TPU v7x, 256 devices: a whole 4x4x8 slice. The times are simulated.
256 devices in a mesh: rep: 4 (over x_lo, core), shard: 32 (over z, y), tp: 2 (over x_hi).
Axes of the slice: x: 4 (x_hi: 2, x_lo: 2; x = x_hi * 2 + x_lo), y: 4, z: 8, core: 2. Of those that a mesh axis runs over, the one named last changes fastest.
Arguments:
- expert_change: float32 [4, 4, 768, 3072], P('rep', None, 'shard', 'tp'), may hold values from -6 to 6
- table_change: float32 [4, 768, 16384], P('rep', 'shard', 'tp'), may hold values from -6 to 6
- expert_master: float32 [4, 3072, 768], P(None, 'shard'), may hold values from -6 to 6
- expert_moment: float32 [4, 3072, 768], P(None, 'shard'), may hold values from -6 to 6
- table_master: float32 [16384, 768], P('shard'), may hold values from -6 to 6
- table_moment: float32 [16384, 768], P('shard'), may hold values from -6 to 6
Outputs:
- expert_weights: float32 [4, 3072, 768], P(None, 'shard')
- expert_velocity: float32 [4, 3072, 768], P(None, 'shard')
- expert_copies: bfloat16 [4, 768, 3072], P(None, 'shard', 'tp')
- table_weights: float32 [16384, 768], P('shard')
- table_velocity: float32 [16384, 768], P('shard')
- table_copies: bfloat16 [768, 16384], P('shard', 'tp')
All inputs are finite; a program needn't handle non-finite values.
Results may differ from a plain program's by a relative error of at most 0.001.
Values may be sent and summed in bfloat16 or wider, within the bound.
A program may use at most 128 MiB of HBM per device.

v0:
```python
import jax
import jax.numpy as jnp
from jax import lax
from jax.sharding import PartitionSpec as P

momentum_coef = 0.9
outer_rate = 0.7


def update(master, moment, mean):
    velocity = momentum_coef * moment + mean
    weights = master - outer_rate * (mean + momentum_coef * velocity)
    return weights, velocity


def local(expert_change, table_change, expert_master, expert_moment, table_master, table_moment):
    groups = lax.axis_size("rep")
    tensor = lax.axis_size("tp")
    shards = lax.axis_size("shard")
    t = lax.axis_index("tp")
    mats, width, half = expert_change.shape[1:]
    rows = expert_master.shape[1]
    vrows = table_master.shape[0]
    per_half = shards // tensor

    summed = lax.psum((expert_change[0], table_change[0]), "rep")
    ge = lax.all_gather(summed[0], "tp", axis=0)
    gt = lax.all_gather(summed[1], "tp", axis=0)

    se = ge.reshape(tensor, mats, width, per_half, rows)
    se = jnp.transpose(se, (0, 3, 1, 2, 4)).reshape(shards, mats, width, rows)
    st = gt.reshape(tensor, width, per_half, vrows)
    st = jnp.transpose(st, (0, 2, 1, 3)).reshape(shards, width, vrows)

    re = lax.all_to_all(se, "shard", 0, 0, tiled=True)
    rt = lax.all_to_all(st, "shard", 0, 0, tiled=True)

    expert_sum = jnp.transpose(re, (1, 3, 0, 2)).reshape(mats, rows, shards * width)
    table_sum = jnp.transpose(rt.reshape(shards * width, vrows))
    expert_weights, expert_velocity = update(expert_master, expert_moment, expert_sum / groups)
    table_weights, table_velocity = update(table_master, table_moment, table_sum / groups)

    le = expert_weights.astype(jnp.bfloat16).reshape(mats, rows, shards, width)
    le = jnp.transpose(le, (2, 0, 3, 1))
    lt = table_weights.astype(jnp.bfloat16).reshape(vrows, shards, width)
    lt = jnp.transpose(lt, (1, 2, 0))
    be = lax.all_to_all(le, "shard", 0, 0, tiled=True)
    bt = lax.all_to_all(lt, "shard", 0, 0, tiled=True)
    be = lax.dynamic_slice_in_dim(be, t * per_half, per_half, 0)
    bt = lax.dynamic_slice_in_dim(bt, t * per_half, per_half, 0)
    expert_copies = jnp.transpose(be, (1, 2, 0, 3)).reshape(mats, width, per_half * rows)
    table_copies = jnp.transpose(bt, (1, 0, 2)).reshape(width, per_half * vrows)
    return (
        expert_weights,
        expert_velocity,
        expert_copies,
        table_weights,
        table_velocity,
        table_copies,
    )


def solution(mesh):
    in_specs = (
        P("rep", None, "shard", "tp"),
        P("rep", "shard", "tp"),
        P(None, "shard", None),
        P(None, "shard", None),
        P("shard", None),
        P("shard", None),
    )
    out_specs = (
        P(None, "shard", None),
        P(None, "shard", None),
        P(None, "shard", "tp"),
        P("shard", None),
        P("shard", None),
        P("shard", "tp"),
    )
    return jax.shard_map(local, mesh=mesh, in_specs=in_specs, out_specs=out_specs, check_vma=False)
```

profile of v0, /device:TPU:1, one launch (start us, length us, event | category | flops | bytes accessed | tf_op | source)
XLA Modules:
  0.0 257.7 jit_solution(11754197058248116986)
XLA Ops:
  7.2 0.0 all-reduce.3.cloned.1.call-start
  7.2 0.7 all-reduce.3.cloned.1.call-update
  7.9 0.0 all-gather.3.cloned.1.call-start
  7.9 57.9 %all-reduce.3.cloned.1.call-done = (f32[1,4,24,1536]{3,2,1,0:T(8,128)}, f32[1,24,8192]{2,1,0:T(8,128)}) async-done(((f32[1,4,24,1536]{3,2,1,0:T(8,128)}, f32[1,24,8192]{2,1,0:T(8,128)}), (f32[1,4,24,1536]{3,2,1,0:T(8,128)}, f32[1,24,8192]{2,1,0:T(8,128)})) %all-reduce.3.cloned.1.call-update) | async-done | bytes 1376272 | tf_op jit(solution)/shard_map/psum | solution.py:26
  65.9 0.0 all-gather.3.cloned.1.call-update
  65.9 32.0 %all-gather.3.cloned.1.call-done = f32[2,4,24,1536]{3,2,1,0:T(8,128)} async-done(((f32[1,4,24,1536]{3,2,1,0:T(8,128)}), f32[2,4,24,1536]{3,2,1,0:T(8,128)}) %all-gather.3.cloned.1.call-update) | async-done | bytes 1179664 | tf_op jit(solution)/shard_map/all_gather | solution.py:27
  97.9 1.8 reshape.42
  99.7 1.6 copy.38
  101.3 9.6 %all-to-all-start = ((f32[32,4,24,96]{3,2,1,0:T(8,128)}), f32[32,4,24,96]{3,2,1,0:T(8,128)S(1)}, u32[]{:S(2)}, u32[]{:S(2)}) async-start(f32[32,4,24,96]{3,2,1,0:T(8,128)} %bitcast.1), calls=%async_computation | async-start | bytes 3145728 | tf_op jit(solution)/shard_map/all_to_all | solution.py:35
  110.9 0.0 all-gather.5.cloned.1.call-start
  111.0 0.7 all-gather.5.cloned.1.call-update
  111.6 35.5 %all-gather.5.cloned.1.call-done = f32[2,24,8192]{2,1,0:T(8,128)} async-done(((f32[1,24,8192]{2,1,0:T(8,128)}), f32[2,24,8192]{2,1,0:T(8,128)}) %all-gather.5.cloned.1.call-update) | async-done | bytes 1572880 | tf_op jit(solution)/shard_map/all_gather | solution.py:28
  147.2 2.7 %copy.55 = f32[2,3,16,8,512]{4,3,1,2,0:T(8,128)} copy(f32[2,3,16,8,512]{4,3,2,1,0:T(8,128)} %bitcast.53) | data formatting | bytes 3145728 | tf_op jit(solution)/shard_map/reshape | solution.py:32
  149.8 0.0 all-to-all-done
  149.9 9.6 %all-to-all-start.2 = ((f32[32,24,512]{2,1,0:T(8,128)}), f32[32,24,512]{2,1,0:T(8,128)S(1)}, u32[]{:S(2)}, u32[]{:S(2)}) async-start(f32[32,24,512]{2,1,0:T(8,128)} %bitcast.49), calls=%async_computation.2 | async-start | bytes 3145728 | tf_op jit(solution)/shard_map/all_to_all | solution.py:36
  159.4 2.9 %copy.41 = f32[4,96,768]{1,2,0:T(8,128)} copy(f32[4,96,768]{2,1,0:T(8,128)} %param.8) | data formatting | bytes 2359296 | tf_op args[2]
  162.3 2.9 %copy.40 = f32[4,96,768]{1,2,0:T(8,128)} copy(f32[4,96,768]{2,1,0:T(8,128)} %param.9) | data formatting | bytes 2359296 | tf_op args[3]
  165.2 0.1 multiply_bitcast_fusion
  165.3 0.0 copy-start.2
  165.3 0.0 copy-start.3
  165.4 0.1 copy.39
  165.5 1.3 copy-done.2
  166.7 0.5 copy-done.3
  167.2 2.1 fusion.6
  169.3 1.0 copy.42
  170.3 27.0 %all-to-all-done.2 = f32[32,24,512]{2,1,0:T(8,128)S(1)} async-done(((f32[32,24,512]{2,1,0:T(8,128)}), f32[32,24,512]{2,1,0:T(8,128)S(1)}, u32[]{:S(2)}, u32[]{:S(2)}) %all-to-all-start.2) | async-done | bytes 1572896 | tf_op jit(solution)/shard_map/all_to_all | solution.py:36
  197.3 5.9 %all-to-all-start.1 = ((bf16[32,4,24,96]{3,2,1,0:T(8,128)(2,1)}), bf16[32,4,24,96]{3,2,1,0:T(8,128)(2,1)}, u32[]{:S(2)}, u32[]{:S(2)}) async-start(bf16[32,4,24,96]{3,2,1,0:T(8,128)(2,1)} %copy.42), calls=%async_computation.1 | async-start | bytes 1572864 | tf_op jit(solution)/shard_map/all_to_all | solution.py:47
  203.2 0.0 copy-done.4
  203.2 1.6 copy.46
  204.9 3.0 %copy.45 = f32[512,768]{0,1:T(8,128)} copy(f32[512,768]{1,0:T(8,128)} %param.11) | data formatting | bytes 3145728 | tf_op args[5]
  207.9 0.0 copy-start
  207.9 0.0 copy-start.1
  207.9 0.2 broadcast_multiply_fusion
  208.0 1.2 copy-done
  209.3 0.5 copy-done.1
  209.8 1.5 fusion.4
  211.3 11.7 %all-to-all-done.1 = bf16[32,4,24,96]{3,2,1,0:T(8,128)(2,1)} async-done(((bf16[32,4,24,96]{3,2,1,0:T(8,128)(2,1)}), bf16[32,4,24,96]{3,2,1,0:T(8,128)(2,1)}, u32[]{:S(2)}, u32[]{:S(2)}) %all-to-all-start.1) | async-done | bytes 589856 | tf_op jit(solution)/shard_map/all_to_all | solution.py:47
  223.0 6.7 %all-to-all-start.3 = ((bf16[32,24,512]{2,1,0:T(8,128)(2,1)}), bf16[32,24,512]{2,1,0:T(8,128)(2,1)}, u32[]{:S(2)}, u32[]{:S(2)}) async-start(bf16[32,24,512]{2,1,0:T(8,128)(2,1)} %bitcast.51), calls=%async_computation.3 | async-start | bytes 1572864 | tf_op jit(solution)/shard_map/all_to_all | solution.py:48
  229.7 2.9 %copy.48 = f32[4,96,768]{2,1,0:T(8,128)} copy(f32[4,96,768]{1,2,0:T(8,128)} %get-tuple-element.29) | data formatting | bytes 2359296
  232.6 2.9 %copy.49 = f32[4,96,768]{2,1,0:T(8,128)} copy(f32[4,96,768]{1,2,0:T(8,128)} %get-tuple-element.31) | data formatting | bytes 2359296
  235.5 1.0 dynamic-slice_bitcast_fusion.1
  236.5 0.2 copy.43
  236.7 1.1 reshape.45
  237.8 1.6 copy.50
  239.4 1.6 copy.51
  241.0 8.4 %all-to-all-done.3 = bf16[32,24,512]{2,1,0:T(8,128)(2,1)} async-done(((bf16[32,24,512]{2,1,0:T(8,128)(2,1)}), bf16[32,24,512]{2,1,0:T(8,128)(2,1)}, u32[]{:S(2)}, u32[]{:S(2)}) %all-to-all-start.3) | async-done | bytes 786464 | tf_op jit(solution)/shard_map/all_to_all | solution.py:48
  249.4 1.0 dynamic-slice_bitcast_fusion
  250.4 0.8 copy.53
  (1 shorter events, 0.0 us)
Async XLA Ops:
  7.2 58.7 %all-reduce.3.cloned.1.call-start = ((), (), s32[]{:S(2)}) async-start(), calls=%async_computation.6 | async-start | bytes 2752512 | tf_op jit(solution)/shard_map/psum | solution.py:26
  7.9 90.0 %all-gather.3.cloned.1.call-start = ((), (), s32[]{:S(2)}) async-start(), calls=%async_computation.4 | async-start | bytes 1769472 | tf_op jit(solution)/shard_map/all_gather | solution.py:27
  101.3 48.5 %all-to-all-start = ((f32[32,4,24,96]{3,2,1,0:T(8,128)}), f32[32,4,24,96]{3,2,1,0:T(8,128)S(1)}, u32[]{:S(2)}, u32[]{:S(2)}) async-start(f32[32,4,24,96]{3,2,1,0:T(8,128)} %bitcast.1), calls=%async_computation | async-start | bytes 3145728 | tf_op jit(solution)/shard_map/all_to_all | solution.py:35
  110.9 36.3 %all-gather.5.cloned.1.call-start = ((), (), s32[]{:S(2)}) async-start(), calls=%async_computation.5 | async-start | bytes 2359296 | tf_op jit(solution)/shard_map/all_gather | solution.py:28
  149.9 47.4 %all-to-all-start.2 = ((f32[32,24,512]{2,1,0:T(8,128)}), f32[32,24,512]{2,1,0:T(8,128)S(1)}, u32[]{:S(2)}, u32[]{:S(2)}) async-start(f32[32,24,512]{2,1,0:T(8,128)} %bitcast.49), calls=%async_computation.2 | async-start | bytes 3145728 | tf_op jit(solution)/shard_map/all_to_all | solution.py:36
  165.3 1.4 copy-start.2
  165.3 1.9 copy-start.3
  169.3 33.9 %copy-start.4 = (f32[512,768]{1,0:T(8,128)S(1)}, f32[512,768]{1,0:T(8,128)}, u32[]{:S(2)}) copy-start(f32[512,768]{1,0:T(8,128)} %param.10) | copy-start | bytes 4718596
  197.3 25.7 %all-to-all-start.1 = ((bf16[32,4,24,96]{3,2,1,0:T(8,128)(2,1)}), bf16[32,4,24,96]{3,2,1,0:T(8,128)(2,1)}, u32[]{:S(2)}, u32[]{:S(2)}) async-start(bf16[32,4,24,96]{3,2,1,0:T(8,128)(2,1)} %copy.42), calls=%async_computation.1 | async-start | bytes 1572864 | tf_op jit(solution)/shard_map/all_to_all | solution.py:47
  207.9 1.4 copy-start
  207.9 1.9 copy-start.1
  223.0 26.4 %all-to-all-start.3 = ((bf16[32,24,512]{2,1,0:T(8,128)(2,1)}), bf16[32,24,512]{2,1,0:T(8,128)(2,1)}, u32[]{:S(2)}, u32[]{:S(2)}) async-start(bf16[32,24,512]{2,1,0:T(8,128)(2,1)} %bitcast.51), calls=%async_computation.3 | async-start | bytes 1572864 | tf_op jit(solution)/shard_map/all_to_all | solution.py:48
Sparse Core Ops, SparseCore 0:
  10.7 55.1 all-reduce.2
  67.8 30.0 all-gather.2
  113.7 33.4 all-gather.4
where the time goes:
time: 261 us; the launch traced here: 258 us
  waiting for transfers between devices  174 us (67%)
  local copies, waits for them, and re-layouts  34.1 us (13%)
  starting transfers between devices  31.9 us (12%)
  between operations  13.9 us (5%)
  other arithmetic  3.92 us (2%)
    psum x1, waiting for transfers between devices, local(): summed = lax.psum((expert_change[0], table_change[0]), 'rep')  57.9 us
    all_gather x1, waiting for transfers between devices, local(): gt = lax.all_gather(summed[1], 'tp', axis=0)  35.5 us
    all_gather x1, waiting for transfers between devices, local(): ge = lax.all_gather(summed[0], 'tp', axis=0)  32 us
    all_to_all x1, waiting for transfers between devices, local(): rt = lax.all_to_all(st, 'shard', 0, 0, tiled=True)  27 us
    unnamed x19, local copies, waits for them, and re-layouts  23.9 us
    all_to_all x1, waiting for transfers between devices, local(): be = lax.all_to_all(le, 'shard', 0, 0, tiled=True)  11.7 us
    all_to_all x1, starting transfers between devices, local(): rt = lax.all_to_all(st, 'shard', 0, 0, tiled=True)  9.57 us
    all_to_all x1, starting transfers between devices, local(): re = lax.all_to_all(se, 'shard', 0, 0, tiled=True)  9.57 us
  transfers between devices with their start and end apart: 7, of which 6 were waited for; matrix products, arithmetic and copies ran while one was open for 11% of the time, Pallas kernels for 0%

commit v1 on v0

--- a/solution.py
+++ b/solution.py
@@ -23,9 +23,19 @@
     vrows = table_master.shape[0]
     per_half = shards // tensor
 
-    summed = lax.psum((expert_change[0], table_change[0]), "rep")
-    ge = lax.all_gather(summed[0], "tp", axis=0)
-    gt = lax.all_gather(summed[1], "tp", axis=0)
+    ex = expert_change[0]
+    tx = table_change[0]
+    flat = jnp.concatenate([ex.reshape(-1), tx.reshape(-1)])
+    quarters = lax.all_to_all(flat.reshape(groups, -1), "rep", 0, 0, tiled=True)
+    part = jnp.sum(quarters, axis=0)
+    whole = lax.all_to_all(
+        jnp.broadcast_to(part[None], (groups, part.size)), "rep", 0, 0, tiled=True
+    ).reshape(-1)
+    both = lax.all_to_all(
+        jnp.broadcast_to(whole[None], (tensor, whole.size)), "tp", 0, 0, tiled=True
+    )
+    ge = both[:, : ex.size].reshape((tensor,) + ex.shape)
+    gt = both[:, ex.size :].reshape((tensor,) + tx.shape)
 
     se = ge.reshape(tensor, mats, width, per_half, rows)
     se = jnp.transpose(se, (0, 3, 1, 2, 4)).reshape(shards, mats, width, rows)

time: 261 us -> 249 us (0.954)
  waiting for transfers between devices: 174 us -> 76.2 us
  blocking collectives: 0 us -> 78.6 us
  local copies, waits for them, and re-layouts: 34.1 us -> 49.8 us
  between operations: 13.9 us -> 0.81 us
  other arithmetic: 3.92 us -> 6.66 us
    all_to_all x0 -> x3, blocking collectives: none -> 78.6 us  [the longest x1 35.3 us: local(): lax.all_to_all(jnp.broadcast_to(whole[None], (tensor, whole.size)), 'tp',...]
    all_gather x2 -> x0, waiting for transfers between devices: 67.6 us -> none  [the longest x1 35.5 us: local(): gt = lax.all_gather(summed[1], 'tp', axis=0)]
    psum x1 -> x0, waiting for transfers between devices: 57.9 us -> none  [local(): summed = lax.psum((expert_change[0], table_change[0]), 'rep')]
    all_to_all x1, waiting for transfers between devices: 0.01 us -> 33.2 us  [local(): re = lax.all_to_all(se, 'shard', 0, 0, tiled=True)]
    broadcast_in_dim x0 -> x2, local copies, waits for them, and re-layouts: none -> 7.15 us  [the longest x1 6.44 us: local(): jnp.broadcast_to(whole[None], (tensor, whole.size))]
    another operation x0 -> x2, local copies, waits for them, and re-layouts: none -> 4.69 us  [the longest x1 3.51 us: local(): se = ge.reshape(tensor, mats, width, per_half, rows)]
    reshape x2 -> x0, local copies, waits for them, and re-layouts: 4.44 us -> none  [the longest x1 2.66 us: local(): st = gt.reshape(tensor, width, per_half, vrows)]
    unnamed x19 -> x22, local copies, waits for them, and re-layouts: 23.9 us -> 27.5 us
  transfers between devices with their start and end apart: 7 -> 4, of which waited for: 6 -> 4; matrix products, arithmetic and copies ran while one was open for 11% -> 12% of each run, Pallas kernels for 0% -> 0%
where the time goes in v1:
time: 249 us; the launch traced here: 244 us
  blocking collectives  78.6 us (32%)
  waiting for transfers between devices  76.2 us (31%)
  local copies, waits for them, and re-layouts  49.8 us (20%)
  starting transfers between devices  32 us (13%)
  other arithmetic  6.66 us (3%)
    all_to_all x1, blocking collectives, local(): lax.all_to_all(jnp.broadcast_to(whole[None], (tensor, whole.size)), 'tp',...  35.3 us
    all_to_all x1, waiting for transfers between devices, local(): re = lax.all_to_all(se, 'shard', 0, 0, tiled=True)  33.2 us
    unnamed x22, local copies, waits for them, and re-layouts  27.5 us
    all_to_all x1, waiting for transfers between devices, local(): rt = lax.all_to_all(st, 'shard', 0, 0, tiled=True)  24.6 us
    all_to_all x1, blocking collectives, local(): quarters = lax.all_to_all(flat.reshape(groups, -1), 'rep', 0, 0, tiled=True)  22.9 us
    all_to_all x1, blocking collectives, local(): lax.all_to_all(jnp.broadcast_to(part[None], (groups, part.size)), 'rep',...  20.4 us
    all_to_all x1, waiting for transfers between devices, local(): be = lax.all_to_all(le, 'shard', 0, 0, tiled=True)  11.3 us
    all_to_all x1, starting transfers between devices, local(): re = lax.all_to_all(se, 'shard', 0, 0, tiled=True)  10.5 us
  transfers between devices with their start and end apart: 4, of which 4 were waited for; matrix products, arithmetic and copies ran while one was open for 12% of the time, Pallas kernels for 0%

profile of v1, /device:TPU:1, one launch (start us, length us, event | category | flops | bytes accessed | tf_op | source)
XLA Modules:
  0.0 244.0 jit_solution(6817830290871463134)
XLA Ops:
  0.6 1.2 reshape_squeeze.6
  1.8 0.1 copy-done.4
  1.9 0.1 copy.81
  2.1 0.1 pad_maximum_fusion
  2.2 22.9 %all_to_all.44 = f32[4,1,86016]{2,1,0:T(1,128)S(1)} all-to-all(f32[4,1,86016]{2,1,0:T(1,128)S(1)} %bitcast.61), channel_id=1, replica_groups=mesh['rep'=4,'shard'=32,'tp'=2] {'rep'}, dimensions={0} | all-to-all | bytes 2752512 | tf_op jit(solution)/shard_map/all_to_all | solution.py:29
  25.1 1.3 reduce_sum.9
  26.3 0.7 broadcast_in_dim.6
  27.1 20.4 %all_to_all.45 = f32[4,1,86016]{2,1,0:T(1,128)S(1)} all-to-all(f32[4,1,86016]{2,1,0:T(1,128)S(1)} %broadcast_in_dim.6), channel_id=1, replica_groups=mesh['rep'=4,'shard'=32,'tp'=2] {'rep'}, dimensions={0} | all-to-all | bytes 2752512 | tf_op jit(solution)/shard_map/all_to_all | solution.py:31
  47.4 6.4 %broadcast_in_dim.15 = f32[2,1,344064]{2,1,0:T(1,128)S(1)} broadcast(f32[344064]{0:T(1024)S(1)} %bitcast.62), dimensions={2} | broadcast | bytes 4128768 | tf_op jit(solution)/shard_map/broadcast_in_dim | solution.py:35
  53.9 35.3 %all_to_all.46 = f32[2,1,344064]{2,1,0:T(1,128)S(1)} all-to-all(f32[2,1,344064]{2,1,0:T(1,128)S(1)} %broadcast_in_dim.15), channel_id=1, replica_groups=mesh['rep'=4,'shard'=32,'tp'=2] {'tp'}, dimensions={0} | all-to-all | bytes 5505024 | tf_op jit(solution)/shard_map/all_to_all | solution.py:34
  89.2 4.6 %copy.84 = f32[2,1,344064]{2,0,1:T(2,128)S(1)} copy(f32[2,1,344064]{2,1,0:T(1,128)S(1)} %all_to_all.46) | data formatting | bytes 5505024
  93.8 1.1 slice.8
  94.8 3.5 %reshape_reshape.6 = f32[2,4,24,16,96]{4,3,2,1,0:T(8,128)} reshape(f32[2,147456]{1,0:T(2,128)} %slice.8) | data formatting | bytes 2359296 | tf_op jit(solution)/shard_map/reshape;reshape | solution.py:40
  98.4 3.0 %copy.64 = f32[2,16,4,24,96]{4,3,2,1,0:T(8,128)} copy(f32[2,16,4,24,96]{4,1,3,2,0:T(8,128)} %bitcast.60) | data formatting | bytes 2359296 | tf_op jit(solution)/shard_map/transpose | solution.py:41
  101.4 10.5 %all-to-all-start.3 = ((f32[32,4,24,96]{3,2,1,0:T(8,128)}), f32[32,4,24,96]{3,2,1,0:T(8,128)}, u32[]{:S(2)}, u32[]{:S(2)}) async-start(f32[32,4,24,96]{3,2,1,0:T(8,128)} %bitcast.57), calls=%async_computation.3 | async-start | bytes 3145728 | tf_op jit(solution)/shard_map/all_to_all | solution.py:45
  111.8 0.2 slice.9
  112.0 0.3 copy.82
  112.3 2.1 copy.70
  114.4 33.2 %all-to-all-done.3 = f32[32,4,24,96]{3,2,1,0:T(8,128)} async-done(((f32[32,4,24,96]{3,2,1,0:T(8,128)}), f32[32,4,24,96]{3,2,1,0:T(8,128)}, u32[]{:S(2)}, u32[]{:S(2)}) %all-to-all-start.3) | async-done | bytes 1179680 | tf_op jit(solution)/shard_map/all_to_all | solution.py:45
  147.6 7.2 %all-to-all-start.5 = ((f32[32,24,512]{2,1,0:T(8,128)}), f32[32,24,512]{2,1,0:T(8,128)S(1)}, u32[]{:S(2)}, u32[]{:S(2)}) async-start(f32[32,24,512]{2,1,0:T(8,128)} %bitcast.10), calls=%async_computation.5 | async-start | bytes 3145728 | tf_op jit(solution)/shard_map/all_to_all | solution.py:46
  154.8 1.7 copy.67
  156.6 2.9 %copy.66 = f32[4,96,768]{1,2,0:T(8,128)} copy(f32[4,96,768]{2,1,0:T(8,128)} %param.9) | data formatting | bytes 2359296 | tf_op args[3]
  159.4 1.5 multiply_bitcast_fusion
  161.0 0.0 copy-start.2
  161.0 0.1 copy.65
  161.1 1.3 copy-done.2
  162.4 2.1 fusion.6
  164.5 1.0 copy.68
  165.5 24.6 %all-to-all-done.5 = f32[32,24,512]{2,1,0:T(8,128)S(1)} async-done(((f32[32,24,512]{2,1,0:T(8,128)}), f32[32,24,512]{2,1,0:T(8,128)S(1)}, u32[]{:S(2)}, u32[]{:S(2)}) %all-to-all-start.5) | async-done | bytes 1572896 | tf_op jit(solution)/shard_map/all_to_all | solution.py:46
  190.1 7.8 %all-to-all-start.4 = ((bf16[32,4,24,96]{3,2,1,0:T(8,128)(2,1)}), bf16[32,4,24,96]{3,2,1,0:T(8,128)(2,1)}, u32[]{:S(2)}, u32[]{:S(2)}) async-start(bf16[32,4,24,96]{3,2,1,0:T(8,128)(2,1)} %copy.68), calls=%async_computation.4 | async-start | bytes 1572864 | tf_op jit(solution)/shard_map/all_to_all | solution.py:57
  197.9 1.6 copy.72
  199.5 3.0 %copy.71 = f32[512,768]{0,1:T(8,128)} copy(f32[512,768]{1,0:T(8,128)} %param.11) | data formatting | bytes 3145728 | tf_op args[5]
  202.5 0.2 broadcast_multiply_fusion
  202.7 1.2 copy-done
  203.9 0.5 copy-done.1
  204.4 1.5 fusion.4
  205.9 11.3 %all-to-all-done.4 = bf16[32,4,24,96]{3,2,1,0:T(8,128)(2,1)} async-done(((bf16[32,4,24,96]{3,2,1,0:T(8,128)(2,1)}), bf16[32,4,24,96]{3,2,1,0:T(8,128)(2,1)}, u32[]{:S(2)}, u32[]{:S(2)}) %all-to-all-start.4) | async-done | bytes 589856 | tf_op jit(solution)/shard_map/all_to_all | solution.py:57
  217.2 6.5 %all-to-all-start.6 = ((bf16[32,24,512]{2,1,0:T(8,128)(2,1)}), bf16[32,24,512]{2,1,0:T(8,128)(2,1)}, u32[]{:S(2)}, u32[]{:S(2)}) async-start(bf16[32,24,512]{2,1,0:T(8,128)(2,1)} %bitcast.63), calls=%async_computation.6 | async-start | bytes 1572864 | tf_op jit(solution)/shard_map/all_to_all | solution.py:58
  223.7 2.9 %copy.74 = f32[4,96,768]{2,1,0:T(8,128)} copy(f32[4,96,768]{1,2,0:T(8,128)} %get-tuple-element.39) | data formatting | bytes 2359296
  226.6 2.9 %copy.75 = f32[4,96,768]{2,1,0:T(8,128)} copy(f32[4,96,768]{1,2,0:T(8,128)} %get-tuple-element.41) | data formatting | bytes 2359296
  229.5 1.6 copy.76
  231.1 1.6 copy.77
  232.7 1.0 dynamic-slice_bitcast_fusion.1
  233.8 0.2 copy.69
  233.9 1.1 reshape.57
  235.1 7.2 %all-to-all-done.6 = bf16[32,24,512]{2,1,0:T(8,128)(2,1)} async-done(((bf16[32,24,512]{2,1,0:T(8,128)(2,1)}), bf16[32,24,512]{2,1,0:T(8,128)(2,1)}, u32[]{:S(2)}, u32[]{:S(2)}) %all-to-all-start.6) | async-done | bytes 786464 | tf_op jit(solution)/shard_map/all_to_all | solution.py:58
  242.2 1.0 dynamic-slice_bitcast_fusion
  243.3 0.8 copy.80
  (5 shorter events, 0.0 us)
Async XLA Ops:
  0.6 1.3 copy-start.4
  101.4 46.2 %all-to-all-start.3 = ((f32[32,4,24,96]{3,2,1,0:T(8,128)}), f32[32,4,24,96]{3,2,1,0:T(8,128)}, u32[]{:S(2)}, u32[]{:S(2)}) async-start(f32[32,4,24,96]{3,2,1,0:T(8,128)} %bitcast.57), calls=%async_computation.3 | async-start | bytes 3145728 | tf_op jit(solution)/shard_map/all_to_all | solution.py:45
  147.6 42.5 %all-to-all-start.5 = ((f32[32,24,512]{2,1,0:T(8,128)}), f32[32,24,512]{2,1,0:T(8,128)S(1)}, u32[]{:S(2)}, u32[]{:S(2)}) async-start(f32[32,24,512]{2,1,0:T(8,128)} %bitcast.10), calls=%async_computation.5 | async-start | bytes 3145728 | tf_op jit(solution)/shard_map/all_to_all | solution.py:46
  161.0 1.4 copy-start.2
  164.5 33.4 %copy-start.3 = (f32[512,768]{1,0:T(8,128)S(1)}, f32[512,768]{1,0:T(8,128)}, u32[]{:S(2)}) copy-start(f32[512,768]{1,0:T(8,128)} %param.10) | copy-start | bytes 4718596
  190.1 27.1 %all-to-all-start.4 = ((bf16[32,4,24,96]{3,2,1,0:T(8,128)(2,1)}), bf16[32,4,24,96]{3,2,1,0:T(8,128)(2,1)}, u32[]{:S(2)}, u32[]{:S(2)}) async-start(bf16[32,4,24,96]{3,2,1,0:T(8,128)(2,1)} %copy.68), calls=%async_computation.4 | async-start | bytes 1572864 | tf_op jit(solution)/shard_map/all_to_all | solution.py:57
  202.5 1.4 copy-start
  202.5 1.9 copy-start.1
  217.2 25.1 %all-to-all-start.6 = ((bf16[32,24,512]{2,1,0:T(8,128)(2,1)}), bf16[32,24,512]{2,1,0:T(8,128)(2,1)}, u32[]{:S(2)}, u32[]{:S(2)}) async-start(bf16[32,24,512]{2,1,0:T(8,128)(2,1)} %bitcast.63), calls=%async_computation.6 | async-start | bytes 1572864 | tf_op jit(solution)/shard_map/all_to_all | solution.py:58

commit v2 on v0

v2 whole, which is shorter than its diff:
```python
import jax
import jax.numpy as jnp
from jax import lax
from jax.sharding import PartitionSpec as P

momentum_coef = 0.9
outer_rate = 0.7


def update(master, moment, mean):
    velocity = momentum_coef * moment + mean
    weights = master - outer_rate * (mean + momentum_coef * velocity)
    return weights, velocity


def pairs(n, flip):
    return [(i, i ^ flip) for i in range(n)]


def rep_scatter(x):
    r = lax.axis_index("rep")
    n = lax.axis_size("rep")
    core, x_lo = r % 2, r // 2
    x4 = x.reshape(2, 2, -1)
    mine = lax.dynamic_index_in_dim(x4, core, 1, keepdims=False)
    other = lax.dynamic_index_in_dim(x4, 1 - core, 1, keepdims=False)
    a = mine + lax.ppermute(other, "rep", pairs(n, 1))
    keep = lax.dynamic_index_in_dim(a, x_lo, 0, keepdims=False)
    send = lax.dynamic_index_in_dim(a, 1 - x_lo, 0, keepdims=False)
    return keep + lax.ppermute(send, "rep", pairs(n, 2))


def rep_gather(x):
    r = lax.axis_index("rep")
    n = lax.axis_size("rep")
    core, x_lo = r % 2, r // 2
    cross = lax.ppermute(x, "rep", pairs(n, 2))
    pair = jnp.where(x_lo == 0, jnp.stack([x, cross]), jnp.stack([cross, x]))
    sib = lax.ppermute(pair, "rep", pairs(n, 1))
    full = jnp.where(core == 0, jnp.stack([pair, sib], 1), jnp.stack([sib, pair], 1))
    return full.reshape((n,) + x.shape)


def local(expert_change, table_change, expert_master, expert_moment, table_master, table_moment):
    groups = lax.axis_size("rep")
    tensor = lax.axis_size("tp")
    shards = lax.axis_size("shard")
    t = lax.axis_index("tp")
    mats, width, half = expert_change.shape[1:]
    rows = expert_master.shape[1]
    vrows = table_master.shape[0]
    per_half = shards // tensor
    sub = vrows // groups
    esize = width * half

    ex = expert_change[0].reshape(mats, esize)
    tx = table_change[0].reshape(width, per_half, groups, sub)
    tx = jnp.transpose(tx, (2, 0, 1, 3)).reshape(groups, -1)
    q = rep_scatter(jnp.concatenate([ex, tx], axis=1))

    other = lax.ppermute(q, "tp", pairs(tensor, 1))
    halves = jnp.where(t == 0, jnp.stack([q, other]), jnp.stack([other, q]))
    he = halves[:, :esize].reshape(tensor, width, per_half, rows)
    he = jnp.transpose(he, (0, 2, 1, 3)).reshape(shards, width * rows)
    ht = halves[:, esize:].reshape(tensor, width, per_half, sub)
    ht = jnp.transpose(ht, (0, 2, 1, 3)).reshape(shards, width * sub)
    got = lax.all_to_all(jnp.concatenate([he, ht], 1), "shard", 0, 0, tiled=True)

    every = rep_gather(got)
    ee = every[:, :, : width * rows].reshape(groups, shards, width, rows)
    expert_sum = jnp.transpose(ee, (0, 3, 1, 2)).reshape(mats, rows, shards * width)
    et = every[:, :, width * rows :].reshape(groups, shards, width, sub)
    table_sum = jnp.transpose(et, (0, 3, 1, 2)).reshape(vrows, shards * width)

    expert_weights, expert_velocity = update(expert_master, expert_moment, expert_sum / groups)
    table_weights, table_velocity = update(table_master, table_moment, table_sum / groups)

    r = lax.axis_index("rep")
    le = lax.dynamic_index_in_dim(expert_weights, r, 0, keepdims=False)
    le = le.astype(jnp.bfloat16).reshape(rows, shards, width)
    le = jnp.transpose(le, (1, 2, 0)).reshape(shards, width * rows)
    lt = lax.dynamic_slice_in_dim(table_weights, r * sub, sub, 0)
    lt = lt.astype(jnp.bfloat16).reshape(sub, shards, width)
    lt = jnp.transpose(lt, (1, 2, 0)).reshape(shards, width * sub)
    back = lax.all_to_all(jnp.concatenate([le, lt], 1), "shard", 0, 0, tiled=True)
    back = lax.dynamic_slice_in_dim(back, t * per_half, per_half, 0)
    allq = rep_gather(back)
    ce = allq[:, :, : width * rows].reshape(groups, per_half, width, rows)
    expert_copies = jnp.transpose(ce, (0, 2, 1, 3)).reshape(mats, width, per_half * rows)
    ct = allq[:, :, width * rows :].reshape(groups, per_half, width, sub)
    table_copies = jnp.transpose(ct, (2, 1, 0, 3)).reshape(width, per_half * vrows)
    return (
        expert_weights,
        expert_velocity,
        expert_copies,
        table_weights,
        table_velocity,
        table_copies,
    )


def solution(mesh):
    in_specs = (
        P("rep", None, "shard", "tp"),
        P("rep", "shard", "tp"),
        P(None, "shard", None),
        P(None, "shard", None),
        P("shard", None),
        P("shard", None),
    )
    out_specs = (
        P(None, "shard", None),
        P(None, "shard", None),
        P(None, "shard", "tp"),
        P("shard", None),
        P("shard", None),
        P("shard", "tp"),
    )
    return jax.shard_map(local, mesh=mesh, in_specs=in_specs, out_specs=out_specs, check_vma=False)
```

time: 261 us -> 149 us (0.57); the launches traced: 258 us -> 149 us
  waiting for transfers between devices: 174 us -> 46.3 us
  blocking collectives: 0 us -> 27.3 us
  between operations: 13.9 us -> 1.01 us
  starting transfers between devices: 31.9 us -> 20.7 us
  other arithmetic: 3.92 us -> 14.6 us
  local copies, waits for them, and re-layouts: 34.1 us -> 38.8 us
    all_gather x2 -> x0, waiting for transfers between devices: 67.6 us -> none  [the longest x1 35.5 us: local(): gt = lax.all_gather(summed[1], 'tp', axis=0)]
    psum x1 -> x0, waiting for transfers between devices: 57.9 us -> none  [local(): summed = lax.psum((expert_change[0], table_change[0]), 'rep')]
    all_to_all x4 -> x1, waiting for transfers between devices: 47.1 us -> 13.5 us  [local(): lax.all_to_all(jnp.concatenate([le, lt], 1), 'shard', 0, 0, tiled=True)]
    ppermute x0 -> x7, waiting for transfers between devices: none -> 32.8 us  [the longest x2 11.7 us: rep_gather(): cross = lax.ppermute(x, 'rep', pairs(n, 2))]
    all_to_all x0 -> x1, blocking collectives: none -> 27.3 us  [local(): lax.all_to_all(jnp.concatenate([he, ht], 1), 'shard', 0, 0, tiled=True)]
    all_to_all x4 -> x1, starting transfers between devices: 31.8 us -> 6.36 us  [local(): lax.all_to_all(jnp.concatenate([le, lt], 1), 'shard', 0, 0, tiled=True)]
    ppermute x0 -> x7, starting transfers between devices: none -> 14.3 us  [the longest x2 7.18 us: rep_gather(): sib = lax.ppermute(pair, 'rep', pairs(n, 1))]
    add x0 -> x4, other arithmetic: none -> 8.28 us  [the longest x2 7.53 us: update(): velocity = momentum_coef * moment + mean]
  transfers between devices with their start and end apart: 7 -> 8, of which waited for: 6 -> 6; matrix products, arithmetic and copies ran while one was open for 11% -> 12% of each run, Pallas kernels for 0% -> 0%
where the time goes in v2:
time: 149 us
  waiting for transfers between devices  46.3 us (31%)
  local copies, waits for them, and re-layouts  38.8 us (26%)
  blocking collectives  27.3 us (18%)
  starting transfers between devices  20.7 us (14%)
  other arithmetic  14.6 us (10%)
    all_to_all x1, blocking collectives, local(): lax.all_to_all(jnp.concatenate([he, ht], 1), 'shard', 0, 0, tiled=True)  27.3 us
    unnamed x26, local copies, waits for them, and re-layouts  22.3 us
    all_to_all x1, waiting for transfers between devices, local(): lax.all_to_all(jnp.concatenate([le, lt], 1), 'shard', 0, 0, tiled=True)  13.5 us
    ppermute x2, waiting for transfers between devices, rep_gather(): cross = lax.ppermute(x, 'rep', pairs(n, 2))  11.7 us
    ppermute x1, waiting for transfers between devices, rep_scatter(): return keep + lax.ppermute(send, 'rep', pairs(n, 2))  9.26 us
    ppermute x1, waiting for transfers between devices, local(): other = lax.ppermute(q, 'tp', pairs(tensor, 1))  8.85 us
    add x2, other arithmetic, update(): velocity = momentum_coef * moment + mean  7.53 us
    ppermute x2, starting transfers between devices, rep_gather(): sib = lax.ppermute(pair, 'rep', pairs(n, 1))  7.18 us
  transfers between devices with their start and end apart: 8, of which 6 were waited for; matrix products, arithmetic and copies ran while one was open for 12% of the time, Pallas kernels for 0%

profile of v2, /device:TPU:1, one launch (start us, length us, event | category | flops | bytes accessed | tf_op | source)
XLA Modules:
  0.0 148.7 jit_solution(957479120610114400)
XLA Ops:
  0.7 1.6 %concatenate.42 = f32[2,2,36864]{2,1,0:T(2,128)S(1)} reshape(f32[1,4,24,1536]{3,2,1,0:T(8,128)} %param.6) | data formatting | bytes 1179648 | tf_op jit(solution)/shard_map/concatenate | solution.py:59
  2.4 0.5 reshape_squeeze.4
  3.0 0.5 concatenate.43
  3.6 1.2 constant_dynamic-slice_fusion.4
  4.8 0.5 copy.112
  5.3 3.3 %collective-permute-start = (f32[2,86016]{1,0:T(2,128)S(1)}, f32[2,86016]{1,0:T(2,128)S(1)}, u32[]{:S(2)}, u32[]{:S(2)}) collective-permute-start(f32[2,86016]{1,0:T(2,128)S(1)} %bitcast.137), channel_id=1, source_target_pairs={{0,64},{64,0},{128,192},{192,128},{1,65},{65,1},{129,193},{193,129... | collective-permute-start | bytes 2064392 | tf_op jit(solution)/shard_map/ppermute | solution.py:27
  8.6 1.8 %collective-permute-done = f32[2,86016]{1,0:T(2,128)S(1)} collective-permute-done((f32[2,86016]{1,0:T(2,128)S(1)}, f32[2,86016]{1,0:T(2,128)S(1)}, u32[]{:S(2)}, u32[]{:S(2)}) %collective-permute-start) | collective-permute-done | bytes 688160 | tf_op jit(solution)/shard_map/ppermute | solution.py:27
  10.4 0.7 bitcast_add_fusion.4
  11.1 0.6 constant_dynamic-slice_fusion.1
  11.8 9.3 %collective-permute-done.1 = f32[86016]{0:T(1024)S(1)} collective-permute-done((f32[86016]{0:T(1024)S(1)}, f32[86016]{0:T(1024)S(1)}, u32[]{:S(2)}, u32[]{:S(2)}) %collective-permute-start.1) | collective-permute-done | bytes 344096 | tf_op jit(solution)/shard_map/ppermute | solution.py:30
  21.1 1.1 collective-permute-start.2
  22.2 8.8 %collective-permute-done.2 = f32[86016]{0:T(1024)S(1)} collective-permute-done((f32[86016]{0:T(1024)S(1)}, f32[86016]{0:T(1024)S(1)}, u32[]{:S(2)}, u32[]{:S(2)}) %collective-permute-start.2) | collective-permute-done | bytes 344096 | tf_op jit(solution)/shard_map/ppermute | solution.py:61
  31.1 1.0 maximum_select_fusion.3
  32.3 0.3 reshape.201
  33.0 0.7 copy.70
  33.7 27.3 %all_to_all.21 = f32[32,1,5376]{2,1,0:T(1,128)S(1)} all-to-all(f32[32,1,5376]{2,1,0:T(1,128)S(1)} %copy.70), channel_id=1, replica_groups=mesh['rep'=4,'shard'=32,'tp'=2] {'shard'}, dimensions={0} | all-to-all | bytes 1376256 | tf_op jit(solution)/shard_map/all_to_all | solution.py:67
  61.1 1.3 collective-permute-start.3
  62.4 11.7 %collective-permute-done.3 = f32[32,5376]{1,0:T(8,128)S(1)} collective-permute-done((f32[32,5376]{1,0:T(8,128)S(1)}, f32[32,5376]{1,0:T(8,128)S(1)}, u32[]{:S(2)}, u32[]{:S(2)}) %collective-permute-start.3) | collective-permute-done | bytes 688160 | tf_op jit(solution)/shard_map/ppermute | solution.py:37
  74.1 1.2 maximum_select_fusion.2
  75.2 4.9 %collective-permute-start.4 = (f32[2,32,5376]{2,1,0:T(8,128)}, f32[2,32,5376]{2,1,0:T(8,128)}, u32[]{:S(2)}, u32[]{:S(2)}) collective-permute-start(f32[2,32,5376]{2,1,0:T(8,128)} %maximum_select_fusion.2), channel_id=1, source_target_pairs={{0,64},{64,0},{128,192},{192,128},{1,65},{65,1},{129,193},{193,129... | collective-permute-start | bytes 4128776 | tf_op jit(solution)/shard_map/ppermute | solution.py:39
  80.2 1.7 %copy.72 = f32[4,96,768]{1,2,0:T(8,128)S(1)} copy(f32[4,96,768]{2,1,0:T(8,128)} %param.8) | data formatting | bytes 2359296 | tf_op args[2]
  81.9 2.9 %copy.71 = f32[4,96,768]{1,2,0:T(8,128)} copy(f32[4,96,768]{2,1,0:T(8,128)} %param.9) | data formatting | bytes 2359296 | tf_op args[3]
  84.8 3.0 %copy.75 = f32[512,768]{0,1:T(8,128)} copy(f32[512,768]{1,0:T(8,128)} %param.10) | data formatting | bytes 3145728 | tf_op args[4]
  87.8 3.0 %copy.74 = f32[512,768]{0,1:T(8,128)} copy(f32[512,768]{1,0:T(8,128)} %param.11) | data formatting | bytes 3145728 | tf_op args[5]
  91.0 2.0 %maximum_select_fusion = f32[2,2,32,5376]{3,2,1,0:T(8,128)S(1)} fusion(f32[2,1,32,5376]{3,2,1,0:T(8,128)} %bitcast.10, f32[2,1,32,5376]{3,2,1,0:T(8,128)S(1)} %maximum_select_fusion.1, pred[]{:T(512)S(6)} %eq.15), kind=kLoop, calls=%fused_computation | loop fusion | flops 2064384 | bytes 5505025 | tf_op jit(solution)/shard_map/jit(_where)/select_n | solution.py:40
  93.6 2.2 %copy.73 = f32[4,128,32,24]{1,0,3,2:T(4,128)} copy(f32[4,128,32,24]{1,3,2,0:T(8,128)S(1)} %bitcast_bitcast_fusion) | data formatting | bytes 3145728 | tf_op jit(solution)/shard_map/div | solution.py:76
  95.8 2.2 %div.39 = f32[4,32,24,96]{3,2,1,0:T(8,128)} reshape(f32[4,32,2304]{2,1,0:T(8,128)S(1)} %slice_multiply_fusion.1) | data formatting | bytes 2359296 | tf_op jit(solution)/shard_map/div | solution.py:75
  98.0 3.4 %bitcast_add_fusion.3 = (f32[4,96,768]{1,2,0:T(8,128)}, f32[4,96,768]{1,2,0:T(8,128)S(1)}) fusion(f32[4,32,24,96]{3,2,1,0:T(8,128)} %div.39, f32[4,96,768]{1,2,0:T(8,128)} %copy.71, f32[4,96,768]{1,2,0:T(8,128)S(1)} %copy.72), kind=kLoop, calls=%fused_computation.8 | loop fusion | flops 1769472 | bytes 5898240 | tf_op jit(solution)/shard_map/add | solution.py:11
  101.5 0.8 reshape.205
  102.3 4.1 %bitcast_add_fusion.1 = (f32[512,768]{0,1:T(8,128)}, f32[512,768]{0,1:T(8,128)S(1)}) fusion(f32[512,768]{0,1:T(8,128)} %copy.74, f32[96,8,4,128]{3,2,1,0:T(4,128)} %bitcast.113, f32[512,768]{0,1:T(8,128)} %copy.75), kind=kLoop, calls=%fused_computation.2 | loop fusion | flops 2359296 | bytes 7864320 | tf_op jit(solution)/shard_map/add | solution.py:11
  106.6 0.5 broadcast.52
  107.1 1.6 %reduce = bf16[32,5376]{1,0:T(8,128)(2,1)} reduce(bf16[32,1,5376]{2,0,1:T(8,128)(2,1)S(1)} %maximum_bitcast_fusion.1, bf16[]{:T(256)} %broadcast.52), dimensions={1}, to_apply=%copy.76.reduce_sub_computation | reduce | bytes 688130 | tf_op jit(solution)/shard_map/all_to_all | solution.py:85
  108.6 1.8 %reshape.212 = bf16[32,2,2688]{2,1,0:T(2,128)(2,1)} reshape(bf16[32,5376]{1,0:T(8,128)(2,1)} %reduce) | data formatting | bytes 688128
  110.4 6.4 %all-to-all-start.1 = ((bf16[32,2,2688]{2,1,0:T(2,128)(2,1)}), bf16[32,2,2688]{2,1,0:T(2,128)(2,1)S(1)}, u32[]{:S(2)}, u32[]{:S(2)}) async-start(bf16[32,2,2688]{2,1,0:T(2,128)(2,1)} %reshape.212), calls=%async_computation.1 | async-start | bytes 688128 | tf_op jit(solution)/shard_map/all_to_all | solution.py:85
  116.8 13.5 %all-to-all-done.1 = bf16[32,2,2688]{2,1,0:T(2,128)(2,1)S(1)} async-done(((bf16[32,2,2688]{2,1,0:T(2,128)(2,1)}), bf16[32,2,2688]{2,1,0:T(2,128)(2,1)S(1)}, u32[]{:S(2)}, u32[]{:S(2)}) %all-to-all-start.1) | async-done | bytes 344096 | tf_op jit(solution)/shard_map/all_to_all | solution.py:85
  130.3 1.0 reshape.213
  131.3 1.3 constant_dynamic-slice_fusion
  132.7 1.3 collective-permute-start.5
  134.0 1.5 copy.80
  135.5 1.6 %copy.82 = f32[512,768]{1,0:T(8,128)} copy(f32[512,768]{0,1:T(8,128)S(1)} %get-tuple-element.37) | data formatting | bytes 3145728
  137.1 3.0 %copy.81 = f32[4,96,768]{2,1,0:T(8,128)} copy(f32[4,96,768]{1,2,0:T(8,128)} %get-tuple-element.38) | data formatting | bytes 2359296
  140.1 1.6 %copy.83 = f32[512,768]{1,0:T(8,128)} copy(f32[512,768]{0,1:T(8,128)S(1)} %copy-done) | data formatting | bytes 3145728
  141.8 2.2 %collective-permute-start.6 = (bf16[2,16,5376]{2,1,0:T(8,128)(2,1)S(1)}, bf16[2,16,5376]{2,1,0:T(8,128)(2,1)S(1)}, u32[]{:S(2)}, u32[]{:S(2)}) collective-permute-start(bf16[2,16,5376]{2,1,0:T(8,128)(2,1)S(1)} %maximum_select_fusion.6), channel_id=1, source_target_pairs={{0,64},{64,0},{128,192},{192,128},{1,65},{65,1},{129,193},{193,129... | collective-permute-start | bytes 1032200 | tf_op jit(solution)/shard_map/ppermute | solution.py:39
  144.0 1.2 collective-permute-done.6
  145.5 0.3 copy.79
  145.8 1.0 reshape.211
  146.9 0.6 reshape.208
  147.6 1.1 reshape.209
  (40 shorter events, 2.2 us)
Async XLA Ops:
  0.6 1.7 %copy-start.1 = (f32[1,24,8192]{2,1,0:T(8,128)S(1)}, f32[1,24,8192]{2,1,0:T(8,128)}, u32[]{:S(2)}) copy-start(f32[1,24,8192]{2,1,0:T(8,128)} %param.7) | copy-start | bytes 2359300
  5.3 5.1 %collective-permute-start = (f32[2,86016]{1,0:T(2,128)S(1)}, f32[2,86016]{1,0:T(2,128)S(1)}, u32[]{:S(2)}, u32[]{:S(2)}) collective-permute-start(f32[2,86016]{1,0:T(2,128)S(1)} %bitcast.137), channel_id=1, source_target_pairs={{0,64},{64,0},{128,192},{192,128},{1,65},{65,1},{129,193},{193,129... | collective-permute-start | bytes 2064392 | tf_op jit(solution)/shard_map/ppermute | solution.py:27
  11.7 9.4 %collective-permute-start.1 = (f32[86016]{0:T(1024)S(1)}, f32[86016]{0:T(1024)S(1)}, u32[]{:S(2)}, u32[]{:S(2)}) collective-permute-start(f32[86016]{0:T(1024)S(1)} %bitcast.142), channel_id=1, source_target_pairs={{0,128},{64,192},{128,0},{192,64},{1,129},{65,193},{129,1},{193,65... | collective-permute-start | bytes 1032200 | tf_op jit(solution)/shard_map/ppermute | solution.py:30
  21.1 9.9 %collective-permute-start.2 = (f32[86016]{0:T(1024)S(1)}, f32[86016]{0:T(1024)S(1)}, u32[]{:S(2)}, u32[]{:S(2)}) collective-permute-start(f32[86016]{0:T(1024)S(1)} %add.57), channel_id=1, source_target_pairs={{0,1},{1,0},{2,3},{3,2},{4,5},{5,4},{6,7},{7,6},{8,9},{9,8},{10,11... | collective-permute-start | bytes 1032200 | tf_op jit(solution)/shard_map/ppermute | solution.py:61
  61.1 13.0 %collective-permute-start.3 = (f32[32,5376]{1,0:T(8,128)S(1)}, f32[32,5376]{1,0:T(8,128)S(1)}, u32[]{:S(2)}, u32[]{:S(2)}) collective-permute-start(f32[32,5376]{1,0:T(8,128)S(1)} %bitcast.114), channel_id=1, source_target_pairs={{0,128},{64,192},{128,0},{192,64},{1,129},{65,193},{129,1},{193,65... | collective-permute-start | bytes 2064392 | tf_op jit(solution)/shard_map/ppermute | solution.py:37
  75.2 15.7 %collective-permute-start.4 = (f32[2,32,5376]{2,1,0:T(8,128)}, f32[2,32,5376]{2,1,0:T(8,128)}, u32[]{:S(2)}, u32[]{:S(2)}) collective-permute-start(f32[2,32,5376]{2,1,0:T(8,128)} %maximum_select_fusion.2), channel_id=1, source_target_pairs={{0,64},{64,0},{128,192},{192,128},{1,65},{65,1},{129,193},{193,129... | collective-permute-start | bytes 4128776 | tf_op jit(solution)/shard_map/ppermute | solution.py:39
  102.3 4.2 %copy-start.2 = (bf16[32,2304]{1,0:T(8,128)(2,1)S(1)}, bf16[32,2304]{1,0:T(8,128)(2,1)}, u32[]{:S(2)}) copy-start(bf16[32,2304]{1,0:T(8,128)(2,1)} %reshape.205) | copy-start | bytes 442372
  110.4 19.9 %all-to-all-start.1 = ((bf16[32,2,2688]{2,1,0:T(2,128)(2,1)}), bf16[32,2,2688]{2,1,0:T(2,128)(2,1)S(1)}, u32[]{:S(2)}, u32[]{:S(2)}) async-start(bf16[32,2,2688]{2,1,0:T(2,128)(2,1)} %reshape.212), calls=%async_computation.1 | async-start | bytes 688128 | tf_op jit(solution)/shard_map/all_to_all | solution.py:85
  132.7 9.0 %collective-permute-start.5 = (bf16[16,5376]{1,0:T(8,128)(2,1)S(1)}, bf16[16,5376]{1,0:T(8,128)(2,1)S(1)}, u32[]{:S(2)}, u32[]{:S(2)}) collective-permute-start(bf16[16,5376]{1,0:T(8,128)(2,1)S(1)} %bitcast.129), channel_id=1, source_target_pairs={{0,128},{64,192},{128,0},{192,64},{1,129},{65,193},{129,1},{193,65... | collective-permute-start | bytes 516104 | tf_op jit(solution)/shard_map/ppermute | solution.py:37
  137.1 3.0 %copy-start = (f32[512,768]{0,1:T(8,128)S(1)}, f32[512,768]{0,1:T(8,128)}, u32[]{:S(2)}) copy-start(f32[512,768]{0,1:T(8,128)} %get-tuple-element.36) | copy-start | bytes 4718596
  141.8 3.5 %collective-permute-start.6 = (bf16[2,16,5376]{2,1,0:T(8,128)(2,1)S(1)}, bf16[2,16,5376]{2,1,0:T(8,128)(2,1)S(1)}, u32[]{:S(2)}, u32[]{:S(2)}) collective-permute-start(bf16[2,16,5376]{2,1,0:T(8,128)(2,1)S(1)} %maximum_select_fusion.6), channel_id=1, source_target_pairs={{0,64},{64,0},{128,192},{192,128},{1,65},{65,1},{129,193},{193,129... | collective-permute-start | bytes 1032200 | tf_op jit(solution)/shard_map/ppermute | solution.py:39

commit v3 on v2

--- a/solution.py
+++ b/solution.py
@@ -2,6 +2,8 @@
 import jax.numpy as jnp
 from jax import lax
 from jax.sharding import PartitionSpec as P
+from jax.experimental import pallas as pl
+from jax.experimental.pallas import tpu as pltpu
 
 momentum_coef = 0.9
 outer_rate = 0.7
@@ -35,10 +37,46 @@
     n = lax.axis_size("rep")
     core, x_lo = r % 2, r // 2
     cross = lax.ppermute(x, "rep", pairs(n, 2))
-    pair = jnp.where(x_lo == 0, jnp.stack([x, cross]), jnp.stack([cross, x]))
+    pair = jax.tree.map(
+        lambda a, b: jnp.where(x_lo == 0, jnp.stack([a, b]), jnp.stack([b, a])), x, cross
+    )
     sib = lax.ppermute(pair, "rep", pairs(n, 1))
-    full = jnp.where(core == 0, jnp.stack([pair, sib], 1), jnp.stack([sib, pair], 1))
-    return full.reshape((n,) + x.shape)
+    full = jax.tree.map(
+        lambda a, b: jnp.where(core == 0, jnp.stack([a, b], 1), jnp.stack([b, a], 1)), pair, sib
+    )
+    return jax.tree.map(lambda a, f: f.reshape((n,) + a.shape), x, full)
+
+
+def update_kernel(scale, mean_ref, master_ref, moment_ref, w_ref, v_ref, low_ref):
+    x = mean_ref[0]
+    x = x.reshape(x.shape[0] * x.shape[1], x.shape[2])
+    mean = x.T * scale
+    weights, velocity = update(master_ref[...], moment_ref[...], mean.reshape(master_ref.shape))
+    w_ref[...] = weights
+    v_ref[...] = velocity
+    low_ref[0] = weights.reshape(mean.shape).T.astype(low_ref.dtype)
+
+
+def fused_update(got, master, moment, scale):
+    quarters, srcs, wdt, cols = got.shape
+    lead = master.shape[:-2]
+    blk = (1,) * len(lead) + master.shape[-2:] if lead else (cols,) + master.shape[-1:]
+    if lead:
+        idx = lambda q: (q, 0, 0)
+    else:
+        idx = lambda q: (q, 0)
+    big = pl.BlockSpec(blk, idx)
+    return pl.pallas_call(
+        lambda *refs: update_kernel(scale, *refs),
+        grid=(quarters,),
+        in_specs=[pl.BlockSpec((1, srcs, wdt, cols), lambda q: (q, 0, 0, 0)), big, big],
+        out_specs=[big, big, pl.BlockSpec((1, srcs * wdt, cols), lambda q: (q, 0, 0))],
+        out_shape=[
+            jax.ShapeDtypeStruct(master.shape, master.dtype),
+            jax.ShapeDtypeStruct(master.shape, master.dtype),
+            jax.ShapeDtypeStruct((quarters, srcs * wdt, cols), jnp.bfloat16),
+        ],
+    )(got, master, moment)
 
 
 def local(expert_change, table_change, expert_master, expert_moment, table_master, table_moment):
@@ -66,22 +104,20 @@
     ht = jnp.transpose(ht, (0, 2, 1, 3)).reshape(shards, width * sub)
     got = lax.all_to_all(jnp.concatenate([he, ht], 1), "shard", 0, 0, tiled=True)
 
-    every = rep_gather(got)
-    ee = every[:, :, : width * rows].reshape(groups, shards, width, rows)
-    expert_sum = jnp.transpose(ee, (0, 3, 1, 2)).reshape(mats, rows, shards * width)
-    et = every[:, :, width * rows :].reshape(groups, shards, width, sub)
-    table_sum = jnp.transpose(et, (0, 3, 1, 2)).reshape(vrows, shards * width)
+    ge = got[:, : width * rows].reshape(shards, width, rows)
+    gt = got[:, width * rows :].reshape(shards, width, sub)
+    every_e, every_t = rep_gather((ge, gt))
 
-    expert_weights, expert_velocity = update(expert_master, expert_moment, expert_sum / groups)
-    table_weights, table_velocity = update(table_master, table_moment, table_sum / groups)
+    expert_weights, expert_velocity, low_e = fused_update(
+        every_e, expert_master, expert_moment, 1.0 / groups
+    )
+    table_weights, table_velocity, low_t = fused_update(
+        every_t, table_master, table_moment, 1.0 / groups
+    )
 
     r = lax.axis_index("rep")
-    le = lax.dynamic_index_in_dim(expert_weights, r, 0, keepdims=False)
-    le = le.astype(jnp.bfloat16).reshape(rows, shards, width)
-    le = jnp.transpose(le, (1, 2, 0)).reshape(shards, width * rows)
-    lt = lax.dynamic_slice_in_dim(table_weights, r * sub, sub, 0)
-    lt = lt.astype(jnp.bfloat16).reshape(sub, shards, width)
-    lt = jnp.transpose(lt, (1, 2, 0)).reshape(shards, width * sub)
+    le = lax.dynamic_index_in_dim(low_e, r, 0, keepdims=False).reshape(shards, width * rows)
+    lt = lax.dynamic_index_in_dim(low_t, r, 0, keepdims=False).reshape(shards, width * sub)
     back = lax.all_to_all(jnp.concatenate([le, lt], 1), "shard", 0, 0, tiled=True)
     back = lax.dynamic_slice_in_dim(back, t * per_half, per_half, 0)
     allq = rep_gather(back)

time: 149 us -> 134 us (0.90)
  local copies, waits for them, and re-layouts: 38.8 us -> 15 us
  Pallas kernels: 0 us -> 9.35 us
  starting transfers between devices: 20.7 us -> 29.4 us
  other arithmetic: 14.6 us -> 9.24 us
  waiting for transfers between devices: 46.3 us -> 42.4 us
    unnamed x26 -> x14, local copies, waits for them, and re-layouts: 22.3 us -> 2.02 us
    pallas_call x0 -> x2, Pallas kernels: none -> 9.35 us  [fused_update(): pl.pallas_call(lambda *refs: update_kernel(scale, *refs), grid=(quarters,...]
    ppermute x2 -> x3, starting transfers between devices: 7.18 us -> 15.6 us  [rep_gather(): sib = lax.ppermute(pair, 'rep', pairs(n, 1))]
    add x2 -> x0, other arithmetic: 7.53 us -> none  [update(): velocity = momentum_coef * moment + mean]
    div x3 -> x0, local copies, waits for them, and re-layouts: 4.52 us -> none  [the longest x2 2.29 us: local(): table_sum / groups]
    ppermute x2 -> x3, waiting for transfers between devices: 11.7 us -> 7.75 us  [rep_gather(): cross = lax.ppermute(x, 'rep', pairs(n, 2))]
    select_n x6 -> x9, other arithmetic: 3.4 us -> 6.6 us  [the longest x3 5.42 us: rep_gather(): jnp.where(core == 0, jnp.stack([a, b], 1), jnp.stack([b, a], 1))]
    dynamic_slice x0 -> x2, local copies, waits for them, and re-layouts: none -> 1.88 us  [the longest x1 0.94 us: local(): lax.dynamic_index_in_dim(low_e, r, 0, keepdims=False)]
  transfers between devices with their start and end apart: 8 -> 10, of which waited for: 6 -> 7; matrix products, arithmetic and copies ran while one was open for 12% -> 4% of each run, Pallas kernels for 0% -> 3%
where the time goes in v3:
time: 134 us
  waiting for transfers between devices  42.4 us (32%)
  starting transfers between devices  29.4 us (22%)
  blocking collectives  27.3 us (20%)
  local copies, waits for them, and re-layouts  15 us (11%)
  Pallas kernels  9.35 us (7%)
  other arithmetic  9.24 us (7%)
    all_to_all x1, blocking collectives, local(): lax.all_to_all(jnp.concatenate([he, ht], 1), 'shard', 0, 0, tiled=True)  27.3 us
    ppermute x3, starting transfers between devices, rep_gather(): sib = lax.ppermute(pair, 'rep', pairs(n, 1))  15.6 us
    all_to_all x1, waiting for transfers between devices, local(): lax.all_to_all(jnp.concatenate([le, lt], 1), 'shard', 0, 0, tiled=True)  13.5 us
    pallas_call x2, Pallas kernels, fused_update(): pl.pallas_call(lambda *refs: update_kernel(scale, *refs), grid=(quarters,...  9.35 us
    ppermute x1, waiting for transfers between devices, rep_scatter(): return keep + lax.ppermute(send, 'rep', pairs(n, 2))  9.26 us
    ppermute x1, waiting for transfers between devices, local(): other = lax.ppermute(q, 'tp', pairs(tensor, 1))  8.85 us
    ppermute x3, waiting for transfers between devices, rep_gather(): cross = lax.ppermute(x, 'rep', pairs(n, 2))  7.75 us
    all_to_all x1, starting transfers between devices, local(): lax.all_to_all(jnp.concatenate([le, lt], 1), 'shard', 0, 0, tiled=True)  6.36 us
  transfers between devices with their start and end apart: 10, of which 7 were waited for; matrix products, arithmetic and copies ran while one was open for 4% of the time, Pallas kernels for 3%

profile of v3, /device:TPU:1, one launch (start us, length us, event | category | flops | bytes accessed | tf_op | source)
XLA Modules:
  0.0 133.8 jit_solution(10468967497646051528)
XLA Ops:
  0.7 1.6 %concatenate.56 = f32[2,2,36864]{2,1,0:T(2,128)S(1)} reshape(f32[1,4,24,1536]{3,2,1,0:T(8,128)} %param.6) | data formatting | bytes 1179648 | tf_op jit(solution)/shard_map/concatenate | solution.py:97
  2.4 0.5 reshape_squeeze.4
  3.0 0.5 concatenate.57
  3.6 1.2 constant_dynamic-slice_fusion.6
  4.8 0.5 copy.52
  5.3 3.3 %collective-permute-start = (f32[2,86016]{1,0:T(2,128)S(1)}, f32[2,86016]{1,0:T(2,128)S(1)}, u32[]{:S(2)}, u32[]{:S(2)}) collective-permute-start(f32[2,86016]{1,0:T(2,128)S(1)} %bitcast.102), channel_id=1, source_target_pairs={{0,64},{64,0},{128,192},{192,128},{1,65},{65,1},{129,193},{193,129... | collective-permute-start | bytes 2064392 | tf_op jit(solution)/shard_map/ppermute | solution.py:29
  8.6 1.8 %collective-permute-done = f32[2,86016]{1,0:T(2,128)S(1)} collective-permute-done((f32[2,86016]{1,0:T(2,128)S(1)}, f32[2,86016]{1,0:T(2,128)S(1)}, u32[]{:S(2)}, u32[]{:S(2)}) %collective-permute-start) | collective-permute-done | bytes 688160 | tf_op jit(solution)/shard_map/ppermute | solution.py:29
  10.4 0.7 bitcast_add_fusion
  11.1 0.6 constant_dynamic-slice_fusion.3
  11.8 9.3 %collective-permute-done.1 = f32[86016]{0:T(1024)S(1)} collective-permute-done((f32[86016]{0:T(1024)S(1)}, f32[86016]{0:T(1024)S(1)}, u32[]{:S(2)}, u32[]{:S(2)}) %collective-permute-start.1) | collective-permute-done | bytes 344096 | tf_op jit(solution)/shard_map/ppermute | solution.py:32
  21.1 1.1 collective-permute-start.2
  22.2 8.8 %collective-permute-done.2 = f32[86016]{0:T(1024)S(1)} collective-permute-done((f32[86016]{0:T(1024)S(1)}, f32[86016]{0:T(1024)S(1)}, u32[]{:S(2)}, u32[]{:S(2)}) %collective-permute-start.2) | collective-permute-done | bytes 344096 | tf_op jit(solution)/shard_map/ppermute | solution.py:99
  31.1 1.0 maximum_select_fusion.6
  32.3 0.3 reshape.254
  32.8 0.1 reshape.255
  33.0 0.7 copy.27
  33.7 27.3 %all_to_all.21 = f32[32,1,5376]{2,1,0:T(1,128)S(1)} all-to-all(f32[32,1,5376]{2,1,0:T(1,128)S(1)} %copy.27), channel_id=1, replica_groups=mesh['rep'=4,'shard'=32,'tp'=2] {'shard'}, dimensions={0} | all-to-all | bytes 1376256 | tf_op jit(solution)/shard_map/all_to_all | solution.py:105
  61.1 0.3 reshape.258
  61.4 1.3 collective-permute-start.3
  62.8 0.3 collective-permute-start.5
  63.1 0.3 stack_reshape.8
  63.4 4.7 %collective-permute-done.3 = f32[32,24,96]{2,1,0:T(8,128)S(1)} collective-permute-done((f32[32,24,96]{2,1,0:T(8,128)S(1)}, f32[32,24,96]{2,1,0:T(8,128)S(1)}, u32[]{:S(2)}, u32[]{:S(2)}) %collective-permute-start.3) | collective-permute-done | bytes 294944 | tf_op jit(solution)/shard_map/ppermute | solution.py:39
  68.1 0.9 maximum_select_fusion.3
  69.0 9.1 %collective-permute-start.4 = (f32[2,32,24,96]{3,2,1,0:T(8,128)}, f32[2,32,24,96]{3,2,1,0:T(8,128)}, u32[]{:S(2)}, u32[]{:S(2)}) collective-permute-start(f32[2,32,24,96]{3,2,1,0:T(8,128)} %maximum_select_fusion.3), channel_id=1, source_target_pairs={{0,64},{64,0},{128,192},{192,128},{1,65},{65,1},{129,193},{193,129... | collective-permute-start | bytes 1769480 | tf_op jit(solution)/shard_map/ppermute | solution.py:43
  78.2 3.4 %collective-permute-start.6 = (f32[2,32,24,128]{3,2,1,0:T(8,128)S(1)}, f32[2,32,24,128]{3,2,1,0:T(8,128)}, u32[]{:S(2)}, u32[]{:S(2)}) collective-permute-start(f32[2,32,24,128]{3,2,1,0:T(8,128)S(1)} %maximum_select_fusion.5), channel_id=1, source_target_pairs={{0,64},{64,0},{128,192},{192,128},{1,65},{65,1},{129,193},{193,129... | collective-permute-start | bytes 2359304 | tf_op jit(solution)/shard_map/ppermute | solution.py:43
  81.5 0.3 stack.112
  81.9 2.7 %maximum_select_fusion = f32[2,2,32,24,96]{4,3,2,1,0:T(8,128)} fusion(f32[2,1,32,24,96]{4,3,2,1,0:T(8,128)} %bitcast.10, f32[2,1,32,24,96]{4,3,2,1,0:T(8,128)S(1)} %maximum_select_fusion.2, pred[]{:T(512)S(6)} %eq.17), kind=kLoop, calls=%fused_computation | loop fusion | flops 884736 | bytes 2359297 | tf_op jit(solution)/shard_map/jit(_where)/select_n | solution.py:45
  84.6 4.5 %shard_map.109 = (f32[4,96,768]{2,1,0:T(8,128)}, f32[4,96,768]{2,1,0:T(8,128)}, bf16[4,768,96]{2,1,0:T(8,128)(2,1)}) custom-call(f32[4,32,24,96]{3,2,1,0:T(8,128)} %bitcast.76, f32[4,96,768]{2,1,0:T(8,128)} %refs_1_.2, f32[4,96,768]{2,1,0:T(8,128)} %refs_2_.2), custom_call_target="tpu_custom_call" | custom-call | tf_op jit(solution)/shard_map/pallas_call | solution.py:69
  89.1 0.9 constant_dynamic-slice_fusion.2
  90.0 0.2 reshape.259
  90.2 2.7 %maximum_select_fusion.1 = f32[2,2,32,24,128]{4,3,2,1,0:T(8,128)} fusion(f32[2,1,32,24,128]{4,3,2,1,0:T(8,128)} %bitcast.14, f32[2,1,32,24,128]{4,3,2,1,0:T(8,128)S(1)} %maximum_select_fusion.4, pred[]{:T(512)S(6)} %eq.17), kind=kLoop, calls=%fused_computation.1 | loop fusion | flops 1179648 | bytes 3145729 | tf_op jit(solution)/shard_map/jit(_where)/select_n | solution.py:45
  92.9 4.9 %shard_map.110 = (f32[512,768]{1,0:T(8,128)}, f32[512,768]{1,0:T(8,128)}, bf16[4,768,128]{2,1,0:T(8,128)(2,1)}) custom-call(f32[4,32,24,128]{3,2,1,0:T(8,128)} %bitcast.77, f32[512,768]{1,0:T(8,128)} %refs_1_.3, f32[512,768]{1,0:T(8,128)} %refs_2_.3), custom_call_target="tpu_custom_call" | custom-call | tf_op jit(solution)/shard_map/pallas_call | solution.py:69
  97.8 0.9 constant_dynamic-slice_fusion.1
  98.8 0.5 broadcast.32
  99.3 0.8 reduce
  100.2 0.8 reshape.266
  101.0 6.4 %all-to-all-start.1 = ((bf16[32,2,2688]{2,1,0:T(2,128)(2,1)}), bf16[32,2,2688]{2,1,0:T(2,128)(2,1)S(1)}, u32[]{:S(2)}, u32[]{:S(2)}) async-start(bf16[32,2,2688]{2,1,0:T(2,128)(2,1)} %reshape.266), calls=%async_computation.1 | async-start | bytes 688128 | tf_op jit(solution)/shard_map/all_to_all | solution.py:121
  107.4 13.5 %all-to-all-done.1 = bf16[32,2,2688]{2,1,0:T(2,128)(2,1)S(1)} async-done(((bf16[32,2,2688]{2,1,0:T(2,128)(2,1)}), bf16[32,2,2688]{2,1,0:T(2,128)(2,1)S(1)}, u32[]{:S(2)}, u32[]{:S(2)}) %all-to-all-start.1) | async-done | bytes 344096 | tf_op jit(solution)/shard_map/all_to_all | solution.py:121
  120.9 0.3 reshape.267
  121.2 0.4 constant_dynamic-slice_fusion
  121.6 1.3 collective-permute-start.7
  122.9 3.0 %collective-permute-done.7 = bf16[16,5376]{1,0:T(8,128)(2,1)S(1)} collective-permute-done((bf16[16,5376]{1,0:T(8,128)(2,1)S(1)}, bf16[16,5376]{1,0:T(8,128)(2,1)S(1)}, u32[]{:S(2)}, u32[]{:S(2)}) %collective-permute-start.7) | collective-permute-done | bytes 172064 | tf_op jit(solution)/shard_map/ppermute | solution.py:39
  126.0 3.1 %collective-permute-start.8 = (bf16[2,16,5376]{2,1,0:T(8,128)(2,1)S(1)}, bf16[2,16,5376]{2,1,0:T(8,128)(2,1)S(1)}, u32[]{:S(2)}, u32[]{:S(2)}) collective-permute-start(bf16[2,16,5376]{2,1,0:T(8,128)(2,1)S(1)} %maximum_select_fusion.9), channel_id=1, source_target_pairs={{0,64},{64,0},{128,192},{192,128},{1,65},{65,1},{129,193},{193,129... | collective-permute-start | bytes 1032200 | tf_op jit(solution)/shard_map/ppermute | solution.py:43
  129.1 1.2 collective-permute-done.8
  130.6 0.3 copy.31
  130.9 1.0 reshape.265
  132.0 0.6 reshape.262
  132.7 1.1 reshape.263
  (35 shorter events, 1.6 us)
Async XLA Ops:
  0.6 1.7 %copy-start = (f32[1,24,8192]{2,1,0:T(8,128)S(1)}, f32[1,24,8192]{2,1,0:T(8,128)}, u32[]{:S(2)}) copy-start(f32[1,24,8192]{2,1,0:T(8,128)} %param.7) | copy-start | bytes 2359300
  5.3 5.1 %collective-permute-start = (f32[2,86016]{1,0:T(2,128)S(1)}, f32[2,86016]{1,0:T(2,128)S(1)}, u32[]{:S(2)}, u32[]{:S(2)}) collective-permute-start(f32[2,86016]{1,0:T(2,128)S(1)} %bitcast.102), channel_id=1, source_target_pairs={{0,64},{64,0},{128,192},{192,128},{1,65},{65,1},{129,193},{193,129... | collective-permute-start | bytes 2064392 | tf_op jit(solution)/shard_map/ppermute | solution.py:29
  11.7 9.4 %collective-permute-start.1 = (f32[86016]{0:T(1024)S(1)}, f32[86016]{0:T(1024)S(1)}, u32[]{:S(2)}, u32[]{:S(2)}) collective-permute-start(f32[86016]{0:T(1024)S(1)} %bitcast.107), channel_id=1, source_target_pairs={{0,128},{64,192},{128,0},{192,64},{1,129},{65,193},{129,1},{193,65... | collective-permute-start | bytes 1032200 | tf_op jit(solution)/shard_map/ppermute | solution.py:32
  21.1 9.9 %collective-permute-start.2 = (f32[86016]{0:T(1024)S(1)}, f32[86016]{0:T(1024)S(1)}, u32[]{:S(2)}, u32[]{:S(2)}) collective-permute-start(f32[86016]{0:T(1024)S(1)} %add.44), channel_id=1, source_target_pairs={{0,1},{1,0},{2,3},{3,2},{4,5},{5,4},{6,7},{7,6},{8,9},{9,8},{10,11... | collective-permute-start | bytes 1032200 | tf_op jit(solution)/shard_map/ppermute | solution.py:99
  61.4 6.7 %collective-permute-start.3 = (f32[32,24,96]{2,1,0:T(8,128)S(1)}, f32[32,24,96]{2,1,0:T(8,128)S(1)}, u32[]{:S(2)}, u32[]{:S(2)}) collective-permute-start(f32[32,24,96]{2,1,0:T(8,128)S(1)} %reshape.258), channel_id=1, source_target_pairs={{0,128},{64,192},{128,0},{192,64},{1,129},{65,193},{129,1},{193,65... | collective-permute-start | bytes 884744 | tf_op jit(solution)/shard_map/ppermute | solution.py:39
  62.8 15.4 %collective-permute-start.5 = (f32[32,24,128]{2,1,0:T(8,128)S(1)}, f32[32,24,128]{2,1,0:T(8,128)S(1)}, u32[]{:S(2)}, u32[]{:S(2)}) collective-permute-start(f32[32,24,128]{2,1,0:T(8,128)S(1)} %bitcast.78), channel_id=1, source_target_pairs={{0,128},{64,192},{128,0},{192,64},{1,129},{65,193},{129,1},{193,65... | collective-permute-start | bytes 1179656 | tf_op jit(solution)/shard_map/ppermute | solution.py:39
  69.0 12.9 %collective-permute-start.4 = (f32[2,32,24,96]{3,2,1,0:T(8,128)}, f32[2,32,24,96]{3,2,1,0:T(8,128)}, u32[]{:S(2)}, u32[]{:S(2)}) collective-permute-start(f32[2,32,24,96]{3,2,1,0:T(8,128)} %maximum_select_fusion.3), channel_id=1, source_target_pairs={{0,64},{64,0},{128,192},{192,128},{1,65},{65,1},{129,193},{193,129... | collective-permute-start | bytes 1769480 | tf_op jit(solution)/shard_map/ppermute | solution.py:43
  78.2 12.0 %collective-permute-start.6 = (f32[2,32,24,128]{3,2,1,0:T(8,128)S(1)}, f32[2,32,24,128]{3,2,1,0:T(8,128)}, u32[]{:S(2)}, u32[]{:S(2)}) collective-permute-start(f32[2,32,24,128]{3,2,1,0:T(8,128)S(1)} %maximum_select_fusion.5), channel_id=1, source_target_pairs={{0,64},{64,0},{128,192},{192,128},{1,65},{65,1},{129,193},{193,129... | collective-permute-start | bytes 2359304 | tf_op jit(solution)/shard_map/ppermute | solution.py:43
  101.0 19.9 %all-to-all-start.1 = ((bf16[32,2,2688]{2,1,0:T(2,128)(2,1)}), bf16[32,2,2688]{2,1,0:T(2,128)(2,1)S(1)}, u32[]{:S(2)}, u32[]{:S(2)}) async-start(bf16[32,2,2688]{2,1,0:T(2,128)(2,1)} %reshape.266), calls=%async_computation.1 | async-start | bytes 688128 | tf_op jit(solution)/shard_map/all_to_all | solution.py:121
  121.6 4.3 %collective-permute-start.7 = (bf16[16,5376]{1,0:T(8,128)(2,1)S(1)}, bf16[16,5376]{1,0:T(8,128)(2,1)S(1)}, u32[]{:S(2)}, u32[]{:S(2)}) collective-permute-start(bf16[16,5376]{1,0:T(8,128)(2,1)S(1)} %bitcast.97), channel_id=1, source_target_pairs={{0,128},{64,192},{128,0},{192,64},{1,129},{65,193},{129,1},{193,65... | collective-permute-start | bytes 516104 | tf_op jit(solution)/shard_map/ppermute | solution.py:39
  126.0 4.4 %collective-permute-start.8 = (bf16[2,16,5376]{2,1,0:T(8,128)(2,1)S(1)}, bf16[2,16,5376]{2,1,0:T(8,128)(2,1)S(1)}, u32[]{:S(2)}, u32[]{:S(2)}) collective-permute-start(bf16[2,16,5376]{2,1,0:T(8,128)(2,1)S(1)} %maximum_select_fusion.9), channel_id=1, source_target_pairs={{0,64},{64,0},{128,192},{192,128},{1,65},{65,1},{129,193},{193,129... | collective-permute-start | bytes 1032200 | tf_op jit(solution)/shard_map/ppermute | solution.py:43

commit v4 on v3

--- a/solution.py
+++ b/solution.py
@@ -79,6 +79,55 @@
     )(got, master, moment)
 
 
+def shard_all_to_all(x):
+    n = x.shape[0]
+
+    def copy(x_ref, y_ref, send, recv, src, dst, peer):
+        return pltpu.make_async_remote_copy(
+            src_ref=x_ref.at[src],
+            dst_ref=y_ref.at[dst],
+            send_sem=send.at[src],
+            recv_sem=recv.at[dst],
+            device_id={"shard": peer},
+            device_id_type=pl.DeviceIdType.MESH,
+        )
+
+    def kernel(x_ref, y_ref, send, recv, local_sem):
+        me = lax.axis_index("shard")
+        local = pltpu.make_async_copy(x_ref.at[me], y_ref.at[me], local_sem)
+        local.start()
+
+        def start(i, c):
+            k = lax.rem(me + i, n)
+            copy(x_ref, y_ref, send, recv, k, me, k).start()
+            return c
+
+        lax.fori_loop(1, n, start, 0)
+
+        def wait(i, c):
+            k = lax.rem(me + i, n)
+            src = lax.rem(me + n - i, n)
+            copy(x_ref, y_ref, send, recv, k, me, k).wait_send()
+            copy(x_ref, y_ref, send, recv, src, src, src).wait_recv()
+            return c
+
+        lax.fori_loop(1, n, wait, 0)
+        local.wait()
+
+    return pl.pallas_call(
+        kernel,
+        out_shape=jax.ShapeDtypeStruct(x.shape, x.dtype),
+        in_specs=[pl.BlockSpec(memory_space=pl.ANY)],
+        out_specs=pl.BlockSpec(memory_space=pl.ANY),
+        scratch_shapes=[
+            pltpu.SemaphoreType.DMA((n,)),
+            pltpu.SemaphoreType.DMA((n,)),
+            pltpu.SemaphoreType.DMA,
+        ],
+        compiler_params=pltpu.CompilerParams(has_side_effects=True),
+    )(x)
+
+
 def local(expert_change, table_change, expert_master, expert_moment, table_master, table_moment):
     groups = lax.axis_size("rep")
     tensor = lax.axis_size("tp")
@@ -102,7 +151,7 @@
     he = jnp.transpose(he, (0, 2, 1, 3)).reshape(shards, width * rows)
     ht = halves[:, esize:].reshape(tensor, width, per_half, sub)
     ht = jnp.transpose(ht, (0, 2, 1, 3)).reshape(shards, width * sub)
-    got = lax.all_to_all(jnp.concatenate([he, ht], 1), "shard", 0, 0, tiled=True)
+    got = shard_all_to_all(jnp.concatenate([he, ht], 1)[:, None])[:, 0]
 
     ge = got[:, : width * rows].reshape(shards, width, rows)
     gt = got[:, width * rows :].reshape(shards, width, sub)
@@ -118,7 +167,8 @@
     r = lax.axis_index("rep")
     le = lax.dynamic_index_in_dim(low_e, r, 0, keepdims=False).reshape(shards, width * rows)
     lt = lax.dynamic_index_in_dim(low_t, r, 0, keepdims=False).reshape(shards, width * sub)
-    back = lax.all_to_all(jnp.concatenate([le, lt], 1), "shard", 0, 0, tiled=True)
+    back = jnp.concatenate([le, lt], 1)
+    back = shard_all_to_all(back.reshape(shards, 2, -1)).reshape(shards, -1)
     back = lax.dynamic_slice_in_dim(back, t * per_half, per_half, 0)
     allq = rep_gather(back)
     ce = allq[:, :, : width * rows].reshape(groups, per_half, width, rows)

time: 134 us -> 144 us (1.075)
  Pallas kernels: 9.35 us -> 65.9 us
  blocking collectives: 27.3 us -> 0 us
  starting transfers between devices: 29.4 us -> 19 us
  waiting for transfers between devices: 42.4 us -> 32.8 us
  local copies, waits for them, and re-layouts: 15 us -> 16.6 us
    pallas_call x0 -> x2, Pallas kernels: none -> 56.5 us  [shard_all_to_all(): pl.pallas_call(kernel, out_shape=jax.ShapeDtypeStruct(x.shape, x.dtype),...]
    all_to_all x1 -> x0, blocking collectives: 27.3 us -> none  [local(): lax.all_to_all(jnp.concatenate([he, ht], 1), 'shard', 0, 0, tiled=True)]
    all_to_all x1 -> x0, waiting for transfers between devices: 13.5 us -> none  [local(): lax.all_to_all(jnp.concatenate([le, lt], 1), 'shard', 0, 0, tiled=True)]
    all_to_all x1 -> x0, starting transfers between devices: 6.36 us -> none  [local(): lax.all_to_all(jnp.concatenate([le, lt], 1), 'shard', 0, 0, tiled=True)]
    ppermute x3, starting transfers between devices: 15.6 us -> 11.6 us  [rep_gather(): sib = lax.ppermute(pair, 'rep', pairs(n, 1))]
    ppermute x3, waiting for transfers between devices: 7.75 us -> 11.7 us  [rep_gather(): cross = lax.ppermute(x, 'rep', pairs(n, 2))]
    unnamed x14 -> x12, local copies, waits for them, and re-layouts: 2.02 us -> 3.02 us
  transfers between devices with their start and end apart: 10 -> 9, of which waited for: 7 -> 7; matrix products, arithmetic and copies ran while one was open for 4% -> 4% of each run, Pallas kernels for 3% -> 3%
where the time goes in v4:
time: 144 us
  Pallas kernels  65.9 us (46%)
  waiting for transfers between devices  32.8 us (23%)
  starting transfers between devices  19 us (13%)
  local copies, waits for them, and re-layouts  16.6 us (12%)
  other arithmetic  8.39 us (6%)
    pallas_call x2, Pallas kernels, shard_all_to_all(): pl.pallas_call(kernel, out_shape=jax.ShapeDtypeStruct(x.shape, x.dtype),...  56.5 us
    ppermute x3, waiting for transfers between devices, rep_gather(): cross = lax.ppermute(x, 'rep', pairs(n, 2))  11.7 us
    ppermute x3, starting transfers between devices, rep_gather(): sib = lax.ppermute(pair, 'rep', pairs(n, 1))  11.6 us
    pallas_call x2, Pallas kernels, fused_update(): pl.pallas_call(lambda *refs: update_kernel(scale, *refs), grid=(quarters,...  9.35 us
    ppermute x1, waiting for transfers between devices, rep_scatter(): return keep + lax.ppermute(send, 'rep', pairs(n, 2))  9.26 us
    ppermute x1, waiting for transfers between devices, local(): other = lax.ppermute(q, 'tp', pairs(tensor, 1))  8.85 us
    select_n x3, other arithmetic, rep_gather(): jnp.where(core == 0, jnp.stack([a, b], 1), jnp.stack([b, a], 1))  5.42 us
    ppermute x1, starting transfers between devices, rep_scatter(): a = mine + lax.ppermute(other, 'rep', pairs(n, 1))  3.33 us
  transfers between devices with their start and end apart: 9, of which 7 were waited for; matrix products, arithmetic and copies ran while one was open for 4% of the time, Pallas kernels for 3%

profile of v4, /device:TPU:1, one launch (start us, length us, event | category | flops | bytes accessed | tf_op | source)
XLA Modules:
  0.0 143.7 jit_solution(857098418834681578)
XLA Ops:
  0.7 1.6 %concatenate.56 = f32[2,2,36864]{2,1,0:T(2,128)S(1)} reshape(f32[1,4,24,1536]{3,2,1,0:T(8,128)} %param.6) | data formatting | bytes 1179648 | tf_op jit(solution)/shard_map/concatenate | solution.py:146
  2.4 0.5 reshape_squeeze.4
  3.0 0.5 concatenate.57
  3.6 1.2 constant_dynamic-slice_fusion.6
  4.8 0.5 copy.37
  5.3 3.3 %collective-permute-start = (f32[2,86016]{1,0:T(2,128)S(1)}, f32[2,86016]{1,0:T(2,128)S(1)}, u32[]{:S(2)}, u32[]{:S(2)}) collective-permute-start(f32[2,86016]{1,0:T(2,128)S(1)} %bitcast.98), channel_id=1, source_target_pairs={{0,64},{64,0},{128,192},{192,128},{1,65},{65,1},{129,193},{193,129... | collective-permute-start | bytes 2064392 | tf_op jit(solution)/shard_map/ppermute | solution.py:29
  8.6 1.8 %collective-permute-done = f32[2,86016]{1,0:T(2,128)S(1)} collective-permute-done((f32[2,86016]{1,0:T(2,128)S(1)}, f32[2,86016]{1,0:T(2,128)S(1)}, u32[]{:S(2)}, u32[]{:S(2)}) %collective-permute-start) | collective-permute-done | bytes 688160 | tf_op jit(solution)/shard_map/ppermute | solution.py:29
  10.4 0.7 bitcast_add_fusion
  11.1 0.6 constant_dynamic-slice_fusion.3
  11.8 9.3 %collective-permute-done.1 = f32[86016]{0:T(1024)S(1)} collective-permute-done((f32[86016]{0:T(1024)S(1)}, f32[86016]{0:T(1024)S(1)}, u32[]{:S(2)}, u32[]{:S(2)}) %collective-permute-start.1) | collective-permute-done | bytes 344096 | tf_op jit(solution)/shard_map/ppermute | solution.py:32
  21.1 1.1 collective-permute-start.2
  22.2 8.8 %collective-permute-done.2 = f32[86016]{0:T(1024)S(1)} collective-permute-done((f32[86016]{0:T(1024)S(1)}, f32[86016]{0:T(1024)S(1)}, u32[]{:S(2)}, u32[]{:S(2)}) %collective-permute-start.2) | collective-permute-done | bytes 344096 | tf_op jit(solution)/shard_map/ppermute | solution.py:148
  31.1 1.0 maximum_select_fusion.6
  32.1 0.1 copy.17
  32.3 0.3 reshape.254
  32.6 0.1 copy.16
  32.8 0.1 reshape.255
  33.0 1.3 broadcast_in_dim.3.x_ref
  34.3 32.6 %shard_map.109 = f32[32,1,5376]{2,1,0:T(1,128)} custom-call(f32[32,1,5376]{2,1,0:T(1,128)} %broadcast_in_dim.3.x_ref), custom_call_target="tpu_custom_call" | custom-call | tf_op jit(solution)/shard_map/pallas_call | solution.py:117
  66.9 1.1 copy.36
  68.1 0.3 reshape.258
  68.3 1.3 collective-permute-start.3
  69.7 0.4 collective-permute-start.5
  70.1 0.3 stack_reshape.8
  70.4 6.7 %collective-permute-done.3 = f32[32,24,96]{2,1,0:T(8,128)S(1)} collective-permute-done((f32[32,24,96]{2,1,0:T(8,128)S(1)}, f32[32,24,96]{2,1,0:T(8,128)S(1)}, u32[]{:S(2)}, u32[]{:S(2)}) %collective-permute-start.3) | collective-permute-done | bytes 294944 | tf_op jit(solution)/shard_map/ppermute | solution.py:39
  77.0 0.9 maximum_select_fusion.3
  78.0 5.5 %collective-permute-start.4 = (f32[2,32,24,96]{3,2,1,0:T(8,128)}, f32[2,32,24,96]{3,2,1,0:T(8,128)}, u32[]{:S(2)}, u32[]{:S(2)}) collective-permute-start(f32[2,32,24,96]{3,2,1,0:T(8,128)} %maximum_select_fusion.3), channel_id=1, source_target_pairs={{0,64},{64,0},{128,192},{192,128},{1,65},{65,1},{129,193},{193,129... | collective-permute-start | bytes 1769480 | tf_op jit(solution)/shard_map/ppermute | solution.py:43
  83.4 2.0 %collective-permute-done.5 = f32[32,24,128]{2,1,0:T(8,128)S(1)} collective-permute-done((f32[32,24,128]{2,1,0:T(8,128)S(1)}, f32[32,24,128]{2,1,0:T(8,128)S(1)}, u32[]{:S(2)}, u32[]{:S(2)}) %collective-permute-start.5) | collective-permute-done | bytes 393248 | tf_op jit(solution)/shard_map/ppermute | solution.py:39
  85.5 3.0 %collective-permute-start.6 = (f32[2,32,24,128]{3,2,1,0:T(8,128)S(1)}, f32[2,32,24,128]{3,2,1,0:T(8,128)}, u32[]{:S(2)}, u32[]{:S(2)}) collective-permute-start(f32[2,32,24,128]{3,2,1,0:T(8,128)S(1)} %maximum_select_fusion.5), channel_id=1, source_target_pairs={{0,64},{64,0},{128,192},{192,128},{1,65},{65,1},{129,193},{193,129... | collective-permute-start | bytes 2359304 | tf_op jit(solution)/shard_map/ppermute | solution.py:43
  88.5 0.3 stack.112
  88.9 2.7 %maximum_select_fusion = f32[2,2,32,24,96]{4,3,2,1,0:T(8,128)} fusion(f32[2,1,32,24,96]{4,3,2,1,0:T(8,128)} %bitcast.9, f32[2,1,32,24,96]{4,3,2,1,0:T(8,128)S(1)} %maximum_select_fusion.2, pred[]{:T(512)S(6)} %eq.17), kind=kLoop, calls=%fused_computation | loop fusion | flops 884736 | bytes 2359297 | tf_op jit(solution)/shard_map/jit(_where)/select_n | solution.py:45
  91.6 4.5 %shard_map.110 = (f32[4,96,768]{2,1,0:T(8,128)}, f32[4,96,768]{2,1,0:T(8,128)}, bf16[4,768,96]{2,1,0:T(8,128)(2,1)}) custom-call(f32[4,32,24,96]{3,2,1,0:T(8,128)} %bitcast.71, f32[4,96,768]{2,1,0:T(8,128)} %refs_1_.2, f32[4,96,768]{2,1,0:T(8,128)} %refs_2_.2), custom_call_target="tpu_custom_call" | custom-call | tf_op jit(solution)/shard_map/pallas_call | solution.py:69
  96.1 0.9 constant_dynamic-slice_fusion.2
  97.0 0.2 reshape.259
  97.2 2.7 %maximum_select_fusion.1 = f32[2,2,32,24,128]{4,3,2,1,0:T(8,128)} fusion(f32[2,1,32,24,128]{4,3,2,1,0:T(8,128)} %bitcast.13, f32[2,1,32,24,128]{4,3,2,1,0:T(8,128)S(1)} %maximum_select_fusion.4, pred[]{:T(512)S(6)} %eq.17), kind=kLoop, calls=%fused_computation.1 | loop fusion | flops 1179648 | bytes 3145729 | tf_op jit(solution)/shard_map/jit(_where)/select_n | solution.py:45
  99.9 4.9 %shard_map.111 = (f32[512,768]{1,0:T(8,128)}, f32[512,768]{1,0:T(8,128)}, bf16[4,768,128]{2,1,0:T(8,128)(2,1)}) custom-call(f32[4,32,24,128]{3,2,1,0:T(8,128)} %bitcast.72, f32[512,768]{1,0:T(8,128)} %refs_1_.3, f32[512,768]{1,0:T(8,128)} %refs_2_.3), custom_call_target="tpu_custom_call" | custom-call | tf_op jit(solution)/shard_map/pallas_call | solution.py:69
  104.7 0.9 constant_dynamic-slice_fusion.1
  105.8 0.8 reshape.262.x_ref
  106.6 23.9 %shard_map.112 = bf16[32,2,2688]{2,1,0:T(2,128)(2,1)} custom-call(bf16[32,2,2688]{2,1,0:T(2,128)(2,1)} %reshape.262.x_ref), custom_call_target="tpu_custom_call" | custom-call | tf_op jit(solution)/shard_map/pallas_call | solution.py:117
  130.6 1.0 copy.28
  131.6 1.3 collective-permute-start.7
  132.9 3.0 %collective-permute-done.7 = bf16[16,5376]{1,0:T(8,128)(2,1)S(1)} collective-permute-done((bf16[16,5376]{1,0:T(8,128)(2,1)S(1)}, bf16[16,5376]{1,0:T(8,128)(2,1)S(1)}, u32[]{:S(2)}, u32[]{:S(2)}) %collective-permute-start.7) | collective-permute-done | bytes 172064 | tf_op jit(solution)/shard_map/ppermute | solution.py:39
  136.0 3.0 %collective-permute-start.8 = (bf16[2,16,5376]{2,1,0:T(8,128)(2,1)S(1)}, bf16[2,16,5376]{2,1,0:T(8,128)(2,1)S(1)}, u32[]{:S(2)}, u32[]{:S(2)}) collective-permute-start(bf16[2,16,5376]{2,1,0:T(8,128)(2,1)S(1)} %maximum_select_fusion.9), channel_id=1, source_target_pairs={{0,64},{64,0},{128,192},{192,128},{1,65},{65,1},{129,193},{193,129... | collective-permute-start | bytes 1032200 | tf_op jit(solution)/shard_map/ppermute | solution.py:43
  139.1 1.2 collective-permute-done.8
  140.6 0.3 copy.19
  140.9 1.0 reshape.267
  141.9 0.6 reshape.264
  142.6 1.1 reshape.265
  (33 shorter events, 1.4 us)
Async XLA Ops:
  0.6 1.7 %copy-start = (f32[1,24,8192]{2,1,0:T(8,128)S(1)}, f32[1,24,8192]{2,1,0:T(8,128)}, u32[]{:S(2)}) copy-start(f32[1,24,8192]{2,1,0:T(8,128)} %param.7) | copy-start | bytes 2359300
  5.3 5.1 %collective-permute-start = (f32[2,86016]{1,0:T(2,128)S(1)}, f32[2,86016]{1,0:T(2,128)S(1)}, u32[]{:S(2)}, u32[]{:S(2)}) collective-permute-start(f32[2,86016]{1,0:T(2,128)S(1)} %bitcast.98), channel_id=1, source_target_pairs={{0,64},{64,0},{128,192},{192,128},{1,65},{65,1},{129,193},{193,129... | collective-permute-start | bytes 2064392 | tf_op jit(solution)/shard_map/ppermute | solution.py:29
  11.7 9.4 %collective-permute-start.1 = (f32[86016]{0:T(1024)S(1)}, f32[86016]{0:T(1024)S(1)}, u32[]{:S(2)}, u32[]{:S(2)}) collective-permute-start(f32[86016]{0:T(1024)S(1)} %bitcast.103), channel_id=1, source_target_pairs={{0,128},{64,192},{128,0},{192,64},{1,129},{65,193},{129,1},{193,65... | collective-permute-start | bytes 1032200 | tf_op jit(solution)/shard_map/ppermute | solution.py:32
  21.1 9.9 %collective-permute-start.2 = (f32[86016]{0:T(1024)S(1)}, f32[86016]{0:T(1024)S(1)}, u32[]{:S(2)}, u32[]{:S(2)}) collective-permute-start(f32[86016]{0:T(1024)S(1)} %add.44), channel_id=1, source_target_pairs={{0,1},{1,0},{2,3},{3,2},{4,5},{5,4},{6,7},{7,6},{8,9},{9,8},{10,11... | collective-permute-start | bytes 1032200 | tf_op jit(solution)/shard_map/ppermute | solution.py:148
  68.3 8.7 %collective-permute-start.3 = (f32[32,24,96]{2,1,0:T(8,128)S(1)}, f32[32,24,96]{2,1,0:T(8,128)S(1)}, u32[]{:S(2)}, u32[]{:S(2)}) collective-permute-start(f32[32,24,96]{2,1,0:T(8,128)S(1)} %reshape.258), channel_id=1, source_target_pairs={{0,128},{64,192},{128,0},{192,64},{1,129},{65,193},{129,1},{193,65... | collective-permute-start | bytes 884744 | tf_op jit(solution)/shard_map/ppermute | solution.py:39
  69.7 15.7 %collective-permute-start.5 = (f32[32,24,128]{2,1,0:T(8,128)S(1)}, f32[32,24,128]{2,1,0:T(8,128)S(1)}, u32[]{:S(2)}, u32[]{:S(2)}) collective-permute-start(f32[32,24,128]{2,1,0:T(8,128)S(1)} %bitcast.73), channel_id=1, source_target_pairs={{0,128},{64,192},{128,0},{192,64},{1,129},{65,193},{129,1},{193,65... | collective-permute-start | bytes 1179656 | tf_op jit(solution)/shard_map/ppermute | solution.py:39
  78.0 11.0 %collective-permute-start.4 = (f32[2,32,24,96]{3,2,1,0:T(8,128)}, f32[2,32,24,96]{3,2,1,0:T(8,128)}, u32[]{:S(2)}, u32[]{:S(2)}) collective-permute-start(f32[2,32,24,96]{3,2,1,0:T(8,128)} %maximum_select_fusion.3), channel_id=1, source_target_pairs={{0,64},{64,0},{128,192},{192,128},{1,65},{65,1},{129,193},{193,129... | collective-permute-start | bytes 1769480 | tf_op jit(solution)/shard_map/ppermute | solution.py:43
  85.5 11.7 %collective-permute-start.6 = (f32[2,32,24,128]{3,2,1,0:T(8,128)S(1)}, f32[2,32,24,128]{3,2,1,0:T(8,128)}, u32[]{:S(2)}, u32[]{:S(2)}) collective-permute-start(f32[2,32,24,128]{3,2,1,0:T(8,128)S(1)} %maximum_select_fusion.5), channel_id=1, source_target_pairs={{0,64},{64,0},{128,192},{192,128},{1,65},{65,1},{129,193},{193,129... | collective-permute-start | bytes 2359304 | tf_op jit(solution)/shard_map/ppermute | solution.py:43
  131.6 4.3 %collective-permute-start.7 = (bf16[16,5376]{1,0:T(8,128)(2,1)S(1)}, bf16[16,5376]{1,0:T(8,128)(2,1)S(1)}, u32[]{:S(2)}, u32[]{:S(2)}) collective-permute-start(bf16[16,5376]{1,0:T(8,128)(2,1)S(1)} %constant_dynamic-slice_fusion), channel_id=1, source_target_pairs={{0,128},{64,192},{128,0},{192,64},{1,129},{65,193},{129,1},{193,65... | collective-permute-start | bytes 516104 | tf_op jit(solution)/shard_map/ppermute | solution.py:39
  136.0 4.3 %collective-permute-start.8 = (bf16[2,16,5376]{2,1,0:T(8,128)(2,1)S(1)}, bf16[2,16,5376]{2,1,0:T(8,128)(2,1)S(1)}, u32[]{:S(2)}, u32[]{:S(2)}) collective-permute-start(bf16[2,16,5376]{2,1,0:T(8,128)(2,1)S(1)} %maximum_select_fusion.9), channel_id=1, source_target_pairs={{0,64},{64,0},{128,192},{192,128},{1,65},{65,1},{129,193},{193,129... | collective-permute-start | bytes 1032200 | tf_op jit(solution)/shard_map/ppermute | solution.py:43

commit v5 on v3

--- a/solution.py
+++ b/solution.py
@@ -91,22 +91,27 @@
     sub = vrows // groups
     esize = width * half
 
+    r = lax.axis_index("rep")
+
+    def forward(x, cols):
+        q = rep_scatter(x)
+        other = lax.ppermute(q, "tp", pairs(tensor, 1))
+        h = jnp.where(t == 0, jnp.stack([q, other]), jnp.stack([other, q]))
+        h = jnp.transpose(h.reshape(tensor, width, per_half, cols), (0, 2, 1, 3))
+        got = lax.all_to_all(h.reshape(shards, width * cols), "shard", 0, 0, tiled=True)
+        return rep_gather(got.reshape(shards, width, cols))
+
+    def backward(low, cols):
+        mine = lax.dynamic_index_in_dim(low, r, 0, keepdims=False).reshape(shards, width * cols)
+        back = lax.all_to_all(mine, "shard", 0, 0, tiled=True)
+        back = lax.dynamic_slice_in_dim(back, t * per_half, per_half, 0)
+        return rep_gather(back.reshape(per_half, width, cols))
+
     ex = expert_change[0].reshape(mats, esize)
     tx = table_change[0].reshape(width, per_half, groups, sub)
     tx = jnp.transpose(tx, (2, 0, 1, 3)).reshape(groups, -1)
-    q = rep_scatter(jnp.concatenate([ex, tx], axis=1))
-
-    other = lax.ppermute(q, "tp", pairs(tensor, 1))
-    halves = jnp.where(t == 0, jnp.stack([q, other]), jnp.stack([other, q]))
-    he = halves[:, :esize].reshape(tensor, width, per_half, rows)
-    he = jnp.transpose(he, (0, 2, 1, 3)).reshape(shards, width * rows)
-    ht = halves[:, esize:].reshape(tensor, width, per_half, sub)
-    ht = jnp.transpose(ht, (0, 2, 1, 3)).reshape(shards, width * sub)
-    got = lax.all_to_all(jnp.concatenate([he, ht], 1), "shard", 0, 0, tiled=True)
-
-    ge = got[:, : width * rows].reshape(shards, width, rows)
-    gt = got[:, width * rows :].reshape(shards, width, sub)
-    every_e, every_t = rep_gather((ge, gt))
+    every_e = forward(ex, rows)
+    every_t = forward(tx, sub)
 
     expert_weights, expert_velocity, low_e = fused_update(
         every_e, expert_master, expert_moment, 1.0 / groups
@@ -115,15 +120,9 @@
         every_t, table_master, table_moment, 1.0 / groups
     )
 
-    r = lax.axis_index("rep")
-    le = lax.dynamic_index_in_dim(low_e, r, 0, keepdims=False).reshape(shards, width * rows)
-    lt = lax.dynamic_index_in_dim(low_t, r, 0, keepdims=False).reshape(shards, width * sub)
-    back = lax.all_to_all(jnp.concatenate([le, lt], 1), "shard", 0, 0, tiled=True)
-    back = lax.dynamic_slice_in_dim(back, t * per_half, per_half, 0)
-    allq = rep_gather(back)
-    ce = allq[:, :, : width * rows].reshape(groups, per_half, width, rows)
+    ce = backward(low_e, rows)
     expert_copies = jnp.transpose(ce, (0, 2, 1, 3)).reshape(mats, width, per_half * rows)
-    ct = allq[:, :, width * rows :].reshape(groups, per_half, width, sub)
+    ct = backward(low_t, sub)
     table_copies = jnp.transpose(ct, (2, 1, 0, 3)).reshape(width, per_half * vrows)
     return (
         expert_weights,

time: 134 us -> 138 us (1.030)
  starting transfers between devices: 29.4 us -> 62.9 us
  blocking collectives: 27.3 us -> 0 us
  waiting for transfers between devices: 42.4 us -> 36.7 us
  local copies, waits for them, and re-layouts: 15 us -> 16.6 us
  other arithmetic: 9.24 us -> 10.7 us
    all_to_all x1 -> x4, starting transfers between devices: 6.36 us -> 34.1 us  [the longest x2 18.7 us: forward(): lax.all_to_all(h.reshape(shards, width * cols), 'shard', 0, 0, tiled=True)]
    all_to_all x1 -> x0, blocking collectives: 27.3 us -> none  [local(): lax.all_to_all(jnp.concatenate([he, ht], 1), 'shard', 0, 0, tiled=True)]
    all_to_all x3, other arithmetic: 0.91 us -> 3.97 us  [the longest x2 3.28 us: backward(): back = lax.all_to_all(mine, 'shard', 0, 0, tiled=True)]
    ppermute x1 -> x2, starting transfers between devices: 1.09 us -> 3.93 us  [forward(): other = lax.ppermute(q, 'tp', pairs(tensor, 1))]
    ppermute x3 -> x4, starting transfers between devices: 15.6 us -> 18.4 us  [rep_gather(): sib = lax.ppermute(pair, 'rep', pairs(n, 1))]
    another operation x0 -> x4, local copies, waits for them, and re-layouts: none -> 2.3 us  [the longest x2 2.1 us: rep_scatter(): x4 = x.reshape(2, 2, -1)]
    ppermute x3 -> x4, waiting for transfers between devices: 7.75 us -> 5.47 us  [rep_gather(): cross = lax.ppermute(x, 'rep', pairs(n, 2))]
    concatenate x3 -> x0, local copies, waits for them, and re-layouts: 2.21 us -> none  [local(): q = rep_scatter(jnp.concatenate([ex, tx], axis=1))]
  transfers between devices with their start and end apart: 10 -> 18, of which waited for: 7 -> 8; matrix products, arithmetic and copies ran while one was open for 4% -> 16% of each run, Pallas kernels for 3% -> 7%
where the time goes in v5:
time: 138 us; the launch traced here: 137 us
  starting transfers between devices  62.9 us (46%)
  waiting for transfers between devices  36.7 us (27%)
  local copies, waits for them, and re-layouts  16.6 us (12%)
  other arithmetic  10.7 us (8%)
  Pallas kernels  9.36 us (7%)
    all_to_all x2, starting transfers between devices, forward(): lax.all_to_all(h.reshape(shards, width * cols), 'shard', 0, 0, tiled=True)  18.7 us
    ppermute x4, starting transfers between devices, rep_gather(): sib = lax.ppermute(pair, 'rep', pairs(n, 1))  18.4 us
    all_to_all x2, starting transfers between devices, backward(): back = lax.all_to_all(mine, 'shard', 0, 0, tiled=True)  15.5 us
    all_to_all x2, waiting for transfers between devices, forward(): lax.all_to_all(h.reshape(shards, width * cols), 'shard', 0, 0, tiled=True)  10.5 us
    pallas_call x2, Pallas kernels, fused_update(): pl.pallas_call(lambda *refs: update_kernel(scale, *refs), grid=(quarters,...  9.36 us
    ppermute x2, waiting for transfers between devices, forward(): other = lax.ppermute(q, 'tp', pairs(tensor, 1))  8.91 us
    ppermute x2, waiting for transfers between devices, rep_scatter(): return keep + lax.ppermute(send, 'rep', pairs(n, 2))  8.25 us
    select_n x4, other arithmetic, rep_gather(): jnp.where(core == 0, jnp.stack([a, b], 1), jnp.stack([b, a], 1))  5.55 us
  transfers between devices with their start and end apart: 18, of which 8 were waited for; matrix products, arithmetic and copies ran while one was open for 16% of the time, Pallas kernels for 7%

profile of v5, /device:TPU:1, one launch (start us, length us, event | category | flops | bytes accessed | tf_op | source)
XLA Modules:
  0.0 137.3 jit_solution(9573422437683198173)
XLA Ops:
  0.7 1.6 %reshape_reshape_squeeze.3 = f32[2,2,36864]{2,1,0:T(2,128)S(1)} reshape(f32[1,4,24,1536]{3,2,1,0:T(8,128)} %param.6) | data formatting | bytes 1179648 | tf_op jit(solution)/shard_map/reshape;reshape;squeeze | solution.py:26
  2.3 0.5 constant_dynamic-slice_fusion.9
  3.1 3.3 %collective-permute-start = (f32[2,36864]{1,0:T(2,128)S(1)}, f32[2,36864]{1,0:T(2,128)S(1)}, u32[]{:S(2)}, u32[]{:S(2)}) collective-permute-start(f32[2,36864]{1,0:T(2,128)S(1)} %bitcast.89), channel_id=1, source_target_pairs={{0,64},{64,0},{128,192},{192,128},{1,65},{65,1},{129,193},{193,129... | collective-permute-start | bytes 884744 | tf_op jit(solution)/shard_map/ppermute | solution.py:29
  6.4 0.5 reshape_squeeze.3
  7.0 0.5 reshape_reshape.3
  7.5 0.7 constant_dynamic-slice_fusion.4
  9.3 4.9 %collective-permute-done.1 = f32[36864]{0:T(1024)S(1)} collective-permute-done((f32[36864]{0:T(1024)S(1)}, f32[36864]{0:T(1024)S(1)}, u32[]{:S(2)}, u32[]{:S(2)}) %collective-permute-start.1) | collective-permute-done | bytes 147488 | tf_op jit(solution)/shard_map/ppermute | solution.py:32
  14.3 1.1 collective-permute-start.2
  15.4 0.4 bitcast_add_fusion
  15.9 4.0 %collective-permute-done.2 = f32[36864]{0:T(1024)S(1)} collective-permute-done((f32[36864]{0:T(1024)S(1)}, f32[36864]{0:T(1024)S(1)}, u32[]{:S(2)}, u32[]{:S(2)}) %collective-permute-start.2) | collective-permute-done | bytes 147488 | tf_op jit(solution)/shard_map/ppermute | solution.py:98
  20.1 1.1 all_to_all.32
  21.2 9.5 %all-to-all-start = ((f32[32,1,2304]{2,1,0:T(1,128)}), f32[32,1,2304]{2,1,0:T(1,128)S(1)}, u32[]{:S(2)}, u32[]{:S(2)}) async-start(f32[32,1,2304]{2,1,0:T(1,128)} %all_to_all.32), calls=%async_computation | async-start | bytes 589824 | tf_op jit(solution)/shard_map/all_to_all | solution.py:101
  30.7 0.3 constant_dynamic-slice_fusion.1
  31.1 1.3 collective-permute-start.8
  32.4 3.3 %collective-permute-done.8 = f32[49152]{0:T(1024)S(1)} collective-permute-done((f32[49152]{0:T(1024)S(1)}, f32[49152]{0:T(1024)S(1)}, u32[]{:S(2)}, u32[]{:S(2)}) %collective-permute-start.8) | collective-permute-done | bytes 196640 | tf_op jit(solution)/shard_map/ppermute | solution.py:32
  35.7 2.8 %collective-permute-start.9 = (f32[49152]{0:T(1024)S(1)}, f32[49152]{0:T(1024)S(1)}, u32[]{:S(2)}, u32[]{:S(2)}) collective-permute-start(f32[49152]{0:T(1024)S(1)} %add.64), channel_id=1, source_target_pairs={{0,1},{1,0},{2,3},{3,2},{4,5},{5,4},{6,7},{7,6},{8,9},{9,8},{10,11... | collective-permute-start | bytes 589832 | tf_op jit(solution)/shard_map/ppermute | solution.py:98
  38.5 4.9 %collective-permute-done.9 = f32[49152]{0:T(1024)S(1)} collective-permute-done((f32[49152]{0:T(1024)S(1)}, f32[49152]{0:T(1024)S(1)}, u32[]{:S(2)}, u32[]{:S(2)}) %collective-permute-start.9) | collective-permute-done | bytes 196640 | tf_op jit(solution)/shard_map/ppermute | solution.py:98
  43.5 0.9 copy.41
  44.4 9.2 %all-to-all-start.2 = ((f32[32,1,3072]{2,1,0:T(1,128)}), f32[32,1,3072]{2,1,0:T(1,128)S(1)}, u32[]{:S(2)}, u32[]{:S(2)}) async-start(f32[32,1,3072]{2,1,0:T(1,128)} %bitcast.18), calls=%async_computation.2 | async-start | bytes 786432 | tf_op jit(solution)/shard_map/all_to_all | solution.py:101
  53.6 0.7 reduce
  54.7 10.5 %all-to-all-done.2 = f32[32,1,3072]{2,1,0:T(1,128)S(1)} async-done(((f32[32,1,3072]{2,1,0:T(1,128)}), f32[32,1,3072]{2,1,0:T(1,128)S(1)}, u32[]{:S(2)}, u32[]{:S(2)}) %all-to-all-start.2) | async-done | bytes 393248 | tf_op jit(solution)/shard_map/all_to_all | solution.py:101
  65.5 6.7 %collective-permute-start.4 = (f32[2,32,24,96]{3,2,1,0:T(8,128)S(1)}, f32[2,32,24,96]{3,2,1,0:T(8,128)}, u32[]{:S(2)}, u32[]{:S(2)}) collective-permute-start(f32[2,32,24,96]{3,2,1,0:T(8,128)S(1)} %maximum_select_fusion.3), channel_id=1, source_target_pairs={{0,64},{64,0},{128,192},{192,128},{1,65},{65,1},{129,193},{193,129... | collective-permute-start | bytes 1769480 | tf_op jit(solution)/shard_map/ppermute | solution.py:43
  72.3 5.9 %collective-permute-start.11 = (f32[2,32,24,128]{3,2,1,0:T(8,128)S(1)}, f32[2,32,24,128]{3,2,1,0:T(8,128)}, u32[]{:S(2)}, u32[]{:S(2)}) collective-permute-start(f32[2,32,24,128]{3,2,1,0:T(8,128)S(1)} %maximum_select_fusion.5), channel_id=1, source_target_pairs={{0,64},{64,0},{128,192},{192,128},{1,65},{65,1},{129,193},{193,129... | collective-permute-start | bytes 2359304 | tf_op jit(solution)/shard_map/ppermute | solution.py:43
  78.5 2.7 %maximum_select_fusion = f32[2,2,32,24,96]{4,3,2,1,0:T(8,128)} fusion(f32[2,1,32,24,96]{4,3,2,1,0:T(8,128)} %bitcast.5, f32[2,1,32,24,96]{4,3,2,1,0:T(8,128)S(1)} %maximum_select_fusion.2, pred[]{:T(512)S(6)} %eq.23), kind=kLoop, calls=%fused_computation | loop fusion | flops 884736 | bytes 2359297 | tf_op jit(solution)/shard_map/jit(_where)/select_n | solution.py:45
  81.2 4.5 %shard_map.109 = (f32[4,96,768]{2,1,0:T(8,128)}, f32[4,96,768]{2,1,0:T(8,128)}, bf16[4,768,96]{2,1,0:T(8,128)(2,1)}) custom-call(f32[4,32,24,96]{3,2,1,0:T(8,128)} %bitcast.65, f32[4,96,768]{2,1,0:T(8,128)} %refs_1_.2, f32[4,96,768]{2,1,0:T(8,128)} %refs_2_.2), custom_call_target="tpu_custom_call" | custom-call | tf_op jit(solution)/shard_map/pallas_call | solution.py:69
  85.7 0.9 constant_dynamic-slice_fusion.5
  86.9 0.5 broadcast.53
  87.5 1.5 %reduce.11 = bf16[32,2304]{1,0:T(8,128)(2,1)S(1)} reduce(bf16[32,1,2304]{2,1,0:T(2,128)(2,1)S(1)} %all_to_all.33, bf16[]{:T(256)} %broadcast.53), dimensions={1}, to_apply=%all_to_all.33.reduce_sub_computation | reduce | bytes 294914 | tf_op jit(solution)/shard_map/all_to_all | solution.py:106
  89.0 0.7 reshape.347
  89.7 6.2 %all-to-all-start.1 = ((bf16[32,2,1152]{2,1,0:T(2,128)(2,1)}), bf16[32,2,1152]{2,1,0:T(2,128)(2,1)S(1)}, u32[]{:S(2)}, u32[]{:S(2)}) async-start(bf16[32,2,1152]{2,1,0:T(2,128)(2,1)} %reshape.347), calls=%async_computation.1 | async-start | bytes 294912 | tf_op jit(solution)/shard_map/all_to_all | solution.py:106
  96.0 2.7 %maximum_select_fusion.1 = f32[2,2,32,24,128]{4,3,2,1,0:T(8,128)} fusion(f32[2,1,32,24,128]{4,3,2,1,0:T(8,128)} %bitcast.24, f32[2,1,32,24,128]{4,3,2,1,0:T(8,128)S(1)} %maximum_select_fusion.4, pred[]{:T(512)S(6)} %eq.23), kind=kLoop, calls=%fused_computation.1 | loop fusion | flops 1179648 | bytes 3145729 | tf_op jit(solution)/shard_map/jit(_where)/select_n | solution.py:45
  98.7 4.9 %shard_map.110 = (f32[512,768]{1,0:T(8,128)}, f32[512,768]{1,0:T(8,128)}, bf16[4,768,128]{2,1,0:T(8,128)(2,1)}) custom-call(f32[4,32,24,128]{3,2,1,0:T(8,128)} %bitcast.66, f32[512,768]{1,0:T(8,128)} %refs_1_.3, f32[512,768]{1,0:T(8,128)} %refs_2_.3), custom_call_target="tpu_custom_call" | custom-call | tf_op jit(solution)/shard_map/pallas_call | solution.py:69
  103.6 0.9 constant_dynamic-slice_fusion
  104.6 1.8 %reduce.12 = bf16[32,3072]{1,0:T(8,128)(2,1)S(1)} reduce(bf16[32,1,3072]{2,1,0:T(2,128)(2,1)S(1)} %all_to_all.34, bf16[]{:T(256)} %broadcast.53), dimensions={1}, to_apply=%all_to_all.34.reduce_sub_computation | reduce | bytes 393218 | tf_op jit(solution)/shard_map/all_to_all | solution.py:106
  106.4 0.8 reshape.349
  107.2 9.2 %all-to-all-start.3 = ((bf16[32,2,1536]{2,1,0:T(2,128)(2,1)}), bf16[32,2,1536]{2,1,0:T(2,128)(2,1)S(1)}, u32[]{:S(2)}, u32[]{:S(2)}) async-start(bf16[32,2,1536]{2,1,0:T(2,128)(2,1)} %reshape.349), calls=%async_computation.3 | async-start | bytes 393216 | tf_op jit(solution)/shard_map/all_to_all | solution.py:106
  116.5 0.4 dynamic-slice_reduce_fusion.1
  117.1 0.8 collective-permute-start.5
  118.2 2.8 %collective-permute-done.5 = bf16[16,24,96]{2,1,0:T(8,128)(2,1)S(1)} collective-permute-done((bf16[16,24,96]{2,1,0:T(8,128)(2,1)S(1)}, bf16[16,24,96]{2,1,0:T(8,128)(2,1)S(1)}, u32[]{:S(2)}, u32[]{:S(2)}) %collective-permute-start.5) | collective-permute-done | bytes 73760 | tf_op jit(solution)/shard_map/ppermute | solution.py:39
  121.0 1.8 %collective-permute-start.6 = (bf16[2,16,24,96]{3,2,1,0:T(8,128)(2,1)S(1)}, bf16[2,16,24,96]{3,2,1,0:T(8,128)(2,1)S(1)}, u32[]{:S(2)}, u32[]{:S(2)}) collective-permute-start(bf16[2,16,24,96]{3,2,1,0:T(8,128)(2,1)S(1)} %maximum_select_fusion.11), channel_id=1, source_target_pairs={{0,64},{64,0},{128,192},{192,128},{1,65},{65,1},{129,193},{193,129... | collective-permute-start | bytes 442376 | tf_op jit(solution)/shard_map/ppermute | solution.py:43
  122.8 3.5 %all-to-all-done.3 = bf16[32,2,1536]{2,1,0:T(2,128)(2,1)S(1)} async-done(((bf16[32,2,1536]{2,1,0:T(2,128)(2,1)}), bf16[32,2,1536]{2,1,0:T(2,128)(2,1)S(1)}, u32[]{:S(2)}, u32[]{:S(2)}) %all-to-all-start.3) | async-done | bytes 196640 | tf_op jit(solution)/shard_map/all_to_all | solution.py:106
  126.5 0.5 dynamic-slice_reduce_fusion
  127.1 0.8 collective-permute-start.12
  127.9 2.7 %collective-permute-done.12 = bf16[16,24,128]{2,1,0:T(8,128)(2,1)S(1)} collective-permute-done((bf16[16,24,128]{2,1,0:T(8,128)(2,1)S(1)}, bf16[16,24,128]{2,1,0:T(8,128)(2,1)S(1)}, u32[]{:S(2)}, u32[]{:S(2)}) %collective-permute-start.12) | collective-permute-done | bytes 98336 | tf_op jit(solution)/shard_map/ppermute | solution.py:39
  130.7 3.9 %collective-permute-start.13 = (bf16[2,16,24,128]{3,2,1,0:T(8,128)(2,1)S(1)}, bf16[2,16,24,128]{3,2,1,0:T(8,128)(2,1)S(1)}, u32[]{:S(2)}, u32[]{:S(2)}) collective-permute-start(bf16[2,16,24,128]{3,2,1,0:T(8,128)(2,1)S(1)} %maximum_select_fusion.13), channel_id=1, source_target_pairs={{0,64},{64,0},{128,192},{192,128},{1,65},{65,1},{129,193},{193,129... | collective-permute-start | bytes 589832 | tf_op jit(solution)/shard_map/ppermute | solution.py:43
  134.8 1.1 reshape.334
  136.0 0.3 copy.46
  136.3 1.0 reshape.337
  (50 shorter events, 4.5 us)
Async XLA Ops:
  0.6 5.8 %copy-start = (f32[1,24,8192]{2,1,0:T(8,128)S(1)}, f32[1,24,8192]{2,1,0:T(8,128)}, u32[]{:S(2)}) copy-start(f32[1,24,8192]{2,1,0:T(8,128)} %param.7) | copy-start | bytes 2359300
  3.1 5.5 %collective-permute-start = (f32[2,36864]{1,0:T(2,128)S(1)}, f32[2,36864]{1,0:T(2,128)S(1)}, u32[]{:S(2)}, u32[]{:S(2)}) collective-permute-start(f32[2,36864]{1,0:T(2,128)S(1)} %bitcast.89), channel_id=1, source_target_pairs={{0,64},{64,0},{128,192},{192,128},{1,65},{65,1},{129,193},{193,129... | collective-permute-start | bytes 884744 | tf_op jit(solution)/shard_map/ppermute | solution.py:29
  8.5 6.9 %collective-permute-start.7 = (f32[2,49152]{1,0:T(2,128)S(1)}, f32[2,49152]{1,0:T(2,128)S(1)}, u32[]{:S(2)}, u32[]{:S(2)}) collective-permute-start(f32[2,49152]{1,0:T(2,128)S(1)} %bitcast.83), channel_id=1, source_target_pairs={{0,64},{64,0},{128,192},{192,128},{1,65},{65,1},{129,193},{193,129... | collective-permute-start | bytes 1179656 | tf_op jit(solution)/shard_map/ppermute | solution.py:29
  9.2 5.0 %collective-permute-start.1 = (f32[36864]{0:T(1024)S(1)}, f32[36864]{0:T(1024)S(1)}, u32[]{:S(2)}, u32[]{:S(2)}) collective-permute-start(f32[36864]{0:T(1024)S(1)} %bitcast.94), channel_id=1, source_target_pairs={{0,128},{64,192},{128,0},{192,64},{1,129},{65,193},{129,1},{193,65... | collective-permute-start | bytes 442376 | tf_op jit(solution)/shard_map/ppermute | solution.py:32
  14.3 5.6 %collective-permute-start.2 = (f32[36864]{0:T(1024)S(1)}, f32[36864]{0:T(1024)S(1)}, u32[]{:S(2)}, u32[]{:S(2)}) collective-permute-start(f32[36864]{0:T(1024)S(1)} %add.60), channel_id=1, source_target_pairs={{0,1},{1,0},{2,3},{3,2},{4,5},{5,4},{6,7},{7,6},{8,9},{9,8},{10,11... | collective-permute-start | bytes 442376 | tf_op jit(solution)/shard_map/ppermute | solution.py:98
  21.2 23.1 %all-to-all-start = ((f32[32,1,2304]{2,1,0:T(1,128)}), f32[32,1,2304]{2,1,0:T(1,128)S(1)}, u32[]{:S(2)}, u32[]{:S(2)}) async-start(f32[32,1,2304]{2,1,0:T(1,128)} %all_to_all.32), calls=%async_computation | async-start | bytes 589824 | tf_op jit(solution)/shard_map/all_to_all | solution.py:101
  31.1 4.6 %collective-permute-start.8 = (f32[49152]{0:T(1024)S(1)}, f32[49152]{0:T(1024)S(1)}, u32[]{:S(2)}, u32[]{:S(2)}) collective-permute-start(f32[49152]{0:T(1024)S(1)} %bitcast.92), channel_id=1, source_target_pairs={{0,128},{64,192},{128,0},{192,64},{1,129},{65,193},{129,1},{193,65... | collective-permute-start | bytes 589832 | tf_op jit(solution)/shard_map/ppermute | solution.py:32
  35.7 7.8 %collective-permute-start.9 = (f32[49152]{0:T(1024)S(1)}, f32[49152]{0:T(1024)S(1)}, u32[]{:S(2)}, u32[]{:S(2)}) collective-permute-start(f32[49152]{0:T(1024)S(1)} %add.64), channel_id=1, source_target_pairs={{0,1},{1,0},{2,3},{3,2},{4,5},{5,4},{6,7},{7,6},{8,9},{9,8},{10,11... | collective-permute-start | bytes 589832 | tf_op jit(solution)/shard_map/ppermute | solution.py:98
  44.4 20.8 %all-to-all-start.2 = ((f32[32,1,3072]{2,1,0:T(1,128)}), f32[32,1,3072]{2,1,0:T(1,128)S(1)}, u32[]{:S(2)}, u32[]{:S(2)}) async-start(f32[32,1,3072]{2,1,0:T(1,128)} %bitcast.18), calls=%async_computation.2 | async-start | bytes 786432 | tf_op jit(solution)/shard_map/all_to_all | solution.py:101
  54.6 10.9 %collective-permute-start.3 = (f32[32,24,96]{2,1,0:T(8,128)S(1)}, f32[32,24,96]{2,1,0:T(8,128)S(1)}, u32[]{:S(2)}, u32[]{:S(2)}) collective-permute-start(f32[32,24,96]{2,1,0:T(8,128)S(1)} %reshape.332), channel_id=1, source_target_pairs={{0,128},{64,192},{128,0},{192,64},{1,129},{65,193},{129,1},{193,65... | collective-permute-start | bytes 884744 | tf_op jit(solution)/shard_map/ppermute | solution.py:39
  65.1 7.1 %collective-permute-start.10 = (f32[32,24,128]{2,1,0:T(8,128)S(1)}, f32[32,24,128]{2,1,0:T(8,128)S(1)}, u32[]{:S(2)}, u32[]{:S(2)}) collective-permute-start(f32[32,24,128]{2,1,0:T(8,128)S(1)} %bitcast.67), channel_id=1, source_target_pairs={{0,128},{64,192},{128,0},{192,64},{1,129},{65,193},{129,1},{193,65... | collective-permute-start | bytes 1179656 | tf_op jit(solution)/shard_map/ppermute | solution.py:39
  65.5 13.0 %collective-permute-start.4 = (f32[2,32,24,96]{3,2,1,0:T(8,128)S(1)}, f32[2,32,24,96]{3,2,1,0:T(8,128)}, u32[]{:S(2)}, u32[]{:S(2)}) collective-permute-start(f32[2,32,24,96]{3,2,1,0:T(8,128)S(1)} %maximum_select_fusion.3), channel_id=1, source_target_pairs={{0,64},{64,0},{128,192},{192,128},{1,65},{65,1},{129,193},{193,129... | collective-permute-start | bytes 1769480 | tf_op jit(solution)/shard_map/ppermute | solution.py:43
  72.3 23.7 %collective-permute-start.11 = (f32[2,32,24,128]{3,2,1,0:T(8,128)S(1)}, f32[2,32,24,128]{3,2,1,0:T(8,128)}, u32[]{:S(2)}, u32[]{:S(2)}) collective-permute-start(f32[2,32,24,128]{3,2,1,0:T(8,128)S(1)} %maximum_select_fusion.5), channel_id=1, source_target_pairs={{0,64},{64,0},{128,192},{192,128},{1,65},{65,1},{129,193},{193,129... | collective-permute-start | bytes 2359304 | tf_op jit(solution)/shard_map/ppermute | solution.py:43
  89.7 17.5 %all-to-all-start.1 = ((bf16[32,2,1152]{2,1,0:T(2,128)(2,1)}), bf16[32,2,1152]{2,1,0:T(2,128)(2,1)S(1)}, u32[]{:S(2)}, u32[]{:S(2)}) async-start(bf16[32,2,1152]{2,1,0:T(2,128)(2,1)} %reshape.347), calls=%async_computation.1 | async-start | bytes 294912 | tf_op jit(solution)/shard_map/all_to_all | solution.py:106
  107.2 19.2 %all-to-all-start.3 = ((bf16[32,2,1536]{2,1,0:T(2,128)(2,1)}), bf16[32,2,1536]{2,1,0:T(2,128)(2,1)S(1)}, u32[]{:S(2)}, u32[]{:S(2)}) async-start(bf16[32,2,1536]{2,1,0:T(2,128)(2,1)} %reshape.349), calls=%async_computation.3 | async-start | bytes 393216 | tf_op jit(solution)/shard_map/all_to_all | solution.py:106
  117.1 3.8 %collective-permute-start.5 = (bf16[16,24,96]{2,1,0:T(8,128)(2,1)S(1)}, bf16[16,24,96]{2,1,0:T(8,128)(2,1)S(1)}, u32[]{:S(2)}, u32[]{:S(2)}) collective-permute-start(bf16[16,24,96]{2,1,0:T(8,128)(2,1)S(1)} %reshape.333), channel_id=1, source_target_pairs={{0,128},{64,192},{128,0},{192,64},{1,129},{65,193},{129,1},{193,65... | collective-permute-start | bytes 221192 | tf_op jit(solution)/shard_map/ppermute | solution.py:39
  121.0 13.6 %collective-permute-start.6 = (bf16[2,16,24,96]{3,2,1,0:T(8,128)(2,1)S(1)}, bf16[2,16,24,96]{3,2,1,0:T(8,128)(2,1)S(1)}, u32[]{:S(2)}, u32[]{:S(2)}) collective-permute-start(bf16[2,16,24,96]{3,2,1,0:T(8,128)(2,1)S(1)} %maximum_select_fusion.11), channel_id=1, source_target_pairs={{0,64},{64,0},{128,192},{192,128},{1,65},{65,1},{129,193},{193,129... | collective-permute-start | bytes 442376 | tf_op jit(solution)/shard_map/ppermute | solution.py:43
  127.1 3.6 %collective-permute-start.12 = (bf16[16,24,128]{2,1,0:T(8,128)(2,1)S(1)}, bf16[16,24,128]{2,1,0:T(8,128)(2,1)S(1)}, u32[]{:S(2)}, u32[]{:S(2)}) collective-permute-start(bf16[16,24,128]{2,1,0:T(8,128)(2,1)S(1)} %bitcast.77), channel_id=1, source_target_pairs={{0,128},{64,192},{128,0},{192,64},{1,129},{65,193},{129,1},{193,65... | collective-permute-start | bytes 294920 | tf_op jit(solution)/shard_map/ppermute | solution.py:39
  130.7 5.3 %collective-permute-start.13 = (bf16[2,16,24,128]{3,2,1,0:T(8,128)(2,1)S(1)}, bf16[2,16,24,128]{3,2,1,0:T(8,128)(2,1)S(1)}, u32[]{:S(2)}, u32[]{:S(2)}) collective-permute-start(bf16[2,16,24,128]{3,2,1,0:T(8,128)(2,1)S(1)} %maximum_select_fusion.13), channel_id=1, source_target_pairs={{0,64},{64,0},{128,192},{192,128},{1,65},{65,1},{129,193},{193,129... | collective-permute-start | bytes 589832 | tf_op jit(solution)/shard_map/ppermute | solution.py:43

commit v6 on v3

--- a/solution.py
+++ b/solution.py
@@ -19,9 +19,11 @@
     return [(i, i ^ flip) for i in range(n)]
 
 
-def rep_scatter(x):
+def scatter_both_halves(x):
     r = lax.axis_index("rep")
     n = lax.axis_size("rep")
+    t = lax.axis_index("tp")
+    tensor = lax.axis_size("tp")
     core, x_lo = r % 2, r // 2
     x4 = x.reshape(2, 2, -1)
     mine = lax.dynamic_index_in_dim(x4, core, 1, keepdims=False)
@@ -29,7 +31,15 @@
     a = mine + lax.ppermute(other, "rep", pairs(n, 1))
     keep = lax.dynamic_index_in_dim(a, x_lo, 0, keepdims=False)
     send = lax.dynamic_index_in_dim(a, 1 - x_lo, 0, keepdims=False)
-    return keep + lax.ppermute(send, "rep", pairs(n, 2))
+    diagonal = [
+        (i * tensor + j, (i ^ 2) * tensor + (j ^ 1)) for i in range(n) for j in range(tensor)
+    ]
+    from_cross = lax.ppermute(send, "rep", pairs(n, 2))
+    from_partner = lax.ppermute(keep, "tp", pairs(tensor, 1))
+    from_diagonal = lax.ppermute(send, ("rep", "tp"), diagonal)
+    own = keep + from_cross
+    far = from_partner + from_diagonal
+    return jnp.where(t == 0, jnp.stack([own, far]), jnp.stack([far, own]))
 
 
 def rep_gather(x):
@@ -94,10 +104,7 @@
     ex = expert_change[0].reshape(mats, esize)
     tx = table_change[0].reshape(width, per_half, groups, sub)
     tx = jnp.transpose(tx, (2, 0, 1, 3)).reshape(groups, -1)
-    q = rep_scatter(jnp.concatenate([ex, tx], axis=1))
-
-    other = lax.ppermute(q, "tp", pairs(tensor, 1))
-    halves = jnp.where(t == 0, jnp.stack([q, other]), jnp.stack([other, q]))
+    halves = scatter_both_halves(jnp.concatenate([ex, tx], axis=1))
     he = halves[:, :esize].reshape(tensor, width, per_half, rows)
     he = jnp.transpose(he, (0, 2, 1, 3)).reshape(shards, width * rows)
     ht = halves[:, esize:].reshape(tensor, width, per_half, sub)

time: 134 us -> 136 us (1.015)
  blocking collectives: 27.3 us -> 29.1 us
  starting transfers between devices: 29.4 us -> 31.2 us
  waiting for transfers between devices: 42.4 us -> 40.6 us
    ppermute x3 -> x4, waiting for transfers between devices: 19.9 us -> 17 us  [the longest x1 7.84 us: scatter_both_halves(): from_partner = lax.ppermute(keep, 'tp', pairs(tensor, 1))]
    ppermute x3 -> x4, starting transfers between devices: 4.51 us -> 7.27 us  [the longest x1 3.33 us: scatter_both_halves(): a = mine + lax.ppermute(other, 'rep', pairs(n, 1))]
    all_to_all x1, blocking collectives: 27.3 us -> 29.1 us  [local(): lax.all_to_all(jnp.concatenate([he, ht], 1), 'shard', 0, 0, tiled=True)]
  transfers between devices with their start and end apart: 10 -> 11, of which waited for: 7 -> 8; matrix products, arithmetic and copies ran while one was open for 4% -> 4% of each run, Pallas kernels for 3% -> 3%
where the time goes in v6:
time: 136 us
  waiting for transfers between devices  40.6 us (30%)
  starting transfers between devices  31.2 us (23%)
  blocking collectives  29.1 us (21%)
  local copies, waits for them, and re-layouts  15 us (11%)
  Pallas kernels  9.36 us (7%)
  other arithmetic  9.28 us (7%)
    all_to_all x1, blocking collectives, local(): lax.all_to_all(jnp.concatenate([he, ht], 1), 'shard', 0, 0, tiled=True)  29.1 us
    ppermute x3, starting transfers between devices, rep_gather(): sib = lax.ppermute(pair, 'rep', pairs(n, 1))  15.6 us
    all_to_all x1, waiting for transfers between devices, local(): lax.all_to_all(jnp.concatenate([le, lt], 1), 'shard', 0, 0, tiled=True)  13.5 us
    pallas_call x2, Pallas kernels, fused_update(): pl.pallas_call(lambda *refs: update_kernel(scale, *refs), grid=(quarters,...  9.36 us
    ppermute x3, waiting for transfers between devices, rep_gather(): cross = lax.ppermute(x, 'rep', pairs(n, 2))  8.76 us
    ppermute x1, waiting for transfers between devices, scatter_both_halves(): from_partner = lax.ppermute(keep, 'tp', pairs(tensor, 1))  7.84 us
    all_to_all x1, starting transfers between devices, local(): lax.all_to_all(jnp.concatenate([le, lt], 1), 'shard', 0, 0, tiled=True)  6.5 us
    select_n x3, other arithmetic, rep_gather(): jnp.where(core == 0, jnp.stack([a, b], 1), jnp.stack([b, a], 1))  5.43 us
  transfers between devices with their start and end apart: 11, of which 8 were waited for; matrix products, arithmetic and copies ran while one was open for 4% of the time, Pallas kernels for 3%

profile of v6, /device:TPU:1, one launch (start us, length us, event | category | flops | bytes accessed | tf_op | source)
XLA Modules:
  0.0 135.6 jit_solution(9526820344621053363)
XLA Ops:
  0.7 1.6 %concatenate.56 = f32[2,2,36864]{2,1,0:T(2,128)S(1)} reshape(f32[1,4,24,1536]{3,2,1,0:T(8,128)} %param.6) | data formatting | bytes 1179648 | tf_op jit(solution)/shard_map/concatenate | solution.py:107
  2.4 0.5 reshape_squeeze.4
  3.0 0.5 concatenate.57
  3.6 1.2 constant_dynamic-slice_fusion.6
  4.8 0.5 copy.52
  5.3 3.3 %collective-permute-start = (f32[2,86016]{1,0:T(2,128)S(1)}, f32[2,86016]{1,0:T(2,128)S(1)}, u32[]{:S(2)}, u32[]{:S(2)}) collective-permute-start(f32[2,86016]{1,0:T(2,128)S(1)} %bitcast.104), channel_id=1, source_target_pairs={{0,64},{64,0},{128,192},{192,128},{1,65},{65,1},{129,193},{193,129... | collective-permute-start | bytes 2064392 | tf_op jit(solution)/shard_map/ppermute | solution.py:31
  8.6 1.8 %collective-permute-done = f32[2,86016]{1,0:T(2,128)S(1)} collective-permute-done((f32[2,86016]{1,0:T(2,128)S(1)}, f32[2,86016]{1,0:T(2,128)S(1)}, u32[]{:S(2)}, u32[]{:S(2)}) %collective-permute-start) | collective-permute-done | bytes 688160 | tf_op jit(solution)/shard_map/ppermute | solution.py:31
  10.4 0.7 bitcast_add_fusion
  11.1 0.6 constant_dynamic-slice_fusion.3
  11.8 1.9 %collective-permute-start.2 = (f32[86016]{0:T(1024)S(1)}, f32[86016]{0:T(1024)S(1)}, u32[]{:S(2)}, u32[]{:S(2)}) collective-permute-start(f32[86016]{0:T(1024)S(1)} %bitcast.100), channel_id=1, source_target_pairs={{0,1},{1,0},{2,3},{3,2},{4,5},{5,4},{6,7},{7,6},{8,9},{9,8},{10,11... | collective-permute-start | bytes 1032200 | tf_op jit(solution)/shard_map/ppermute | solution.py:38
  13.7 1.9 %collective-permute-start.3 = (f32[86016]{0:T(1024)S(1)}, f32[86016]{0:T(1024)S(1)}, u32[]{:S(2)}, u32[]{:S(2)}) collective-permute-start(f32[86016]{0:T(1024)S(1)} %bitcast.108), channel_id=1, source_target_pairs={{0,129},{1,128},{64,193},{65,192},{128,1},{129,0},{192,65},{193,64... | collective-permute-start | bytes 1032200 | tf_op jit(solution)/shard_map/ppermute | solution.py:39
  15.7 5.4 %collective-permute-done.1 = f32[86016]{0:T(1024)S(1)} collective-permute-done((f32[86016]{0:T(1024)S(1)}, f32[86016]{0:T(1024)S(1)}, u32[]{:S(2)}, u32[]{:S(2)}) %collective-permute-start.1) | collective-permute-done | bytes 344096 | tf_op jit(solution)/shard_map/ppermute | solution.py:37
  21.1 7.8 %collective-permute-done.2 = f32[86016]{0:T(1024)S(1)} collective-permute-done((f32[86016]{0:T(1024)S(1)}, f32[86016]{0:T(1024)S(1)}, u32[]{:S(2)}, u32[]{:S(2)}) %collective-permute-start.2) | collective-permute-done | bytes 344096 | tf_op jit(solution)/shard_map/ppermute | solution.py:38
  28.9 2.0 %collective-permute-done.3 = f32[86016]{0:T(1024)S(1)} collective-permute-done((f32[86016]{0:T(1024)S(1)}, f32[86016]{0:T(1024)S(1)}, u32[]{:S(2)}, u32[]{:S(2)}) %collective-permute-start.3) | collective-permute-done | bytes 344096 | tf_op jit(solution)/shard_map/ppermute | solution.py:39
  31.0 1.0 maximum_select_fusion.6
  32.3 0.3 reshape.254
  32.7 0.1 reshape.255
  32.9 0.7 copy.27
  33.6 29.1 %all_to_all.21 = f32[32,1,5376]{2,1,0:T(1,128)S(1)} all-to-all(f32[32,1,5376]{2,1,0:T(1,128)S(1)} %copy.27), channel_id=1, replica_groups=mesh['rep'=4,'shard'=32,'tp'=2] {'shard'}, dimensions={0} | all-to-all | bytes 1376256 | tf_op jit(solution)/shard_map/all_to_all | solution.py:112
  62.8 0.3 reshape.258
  63.3 1.7 %collective-permute-start.6 = (f32[32,24,128]{2,1,0:T(8,128)S(1)}, f32[32,24,128]{2,1,0:T(8,128)S(1)}, u32[]{:S(2)}, u32[]{:S(2)}) collective-permute-start(f32[32,24,128]{2,1,0:T(8,128)S(1)} %bitcast.78), channel_id=1, source_target_pairs={{0,128},{64,192},{128,0},{192,64},{1,129},{65,193},{129,1},{193,65... | collective-permute-start | bytes 1179656 | tf_op jit(solution)/shard_map/ppermute | solution.py:49
  65.0 0.3 stack_reshape.8
  65.2 4.5 %collective-permute-done.4 = f32[32,24,96]{2,1,0:T(8,128)S(1)} collective-permute-done((f32[32,24,96]{2,1,0:T(8,128)S(1)}, f32[32,24,96]{2,1,0:T(8,128)S(1)}, u32[]{:S(2)}, u32[]{:S(2)}) %collective-permute-start.4) | collective-permute-done | bytes 294944 | tf_op jit(solution)/shard_map/ppermute | solution.py:49
  69.8 0.9 maximum_select_fusion.3
  70.7 9.1 %collective-permute-start.5 = (f32[2,32,24,96]{3,2,1,0:T(8,128)}, f32[2,32,24,96]{3,2,1,0:T(8,128)}, u32[]{:S(2)}, u32[]{:S(2)}) collective-permute-start(f32[2,32,24,96]{3,2,1,0:T(8,128)} %maximum_select_fusion.3), channel_id=1, source_target_pairs={{0,64},{64,0},{128,192},{192,128},{1,65},{65,1},{129,193},{193,129... | collective-permute-start | bytes 1769480 | tf_op jit(solution)/shard_map/ppermute | solution.py:53
  79.9 3.4 %collective-permute-start.7 = (f32[2,32,24,128]{3,2,1,0:T(8,128)S(1)}, f32[2,32,24,128]{3,2,1,0:T(8,128)}, u32[]{:S(2)}, u32[]{:S(2)}) collective-permute-start(f32[2,32,24,128]{3,2,1,0:T(8,128)S(1)} %maximum_select_fusion.5), channel_id=1, source_target_pairs={{0,64},{64,0},{128,192},{192,128},{1,65},{65,1},{129,193},{193,129... | collective-permute-start | bytes 2359304 | tf_op jit(solution)/shard_map/ppermute | solution.py:53
  83.2 0.3 stack.112
  83.6 2.7 %maximum_select_fusion = f32[2,2,32,24,96]{4,3,2,1,0:T(8,128)} fusion(f32[2,1,32,24,96]{4,3,2,1,0:T(8,128)} %bitcast.10, f32[2,1,32,24,96]{4,3,2,1,0:T(8,128)S(1)} %maximum_select_fusion.2, pred[]{:T(512)S(6)} %eq.17), kind=kLoop, calls=%fused_computation | loop fusion | flops 884736 | bytes 2359297 | tf_op jit(solution)/shard_map/jit(_where)/select_n | solution.py:55
  86.3 4.5 %shard_map.109 = (f32[4,96,768]{2,1,0:T(8,128)}, f32[4,96,768]{2,1,0:T(8,128)}, bf16[4,768,96]{2,1,0:T(8,128)(2,1)}) custom-call(f32[4,32,24,96]{3,2,1,0:T(8,128)} %bitcast.76, f32[4,96,768]{2,1,0:T(8,128)} %refs_1_.2, f32[4,96,768]{2,1,0:T(8,128)} %refs_2_.2), custom_call_target="tpu_custom_call" | custom-call | tf_op jit(solution)/shard_map/pallas_call | solution.py:79
  90.8 0.9 constant_dynamic-slice_fusion.2
  91.7 0.2 reshape.259
  91.9 2.7 %maximum_select_fusion.1 = f32[2,2,32,24,128]{4,3,2,1,0:T(8,128)} fusion(f32[2,1,32,24,128]{4,3,2,1,0:T(8,128)} %bitcast.14, f32[2,1,32,24,128]{4,3,2,1,0:T(8,128)S(1)} %maximum_select_fusion.4, pred[]{:T(512)S(6)} %eq.17), kind=kLoop, calls=%fused_computation.1 | loop fusion | flops 1179648 | bytes 3145729 | tf_op jit(solution)/shard_map/jit(_where)/select_n | solution.py:55
  94.6 4.9 %shard_map.110 = (f32[512,768]{1,0:T(8,128)}, f32[512,768]{1,0:T(8,128)}, bf16[4,768,128]{2,1,0:T(8,128)(2,1)}) custom-call(f32[4,32,24,128]{3,2,1,0:T(8,128)} %bitcast.77, f32[512,768]{1,0:T(8,128)} %refs_1_.3, f32[512,768]{1,0:T(8,128)} %refs_2_.3), custom_call_target="tpu_custom_call" | custom-call | tf_op jit(solution)/shard_map/pallas_call | solution.py:79
  99.5 0.9 constant_dynamic-slice_fusion.1
  100.5 0.5 broadcast.32
  101.1 0.8 reduce
  101.9 0.8 reshape.266
  102.7 6.5 %all-to-all-start.1 = ((bf16[32,2,2688]{2,1,0:T(2,128)(2,1)}), bf16[32,2,2688]{2,1,0:T(2,128)(2,1)S(1)}, u32[]{:S(2)}, u32[]{:S(2)}) async-start(bf16[32,2,2688]{2,1,0:T(2,128)(2,1)} %reshape.266), calls=%async_computation.1 | async-start | bytes 688128 | tf_op jit(solution)/shard_map/all_to_all | solution.py:128
  109.2 13.5 %all-to-all-done.1 = bf16[32,2,2688]{2,1,0:T(2,128)(2,1)S(1)} async-done(((bf16[32,2,2688]{2,1,0:T(2,128)(2,1)}), bf16[32,2,2688]{2,1,0:T(2,128)(2,1)S(1)}, u32[]{:S(2)}, u32[]{:S(2)}) %all-to-all-start.1) | async-done | bytes 344096 | tf_op jit(solution)/shard_map/all_to_all | solution.py:128
  122.8 0.3 reshape.267
  123.1 0.4 constant_dynamic-slice_fusion
  123.6 4.2 %collective-permute-done.8 = bf16[16,5376]{1,0:T(8,128)(2,1)S(1)} collective-permute-done((bf16[16,5376]{1,0:T(8,128)(2,1)S(1)}, bf16[16,5376]{1,0:T(8,128)(2,1)S(1)}, u32[]{:S(2)}, u32[]{:S(2)}) %collective-permute-start.8) | collective-permute-done | bytes 172064 | tf_op jit(solution)/shard_map/ppermute | solution.py:49
  127.8 3.1 %collective-permute-start.9 = (bf16[2,16,5376]{2,1,0:T(8,128)(2,1)S(1)}, bf16[2,16,5376]{2,1,0:T(8,128)(2,1)S(1)}, u32[]{:S(2)}, u32[]{:S(2)}) collective-permute-start(bf16[2,16,5376]{2,1,0:T(8,128)(2,1)S(1)} %maximum_select_fusion.9), channel_id=1, source_target_pairs={{0,64},{64,0},{128,192},{192,128},{1,65},{65,1},{129,193},{193,129... | collective-permute-start | bytes 1032200 | tf_op jit(solution)/shard_map/ppermute | solution.py:53
  131.0 1.2 collective-permute-done.9
  132.5 0.3 copy.31
  132.8 1.0 reshape.265
  133.8 0.6 reshape.262
  134.5 1.1 reshape.263
  (38 shorter events, 1.8 us)
Async XLA Ops:
  0.6 1.7 %copy-start = (f32[1,24,8192]{2,1,0:T(8,128)S(1)}, f32[1,24,8192]{2,1,0:T(8,128)}, u32[]{:S(2)}) copy-start(f32[1,24,8192]{2,1,0:T(8,128)} %param.7) | copy-start | bytes 2359300
  5.3 5.1 %collective-permute-start = (f32[2,86016]{1,0:T(2,128)S(1)}, f32[2,86016]{1,0:T(2,128)S(1)}, u32[]{:S(2)}, u32[]{:S(2)}) collective-permute-start(f32[2,86016]{1,0:T(2,128)S(1)} %bitcast.104), channel_id=1, source_target_pairs={{0,64},{64,0},{128,192},{192,128},{1,65},{65,1},{129,193},{193,129... | collective-permute-start | bytes 2064392 | tf_op jit(solution)/shard_map/ppermute | solution.py:31
  11.7 9.4 %collective-permute-start.1 = (f32[86016]{0:T(1024)S(1)}, f32[86016]{0:T(1024)S(1)}, u32[]{:S(2)}, u32[]{:S(2)}) collective-permute-start(f32[86016]{0:T(1024)S(1)} %bitcast.107), channel_id=1, source_target_pairs={{0,128},{64,192},{128,0},{192,64},{1,129},{65,193},{129,1},{193,65... | collective-permute-start | bytes 1032200 | tf_op jit(solution)/shard_map/ppermute | solution.py:37
  11.8 17.1 %collective-permute-start.2 = (f32[86016]{0:T(1024)S(1)}, f32[86016]{0:T(1024)S(1)}, u32[]{:S(2)}, u32[]{:S(2)}) collective-permute-start(f32[86016]{0:T(1024)S(1)} %bitcast.100), channel_id=1, source_target_pairs={{0,1},{1,0},{2,3},{3,2},{4,5},{5,4},{6,7},{7,6},{8,9},{9,8},{10,11... | collective-permute-start | bytes 1032200 | tf_op jit(solution)/shard_map/ppermute | solution.py:38
  13.7 17.2 %collective-permute-start.3 = (f32[86016]{0:T(1024)S(1)}, f32[86016]{0:T(1024)S(1)}, u32[]{:S(2)}, u32[]{:S(2)}) collective-permute-start(f32[86016]{0:T(1024)S(1)} %bitcast.108), channel_id=1, source_target_pairs={{0,129},{1,128},{64,193},{65,192},{128,1},{129,0},{192,65},{193,64... | collective-permute-start | bytes 1032200 | tf_op jit(solution)/shard_map/ppermute | solution.py:39
  63.1 6.7 %collective-permute-start.4 = (f32[32,24,96]{2,1,0:T(8,128)S(1)}, f32[32,24,96]{2,1,0:T(8,128)S(1)}, u32[]{:S(2)}, u32[]{:S(2)}) collective-permute-start(f32[32,24,96]{2,1,0:T(8,128)S(1)} %reshape.258), channel_id=1, source_target_pairs={{0,128},{64,192},{128,0},{192,64},{1,129},{65,193},{129,1},{193,65... | collective-permute-start | bytes 884744 | tf_op jit(solution)/shard_map/ppermute | solution.py:49
  63.3 16.6 %collective-permute-start.6 = (f32[32,24,128]{2,1,0:T(8,128)S(1)}, f32[32,24,128]{2,1,0:T(8,128)S(1)}, u32[]{:S(2)}, u32[]{:S(2)}) collective-permute-start(f32[32,24,128]{2,1,0:T(8,128)S(1)} %bitcast.78), channel_id=1, source_target_pairs={{0,128},{64,192},{128,0},{192,64},{1,129},{65,193},{129,1},{193,65... | collective-permute-start | bytes 1179656 | tf_op jit(solution)/shard_map/ppermute | solution.py:49
  70.7 12.9 %collective-permute-start.5 = (f32[2,32,24,96]{3,2,1,0:T(8,128)}, f32[2,32,24,96]{3,2,1,0:T(8,128)}, u32[]{:S(2)}, u32[]{:S(2)}) collective-permute-start(f32[2,32,24,96]{3,2,1,0:T(8,128)} %maximum_select_fusion.3), channel_id=1, source_target_pairs={{0,64},{64,0},{128,192},{192,128},{1,65},{65,1},{129,193},{193,129... | collective-permute-start | bytes 1769480 | tf_op jit(solution)/shard_map/ppermute | solution.py:53
  79.9 12.0 %collective-permute-start.7 = (f32[2,32,24,128]{3,2,1,0:T(8,128)S(1)}, f32[2,32,24,128]{3,2,1,0:T(8,128)}, u32[]{:S(2)}, u32[]{:S(2)}) collective-permute-start(f32[2,32,24,128]{3,2,1,0:T(8,128)S(1)} %maximum_select_fusion.5), channel_id=1, source_target_pairs={{0,64},{64,0},{128,192},{192,128},{1,65},{65,1},{129,193},{193,129... | collective-permute-start | bytes 2359304 | tf_op jit(solution)/shard_map/ppermute | solution.py:53
  102.7 20.1 %all-to-all-start.1 = ((bf16[32,2,2688]{2,1,0:T(2,128)(2,1)}), bf16[32,2,2688]{2,1,0:T(2,128)(2,1)S(1)}, u32[]{:S(2)}, u32[]{:S(2)}) async-start(bf16[32,2,2688]{2,1,0:T(2,128)(2,1)} %reshape.266), calls=%async_computation.1 | async-start | bytes 688128 | tf_op jit(solution)/shard_map/all_to_all | solution.py:128
  123.5 4.3 %collective-permute-start.8 = (bf16[16,5376]{1,0:T(8,128)(2,1)S(1)}, bf16[16,5376]{1,0:T(8,128)(2,1)S(1)}, u32[]{:S(2)}, u32[]{:S(2)}) collective-permute-start(bf16[16,5376]{1,0:T(8,128)(2,1)S(1)} %bitcast.97), channel_id=1, source_target_pairs={{0,128},{64,192},{128,0},{192,64},{1,129},{65,193},{129,1},{193,65... | collective-permute-start | bytes 516104 | tf_op jit(solution)/shard_map/ppermute | solution.py:49
  127.8 4.4 %collective-permute-start.9 = (bf16[2,16,5376]{2,1,0:T(8,128)(2,1)S(1)}, bf16[2,16,5376]{2,1,0:T(8,128)(2,1)S(1)}, u32[]{:S(2)}, u32[]{:S(2)}) collective-permute-start(bf16[2,16,5376]{2,1,0:T(8,128)(2,1)S(1)} %maximum_select_fusion.9), channel_id=1, source_target_pairs={{0,64},{64,0},{128,192},{192,128},{1,65},{65,1},{129,193},{193,129... | collective-permute-start | bytes 1032200 | tf_op jit(solution)/shard_map/ppermute | solution.py:53

commit v7 on v3

--- a/solution.py
+++ b/solution.py
@@ -47,14 +47,13 @@
     return jax.tree.map(lambda a, f: f.reshape((n,) + a.shape), x, full)
 
 
-def update_kernel(scale, mean_ref, master_ref, moment_ref, w_ref, v_ref, low_ref):
+def update_kernel(scale, mean_ref, master_ref, moment_ref, w_ref, v_ref):
     x = mean_ref[0]
     x = x.reshape(x.shape[0] * x.shape[1], x.shape[2])
     mean = x.T * scale
     weights, velocity = update(master_ref[...], moment_ref[...], mean.reshape(master_ref.shape))
     w_ref[...] = weights
     v_ref[...] = velocity
-    low_ref[0] = weights.reshape(mean.shape).T.astype(low_ref.dtype)
 
 
 def fused_update(got, master, moment, scale):
@@ -70,11 +69,10 @@
         lambda *refs: update_kernel(scale, *refs),
         grid=(quarters,),
         in_specs=[pl.BlockSpec((1, srcs, wdt, cols), lambda q: (q, 0, 0, 0)), big, big],
-        out_specs=[big, big, pl.BlockSpec((1, srcs * wdt, cols), lambda q: (q, 0, 0))],
+        out_specs=[big, big],
         out_shape=[
             jax.ShapeDtypeStruct(master.shape, master.dtype),
             jax.ShapeDtypeStruct(master.shape, master.dtype),
-            jax.ShapeDtypeStruct((quarters, srcs * wdt, cols), jnp.bfloat16),
         ],
     )(got, master, moment)
 
@@ -106,19 +104,33 @@
 
     ge = got[:, : width * rows].reshape(shards, width, rows)
     gt = got[:, width * rows :].reshape(shards, width, sub)
+
+    r = lax.axis_index("rep")
+    own_e = jnp.transpose(ge.reshape(shards * width, rows)) / groups
+    own_e, _ = update(
+        lax.dynamic_index_in_dim(expert_master, r, 0, keepdims=False),
+        lax.dynamic_index_in_dim(expert_moment, r, 0, keepdims=False),
+        own_e,
+    )
+    le = jnp.transpose(own_e.astype(jnp.bfloat16).reshape(rows, shards, width), (1, 2, 0))
+    own_t = jnp.transpose(gt.reshape(shards * width, sub)) / groups
+    own_t, _ = update(
+        lax.dynamic_slice_in_dim(table_master, r * sub, sub, 0),
+        lax.dynamic_slice_in_dim(table_moment, r * sub, sub, 0),
+        own_t,
+    )
+    lt = jnp.transpose(own_t.astype(jnp.bfloat16).reshape(sub, shards, width), (1, 2, 0))
+    back = jnp.concatenate([le.reshape(shards, -1), lt.reshape(shards, -1)], 1)
+    back = lax.all_to_all(back, "shard", 0, 0, tiled=True)
+
     every_e, every_t = rep_gather((ge, gt))
-
-    expert_weights, expert_velocity, low_e = fused_update(
+    expert_weights, expert_velocity = fused_update(
         every_e, expert_master, expert_moment, 1.0 / groups
     )
-    table_weights, table_velocity, low_t = fused_update(
+    table_weights, table_velocity = fused_update(
         every_t, table_master, table_moment, 1.0 / groups
     )
 
-    r = lax.axis_index("rep")
-    le = lax.dynamic_index_in_dim(low_e, r, 0, keepdims=False).reshape(shards, width * rows)
-    lt = lax.dynamic_index_in_dim(low_t, r, 0, keepdims=False).reshape(shards, width * sub)
-    back = lax.all_to_all(jnp.concatenate([le, lt], 1), "shard", 0, 0, tiled=True)
     back = lax.dynamic_slice_in_dim(back, t * per_half, per_half, 0)
     allq = rep_gather(back)
     ce = allq[:, :, : width * rows].reshape(groups, per_half, width, rows)

time: 134 us -> 115 us (0.86)
  blocking collectives: 27.3 us -> 0 us
  starting transfers between devices: 29.4 us -> 35.6 us
  local copies, waits for them, and re-layouts: 15 us -> 17.2 us
  waiting for transfers between devices: 42.4 us -> 41 us
    all_to_all x1 -> x0, blocking collectives: 27.3 us -> none  [local(): lax.all_to_all(jnp.concatenate([he, ht], 1), 'shard', 0, 0, tiled=True)]
    all_to_all x1 -> x2, starting transfers between devices: 6.36 us -> 15.8 us  [the longest x1 9.47 us: local(): lax.all_to_all(jnp.concatenate([he, ht], 1), 'shard', 0, 0, tiled=True)]
    ppermute x3, starting transfers between devices: 15.6 us -> 12.4 us  [rep_gather(): sib = lax.ppermute(pair, 'rep', pairs(n, 1))]
    ppermute x3, waiting for transfers between devices: 7.75 us -> 5.99 us  [rep_gather(): cross = lax.ppermute(x, 'rep', pairs(n, 2))]
    all_to_all x1 -> x2, waiting for transfers between devices: 13.5 us -> 15.1 us  [the longest x1 15.1 us: local(): lax.all_to_all(jnp.concatenate([he, ht], 1), 'shard', 0, 0, tiled=True)]
  transfers between devices with their start and end apart: 10 -> 11, of which waited for: 7 -> 5; matrix products, arithmetic and copies ran while one was open for 4% -> 10% of each run, Pallas kernels for 3% -> 8%
where the time goes in v7:
time: 115 us; the launch traced here: 114 us
  waiting for transfers between devices  41 us (36%)
  starting transfers between devices  35.6 us (31%)
  local copies, waits for them, and re-layouts  17.2 us (15%)
  other arithmetic  10.3 us (9%)
  Pallas kernels  9.04 us (8%)
    all_to_all x1, waiting for transfers between devices, local(): lax.all_to_all(jnp.concatenate([he, ht], 1), 'shard', 0, 0, tiled=True)  15.1 us
    ppermute x3, starting transfers between devices, rep_gather(): sib = lax.ppermute(pair, 'rep', pairs(n, 1))  12.4 us
    all_to_all x1, starting transfers between devices, local(): lax.all_to_all(jnp.concatenate([he, ht], 1), 'shard', 0, 0, tiled=True)  9.47 us
    ppermute x1, waiting for transfers between devices, rep_scatter(): return keep + lax.ppermute(send, 'rep', pairs(n, 2))  9.26 us
    pallas_call x2, Pallas kernels, fused_update(): pl.pallas_call(lambda *refs: update_kernel(scale, *refs), grid=(quarters,...  9.04 us
    ppermute x1, waiting for transfers between devices, local(): other = lax.ppermute(q, 'tp', pairs(tensor, 1))  8.85 us
    all_to_all x1, starting transfers between devices, local(): back = lax.all_to_all(back, 'shard', 0, 0, tiled=True)  6.35 us
    ppermute x3, waiting for transfers between devices, rep_gather(): cross = lax.ppermute(x, 'rep', pairs(n, 2))  5.99 us
  transfers between devices with their start and end apart: 11, of which 5 were waited for; matrix products, arithmetic and copies ran while one was open for 10% of the time, Pallas kernels for 8%

profile of v7, /device:TPU:1, one launch (start us, length us, event | category | flops | bytes accessed | tf_op | source)
XLA Modules:
  0.0 114.2 jit_solution(17863341515088116787)
XLA Ops:
  0.7 1.6 %concatenate.56 = f32[2,2,36864]{2,1,0:T(2,128)S(1)} reshape(f32[1,4,24,1536]{3,2,1,0:T(8,128)} %param.6) | data formatting | bytes 1179648 | tf_op jit(solution)/shard_map/concatenate | solution.py:95
  2.4 0.5 reshape_squeeze.4
  3.0 0.5 concatenate.57
  3.6 1.2 %constant_dynamic-slice_fusion.8 = (f32[2,1,86016]{2,1,0:T(1,128)S(1)}, f32[2,1,86016]{2,1,0:T(1,128)S(1)}) fusion(f32[2,2,86016]{2,1,0:T(2,128)S(1)} %constant_dynamic-update-slice_fusion, s32[]{:T(128)S(6)} %select_n.149, s32[]{:T(128)S(6)} %select_n.150), kind=kLoop, calls=%fused_computation.45 | loop fusion | bytes 2752520 | tf_op jit(solution)/shard_map/jit(dynamic_index_in_dim)/dynamic_slice | solution.py:27
  4.8 0.5 copy.74
  5.3 3.3 %collective-permute-start = (f32[2,86016]{1,0:T(2,128)S(1)}, f32[2,86016]{1,0:T(2,128)S(1)}, u32[]{:S(2)}, u32[]{:S(2)}) collective-permute-start(f32[2,86016]{1,0:T(2,128)S(1)} %bitcast.144), channel_id=1, source_target_pairs={{0,64},{64,0},{128,192},{192,128},{1,65},{65,1},{129,193},{193,129... | collective-permute-start | bytes 2064392 | tf_op jit(solution)/shard_map/ppermute | solution.py:29
  8.6 1.8 %collective-permute-done = f32[2,86016]{1,0:T(2,128)S(1)} collective-permute-done((f32[2,86016]{1,0:T(2,128)S(1)}, f32[2,86016]{1,0:T(2,128)S(1)}, u32[]{:S(2)}, u32[]{:S(2)}) %collective-permute-start) | collective-permute-done | bytes 688160 | tf_op jit(solution)/shard_map/ppermute | solution.py:29
  10.4 0.7 bitcast_add_fusion
  11.1 0.6 constant_dynamic-slice_fusion.5
  11.8 9.3 %collective-permute-done.1 = f32[86016]{0:T(1024)S(1)} collective-permute-done((f32[86016]{0:T(1024)S(1)}, f32[86016]{0:T(1024)S(1)}, u32[]{:S(2)}, u32[]{:S(2)}) %collective-permute-start.1) | collective-permute-done | bytes 344096 | tf_op jit(solution)/shard_map/ppermute | solution.py:32
  21.1 1.1 collective-permute-start.2
  22.2 8.8 %collective-permute-done.2 = f32[86016]{0:T(1024)S(1)} collective-permute-done((f32[86016]{0:T(1024)S(1)}, f32[86016]{0:T(1024)S(1)}, u32[]{:S(2)}, u32[]{:S(2)}) %collective-permute-start.2) | collective-permute-done | bytes 344096 | tf_op jit(solution)/shard_map/ppermute | solution.py:97
  31.1 1.0 maximum_select_fusion.6
  32.3 0.3 reshape.264
  33.0 1.6 %copy.40 = f32[32,1,5376]{2,1,0:T(1,128)} copy(f32[32,1,5376]{2,0,1:T(8,128)S(1)} %maximum_bitcast_fusion) | data formatting | bytes 1376256 | tf_op jit(solution)/shard_map/all_to_all | solution.py:103
  34.5 9.5 %all-to-all-start = ((f32[32,1,5376]{2,1,0:T(1,128)}), f32[32,1,5376]{2,1,0:T(1,128)S(1)}, u32[]{:S(2)}, u32[]{:S(2)}) async-start(f32[32,1,5376]{2,1,0:T(1,128)} %copy.40), calls=%async_computation | async-start | bytes 1376256 | tf_op jit(solution)/shard_map/all_to_all | solution.py:103
  44.0 1.1 constant_dynamic-slice_fusion.3
  45.1 0.2 copy.52
  45.3 0.2 copy.41
  45.4 1.2 %constant_dynamic-slice_fusion.1 = (f32[128,768]{1,0:T(8,128)S(1)}, f32[128,768]{1,0:T(8,128)S(1)}) fusion(f32[512,768]{1,0:T(8,128)} %refs_2_.3, s32[]{:T(128)S(6)} %select_n.162, f32[512,768]{1,0:T(8,128)} %refs_1_.3), kind=kLoop, calls=%fused_computation.38 | loop fusion | bytes 1572868 | tf_op jit(solution)/shard_map/dynamic_slice | solution.py:119
  47.0 15.1 %all-to-all-done = f32[32,1,5376]{2,1,0:T(1,128)S(1)} async-done(((f32[32,1,5376]{2,1,0:T(1,128)}), f32[32,1,5376]{2,1,0:T(1,128)S(1)}, u32[]{:S(2)}, u32[]{:S(2)}) %all-to-all-start) | async-done | bytes 688160 | tf_op jit(solution)/shard_map/all_to_all | solution.py:103
  62.2 0.3 div.35
  63.0 0.5 broadcast.58
  63.5 0.8 reduce
  64.4 0.8 reshape.278
  65.2 6.3 %all-to-all-start.1 = ((bf16[32,2,2688]{2,1,0:T(2,128)(2,1)}), bf16[32,2,2688]{2,1,0:T(2,128)(2,1)S(1)}, u32[]{:S(2)}, u32[]{:S(2)}) async-start(bf16[32,2,2688]{2,1,0:T(2,128)(2,1)} %reshape.278), calls=%async_computation.1 | async-start | bytes 688128 | tf_op jit(solution)/shard_map/all_to_all | solution.py:124
  71.6 0.3 reshape.268
  71.8 1.3 %collective-permute-start.3 = (f32[32,24,96]{2,1,0:T(8,128)S(1)}, f32[32,24,96]{2,1,0:T(8,128)S(1)}, u32[]{:S(2)}, u32[]{:S(2)}) collective-permute-start(f32[32,24,96]{2,1,0:T(8,128)S(1)} %reshape.268), channel_id=1, source_target_pairs={{0,128},{64,192},{128,0},{192,64},{1,129},{65,193},{129,1},{193,65... | collective-permute-start | bytes 884744 | tf_op jit(solution)/shard_map/ppermute | solution.py:39
  73.1 0.3 stack_reshape.8
  73.4 0.3 stack.112
  73.7 0.3 collective-permute-start.7
  74.1 6.0 %collective-permute-done.3 = f32[32,24,96]{2,1,0:T(8,128)S(1)} collective-permute-done((f32[32,24,96]{2,1,0:T(8,128)S(1)}, f32[32,24,96]{2,1,0:T(8,128)S(1)}, u32[]{:S(2)}, u32[]{:S(2)}) %collective-permute-start.3) | collective-permute-done | bytes 294944 | tf_op jit(solution)/shard_map/ppermute | solution.py:39
  80.1 6.4 %collective-permute-start.4 = (f32[2,32,24,96]{3,2,1,0:T(8,128)S(1)}, f32[2,32,24,96]{3,2,1,0:T(8,128)}, u32[]{:S(2)}, u32[]{:S(2)}) collective-permute-start(f32[2,32,24,96]{3,2,1,0:T(8,128)S(1)} %maximum_select_fusion.3), channel_id=1, source_target_pairs={{0,64},{64,0},{128,192},{192,128},{1,65},{65,1},{129,193},{193,129... | collective-permute-start | bytes 1769480 | tf_op jit(solution)/shard_map/ppermute | solution.py:43
  86.6 0.3 reshape.279
  86.9 0.4 constant_dynamic-slice_fusion
  87.3 1.3 %collective-permute-start.5 = (bf16[16,5376]{1,0:T(8,128)(2,1)S(1)}, bf16[16,5376]{1,0:T(8,128)(2,1)S(1)}, u32[]{:S(2)}, u32[]{:S(2)}) collective-permute-start(bf16[16,5376]{1,0:T(8,128)(2,1)S(1)} %bitcast.136), channel_id=1, source_target_pairs={{0,128},{64,192},{128,0},{192,64},{1,129},{65,193},{129,1},{193,65... | collective-permute-start | bytes 516104 | tf_op jit(solution)/shard_map/ppermute | solution.py:39
  88.6 0.9 maximum_select_fusion.5
  89.6 4.5 %collective-permute-start.8 = (f32[2,32,24,128]{3,2,1,0:T(8,128)}, f32[2,32,24,128]{3,2,1,0:T(8,128)}, u32[]{:S(2)}, u32[]{:S(2)}) collective-permute-start(f32[2,32,24,128]{3,2,1,0:T(8,128)} %maximum_select_fusion.5), channel_id=1, source_target_pairs={{0,64},{64,0},{128,192},{192,128},{1,65},{65,1},{129,193},{193,129... | collective-permute-start | bytes 2359304 | tf_op jit(solution)/shard_map/ppermute | solution.py:43
  94.1 0.8 maximum_select_fusion.9
  94.9 1.4 %collective-permute-start.6 = (bf16[2,16,5376]{2,1,0:T(8,128)(2,1)}, bf16[2,16,5376]{2,1,0:T(8,128)(2,1)S(1)}, u32[]{:S(2)}, u32[]{:S(2)}) collective-permute-start(bf16[2,16,5376]{2,1,0:T(8,128)(2,1)} %maximum_select_fusion.9), channel_id=1, source_target_pairs={{0,64},{64,0},{128,192},{192,128},{1,65},{65,1},{129,193},{193,129... | collective-permute-start | bytes 1032200 | tf_op jit(solution)/shard_map/ppermute | solution.py:43
  96.4 2.7 %maximum_select_fusion = f32[2,2,32,24,96]{4,3,2,1,0:T(8,128)} fusion(f32[2,1,32,24,96]{4,3,2,1,0:T(8,128)} %bitcast.10, f32[2,1,32,24,96]{4,3,2,1,0:T(8,128)S(1)} %maximum_select_fusion.2, pred[]{:T(512)S(6)} %eq.17), kind=kLoop, calls=%fused_computation | loop fusion | flops 884736 | bytes 2359297 | tf_op jit(solution)/shard_map/jit(_where)/select_n | solution.py:45
  99.1 4.4 %shard_map.109 = (f32[4,96,768]{2,1,0:T(8,128)}, f32[4,96,768]{2,1,0:T(8,128)}) custom-call(f32[4,32,24,96]{3,2,1,0:T(8,128)} %bitcast.115, f32[4,96,768]{2,1,0:T(8,128)} %refs_1_.2, f32[4,96,768]{2,1,0:T(8,128)} %refs_2_.2), custom_call_target="tpu_custom_call" | custom-call | tf_op jit(solution)/shard_map/pallas_call | solution.py:68
  103.4 2.7 %maximum_select_fusion.1 = f32[2,2,32,24,128]{4,3,2,1,0:T(8,128)} fusion(f32[2,1,32,24,128]{4,3,2,1,0:T(8,128)} %bitcast.31, f32[2,1,32,24,128]{4,3,2,1,0:T(8,128)S(1)} %maximum_select_fusion.4, pred[]{:T(512)S(6)} %eq.17), kind=kLoop, calls=%fused_computation.1 | loop fusion | flops 1179648 | bytes 3145729 | tf_op jit(solution)/shard_map/jit(_where)/select_n | solution.py:45
  106.1 4.7 %shard_map.110 = (f32[512,768]{1,0:T(8,128)}, f32[512,768]{1,0:T(8,128)}) custom-call(f32[4,32,24,128]{3,2,1,0:T(8,128)} %bitcast.116, f32[512,768]{1,0:T(8,128)} %refs_1_.3, f32[512,768]{1,0:T(8,128)} %refs_2_.3), custom_call_target="tpu_custom_call" | custom-call | tf_op jit(solution)/shard_map/pallas_call | solution.py:68
  111.1 0.3 copy.48
  111.4 1.0 reshape.277
  112.4 0.6 reshape.273
  113.1 1.1 reshape.274
  (44 shorter events, 2.5 us)
Async XLA Ops:
  0.6 1.7 %copy-start = (f32[1,24,8192]{2,1,0:T(8,128)S(1)}, f32[1,24,8192]{2,1,0:T(8,128)}, u32[]{:S(2)}) copy-start(f32[1,24,8192]{2,1,0:T(8,128)} %param.7) | copy-start | bytes 2359300
  5.3 5.1 %collective-permute-start = (f32[2,86016]{1,0:T(2,128)S(1)}, f32[2,86016]{1,0:T(2,128)S(1)}, u32[]{:S(2)}, u32[]{:S(2)}) collective-permute-start(f32[2,86016]{1,0:T(2,128)S(1)} %bitcast.144), channel_id=1, source_target_pairs={{0,64},{64,0},{128,192},{192,128},{1,65},{65,1},{129,193},{193,129... | collective-permute-start | bytes 2064392 | tf_op jit(solution)/shard_map/ppermute | solution.py:29
  11.7 9.4 %collective-permute-start.1 = (f32[86016]{0:T(1024)S(1)}, f32[86016]{0:T(1024)S(1)}, u32[]{:S(2)}, u32[]{:S(2)}) collective-permute-start(f32[86016]{0:T(1024)S(1)} %bitcast.149), channel_id=1, source_target_pairs={{0,128},{64,192},{128,0},{192,64},{1,129},{65,193},{129,1},{193,65... | collective-permute-start | bytes 1032200 | tf_op jit(solution)/shard_map/ppermute | solution.py:32
  21.1 9.9 %collective-permute-start.2 = (f32[86016]{0:T(1024)S(1)}, f32[86016]{0:T(1024)S(1)}, u32[]{:S(2)}, u32[]{:S(2)}) collective-permute-start(f32[86016]{0:T(1024)S(1)} %add.59), channel_id=1, source_target_pairs={{0,1},{1,0},{2,3},{3,2},{4,5},{5,4},{6,7},{7,6},{8,9},{9,8},{10,11... | collective-permute-start | bytes 1032200 | tf_op jit(solution)/shard_map/ppermute | solution.py:97
  34.5 27.5 %all-to-all-start = ((f32[32,1,5376]{2,1,0:T(1,128)}), f32[32,1,5376]{2,1,0:T(1,128)S(1)}, u32[]{:S(2)}, u32[]{:S(2)}) async-start(f32[32,1,5376]{2,1,0:T(1,128)} %copy.40), calls=%async_computation | async-start | bytes 1376256 | tf_op jit(solution)/shard_map/all_to_all | solution.py:103
  65.2 21.4 %all-to-all-start.1 = ((bf16[32,2,2688]{2,1,0:T(2,128)(2,1)}), bf16[32,2,2688]{2,1,0:T(2,128)(2,1)S(1)}, u32[]{:S(2)}, u32[]{:S(2)}) async-start(bf16[32,2,2688]{2,1,0:T(2,128)(2,1)} %reshape.278), calls=%async_computation.1 | async-start | bytes 688128 | tf_op jit(solution)/shard_map/all_to_all | solution.py:124
  71.8 8.2 %collective-permute-start.3 = (f32[32,24,96]{2,1,0:T(8,128)S(1)}, f32[32,24,96]{2,1,0:T(8,128)S(1)}, u32[]{:S(2)}, u32[]{:S(2)}) collective-permute-start(f32[32,24,96]{2,1,0:T(8,128)S(1)} %reshape.268), channel_id=1, source_target_pairs={{0,128},{64,192},{128,0},{192,64},{1,129},{65,193},{129,1},{193,65... | collective-permute-start | bytes 884744 | tf_op jit(solution)/shard_map/ppermute | solution.py:39
  73.7 14.9 %collective-permute-start.7 = (f32[32,24,128]{2,1,0:T(8,128)S(1)}, f32[32,24,128]{2,1,0:T(8,128)S(1)}, u32[]{:S(2)}, u32[]{:S(2)}) collective-permute-start(f32[32,24,128]{2,1,0:T(8,128)S(1)} %bitcast.117), channel_id=1, source_target_pairs={{0,128},{64,192},{128,0},{192,64},{1,129},{65,193},{129,1},{193,65... | collective-permute-start | bytes 1179656 | tf_op jit(solution)/shard_map/ppermute | solution.py:39
  80.1 16.2 %collective-permute-start.4 = (f32[2,32,24,96]{3,2,1,0:T(8,128)S(1)}, f32[2,32,24,96]{3,2,1,0:T(8,128)}, u32[]{:S(2)}, u32[]{:S(2)}) collective-permute-start(f32[2,32,24,96]{3,2,1,0:T(8,128)S(1)} %maximum_select_fusion.3), channel_id=1, source_target_pairs={{0,64},{64,0},{128,192},{192,128},{1,65},{65,1},{129,193},{193,129... | collective-permute-start | bytes 1769480 | tf_op jit(solution)/shard_map/ppermute | solution.py:43
  87.3 6.8 %collective-permute-start.5 = (bf16[16,5376]{1,0:T(8,128)(2,1)S(1)}, bf16[16,5376]{1,0:T(8,128)(2,1)S(1)}, u32[]{:S(2)}, u32[]{:S(2)}) collective-permute-start(bf16[16,5376]{1,0:T(8,128)(2,1)S(1)} %bitcast.136), channel_id=1, source_target_pairs={{0,128},{64,192},{128,0},{192,64},{1,129},{65,193},{129,1},{193,65... | collective-permute-start | bytes 516104 | tf_op jit(solution)/shard_map/ppermute | solution.py:39
  89.6 13.8 %collective-permute-start.8 = (f32[2,32,24,128]{3,2,1,0:T(8,128)}, f32[2,32,24,128]{3,2,1,0:T(8,128)}, u32[]{:S(2)}, u32[]{:S(2)}) collective-permute-start(f32[2,32,24,128]{3,2,1,0:T(8,128)} %maximum_select_fusion.5), channel_id=1, source_target_pairs={{0,64},{64,0},{128,192},{192,128},{1,65},{65,1},{129,193},{193,129... | collective-permute-start | bytes 2359304 | tf_op jit(solution)/shard_map/ppermute | solution.py:43
  94.9 15.9 %collective-permute-start.6 = (bf16[2,16,5376]{2,1,0:T(8,128)(2,1)}, bf16[2,16,5376]{2,1,0:T(8,128)(2,1)S(1)}, u32[]{:S(2)}, u32[]{:S(2)}) collective-permute-start(bf16[2,16,5376]{2,1,0:T(8,128)(2,1)} %maximum_select_fusion.9), channel_id=1, source_target_pairs={{0,64},{64,0},{128,192},{192,128},{1,65},{65,1},{129,193},{193,129... | collective-permute-start | bytes 1032200 | tf_op jit(solution)/shard_map/ppermute | solution.py:43

commit v8 on v7

--- a/solution.py
+++ b/solution.py
@@ -47,34 +47,55 @@
     return jax.tree.map(lambda a, f: f.reshape((n,) + a.shape), x, full)
 
 
-def update_kernel(scale, mean_ref, master_ref, moment_ref, w_ref, v_ref):
-    x = mean_ref[0]
-    x = x.reshape(x.shape[0] * x.shape[1], x.shape[2])
-    mean = x.T * scale
-    weights, velocity = update(master_ref[...], moment_ref[...], mean.reshape(master_ref.shape))
-    w_ref[...] = weights
-    v_ref[...] = velocity
+def gather_pieces(x):
+    r = lax.axis_index("rep")
+    n = lax.axis_size("rep")
+    cross = lax.ppermute(x, "rep", pairs(n, 2))
+    sib, sib_cross = lax.ppermute((x, cross), "rep", pairs(n, 1))
+    return x, sib, cross, sib_cross
 
 
-def fused_update(got, master, moment, scale):
-    quarters, srcs, wdt, cols = got.shape
+def update_kernel(scale, r_ref, p0, p1, p2, p3, master_ref, moment_ref, w_ref, v_ref):
+    p = pl.program_id(0)
+    for i, piece in enumerate((p0, p1, p2, p3)):
+
+        @pl.when(p == i)
+        def _():
+            x = piece[...]
+            x = x.reshape(x.shape[0] * x.shape[1], x.shape[2])
+            mean = x.T * scale
+            weights, velocity = update(
+                master_ref[...], moment_ref[...], mean.reshape(master_ref.shape)
+            )
+            w_ref[...] = weights
+            v_ref[...] = velocity
+
+
+def fused_update(pieces, master, moment, scale):
+    srcs, wdt, cols = pieces[0].shape
     lead = master.shape[:-2]
-    blk = (1,) * len(lead) + master.shape[-2:] if lead else (cols,) + master.shape[-1:]
     if lead:
-        idx = lambda q: (q, 0, 0)
+        blk = (1,) * len(lead) + master.shape[-2:]
+        idx = lambda p, r_ref: (lax.bitwise_xor(r_ref[0], p), 0, 0)
     else:
-        idx = lambda q: (q, 0)
+        blk = (cols,) + master.shape[-1:]
+        idx = lambda p, r_ref: (lax.bitwise_xor(r_ref[0], p), 0)
     big = pl.BlockSpec(blk, idx)
+    whole = pl.BlockSpec((srcs, wdt, cols), lambda p, r_ref: (0, 0, 0))
+    r = lax.axis_index("rep").astype(jnp.int32).reshape(1)
     return pl.pallas_call(
         lambda *refs: update_kernel(scale, *refs),
-        grid=(quarters,),
-        in_specs=[pl.BlockSpec((1, srcs, wdt, cols), lambda q: (q, 0, 0, 0)), big, big],
-        out_specs=[big, big],
+        grid_spec=pltpu.PrefetchScalarGridSpec(
+            num_scalar_prefetch=1,
+            grid=(len(pieces),),
+            in_specs=[whole] * len(pieces) + [big, big],
+            out_specs=[big, big],
+        ),
         out_shape=[
             jax.ShapeDtypeStruct(master.shape, master.dtype),
             jax.ShapeDtypeStruct(master.shape, master.dtype),
         ],
-    )(got, master, moment)
+    )(r, *pieces, master, moment)
 
 
 def local(expert_change, table_change, expert_master, expert_moment, table_master, table_moment):
@@ -123,12 +144,13 @@
     back = jnp.concatenate([le.reshape(shards, -1), lt.reshape(shards, -1)], 1)
     back = lax.all_to_all(back, "shard", 0, 0, tiled=True)
 
-    every_e, every_t = rep_gather((ge, gt))
+    pieces_e = gather_pieces(ge)
+    pieces_t = gather_pieces(gt)
     expert_weights, expert_velocity = fused_update(
-        every_e, expert_master, expert_moment, 1.0 / groups
+        pieces_e, expert_master, expert_moment, 1.0 / groups
     )
     table_weights, table_velocity = fused_update(
-        every_t, table_master, table_moment, 1.0 / groups
+        pieces_t, table_master, table_moment, 1.0 / groups
     )
 
     back = lax.dynamic_slice_in_dim(back, t * per_half, per_half, 0)

time: 115 us -> 111 us (0.965)
  other arithmetic: 10.3 us -> 3.09 us
  waiting for transfers between devices: 41 us -> 48 us
  starting transfers between devices: 35.6 us -> 30.5 us
    ppermute x0 -> x6, waiting for transfers between devices: none -> 11.7 us  [the longest x2 11.7 us: gather_pieces(): cross = lax.ppermute(x, 'rep', pairs(n, 2))]
    ppermute x3 -> x1, starting transfers between devices: 12.4 us -> 0.78 us  [rep_gather(): sib = lax.ppermute(pair, 'rep', pairs(n, 1))]
    ppermute x0 -> x6, starting transfers between devices: none -> 8.14 us  [the longest x4 6.5 us: gather_pieces(): sib, sib_cross = lax.ppermute((x, cross), 'rep', pairs(n, 1))]
    ppermute x3 -> x1, waiting for transfers between devices: 5.99 us -> 0.01 us  [rep_gather(): cross = lax.ppermute(x, 'rep', pairs(n, 2))]
    select_n x3 -> x1, other arithmetic: 5.44 us -> 0.07 us  [rep_gather(): jnp.where(core == 0, jnp.stack([a, b], 1), jnp.stack([b, a], 1))]
    select_n x6 -> x2, other arithmetic: 1.9 us -> 0.08 us  [rep_gather(): jnp.where(x_lo == 0, jnp.stack([a, b]), jnp.stack([b, a]))]
    ppermute x3 -> x1, starting transfers between devices: 2.94 us -> 1.3 us  [rep_gather(): cross = lax.ppermute(x, 'rep', pairs(n, 2))]
    unnamed x17 -> x29, local copies, waits for them, and re-layouts: 2.53 us -> 3.97 us
  transfers between devices with their start and end apart: 11 -> 13, of which waited for: 5 -> 6; matrix products, arithmetic and copies ran while one was open for 10% -> 4% of each run, Pallas kernels for 8% -> 9%
where the time goes in v8:
time: 111 us; the launch traced here: 110 us
  waiting for transfers between devices  48 us (43%)
  starting transfers between devices  30.5 us (27%)
  local copies, waits for them, and re-layouts  18.1 us (16%)
  Pallas kernels  9.48 us (9%)
  other arithmetic  3.09 us (3%)
  between operations  1.11 us (1%)
    all_to_all x1, waiting for transfers between devices, local(): lax.all_to_all(jnp.concatenate([he, ht], 1), 'shard', 0, 0, tiled=True)  15.1 us
    ppermute x2, waiting for transfers between devices, gather_pieces(): cross = lax.ppermute(x, 'rep', pairs(n, 2))  11.7 us
    pallas_call x2, Pallas kernels, fused_update(): pl.pallas_call(lambda *refs: update_kernel(scale, *refs), grid_spec=pltpu...  9.48 us
    all_to_all x1, starting transfers between devices, local(): lax.all_to_all(jnp.concatenate([he, ht], 1), 'shard', 0, 0, tiled=True)  9.47 us
    ppermute x1, waiting for transfers between devices, rep_scatter(): return keep + lax.ppermute(send, 'rep', pairs(n, 2))  9.26 us
    ppermute x1, waiting for transfers between devices, local(): other = lax.ppermute(q, 'tp', pairs(tensor, 1))  8.85 us
    ppermute x4, starting transfers between devices, gather_pieces(): sib, sib_cross = lax.ppermute((x, cross), 'rep', pairs(n, 1))  6.5 us
    all_to_all x1, starting transfers between devices, local(): back = lax.all_to_all(back, 'shard', 0, 0, tiled=True)  6.35 us
  transfers between devices with their start and end apart: 13, of which 6 were waited for; matrix products, arithmetic and copies ran while one was open for 4% of the time, Pallas kernels for 9%

profile of v8, /device:TPU:1, one launch (start us, length us, event | category | flops | bytes accessed | tf_op | source)
XLA Modules:
  0.0 110.3 jit_solution(14418558411143515025)
XLA Ops:
  0.7 1.6 %concatenate.28 = f32[2,2,36864]{2,1,0:T(2,128)S(1)} reshape(f32[1,4,24,1536]{3,2,1,0:T(8,128)} %param.6) | data formatting | bytes 1179648 | tf_op jit(solution)/shard_map/concatenate | solution.py:116
  2.4 0.5 reshape_squeeze.4
  3.0 0.5 concatenate.29
  3.6 1.2 %constant_dynamic-slice_fusion.8 = (f32[2,1,86016]{2,1,0:T(1,128)S(1)}, f32[2,1,86016]{2,1,0:T(1,128)S(1)}) fusion(f32[2,2,86016]{2,1,0:T(2,128)S(1)} %constant_dynamic-update-slice_fusion, s32[]{:T(128)S(6)} %select_n.81, s32[]{:T(128)S(6)} %select_n.82), kind=kLoop, calls=%fused_computation.39 | loop fusion | bytes 2752520 | tf_op jit(solution)/shard_map/jit(dynamic_index_in_dim)/dynamic_slice | solution.py:27
  4.8 0.5 copy.72
  5.3 3.3 %collective-permute-start = (f32[2,86016]{1,0:T(2,128)S(1)}, f32[2,86016]{1,0:T(2,128)S(1)}, u32[]{:S(2)}, u32[]{:S(2)}) collective-permute-start(f32[2,86016]{1,0:T(2,128)S(1)} %bitcast.125), channel_id=1, source_target_pairs={{0,64},{64,0},{128,192},{192,128},{1,65},{65,1},{129,193},{193,129... | collective-permute-start | bytes 2064392 | tf_op jit(solution)/shard_map/ppermute | solution.py:29
  8.6 1.8 %collective-permute-done = f32[2,86016]{1,0:T(2,128)S(1)} collective-permute-done((f32[2,86016]{1,0:T(2,128)S(1)}, f32[2,86016]{1,0:T(2,128)S(1)}, u32[]{:S(2)}, u32[]{:S(2)}) %collective-permute-start) | collective-permute-done | bytes 688160 | tf_op jit(solution)/shard_map/ppermute | solution.py:29
  10.4 0.7 bitcast_add_fusion
  11.1 0.6 constant_dynamic-slice_fusion.5
  11.8 9.3 %collective-permute-done.1 = f32[86016]{0:T(1024)S(1)} collective-permute-done((f32[86016]{0:T(1024)S(1)}, f32[86016]{0:T(1024)S(1)}, u32[]{:S(2)}, u32[]{:S(2)}) %collective-permute-start.1) | collective-permute-done | bytes 344096 | tf_op jit(solution)/shard_map/ppermute | solution.py:32
  21.1 1.1 collective-permute-start.2
  22.2 8.8 %collective-permute-done.2 = f32[86016]{0:T(1024)S(1)} collective-permute-done((f32[86016]{0:T(1024)S(1)}, f32[86016]{0:T(1024)S(1)}, u32[]{:S(2)}, u32[]{:S(2)}) %collective-permute-start.2) | collective-permute-done | bytes 344096 | tf_op jit(solution)/shard_map/ppermute | solution.py:118
  31.1 1.0 maximum_select_fusion
  32.3 0.3 reshape.141
  33.0 1.6 %copy.40 = f32[32,1,5376]{2,1,0:T(1,128)} copy(f32[32,1,5376]{2,0,1:T(8,128)S(1)} %maximum_bitcast_fusion) | data formatting | bytes 1376256 | tf_op jit(solution)/shard_map/all_to_all | solution.py:124
  34.5 9.5 %all-to-all-start = ((f32[32,1,5376]{2,1,0:T(1,128)}), f32[32,1,5376]{2,1,0:T(1,128)S(1)}, u32[]{:S(2)}, u32[]{:S(2)}) async-start(f32[32,1,5376]{2,1,0:T(1,128)} %copy.40), calls=%async_computation | async-start | bytes 1376256 | tf_op jit(solution)/shard_map/all_to_all | solution.py:124
  44.0 1.1 constant_dynamic-slice_fusion.3
  45.1 0.2 copy.52
  45.3 0.2 copy.41
  45.4 1.2 %constant_dynamic-slice_fusion.1 = (f32[128,768]{1,0:T(8,128)S(1)}, f32[128,768]{1,0:T(8,128)S(1)}) fusion(f32[512,768]{1,0:T(8,128)} %refs_6_.3, s32[]{:T(128)S(6)} %select_n.90, f32[512,768]{1,0:T(8,128)} %refs_5_.3), kind=kLoop, calls=%fused_computation.32 | loop fusion | bytes 1572868 | tf_op jit(solution)/shard_map/dynamic_slice | solution.py:140
  46.6 0.2 copy.54
  46.8 0.2 copy.53
  47.0 15.1 %all-to-all-done = f32[32,1,5376]{2,1,0:T(1,128)S(1)} async-done(((f32[32,1,5376]{2,1,0:T(1,128)}), f32[32,1,5376]{2,1,0:T(1,128)S(1)}, u32[]{:S(2)}, u32[]{:S(2)}) %all-to-all-start) | async-done | bytes 688160 | tf_op jit(solution)/shard_map/all_to_all | solution.py:124
  62.2 0.3 div.34
  62.6 0.2 reshape.147
  63.0 0.5 broadcast.38
  63.5 0.8 reduce
  64.4 0.8 reshape.155
  65.2 6.3 %all-to-all-start.1 = ((bf16[32,2,2688]{2,1,0:T(2,128)(2,1)}), bf16[32,2,2688]{2,1,0:T(2,128)(2,1)S(1)}, u32[]{:S(2)}, u32[]{:S(2)}) async-start(bf16[32,2,2688]{2,1,0:T(2,128)(2,1)} %reshape.155), calls=%async_computation.1 | async-start | bytes 688128 | tf_op jit(solution)/shard_map/all_to_all | solution.py:145
  71.6 1.3 %collective-permute-start.9 = (f32[32,24,128]{2,1,0:T(8,128)S(1)}, f32[32,24,128]{2,1,0:T(8,128)S(1)}, u32[]{:S(2)}, u32[]{:S(2)}) collective-permute-start(f32[32,24,128]{2,1,0:T(8,128)S(1)} %bitcast.107), channel_id=1, source_target_pairs={{0,128},{64,192},{128,0},{192,64},{1,129},{65,193},{129,1},{193,65... | collective-permute-start | bytes 1179656 | tf_op jit(solution)/shard_map/ppermute | solution.py:53
  72.9 0.3 reshape.145.refs_1_
  73.2 0.3 collective-permute-start.4
  73.6 3.0 %collective-permute-start.3 = (f32[32,24,96]{2,1,0:T(8,128)S(1)}, f32[32,24,96]{2,1,0:T(8,128)S(1)}, u32[]{:S(2)}, u32[]{:S(2)}) collective-permute-start(f32[32,24,96]{2,1,0:T(8,128)S(1)} %reshape.145.refs_1_), channel_id=1, source_target_pairs={{0,64},{64,0},{128,192},{192,128},{1,65},{65,1},{129,193},{193,129... | collective-permute-start | bytes 884744 | tf_op jit(solution)/shard_map/ppermute | solution.py:54
  76.6 11.7 %collective-permute-done.4.refs_3_ = f32[32,24,96]{2,1,0:T(8,128)S(1)} collective-permute-done((f32[32,24,96]{2,1,0:T(8,128)S(1)}, f32[32,24,96]{2,1,0:T(8,128)S(1)}, u32[]{:S(2)}, u32[]{:S(2)}) %collective-permute-start.4) | collective-permute-done | bytes 294944 | tf_op jit(solution)/shard_map/ppermute | solution.py:53
  88.3 3.4 %collective-permute-start.5 = (f32[32,24,96]{2,1,0:T(8,128)S(1)}, f32[32,24,96]{2,1,0:T(8,128)}, u32[]{:S(2)}, u32[]{:S(2)}) collective-permute-start(f32[32,24,96]{2,1,0:T(8,128)S(1)} %collective-permute-done.4.refs_3_), channel_id=1, source_target_pairs={{0,64},{64,0},{128,192},{192,128},{1,65},{65,1},{129,193},{193,129... | collective-permute-start | bytes 884744 | tf_op jit(solution)/shard_map/ppermute | solution.py:54
  91.8 0.3 reshape.156
  92.1 0.4 constant_dynamic-slice_fusion
  92.5 1.3 %collective-permute-start.6 = (bf16[16,5376]{1,0:T(8,128)(2,1)S(1)}, bf16[16,5376]{1,0:T(8,128)(2,1)S(1)}, u32[]{:S(2)}, u32[]{:S(2)}) collective-permute-start(bf16[16,5376]{1,0:T(8,128)(2,1)S(1)} %bitcast.117), channel_id=1, source_target_pairs={{0,128},{64,192},{128,0},{192,64},{1,129},{65,193},{129,1},{193,65... | collective-permute-start | bytes 516104 | tf_op jit(solution)/shard_map/ppermute | solution.py:39
  93.8 0.7 copy-done.6
  94.5 4.6 %shard_map.109 = (f32[4,96,768]{2,1,0:T(8,128)}, f32[4,96,768]{2,1,0:T(8,128)}) custom-call(s32[1]{0:T(128)} %bitcast.refs_0_, f32[32,24,96]{2,1,0:T(8,128)} %copy-done.1, f32[32,24,96]{2,1,0:T(8,128)} %copy-done.6, f32[32,24,96]{2,1,0:T(8,128)} %copy-done.4, f32[32,24,96]{2,1,0:T(8,128)} %collective-permute-done.5.refs_4_, f32[4,96,768]{2,1,0:T(8,128)} %refs_5_.2, ...), custom_call_target="tpu_custom_call" | custom-call | tf_op jit(solution)/shard_map/pallas_call | solution.py:86
  99.2 0.7 copy-done.5
  99.9 4.9 %shard_map.110 = (f32[512,768]{1,0:T(8,128)}, f32[512,768]{1,0:T(8,128)}) custom-call(s32[1]{0:T(128)} %bitcast.refs_0_, f32[32,24,128]{2,1,0:T(8,128)} %bitcast.109, f32[32,24,128]{2,1,0:T(8,128)} %copy-done.5, f32[32,24,128]{2,1,0:T(8,128)} %copy-done.3, f32[32,24,128]{2,1,0:T(8,128)} %collective-permute-done.10.refs_4_, f32[512,768]{1,0:T(8,128)} %refs_5_.3, ...), custom_call_target="tpu_custom_call" | custom-call | tf_op jit(solution)/shard_map/pallas_call | solution.py:86
  104.8 0.8 collective-permute-start.7
  105.7 1.2 %collective-permute-done.7 = bf16[2,16,5376]{2,1,0:T(8,128)(2,1)S(1)} collective-permute-done((bf16[2,16,5376]{2,1,0:T(8,128)(2,1)S(1)}, bf16[2,16,5376]{2,1,0:T(8,128)(2,1)S(1)}, u32[]{:S(2)}, u32[]{:S(2)}) %collective-permute-start.7) | collective-permute-done | bytes 344096 | tf_op jit(solution)/shard_map/ppermute | solution.py:43
  107.1 0.3 copy.48
  107.5 1.0 reshape.154
  108.5 0.6 reshape.150
  109.2 1.1 %reshape.151 = bf16[4,24,1536]{2,1,0:T(8,128)(2,1)} reshape(bf16[4,24,16,96]{3,2,1,0:T(8,128)(2,1)S(1)} %copy.47) | data formatting | bytes 589824 | tf_op jit(solution)/shard_map/reshape | solution.py:159
  (52 shorter events, 2.0 us)
Async XLA Ops:
  0.6 1.7 %copy-start.2 = (f32[1,24,8192]{2,1,0:T(8,128)S(1)}, f32[1,24,8192]{2,1,0:T(8,128)}, u32[]{:S(2)}) copy-start(f32[1,24,8192]{2,1,0:T(8,128)} %param.7) | copy-start | bytes 2359300
  5.3 5.1 %collective-permute-start = (f32[2,86016]{1,0:T(2,128)S(1)}, f32[2,86016]{1,0:T(2,128)S(1)}, u32[]{:S(2)}, u32[]{:S(2)}) collective-permute-start(f32[2,86016]{1,0:T(2,128)S(1)} %bitcast.125), channel_id=1, source_target_pairs={{0,64},{64,0},{128,192},{192,128},{1,65},{65,1},{129,193},{193,129... | collective-permute-start | bytes 2064392 | tf_op jit(solution)/shard_map/ppermute | solution.py:29
  11.7 9.4 %collective-permute-start.1 = (f32[86016]{0:T(1024)S(1)}, f32[86016]{0:T(1024)S(1)}, u32[]{:S(2)}, u32[]{:S(2)}) collective-permute-start(f32[86016]{0:T(1024)S(1)} %bitcast.130), channel_id=1, source_target_pairs={{0,128},{64,192},{128,0},{192,64},{1,129},{65,193},{129,1},{193,65... | collective-permute-start | bytes 1032200 | tf_op jit(solution)/shard_map/ppermute | solution.py:32
  21.1 9.9 %collective-permute-start.2 = (f32[86016]{0:T(1024)S(1)}, f32[86016]{0:T(1024)S(1)}, u32[]{:S(2)}, u32[]{:S(2)}) collective-permute-start(f32[86016]{0:T(1024)S(1)} %add.58), channel_id=1, source_target_pairs={{0,1},{1,0},{2,3},{3,2},{4,5},{5,4},{6,7},{7,6},{8,9},{9,8},{10,11... | collective-permute-start | bytes 1032200 | tf_op jit(solution)/shard_map/ppermute | solution.py:118
  34.5 27.5 %all-to-all-start = ((f32[32,1,5376]{2,1,0:T(1,128)}), f32[32,1,5376]{2,1,0:T(1,128)S(1)}, u32[]{:S(2)}, u32[]{:S(2)}) async-start(f32[32,1,5376]{2,1,0:T(1,128)} %copy.40), calls=%async_computation | async-start | bytes 1376256 | tf_op jit(solution)/shard_map/all_to_all | solution.py:124
  65.2 26.6 %all-to-all-start.1 = ((bf16[32,2,2688]{2,1,0:T(2,128)(2,1)}), bf16[32,2,2688]{2,1,0:T(2,128)(2,1)S(1)}, u32[]{:S(2)}, u32[]{:S(2)}) async-start(bf16[32,2,2688]{2,1,0:T(2,128)(2,1)} %reshape.155), calls=%async_computation.1 | async-start | bytes 688128 | tf_op jit(solution)/shard_map/all_to_all | solution.py:145
  71.6 20.9 %copy-start = (f32[4,8,24,128]{3,2,1,0:T(8,128)}, f32[4,8,24,128]{3,2,1,0:T(8,128)S(1)}, u32[]{:S(2)}) copy-start(f32[4,8,24,128]{3,2,1,0:T(8,128)S(1)} %copy.59) | copy-start | bytes 1179652
  71.6 20.0 %collective-permute-start.9 = (f32[32,24,128]{2,1,0:T(8,128)S(1)}, f32[32,24,128]{2,1,0:T(8,128)S(1)}, u32[]{:S(2)}, u32[]{:S(2)}) collective-permute-start(f32[32,24,128]{2,1,0:T(8,128)S(1)} %bitcast.107), channel_id=1, source_target_pairs={{0,128},{64,192},{128,0},{192,64},{1,129},{65,193},{129,1},{193,65... | collective-permute-start | bytes 1179656 | tf_op jit(solution)/shard_map/ppermute | solution.py:53
  73.2 20.6 %copy-start.1 = (f32[32,24,96]{2,1,0:T(8,128)}, f32[32,24,96]{2,1,0:T(8,128)S(1)}, u32[]{:S(2)}) copy-start(f32[32,24,96]{2,1,0:T(8,128)S(1)} %reshape.145.refs_1_) | copy-start | bytes 884740
  73.2 15.1 %collective-permute-start.4 = (f32[32,24,96]{2,1,0:T(8,128)S(1)}, f32[32,24,96]{2,1,0:T(8,128)S(1)}, u32[]{:S(2)}, u32[]{:S(2)}) collective-permute-start(f32[32,24,96]{2,1,0:T(8,128)S(1)} %reshape.145.refs_1_), channel_id=1, source_target_pairs={{0,128},{64,192},{128,0},{192,64},{1,129},{65,193},{129,1},{193,65... | collective-permute-start | bytes 884744 | tf_op jit(solution)/shard_map/ppermute | solution.py:53
  73.6 20.2 %collective-permute-start.3 = (f32[32,24,96]{2,1,0:T(8,128)S(1)}, f32[32,24,96]{2,1,0:T(8,128)S(1)}, u32[]{:S(2)}, u32[]{:S(2)}) collective-permute-start(f32[32,24,96]{2,1,0:T(8,128)S(1)} %reshape.145.refs_1_), channel_id=1, source_target_pairs={{0,64},{64,0},{128,192},{192,128},{1,65},{65,1},{129,193},{193,129... | collective-permute-start | bytes 884744 | tf_op jit(solution)/shard_map/ppermute | solution.py:54
  76.6 22.6 %collective-permute-start.8 = (f32[32,24,128]{2,1,0:T(8,128)S(1)}, f32[32,24,128]{2,1,0:T(8,128)S(1)}, u32[]{:S(2)}, u32[]{:S(2)}) collective-permute-start(f32[32,24,128]{2,1,0:T(8,128)S(1)} %bitcast.108), channel_id=1, source_target_pairs={{0,64},{64,0},{128,192},{192,128},{1,65},{65,1},{129,193},{193,129... | collective-permute-start | bytes 1179656 | tf_op jit(solution)/shard_map/ppermute | solution.py:54
  88.3 5.5 %copy-start.4 = (f32[32,24,96]{2,1,0:T(8,128)}, f32[32,24,96]{2,1,0:T(8,128)S(1)}, u32[]{:S(2)}) copy-start(f32[32,24,96]{2,1,0:T(8,128)S(1)} %collective-permute-done.4.refs_3_) | copy-start | bytes 884740
  88.3 5.5 %collective-permute-start.5 = (f32[32,24,96]{2,1,0:T(8,128)S(1)}, f32[32,24,96]{2,1,0:T(8,128)}, u32[]{:S(2)}, u32[]{:S(2)}) collective-permute-start(f32[32,24,96]{2,1,0:T(8,128)S(1)} %collective-permute-done.4.refs_3_), channel_id=1, source_target_pairs={{0,64},{64,0},{128,192},{192,128},{1,65},{65,1},{129,193},{193,129... | collective-permute-start | bytes 884744 | tf_op jit(solution)/shard_map/ppermute | solution.py:54
  91.7 7.5 %copy-start.3 = (f32[32,24,128]{2,1,0:T(8,128)}, f32[32,24,128]{2,1,0:T(8,128)S(1)}, u32[]{:S(2)}) copy-start(f32[32,24,128]{2,1,0:T(8,128)S(1)} %collective-permute-done.9.refs_3_) | copy-start | bytes 1179652
  91.7 7.5 %collective-permute-start.10 = (f32[32,24,128]{2,1,0:T(8,128)S(1)}, f32[32,24,128]{2,1,0:T(8,128)}, u32[]{:S(2)}, u32[]{:S(2)}) collective-permute-start(f32[32,24,128]{2,1,0:T(8,128)S(1)} %collective-permute-done.9.refs_3_), channel_id=1, source_target_pairs={{0,64},{64,0},{128,192},{192,128},{1,65},{65,1},{129,193},{193,129... | collective-permute-start | bytes 1179656 | tf_op jit(solution)/shard_map/ppermute | solution.py:54
  92.5 12.3 %collective-permute-start.6 = (bf16[16,5376]{1,0:T(8,128)(2,1)S(1)}, bf16[16,5376]{1,0:T(8,128)(2,1)S(1)}, u32[]{:S(2)}, u32[]{:S(2)}) collective-permute-start(bf16[16,5376]{1,0:T(8,128)(2,1)S(1)} %bitcast.117), channel_id=1, source_target_pairs={{0,128},{64,192},{128,0},{192,64},{1,129},{65,193},{129,1},{193,65... | collective-permute-start | bytes 516104 | tf_op jit(solution)/shard_map/ppermute | solution.py:39
  93.8 0.7 copy-start.6
  99.2 0.7 copy-start.5
  104.8 2.1 %collective-permute-start.7 = (bf16[2,16,5376]{2,1,0:T(8,128)(2,1)S(1)}, bf16[2,16,5376]{2,1,0:T(8,128)(2,1)S(1)}, u32[]{:S(2)}, u32[]{:S(2)}) collective-permute-start(bf16[2,16,5376]{2,1,0:T(8,128)(2,1)S(1)} %maximum_select_fusion.3), channel_id=1, source_target_pairs={{0,64},{64,0},{128,192},{192,128},{1,65},{65,1},{129,193},{193,129... | collective-permute-start | bytes 1032200 | tf_op jit(solution)/shard_map/ppermute | solution.py:43

commit v9 on v8

--- a/solution.py
+++ b/solution.py
@@ -50,14 +50,18 @@
 def gather_pieces(x):
     r = lax.axis_index("rep")
     n = lax.axis_size("rep")
+    sib = lax.ppermute(x, "rep", pairs(n, 1))
     cross = lax.ppermute(x, "rep", pairs(n, 2))
-    sib, sib_cross = lax.ppermute((x, cross), "rep", pairs(n, 1))
+    sib_cross = lax.ppermute(cross, "rep", pairs(n, 1))
     return x, sib, cross, sib_cross
 
 
-def update_kernel(scale, r_ref, p0, p1, p2, p3, master_ref, moment_ref, w_ref, v_ref):
+def update_kernel(scale, count, r_ref, *refs):
+    pieces = refs[:count]
+    master_ref, moment_ref = refs[count : count + 2]
+    w_ref, v_ref = refs[-2:]
     p = pl.program_id(0)
-    for i, piece in enumerate((p0, p1, p2, p3)):
+    for i, piece in enumerate(pieces):
 
         @pl.when(p == i)
         def _():
@@ -71,31 +75,40 @@
             v_ref[...] = velocity
 
 
-def fused_update(pieces, master, moment, scale):
+def fused_update(pieces, first, master, moment, scale, into=None):
     srcs, wdt, cols = pieces[0].shape
+    count = len(pieces)
     lead = master.shape[:-2]
     if lead:
         blk = (1,) * len(lead) + master.shape[-2:]
-        idx = lambda p, r_ref: (lax.bitwise_xor(r_ref[0], p), 0, 0)
+        idx = lambda p, r_ref: (lax.bitwise_xor(r_ref[0], p + first), 0, 0)
     else:
         blk = (cols,) + master.shape[-1:]
-        idx = lambda p, r_ref: (lax.bitwise_xor(r_ref[0], p), 0)
+        idx = lambda p, r_ref: (lax.bitwise_xor(r_ref[0], p + first), 0)
     big = pl.BlockSpec(blk, idx)
     whole = pl.BlockSpec((srcs, wdt, cols), lambda p, r_ref: (0, 0, 0))
     r = lax.axis_index("rep").astype(jnp.int32).reshape(1)
+    args = [r, *pieces, master, moment]
+    in_specs = [whole] * count + [big, big]
+    aliases = {}
+    if into is not None:
+        aliases = {len(args): 0, len(args) + 1: 1}
+        args += list(into)
+        in_specs += [pl.BlockSpec(memory_space=pl.ANY)] * 2
     return pl.pallas_call(
-        lambda *refs: update_kernel(scale, *refs),
+        lambda *refs: update_kernel(scale, count, *refs),
         grid_spec=pltpu.PrefetchScalarGridSpec(
             num_scalar_prefetch=1,
-            grid=(len(pieces),),
-            in_specs=[whole] * len(pieces) + [big, big],
+            grid=(count,),
+            in_specs=in_specs,
             out_specs=[big, big],
         ),
         out_shape=[
             jax.ShapeDtypeStruct(master.shape, master.dtype),
             jax.ShapeDtypeStruct(master.shape, master.dtype),
         ],
-    )(r, *pieces, master, moment)
+        input_output_aliases=aliases,
+    )(*args)
 
 
 def local(expert_change, table_change, expert_master, expert_moment, table_master, table_moment):
@@ -146,11 +159,14 @@
 
     pieces_e = gather_pieces(ge)
     pieces_t = gather_pieces(gt)
+    scale = 1.0 / groups
+    early_e = fused_update(pieces_e[:2], 0, expert_master, expert_moment, scale)
+    early_t = fused_update(pieces_t[:2], 0, table_master, table_moment, scale)
     expert_weights, expert_velocity = fused_update(
-        pieces_e, expert_master, expert_moment, 1.0 / groups
+        pieces_e[2:], 2, expert_master, expert_moment, scale, early_e
     )
     table_weights, table_velocity = fused_update(
-        pieces_t, table_master, table_moment, 1.0 / groups
+        pieces_t[2:], 2, table_master, table_moment, scale, early_t
     )
 
     back = lax.dynamic_slice_in_dim(back, t * per_half, per_half, 0)

time: 111 us -> 112 us (level)
    concatenate x3, local copies, waits for them, and re-layouts: 2.21 us -> 1.07 us  [local(): q = rep_scatter(jnp.concatenate([ex, tx], axis=1))]
    another operation x2, local copies, waits for them, and re-layouts: 0.59 us -> 1.72 us  [local(): tx = table_change[0].reshape(width, per_half, groups, sub)]
    pallas_call x2 -> x4, Pallas kernels: 9.48 us -> 10.4 us  [fused_update(): pl.pallas_call(lambda *refs: update_kernel(scale, count, *refs), grid_spe...]
where the time goes in v9:
time: 112 us
  waiting for transfers between devices  48 us (43%)
  starting transfers between devices  30.5 us (27%)
  local copies, waits for them, and re-layouts  18.6 us (17%)
  Pallas kernels  10.4 us (9%)
  other arithmetic  3.09 us (3%)
    all_to_all x1, waiting for transfers between devices, local(): lax.all_to_all(jnp.concatenate([he, ht], 1), 'shard', 0, 0, tiled=True)  15.1 us
    ppermute x2, waiting for transfers between devices, gather_pieces(): cross = lax.ppermute(x, 'rep', pairs(n, 2))  11.7 us
    pallas_call x4, Pallas kernels, fused_update(): pl.pallas_call(lambda *refs: update_kernel(scale, count, *refs), grid_spe...  10.4 us
    all_to_all x1, starting transfers between devices, local(): lax.all_to_all(jnp.concatenate([he, ht], 1), 'shard', 0, 0, tiled=True)  9.47 us
    ppermute x1, waiting for transfers between devices, rep_scatter(): return keep + lax.ppermute(send, 'rep', pairs(n, 2))  9.26 us
    ppermute x1, waiting for transfers between devices, local(): other = lax.ppermute(q, 'tp', pairs(tensor, 1))  8.85 us
    all_to_all x1, starting transfers between devices, local(): back = lax.all_to_all(back, 'shard', 0, 0, tiled=True)  6.35 us
    unnamed x29, local copies, waits for them, and re-layouts  4.51 us
  transfers between devices with their start and end apart: 13, of which 6 were waited for; matrix products, arithmetic and copies ran while one was open for 4% of the time, Pallas kernels for 9%

profile of v9, /device:TPU:1, one launch (start us, length us, event | category | flops | bytes accessed | tf_op | source)
XLA Modules:
  0.0 111.8 jit_solution(15948612690360703826)
XLA Ops:
  0.7 1.7 %reshape_squeeze.4 = f32[24,16,4,128]{3,2,1,0:T(4,128)S(1)} reshape(f32[1,24,8192]{2,1,0:T(8,128)} %param.7) | data formatting | bytes 1572864 | tf_op jit(solution)/shard_map/reshape;squeeze | solution.py:127
  2.4 0.5 concatenate.29
  2.9 0.5 copy-done.2
  3.4 0.5 concatenate.28
  4.1 1.2 %constant_dynamic-slice_fusion.8 = (f32[2,1,86016]{2,1,0:T(1,128)S(1)}, f32[2,1,86016]{2,1,0:T(1,128)S(1)}) fusion(f32[2,2,86016]{2,1,0:T(2,128)S(1)} %constant_dynamic-update-slice_fusion, s32[]{:T(128)S(6)} %select_n.81, s32[]{:T(128)S(6)} %select_n.82), kind=kLoop, calls=%fused_computation.39 | loop fusion | bytes 2752520 | tf_op jit(solution)/shard_map/jit(dynamic_index_in_dim)/dynamic_slice | solution.py:27
  5.2 0.5 copy.76
  5.8 3.3 %collective-permute-start = (f32[2,86016]{1,0:T(2,128)S(1)}, f32[2,86016]{1,0:T(2,128)S(1)}, u32[]{:S(2)}, u32[]{:S(2)}) collective-permute-start(f32[2,86016]{1,0:T(2,128)S(1)} %bitcast.125), channel_id=1, source_target_pairs={{0,64},{64,0},{128,192},{192,128},{1,65},{65,1},{129,193},{193,129... | collective-permute-start | bytes 2064392 | tf_op jit(solution)/shard_map/ppermute | solution.py:29
  9.1 1.8 %collective-permute-done = f32[2,86016]{1,0:T(2,128)S(1)} collective-permute-done((f32[2,86016]{1,0:T(2,128)S(1)}, f32[2,86016]{1,0:T(2,128)S(1)}, u32[]{:S(2)}, u32[]{:S(2)}) %collective-permute-start) | collective-permute-done | bytes 688160 | tf_op jit(solution)/shard_map/ppermute | solution.py:29
  10.9 0.7 bitcast_add_fusion
  11.6 0.6 constant_dynamic-slice_fusion.5
  12.3 9.3 %collective-permute-done.1 = f32[86016]{0:T(1024)S(1)} collective-permute-done((f32[86016]{0:T(1024)S(1)}, f32[86016]{0:T(1024)S(1)}, u32[]{:S(2)}, u32[]{:S(2)}) %collective-permute-start.1) | collective-permute-done | bytes 344096 | tf_op jit(solution)/shard_map/ppermute | solution.py:32
  21.6 1.1 collective-permute-start.2
  22.7 8.8 %collective-permute-done.2 = f32[86016]{0:T(1024)S(1)} collective-permute-done((f32[86016]{0:T(1024)S(1)}, f32[86016]{0:T(1024)S(1)}, u32[]{:S(2)}, u32[]{:S(2)}) %collective-permute-start.2) | collective-permute-done | bytes 344096 | tf_op jit(solution)/shard_map/ppermute | solution.py:131
  31.5 1.0 maximum_select_fusion
  32.8 0.3 reshape.143
  33.5 1.6 %copy.44 = f32[32,1,5376]{2,1,0:T(1,128)} copy(f32[32,1,5376]{2,0,1:T(8,128)S(1)} %maximum_bitcast_fusion) | data formatting | bytes 1376256 | tf_op jit(solution)/shard_map/all_to_all | solution.py:137
  35.0 9.5 %all-to-all-start = ((f32[32,1,5376]{2,1,0:T(1,128)}), f32[32,1,5376]{2,1,0:T(1,128)S(1)}, u32[]{:S(2)}, u32[]{:S(2)}) async-start(f32[32,1,5376]{2,1,0:T(1,128)} %copy.44), calls=%async_computation | async-start | bytes 1376256 | tf_op jit(solution)/shard_map/all_to_all | solution.py:137
  44.5 1.2 %constant_dynamic-slice_fusion.1 = (f32[128,768]{1,0:T(8,128)S(1)}, f32[128,768]{1,0:T(8,128)S(1)}) fusion(f32[512,768]{1,0:T(8,128)} %refs_4_.7, s32[]{:T(128)S(6)} %select_n.90, f32[512,768]{1,0:T(8,128)} %refs_3_.7), kind=kLoop, calls=%fused_computation.32 | loop fusion | bytes 1572868 | tf_op jit(solution)/shard_map/dynamic_slice | solution.py:153
  46.0 1.1 constant_dynamic-slice_fusion.3
  47.1 0.2 copy.45
  47.3 0.2 copy.56
  47.4 15.1 %all-to-all-done = f32[32,1,5376]{2,1,0:T(1,128)S(1)} async-done(((f32[32,1,5376]{2,1,0:T(1,128)}), f32[32,1,5376]{2,1,0:T(1,128)S(1)}, u32[]{:S(2)}, u32[]{:S(2)}) %all-to-all-start) | async-done | bytes 688160 | tf_op jit(solution)/shard_map/all_to_all | solution.py:137
  62.9 0.3 div.34
  63.5 0.5 broadcast.38
  64.0 0.8 reduce
  64.9 0.8 reshape.157
  65.7 6.3 %all-to-all-start.1 = ((bf16[32,2,2688]{2,1,0:T(2,128)(2,1)}), bf16[32,2,2688]{2,1,0:T(2,128)(2,1)S(1)}, u32[]{:S(2)}, u32[]{:S(2)}) async-start(bf16[32,2,2688]{2,1,0:T(2,128)(2,1)} %reshape.157), calls=%async_computation.1 | async-start | bytes 688128 | tf_op jit(solution)/shard_map/all_to_all | solution.py:158
  72.1 1.3 %collective-permute-start.8 = (f32[32,24,128]{2,1,0:T(8,128)S(1)}, f32[32,24,128]{2,1,0:T(8,128)S(1)}, u32[]{:S(2)}, u32[]{:S(2)}) collective-permute-start(f32[32,24,128]{2,1,0:T(8,128)S(1)} %bitcast.107), channel_id=1, source_target_pairs={{0,128},{64,192},{128,0},{192,64},{1,129},{65,193},{129,1},{193,65... | collective-permute-start | bytes 1179656 | tf_op jit(solution)/shard_map/ppermute | solution.py:54
  73.4 0.3 reshape.147.refs_1_
  73.7 0.3 collective-permute-start.3
  74.1 3.0 %collective-permute-start.10 = (f32[32,24,128]{2,1,0:T(8,128)S(1)}, f32[32,24,128]{2,1,0:T(8,128)S(1)}, u32[]{:S(2)}, u32[]{:S(2)}) collective-permute-start(f32[32,24,128]{2,1,0:T(8,128)S(1)} %bitcast.108), channel_id=1, source_target_pairs={{0,64},{64,0},{128,192},{192,128},{1,65},{65,1},{129,193},{193,129... | collective-permute-start | bytes 1179656 | tf_op jit(solution)/shard_map/ppermute | solution.py:53
  77.1 11.7 %collective-permute-done.3.refs_1_ = f32[32,24,96]{2,1,0:T(8,128)S(1)} collective-permute-done((f32[32,24,96]{2,1,0:T(8,128)S(1)}, f32[32,24,96]{2,1,0:T(8,128)S(1)}, u32[]{:S(2)}, u32[]{:S(2)}) %collective-permute-start.3) | collective-permute-done | bytes 294944 | tf_op jit(solution)/shard_map/ppermute | solution.py:54
  88.8 3.4 %collective-permute-start.4 = (f32[32,24,96]{2,1,0:T(8,128)S(1)}, f32[32,24,96]{2,1,0:T(8,128)}, u32[]{:S(2)}, u32[]{:S(2)}) collective-permute-start(f32[32,24,96]{2,1,0:T(8,128)S(1)} %collective-permute-done.3.refs_1_), channel_id=1, source_target_pairs={{0,64},{64,0},{128,192},{192,128},{1,65},{65,1},{129,193},{193,129... | collective-permute-start | bytes 884744 | tf_op jit(solution)/shard_map/ppermute | solution.py:55
  92.3 0.3 reshape.158
  92.6 0.4 constant_dynamic-slice_fusion
  93.0 1.3 %collective-permute-start.6 = (bf16[16,5376]{1,0:T(8,128)(2,1)S(1)}, bf16[16,5376]{1,0:T(8,128)(2,1)S(1)}, u32[]{:S(2)}, u32[]{:S(2)}) collective-permute-start(bf16[16,5376]{1,0:T(8,128)(2,1)S(1)} %bitcast.117), channel_id=1, source_target_pairs={{0,128},{64,192},{128,0},{192,64},{1,129},{65,193},{129,1},{193,65... | collective-permute-start | bytes 516104 | tf_op jit(solution)/shard_map/ppermute | solution.py:39
  94.3 2.5 %shard_map.109 = (f32[4,96,768]{2,1,0:T(8,128)}, f32[4,96,768]{2,1,0:T(8,128)}) custom-call(s32[1]{0:T(128)} %bitcast.refs_0_, f32[32,24,96]{2,1,0:T(8,128)} %copy-done.1, f32[32,24,96]{2,1,0:T(8,128)} %collective-permute-done.5.refs_2_, f32[4,96,768]{2,1,0:T(8,128)} %refs_3_.5, f32[4,96,768]{2,1,0:T(8,128)} %refs_4_.5), custom_call_target="tpu_custom_call" | custom-call | tf_op jit(solution)/shard_map/pallas_call | solution.py:98
  96.9 0.7 copy-done.6
  97.6 2.7 %shard_map.111 = (f32[512,768]{1,0:T(8,128)}, f32[512,768]{1,0:T(8,128)}) custom-call(s32[1]{0:T(128)} %bitcast.refs_0_, f32[32,24,128]{2,1,0:T(8,128)} %bitcast.109, f32[32,24,128]{2,1,0:T(8,128)} %copy-done.6, f32[512,768]{1,0:T(8,128)} %refs_3_.7, f32[512,768]{1,0:T(8,128)} %refs_4_.7), custom_call_target="tpu_custom_call" | custom-call | tf_op jit(solution)/shard_map/pallas_call | solution.py:98
  100.3 2.6 %shard_map.110 = (f32[4,96,768]{2,1,0:T(8,128)}, f32[4,96,768]{2,1,0:T(8,128)}) custom-call(s32[1]{0:T(128)} %bitcast.refs_0_, f32[32,24,96]{2,1,0:T(8,128)} %copy-done.5, f32[32,24,96]{2,1,0:T(8,128)} %collective-permute-done.4.refs_2_, f32[4,96,768]{2,1,0:T(8,128)} %refs_3_.5, ...), custom_call_target="tpu_custom_call", output_to_operand_aliasing={{0}: (5, {}), {1}: (6, {})} | custom-call | tf_op jit(solution)/shard_map/pallas_call | solution.py:98
  102.8 0.7 copy-done.4
  103.6 2.7 %shard_map.112 = (f32[512,768]{1,0:T(8,128)}, f32[512,768]{1,0:T(8,128)}) custom-call(s32[1]{0:T(128)} %bitcast.refs_0_, f32[32,24,128]{2,1,0:T(8,128)} %copy-done.3, f32[32,24,128]{2,1,0:T(8,128)} %copy-done.4, f32[512,768]{1,0:T(8,128)} %refs_3_.7, f32[512,768]{1,0:T(8,128)} %refs_4_.7, ...), custom_call_target="tpu_custom_call", output_to_operand_aliasing={{0}: (5, {}), {1}: (6, {})} | custom-call | tf_op jit(solution)/shard_map/pallas_call | solution.py:98
  106.3 0.8 collective-permute-start.7
  107.1 1.2 %collective-permute-done.7 = bf16[2,16,5376]{2,1,0:T(8,128)(2,1)S(1)} collective-permute-done((bf16[2,16,5376]{2,1,0:T(8,128)(2,1)S(1)}, bf16[2,16,5376]{2,1,0:T(8,128)(2,1)S(1)}, u32[]{:S(2)}, u32[]{:S(2)}) %collective-permute-start.7) | collective-permute-done | bytes 344096 | tf_op jit(solution)/shard_map/ppermute | solution.py:43
  108.6 0.3 copy.52
  108.9 1.0 reshape.156
  110.0 0.6 reshape.152
  110.6 1.1 %reshape.153 = bf16[4,24,1536]{2,1,0:T(8,128)(2,1)} reshape(bf16[4,24,16,96]{3,2,1,0:T(8,128)(2,1)S(1)} %copy.51) | data formatting | bytes 589824 | tf_op jit(solution)/shard_map/reshape | solution.py:175
  (54 shorter events, 2.5 us)
Async XLA Ops:
  2.3 1.1 copy-start.2
  5.8 5.1 %collective-permute-start = (f32[2,86016]{1,0:T(2,128)S(1)}, f32[2,86016]{1,0:T(2,128)S(1)}, u32[]{:S(2)}, u32[]{:S(2)}) collective-permute-start(f32[2,86016]{1,0:T(2,128)S(1)} %bitcast.125), channel_id=1, source_target_pairs={{0,64},{64,0},{128,192},{192,128},{1,65},{65,1},{129,193},{193,129... | collective-permute-start | bytes 2064392 | tf_op jit(solution)/shard_map/ppermute | solution.py:29
  12.2 9.4 %collective-permute-start.1 = (f32[86016]{0:T(1024)S(1)}, f32[86016]{0:T(1024)S(1)}, u32[]{:S(2)}, u32[]{:S(2)}) collective-permute-start(f32[86016]{0:T(1024)S(1)} %bitcast.130), channel_id=1, source_target_pairs={{0,128},{64,192},{128,0},{192,64},{1,129},{65,193},{129,1},{193,65... | collective-permute-start | bytes 1032200 | tf_op jit(solution)/shard_map/ppermute | solution.py:32
  21.6 9.9 %collective-permute-start.2 = (f32[86016]{0:T(1024)S(1)}, f32[86016]{0:T(1024)S(1)}, u32[]{:S(2)}, u32[]{:S(2)}) collective-permute-start(f32[86016]{0:T(1024)S(1)} %add.58), channel_id=1, source_target_pairs={{0,1},{1,0},{2,3},{3,2},{4,5},{5,4},{6,7},{7,6},{8,9},{9,8},{10,11... | collective-permute-start | bytes 1032200 | tf_op jit(solution)/shard_map/ppermute | solution.py:131
  35.0 27.5 %all-to-all-start = ((f32[32,1,5376]{2,1,0:T(1,128)}), f32[32,1,5376]{2,1,0:T(1,128)S(1)}, u32[]{:S(2)}, u32[]{:S(2)}) async-start(f32[32,1,5376]{2,1,0:T(1,128)} %copy.44), calls=%async_computation | async-start | bytes 1376256 | tf_op jit(solution)/shard_map/all_to_all | solution.py:137
  65.7 26.6 %all-to-all-start.1 = ((bf16[32,2,2688]{2,1,0:T(2,128)(2,1)}), bf16[32,2,2688]{2,1,0:T(2,128)(2,1)S(1)}, u32[]{:S(2)}, u32[]{:S(2)}) async-start(bf16[32,2,2688]{2,1,0:T(2,128)(2,1)} %reshape.157), calls=%async_computation.1 | async-start | bytes 688128 | tf_op jit(solution)/shard_map/all_to_all | solution.py:158
  72.1 20.9 %copy-start = (f32[4,8,24,128]{3,2,1,0:T(8,128)}, f32[4,8,24,128]{3,2,1,0:T(8,128)S(1)}, u32[]{:S(2)}) copy-start(f32[4,8,24,128]{3,2,1,0:T(8,128)S(1)} %copy.63) | copy-start | bytes 1179652
  72.1 20.0 %collective-permute-start.8 = (f32[32,24,128]{2,1,0:T(8,128)S(1)}, f32[32,24,128]{2,1,0:T(8,128)S(1)}, u32[]{:S(2)}, u32[]{:S(2)}) collective-permute-start(f32[32,24,128]{2,1,0:T(8,128)S(1)} %bitcast.107), channel_id=1, source_target_pairs={{0,128},{64,192},{128,0},{192,64},{1,129},{65,193},{129,1},{193,65... | collective-permute-start | bytes 1179656 | tf_op jit(solution)/shard_map/ppermute | solution.py:54
  73.7 20.6 %copy-start.1 = (f32[32,24,96]{2,1,0:T(8,128)}, f32[32,24,96]{2,1,0:T(8,128)S(1)}, u32[]{:S(2)}) copy-start(f32[32,24,96]{2,1,0:T(8,128)S(1)} %reshape.147.refs_1_) | copy-start | bytes 884740
  73.7 15.1 %collective-permute-start.3 = (f32[32,24,96]{2,1,0:T(8,128)S(1)}, f32[32,24,96]{2,1,0:T(8,128)S(1)}, u32[]{:S(2)}, u32[]{:S(2)}) collective-permute-start(f32[32,24,96]{2,1,0:T(8,128)S(1)} %reshape.147.refs_1_), channel_id=1, source_target_pairs={{0,128},{64,192},{128,0},{192,64},{1,129},{65,193},{129,1},{193,65... | collective-permute-start | bytes 884744 | tf_op jit(solution)/shard_map/ppermute | solution.py:54
  74.1 22.8 %collective-permute-start.10 = (f32[32,24,128]{2,1,0:T(8,128)S(1)}, f32[32,24,128]{2,1,0:T(8,128)S(1)}, u32[]{:S(2)}, u32[]{:S(2)}) collective-permute-start(f32[32,24,128]{2,1,0:T(8,128)S(1)} %bitcast.108), channel_id=1, source_target_pairs={{0,64},{64,0},{128,192},{192,128},{1,65},{65,1},{129,193},{193,129... | collective-permute-start | bytes 1179656 | tf_op jit(solution)/shard_map/ppermute | solution.py:53
  77.1 17.2 %collective-permute-start.5 = (f32[32,24,96]{2,1,0:T(8,128)S(1)}, f32[32,24,96]{2,1,0:T(8,128)}, u32[]{:S(2)}, u32[]{:S(2)}) collective-permute-start(f32[32,24,96]{2,1,0:T(8,128)S(1)} %reshape.147.refs_1_), channel_id=1, source_target_pairs={{0,64},{64,0},{128,192},{192,128},{1,65},{65,1},{129,193},{193,129... | collective-permute-start | bytes 884744 | tf_op jit(solution)/shard_map/ppermute | solution.py:53
  88.8 8.0 %copy-start.5 = (f32[32,24,96]{2,1,0:T(8,128)}, f32[32,24,96]{2,1,0:T(8,128)S(1)}, u32[]{:S(2)}) copy-start(f32[32,24,96]{2,1,0:T(8,128)S(1)} %collective-permute-done.3.refs_1_) | copy-start | bytes 884740
  88.8 11.5 %collective-permute-start.4 = (f32[32,24,96]{2,1,0:T(8,128)S(1)}, f32[32,24,96]{2,1,0:T(8,128)}, u32[]{:S(2)}, u32[]{:S(2)}) collective-permute-start(f32[32,24,96]{2,1,0:T(8,128)S(1)} %collective-permute-done.3.refs_1_), channel_id=1, source_target_pairs={{0,64},{64,0},{128,192},{192,128},{1,65},{65,1},{129,193},{193,129... | collective-permute-start | bytes 884744 | tf_op jit(solution)/shard_map/ppermute | solution.py:55
  92.2 4.7 %copy-start.3 = (f32[32,24,128]{2,1,0:T(8,128)}, f32[32,24,128]{2,1,0:T(8,128)S(1)}, u32[]{:S(2)}) copy-start(f32[32,24,128]{2,1,0:T(8,128)S(1)} %collective-permute-done.8.refs_1_) | copy-start | bytes 1179652
  92.2 10.6 %collective-permute-start.9 = (f32[32,24,128]{2,1,0:T(8,128)S(1)}, f32[32,24,128]{2,1,0:T(8,128)S(1)}, u32[]{:S(2)}, u32[]{:S(2)}) collective-permute-start(f32[32,24,128]{2,1,0:T(8,128)S(1)} %collective-permute-done.8.refs_1_), channel_id=1, source_target_pairs={{0,64},{64,0},{128,192},{192,128},{1,65},{65,1},{129,193},{193,129... | collective-permute-start | bytes 1179656 | tf_op jit(solution)/shard_map/ppermute | solution.py:55
  93.0 13.3 %collective-permute-start.6 = (bf16[16,5376]{1,0:T(8,128)(2,1)S(1)}, bf16[16,5376]{1,0:T(8,128)(2,1)S(1)}, u32[]{:S(2)}, u32[]{:S(2)}) collective-permute-start(bf16[16,5376]{1,0:T(8,128)(2,1)S(1)} %bitcast.117), channel_id=1, source_target_pairs={{0,128},{64,192},{128,0},{192,64},{1,129},{65,193},{129,1},{193,65... | collective-permute-start | bytes 516104 | tf_op jit(solution)/shard_map/ppermute | solution.py:39
  96.9 0.7 copy-start.6
  102.8 0.7 copy-start.4
  106.3 2.1 %collective-permute-start.7 = (bf16[2,16,5376]{2,1,0:T(8,128)(2,1)S(1)}, bf16[2,16,5376]{2,1,0:T(8,128)(2,1)S(1)}, u32[]{:S(2)}, u32[]{:S(2)}) collective-permute-start(bf16[2,16,5376]{2,1,0:T(8,128)(2,1)S(1)} %maximum_select_fusion.3), channel_id=1, source_target_pairs={{0,64},{64,0},{128,192},{192,128},{1,65},{65,1},{129,193},{193,129... | collective-permute-start | bytes 1032200 | tf_op jit(solution)/shard_map/ppermute | solution.py:43

commit v10 on v8

--- a/solution.py
+++ b/solution.py
@@ -23,13 +23,14 @@
     r = lax.axis_index("rep")
     n = lax.axis_size("rep")
     core, x_lo = r % 2, r // 2
-    x4 = x.reshape(2, 2, -1)
-    mine = lax.dynamic_index_in_dim(x4, core, 1, keepdims=False)
-    other = lax.dynamic_index_in_dim(x4, 1 - core, 1, keepdims=False)
-    a = mine + lax.ppermute(other, "rep", pairs(n, 1))
-    keep = lax.dynamic_index_in_dim(a, x_lo, 0, keepdims=False)
-    send = lax.dynamic_index_in_dim(a, 1 - x_lo, 0, keepdims=False)
-    return keep + lax.ppermute(send, "rep", pairs(n, 2))
+    x4 = jax.tree.map(lambda a: a.reshape(2, 2, -1), x)
+    pick = lambda tree, i, axis: jax.tree.map(
+        lambda a: lax.dynamic_index_in_dim(a, i, axis, keepdims=False), tree
+    )
+    got = lax.ppermute(pick(x4, 1 - core, 1), "rep", pairs(n, 1))
+    a = jax.tree.map(jnp.add, pick(x4, core, 1), got)
+    got = lax.ppermute(pick(a, 1 - x_lo, 0), "rep", pairs(n, 2))
+    return jax.tree.map(jnp.add, pick(a, x_lo, 0), got)
 
 
 def rep_gather(x):
@@ -113,13 +114,15 @@
     ex = expert_change[0].reshape(mats, esize)
     tx = table_change[0].reshape(width, per_half, groups, sub)
     tx = jnp.transpose(tx, (2, 0, 1, 3)).reshape(groups, -1)
-    q = rep_scatter(jnp.concatenate([ex, tx], axis=1))
+    q = rep_scatter((ex, tx))
 
     other = lax.ppermute(q, "tp", pairs(tensor, 1))
-    halves = jnp.where(t == 0, jnp.stack([q, other]), jnp.stack([other, q]))
-    he = halves[:, :esize].reshape(tensor, width, per_half, rows)
+    halves = jax.tree.map(
+        lambda a, b: jnp.where(t == 0, jnp.stack([a, b]), jnp.stack([b, a])), q, other
+    )
+    he = halves[0].reshape(tensor, width, per_half, rows)
     he = jnp.transpose(he, (0, 2, 1, 3)).reshape(shards, width * rows)
-    ht = halves[:, esize:].reshape(tensor, width, per_half, sub)
+    ht = halves[1].reshape(tensor, width, per_half, sub)
     ht = jnp.transpose(ht, (0, 2, 1, 3)).reshape(shards, width * sub)
     got = lax.all_to_all(jnp.concatenate([he, ht], 1), "shard", 0, 0, tiled=True)
 

time: 111 us -> 106 us (0.955)
  waiting for transfers between devices: 48 us -> 41.4 us
  starting transfers between devices: 30.5 us -> 33.6 us
    ppermute x2 -> x4, waiting for transfers between devices: 11 us -> 6.74 us  [the longest x2 5.74 us: rep_scatter(): got = lax.ppermute(pick(a, 1 - x_lo, 0), 'rep', pairs(n, 2))]
    ppermute x1 -> x2, waiting for transfers between devices: 8.85 us -> 4.69 us  [local(): other = lax.ppermute(q, 'tp', pairs(tensor, 1))]
    all_to_all x1, starting transfers between devices: 9.47 us -> 12.7 us  [local(): lax.all_to_all(jnp.concatenate([he, ht], 1), 'shard', 0, 0, tiled=True)]
    another operation x0 -> x4, local copies, waits for them, and re-layouts: none -> 2.3 us  [the longest x2 2.1 us: rep_scatter(): x4 = jax.tree.map(lambda a: a.reshape(2, 2, -1), x)]
    concatenate x3 -> x0, local copies, waits for them, and re-layouts: 2.21 us -> none  [local(): q = rep_scatter(jnp.concatenate([ex, tx], axis=1))]
    ppermute x1, starting transfers between devices: 1.3 us -> 0.09 us  [rep_gather(): cross = lax.ppermute(x, 'rep', pairs(n, 2))]
    ppermute x2 -> x4, starting transfers between devices: 3.42 us -> 4.08 us  [the longest x2 3.44 us: rep_scatter(): got = lax.ppermute(pick(x4, 1 - core, 1), 'rep', pairs(n, 1))]
    unnamed x29 -> x27, local copies, waits for them, and re-layouts: 3.97 us -> 3.34 us
  transfers between devices with their start and end apart: 13 -> 16, of which waited for: 6 -> 9; matrix products, arithmetic and copies ran while one was open for 4% -> 7% of each run, Pallas kernels for 9% -> 9%
where the time goes in v10:
time: 106 us; the launch traced here: 105 us
  waiting for transfers between devices  41.4 us (39%)
  starting transfers between devices  33.6 us (32%)
  local copies, waits for them, and re-layouts  17.3 us (16%)
  Pallas kernels  9.48 us (9%)
  other arithmetic  2.17 us (2%)
  between operations  1.17 us (1%)
    all_to_all x1, waiting for transfers between devices, local(): lax.all_to_all(jnp.concatenate([he, ht], 1), 'shard', 0, 0, tiled=True)  15.6 us
    all_to_all x1, starting transfers between devices, local(): lax.all_to_all(jnp.concatenate([he, ht], 1), 'shard', 0, 0, tiled=True)  12.7 us
    ppermute x2, waiting for transfers between devices, gather_pieces(): cross = lax.ppermute(x, 'rep', pairs(n, 2))  12.6 us
    pallas_call x2, Pallas kernels, fused_update(): pl.pallas_call(lambda *refs: update_kernel(scale, *refs), grid_spec=pltpu...  9.48 us
    all_to_all x1, starting transfers between devices, local(): back = lax.all_to_all(back, 'shard', 0, 0, tiled=True)  6.45 us
    ppermute x2, waiting for transfers between devices, rep_scatter(): got = lax.ppermute(pick(a, 1 - x_lo, 0), 'rep', pairs(n, 2))  5.74 us
    ppermute x4, starting transfers between devices, gather_pieces(): sib, sib_cross = lax.ppermute((x, cross), 'rep', pairs(n, 1))  5.67 us
    ppermute x2, waiting for transfers between devices, local(): other = lax.ppermute(q, 'tp', pairs(tensor, 1))  4.69 us
  transfers between devices with their start and end apart: 16, of which 9 were waited for; matrix products, arithmetic and copies ran while one was open for 7% of the time, Pallas kernels for 9%

profile of v10, /device:TPU:1, one launch (start us, length us, event | category | flops | bytes accessed | tf_op | source)
XLA Modules:
  0.0 105.0 jit_solution(11987407639580290922)
XLA Ops:
  0.7 1.6 %reshape_reshape_squeeze.3 = f32[2,2,36864]{2,1,0:T(2,128)S(1)} reshape(f32[1,4,24,1536]{3,2,1,0:T(8,128)} %param.6) | data formatting | bytes 1179648 | tf_op jit(solution)/shard_map/reshape;reshape;squeeze | solution.py:26
  2.3 0.5 constant_dynamic-slice_fusion.12
  2.8 0.2 copy.77
  3.1 3.3 %collective-permute-start = (f32[2,36864]{1,0:T(2,128)S(1)}, f32[2,36864]{1,0:T(2,128)S(1)}, u32[]{:S(2)}, u32[]{:S(2)}) collective-permute-start(f32[2,36864]{1,0:T(2,128)S(1)} %bitcast.132), channel_id=1, source_target_pairs={{0,64},{64,0},{128,192},{192,128},{1,65},{65,1},{129,193},{193,129... | collective-permute-start | bytes 884744 | tf_op jit(solution)/shard_map/ppermute | solution.py:30
  6.4 0.5 reshape_squeeze.3
  7.0 0.5 reshape_reshape.2
  7.5 0.7 constant_dynamic-slice_fusion.8
  8.2 0.3 copy.76
  8.6 0.3 bitcast_add_fusion.4
  8.9 0.3 constant_dynamic-slice_fusion.9
  9.3 1.0 collective-permute-done.3
  10.3 0.4 bitcast_add_fusion
  10.7 0.3 constant_dynamic-slice_fusion.5
  11.0 0.5 collective-permute-start.4
  11.6 2.6 %collective-permute-done.1 = f32[36864]{0:T(1024)S(1)} collective-permute-done((f32[36864]{0:T(1024)S(1)}, f32[36864]{0:T(1024)S(1)}, u32[]{:S(2)}, u32[]{:S(2)}) %collective-permute-start.1) | collective-permute-done | bytes 147488 | tf_op jit(solution)/shard_map/ppermute | solution.py:32
  14.3 1.1 %collective-permute-start.2 = (f32[36864]{0:T(1024)S(1)}, f32[36864]{0:T(1024)S(1)}, u32[]{:S(2)}, u32[]{:S(2)}) collective-permute-start(f32[36864]{0:T(1024)S(1)} %add.70), channel_id=1, source_target_pairs={{0,1},{1,0},{2,3},{3,2},{4,5},{5,4},{6,7},{7,6},{8,9},{9,8},{10,11... | collective-permute-start | bytes 442376 | tf_op jit(solution)/shard_map/ppermute | solution.py:119
  15.4 3.1 %collective-permute-done.4 = f32[49152]{0:T(1024)S(1)} collective-permute-done((f32[49152]{0:T(1024)S(1)}, f32[49152]{0:T(1024)S(1)}, u32[]{:S(2)}, u32[]{:S(2)}) %collective-permute-start.4) | collective-permute-done | bytes 196640 | tf_op jit(solution)/shard_map/ppermute | solution.py:32
  18.5 1.1 %collective-permute-start.5 = (f32[49152]{0:T(1024)S(1)}, f32[49152]{0:T(1024)S(1)}, u32[]{:S(2)}, u32[]{:S(2)}) collective-permute-start(f32[49152]{0:T(1024)S(1)} %add.72), channel_id=1, source_target_pairs={{0,1},{1,0},{2,3},{3,2},{4,5},{5,4},{6,7},{7,6},{8,9},{9,8},{10,11... | collective-permute-start | bytes 589832 | tf_op jit(solution)/shard_map/ppermute | solution.py:119
  19.7 1.8 %collective-permute-done.2 = f32[36864]{0:T(1024)S(1)} collective-permute-done((f32[36864]{0:T(1024)S(1)}, f32[36864]{0:T(1024)S(1)}, u32[]{:S(2)}, u32[]{:S(2)}) %collective-permute-start.2) | collective-permute-done | bytes 147488 | tf_op jit(solution)/shard_map/ppermute | solution.py:119
  21.9 2.9 %collective-permute-done.5 = f32[49152]{0:T(1024)S(1)} collective-permute-done((f32[49152]{0:T(1024)S(1)}, f32[49152]{0:T(1024)S(1)}, u32[]{:S(2)}, u32[]{:S(2)}) %collective-permute-start.5) | collective-permute-done | bytes 196640 | tf_op jit(solution)/shard_map/ppermute | solution.py:119
  25.1 1.6 %copy.40 = f32[32,1,5376]{2,1,0:T(1,128)} copy(f32[32,1,5376]{2,0,1:T(8,128)S(1)} %maximum_bitcast_fusion) | data formatting | bytes 1376256 | tf_op jit(solution)/shard_map/all_to_all | solution.py:127
  26.6 12.7 %all-to-all-start = ((f32[32,1,5376]{2,1,0:T(1,128)}), f32[32,1,5376]{2,1,0:T(1,128)S(1)}, u32[]{:S(2)}, u32[]{:S(2)}) async-start(f32[32,1,5376]{2,1,0:T(1,128)} %copy.40), calls=%async_computation | async-start | bytes 1376256 | tf_op jit(solution)/shard_map/all_to_all | solution.py:127
  39.3 1.1 %constant_dynamic-slice_fusion.3 = (f32[1,96,768]{2,1,0:T(8,128)S(1)}, f32[1,96,768]{2,1,0:T(8,128)S(1)}) fusion(f32[4,96,768]{2,1,0:T(8,128)} %refs_6_.2, s32[]{:T(128)S(6)} %select_n.107, f32[4,96,768]{2,1,0:T(8,128)} %refs_5_.2), kind=kLoop, calls=%fused_computation.36 | loop fusion | bytes 1179652 | tf_op jit(solution)/shard_map/jit(dynamic_index_in_dim)/dynamic_slice | solution.py:136
  40.8 1.2 %constant_dynamic-slice_fusion.1 = (f32[128,768]{1,0:T(8,128)S(1)}, f32[128,768]{1,0:T(8,128)S(1)}) fusion(f32[512,768]{1,0:T(8,128)} %refs_6_.3, s32[]{:T(128)S(6)} %select_n.108, f32[512,768]{1,0:T(8,128)} %refs_5_.3), kind=kLoop, calls=%fused_computation.34 | loop fusion | bytes 1572868 | tf_op jit(solution)/shard_map/dynamic_slice | solution.py:143
  42.3 15.6 %all-to-all-done = f32[32,1,5376]{2,1,0:T(1,128)S(1)} async-done(((f32[32,1,5376]{2,1,0:T(1,128)}), f32[32,1,5376]{2,1,0:T(1,128)S(1)}, u32[]{:S(2)}, u32[]{:S(2)}) %all-to-all-start) | async-done | bytes 688160 | tf_op jit(solution)/shard_map/all_to_all | solution.py:127
  58.1 0.3 div.34
  58.8 0.5 broadcast.40
  59.4 0.8 reduce
  60.2 0.8 reshape.159
  61.0 6.5 %all-to-all-start.1 = ((bf16[32,2,2688]{2,1,0:T(2,128)(2,1)}), bf16[32,2,2688]{2,1,0:T(2,128)(2,1)S(1)}, u32[]{:S(2)}, u32[]{:S(2)}) async-start(bf16[32,2,2688]{2,1,0:T(2,128)(2,1)} %reshape.159), calls=%async_computation.1 | async-start | bytes 688128 | tf_op jit(solution)/shard_map/all_to_all | solution.py:148
  67.7 0.3 reshape.149.refs_1_
  68.0 1.5 %collective-permute-start.7 = (f32[32,24,96]{2,1,0:T(8,128)S(1)}, f32[32,24,96]{2,1,0:T(8,128)S(1)}, u32[]{:S(2)}, u32[]{:S(2)}) collective-permute-start(f32[32,24,96]{2,1,0:T(8,128)S(1)} %reshape.149.refs_1_), channel_id=1, source_target_pairs={{0,128},{64,192},{128,0},{192,64},{1,129},{65,193},{129,1},{193,65... | collective-permute-start | bytes 884744 | tf_op jit(solution)/shard_map/ppermute | solution.py:54
  69.5 2.6 %collective-permute-start.6 = (f32[32,24,96]{2,1,0:T(8,128)S(1)}, f32[32,24,96]{2,1,0:T(8,128)S(1)}, u32[]{:S(2)}, u32[]{:S(2)}) collective-permute-start(f32[32,24,96]{2,1,0:T(8,128)S(1)} %reshape.149.refs_1_), channel_id=1, source_target_pairs={{0,64},{64,0},{128,192},{192,128},{1,65},{65,1},{129,193},{193,129... | collective-permute-start | bytes 884744 | tf_op jit(solution)/shard_map/ppermute | solution.py:55
  72.1 12.6 %collective-permute-done.7.refs_3_ = f32[32,24,96]{2,1,0:T(8,128)S(1)} collective-permute-done((f32[32,24,96]{2,1,0:T(8,128)S(1)}, f32[32,24,96]{2,1,0:T(8,128)S(1)}, u32[]{:S(2)}, u32[]{:S(2)}) %collective-permute-start.7) | collective-permute-done | bytes 294944 | tf_op jit(solution)/shard_map/ppermute | solution.py:54
  84.7 3.0 %collective-permute-start.8 = (f32[32,24,96]{2,1,0:T(8,128)S(1)}, f32[32,24,96]{2,1,0:T(8,128)}, u32[]{:S(2)}, u32[]{:S(2)}) collective-permute-start(f32[32,24,96]{2,1,0:T(8,128)S(1)} %collective-permute-done.7.refs_3_), channel_id=1, source_target_pairs={{0,64},{64,0},{128,192},{192,128},{1,65},{65,1},{129,193},{193,129... | collective-permute-start | bytes 884744 | tf_op jit(solution)/shard_map/ppermute | solution.py:55
  87.7 0.3 reshape.160
  88.0 0.4 constant_dynamic-slice_fusion
  88.6 0.6 collective-permute-done.8.refs_4_
  89.1 0.2 copy-done.6
  89.3 4.6 %shard_map.109 = (f32[4,96,768]{2,1,0:T(8,128)}, f32[4,96,768]{2,1,0:T(8,128)}) custom-call(s32[1]{0:T(128)} %bitcast.refs_0_, f32[32,24,96]{2,1,0:T(8,128)} %copy-done.1, f32[32,24,96]{2,1,0:T(8,128)} %copy-done.6, f32[32,24,96]{2,1,0:T(8,128)} %copy-done.4, f32[32,24,96]{2,1,0:T(8,128)} %collective-permute-done.8.refs_4_, f32[4,96,768]{2,1,0:T(8,128)} %refs_5_.2, ...), custom_call_target="tpu_custom_call" | custom-call | tf_op jit(solution)/shard_map/pallas_call | solution.py:87
  93.9 0.7 copy-done.5
  94.7 4.9 %shard_map.110 = (f32[512,768]{1,0:T(8,128)}, f32[512,768]{1,0:T(8,128)}) custom-call(s32[1]{0:T(128)} %bitcast.refs_0_, f32[32,24,128]{2,1,0:T(8,128)} %bitcast.113, f32[32,24,128]{2,1,0:T(8,128)} %copy-done.5, f32[32,24,128]{2,1,0:T(8,128)} %copy-done.3, f32[32,24,128]{2,1,0:T(8,128)} %collective-permute-done.13.refs_4_, f32[512,768]{1,0:T(8,128)} %refs_5_.3, ...), custom_call_target="tpu_custom_call" | custom-call | tf_op jit(solution)/shard_map/pallas_call | solution.py:87
  99.6 0.8 collective-permute-start.10
  100.4 1.2 %collective-permute-done.10 = bf16[2,16,5376]{2,1,0:T(8,128)(2,1)S(1)} collective-permute-done((bf16[2,16,5376]{2,1,0:T(8,128)(2,1)S(1)}, bf16[2,16,5376]{2,1,0:T(8,128)(2,1)S(1)}, u32[]{:S(2)}, u32[]{:S(2)}) %collective-permute-start.10) | collective-permute-done | bytes 344096 | tf_op jit(solution)/shard_map/ppermute | solution.py:44
  101.9 0.3 copy.48
  102.2 1.0 reshape.158
  103.2 0.6 reshape.154
  103.9 1.1 %reshape.155 = bf16[4,24,1536]{2,1,0:T(8,128)(2,1)} reshape(bf16[4,24,16,96]{3,2,1,0:T(8,128)(2,1)S(1)} %copy.47) | data formatting | bytes 589824 | tf_op jit(solution)/shard_map/reshape | solution.py:162
  (60 shorter events, 3.1 us)
Async XLA Ops:
  0.6 5.8 %copy-start.2 = (f32[1,24,8192]{2,1,0:T(8,128)S(1)}, f32[1,24,8192]{2,1,0:T(8,128)}, u32[]{:S(2)}) copy-start(f32[1,24,8192]{2,1,0:T(8,128)} %param.7) | copy-start | bytes 2359300
  3.1 5.5 %collective-permute-start = (f32[2,36864]{1,0:T(2,128)S(1)}, f32[2,36864]{1,0:T(2,128)S(1)}, u32[]{:S(2)}, u32[]{:S(2)}) collective-permute-start(f32[2,36864]{1,0:T(2,128)S(1)} %bitcast.132), channel_id=1, source_target_pairs={{0,64},{64,0},{128,192},{192,128},{1,65},{65,1},{129,193},{193,129... | collective-permute-start | bytes 884744 | tf_op jit(solution)/shard_map/ppermute | solution.py:30
  8.5 1.8 %collective-permute-start.3 = (f32[2,49152]{1,0:T(2,128)S(1)}, f32[2,49152]{1,0:T(2,128)S(1)}, u32[]{:S(2)}, u32[]{:S(2)}) collective-permute-start(f32[2,49152]{1,0:T(2,128)S(1)} %bitcast.130), channel_id=1, source_target_pairs={{0,64},{64,0},{128,192},{192,128},{1,65},{65,1},{129,193},{193,129... | collective-permute-start | bytes 1179656 | tf_op jit(solution)/shard_map/ppermute | solution.py:30
  9.2 5.0 %collective-permute-start.1 = (f32[36864]{0:T(1024)S(1)}, f32[36864]{0:T(1024)S(1)}, u32[]{:S(2)}, u32[]{:S(2)}) collective-permute-start(f32[36864]{0:T(1024)S(1)} %bitcast.135), channel_id=1, source_target_pairs={{0,128},{64,192},{128,0},{192,64},{1,129},{65,193},{129,1},{193,65... | collective-permute-start | bytes 442376 | tf_op jit(solution)/shard_map/ppermute | solution.py:32
  11.0 7.4 %collective-permute-start.4 = (f32[49152]{0:T(1024)S(1)}, f32[49152]{0:T(1024)S(1)}, u32[]{:S(2)}, u32[]{:S(2)}) collective-permute-start(f32[49152]{0:T(1024)S(1)} %bitcast.134), channel_id=1, source_target_pairs={{0,128},{64,192},{128,0},{192,64},{1,129},{65,193},{129,1},{193,65... | collective-permute-start | bytes 589832 | tf_op jit(solution)/shard_map/ppermute | solution.py:32
  14.3 7.2 %collective-permute-start.2 = (f32[36864]{0:T(1024)S(1)}, f32[36864]{0:T(1024)S(1)}, u32[]{:S(2)}, u32[]{:S(2)}) collective-permute-start(f32[36864]{0:T(1024)S(1)} %add.70), channel_id=1, source_target_pairs={{0,1},{1,0},{2,3},{3,2},{4,5},{5,4},{6,7},{7,6},{8,9},{9,8},{10,11... | collective-permute-start | bytes 442376 | tf_op jit(solution)/shard_map/ppermute | solution.py:119
  18.5 6.3 %collective-permute-start.5 = (f32[49152]{0:T(1024)S(1)}, f32[49152]{0:T(1024)S(1)}, u32[]{:S(2)}, u32[]{:S(2)}) collective-permute-start(f32[49152]{0:T(1024)S(1)} %add.72), channel_id=1, source_target_pairs={{0,1},{1,0},{2,3},{3,2},{4,5},{5,4},{6,7},{7,6},{8,9},{9,8},{10,11... | collective-permute-start | bytes 589832 | tf_op jit(solution)/shard_map/ppermute | solution.py:119
  26.6 31.3 %all-to-all-start = ((f32[32,1,5376]{2,1,0:T(1,128)}), f32[32,1,5376]{2,1,0:T(1,128)S(1)}, u32[]{:S(2)}, u32[]{:S(2)}) async-start(f32[32,1,5376]{2,1,0:T(1,128)} %copy.40), calls=%async_computation | async-start | bytes 1376256 | tf_op jit(solution)/shard_map/all_to_all | solution.py:127
  61.0 26.7 %all-to-all-start.1 = ((bf16[32,2,2688]{2,1,0:T(2,128)(2,1)}), bf16[32,2,2688]{2,1,0:T(2,128)(2,1)S(1)}, u32[]{:S(2)}, u32[]{:S(2)}) async-start(bf16[32,2,2688]{2,1,0:T(2,128)(2,1)} %reshape.159), calls=%async_computation.1 | async-start | bytes 688128 | tf_op jit(solution)/shard_map/all_to_all | solution.py:148
  67.6 26.3 %copy-start = (f32[4,8,24,128]{3,2,1,0:T(8,128)}, f32[4,8,24,128]{3,2,1,0:T(8,128)S(1)}, u32[]{:S(2)}) copy-start(f32[4,8,24,128]{3,2,1,0:T(8,128)S(1)} %copy.60) | copy-start | bytes 1179652
  67.6 20.0 %collective-permute-start.12 = (f32[32,24,128]{2,1,0:T(8,128)S(1)}, f32[32,24,128]{2,1,0:T(8,128)S(1)}, u32[]{:S(2)}, u32[]{:S(2)}) collective-permute-start(f32[32,24,128]{2,1,0:T(8,128)S(1)} %bitcast.111), channel_id=1, source_target_pairs={{0,128},{64,192},{128,0},{192,64},{1,129},{65,193},{129,1},{193,65... | collective-permute-start | bytes 1179656 | tf_op jit(solution)/shard_map/ppermute | solution.py:54
  67.9 21.2 %copy-start.1 = (f32[32,24,96]{2,1,0:T(8,128)}, f32[32,24,96]{2,1,0:T(8,128)S(1)}, u32[]{:S(2)}) copy-start(f32[32,24,96]{2,1,0:T(8,128)S(1)} %reshape.149.refs_1_) | copy-start | bytes 884740
  68.0 16.7 %collective-permute-start.7 = (f32[32,24,96]{2,1,0:T(8,128)S(1)}, f32[32,24,96]{2,1,0:T(8,128)S(1)}, u32[]{:S(2)}, u32[]{:S(2)}) collective-permute-start(f32[32,24,96]{2,1,0:T(8,128)S(1)} %reshape.149.refs_1_), channel_id=1, source_target_pairs={{0,128},{64,192},{128,0},{192,64},{1,129},{65,193},{129,1},{193,65... | collective-permute-start | bytes 884744 | tf_op jit(solution)/shard_map/ppermute | solution.py:54
  69.5 19.0 %collective-permute-start.6 = (f32[32,24,96]{2,1,0:T(8,128)S(1)}, f32[32,24,96]{2,1,0:T(8,128)S(1)}, u32[]{:S(2)}, u32[]{:S(2)}) collective-permute-start(f32[32,24,96]{2,1,0:T(8,128)S(1)} %reshape.149.refs_1_), channel_id=1, source_target_pairs={{0,64},{64,0},{128,192},{192,128},{1,65},{65,1},{129,193},{193,129... | collective-permute-start | bytes 884744 | tf_op jit(solution)/shard_map/ppermute | solution.py:55
  72.1 21.8 %collective-permute-start.11 = (f32[32,24,128]{2,1,0:T(8,128)S(1)}, f32[32,24,128]{2,1,0:T(8,128)S(1)}, u32[]{:S(2)}, u32[]{:S(2)}) collective-permute-start(f32[32,24,128]{2,1,0:T(8,128)S(1)} %bitcast.112), channel_id=1, source_target_pairs={{0,64},{64,0},{128,192},{192,128},{1,65},{65,1},{129,193},{193,129... | collective-permute-start | bytes 1179656 | tf_op jit(solution)/shard_map/ppermute | solution.py:55
  84.7 4.5 %copy-start.4 = (f32[32,24,96]{2,1,0:T(8,128)}, f32[32,24,96]{2,1,0:T(8,128)S(1)}, u32[]{:S(2)}) copy-start(f32[32,24,96]{2,1,0:T(8,128)S(1)} %collective-permute-done.7.refs_3_) | copy-start | bytes 884740
  84.7 4.4 %collective-permute-start.8 = (f32[32,24,96]{2,1,0:T(8,128)S(1)}, f32[32,24,96]{2,1,0:T(8,128)}, u32[]{:S(2)}, u32[]{:S(2)}) collective-permute-start(f32[32,24,96]{2,1,0:T(8,128)S(1)} %collective-permute-done.7.refs_3_), channel_id=1, source_target_pairs={{0,64},{64,0},{128,192},{192,128},{1,65},{65,1},{129,193},{193,129... | collective-permute-start | bytes 884744 | tf_op jit(solution)/shard_map/ppermute | solution.py:55
  87.6 6.3 %copy-start.3 = (f32[32,24,128]{2,1,0:T(8,128)}, f32[32,24,128]{2,1,0:T(8,128)S(1)}, u32[]{:S(2)}) copy-start(f32[32,24,128]{2,1,0:T(8,128)S(1)} %collective-permute-done.12.refs_3_) | copy-start | bytes 1179652
  87.6 6.3 %collective-permute-start.13 = (f32[32,24,128]{2,1,0:T(8,128)S(1)}, f32[32,24,128]{2,1,0:T(8,128)}, u32[]{:S(2)}, u32[]{:S(2)}) collective-permute-start(f32[32,24,128]{2,1,0:T(8,128)S(1)} %collective-permute-done.12.refs_3_), channel_id=1, source_target_pairs={{0,64},{64,0},{128,192},{192,128},{1,65},{65,1},{129,193},{193,129... | collective-permute-start | bytes 1179656 | tf_op jit(solution)/shard_map/ppermute | solution.py:55
  88.4 11.1 %collective-permute-start.9 = (bf16[16,5376]{1,0:T(8,128)(2,1)S(1)}, bf16[16,5376]{1,0:T(8,128)(2,1)S(1)}, u32[]{:S(2)}, u32[]{:S(2)}) collective-permute-start(bf16[16,5376]{1,0:T(8,128)(2,1)S(1)} %bitcast.119), channel_id=1, source_target_pairs={{0,128},{64,192},{128,0},{192,64},{1,129},{65,193},{129,1},{193,65... | collective-permute-start | bytes 516104 | tf_op jit(solution)/shard_map/ppermute | solution.py:40
  88.5 0.7 copy-start.6
  93.9 0.7 copy-start.5
  99.6 2.0 %collective-permute-start.10 = (bf16[2,16,5376]{2,1,0:T(8,128)(2,1)S(1)}, bf16[2,16,5376]{2,1,0:T(8,128)(2,1)S(1)}, u32[]{:S(2)}, u32[]{:S(2)}) collective-permute-start(bf16[2,16,5376]{2,1,0:T(8,128)(2,1)S(1)} %maximum_select_fusion.4), channel_id=1, source_target_pairs={{0,64},{64,0},{128,192},{192,128},{1,65},{65,1},{129,193},{193,129... | collective-permute-start | bytes 1032200 | tf_op jit(solution)/shard_map/ppermute | solution.py:44

commit v11 on v10

--- a/solution.py
+++ b/solution.py
@@ -148,6 +148,7 @@
     back = lax.all_to_all(back, "shard", 0, 0, tiled=True)
 
     pieces_e = gather_pieces(ge)
+    gt, _ = lax.optimization_barrier((gt, pieces_e[2]))
     pieces_t = gather_pieces(gt)
     expert_weights, expert_velocity = fused_update(
         pieces_e, expert_master, expert_moment, 1.0 / groups

time: 106 us -> 102 us (0.962)
  waiting for transfers between devices: 41.4 us -> 33.4 us
  starting transfers between devices: 33.6 us -> 36.7 us
  local copies, waits for them, and re-layouts: 17.3 us -> 18.7 us
    ppermute x2, waiting for transfers between devices: 12.6 us -> 6.33 us  [gather_pieces(): cross = lax.ppermute(x, 'rep', pairs(n, 2))]
    ppermute x4, starting transfers between devices: 5.67 us -> 7.47 us  [gather_pieces(): sib, sib_cross = lax.ppermute((x, cross), 'rep', pairs(n, 1))]
    ppermute x1, starting transfers between devices: 0.09 us -> 1.55 us  [rep_gather(): cross = lax.ppermute(x, 'rep', pairs(n, 2))]
    unnamed x27 -> x31, local copies, waits for them, and re-layouts: 3.34 us -> 4.78 us
    ppermute x2, starting transfers between devices: 1.63 us -> 0.38 us  [gather_pieces(): cross = lax.ppermute(x, 'rep', pairs(n, 2))]
    ppermute x1, waiting for transfers between devices: 1.24 us -> 0.01 us  [rep_gather(): sib = lax.ppermute(pair, 'rep', pairs(n, 1))]
    ppermute x1, starting transfers between devices: 0.75 us -> 1.92 us  [rep_gather(): sib = lax.ppermute(pair, 'rep', pairs(n, 1))]
  transfers between devices with their start and end apart: 16 -> 16, of which waited for: 9 -> 7; matrix products, arithmetic and copies ran while one was open for 7% -> 8% of each run, Pallas kernels for 9% -> 9%
where the time goes in v11:
time: 102 us
  starting transfers between devices  36.7 us (36%)
  waiting for transfers between devices  33.4 us (33%)
  local copies, waits for them, and re-layouts  18.7 us (18%)
  Pallas kernels  9.48 us (9%)
  other arithmetic  2.17 us (2%)
  between operations  1.18 us (1%)
    all_to_all x1, waiting for transfers between devices, local(): lax.all_to_all(jnp.concatenate([he, ht], 1), 'shard', 0, 0, tiled=True)  15.6 us
    all_to_all x1, starting transfers between devices, local(): lax.all_to_all(jnp.concatenate([he, ht], 1), 'shard', 0, 0, tiled=True)  12.7 us
    pallas_call x2, Pallas kernels, fused_update(): pl.pallas_call(lambda *refs: update_kernel(scale, *refs), grid_spec=pltpu...  9.48 us
    ppermute x4, starting transfers between devices, gather_pieces(): sib, sib_cross = lax.ppermute((x, cross), 'rep', pairs(n, 1))  7.47 us
    all_to_all x1, starting transfers between devices, local(): back = lax.all_to_all(back, 'shard', 0, 0, tiled=True)  6.45 us
    ppermute x2, waiting for transfers between devices, gather_pieces(): cross = lax.ppermute(x, 'rep', pairs(n, 2))  6.33 us
    ppermute x2, waiting for transfers between devices, rep_scatter(): got = lax.ppermute(pick(a, 1 - x_lo, 0), 'rep', pairs(n, 2))  5.74 us
    unnamed x31, local copies, waits for them, and re-layouts  4.78 us
  transfers between devices with their start and end apart: 16, of which 7 were waited for; matrix products, arithmetic and copies ran while one was open for 8% of the time, Pallas kernels for 9%

profile of v11, /device:TPU:1, one launch (start us, length us, event | category | flops | bytes accessed | tf_op | source)
XLA Modules:
  0.0 101.7 jit_solution(5631783613817005190)
XLA Ops:
  0.7 1.6 %reshape_reshape_squeeze.3 = f32[2,2,36864]{2,1,0:T(2,128)S(1)} reshape(f32[1,4,24,1536]{3,2,1,0:T(8,128)} %param.6) | data formatting | bytes 1179648 | tf_op jit(solution)/shard_map/reshape;reshape;squeeze | solution.py:26
  2.3 0.5 constant_dynamic-slice_fusion.12
  3.1 3.3 %collective-permute-start = (f32[2,36864]{1,0:T(2,128)S(1)}, f32[2,36864]{1,0:T(2,128)S(1)}, u32[]{:S(2)}, u32[]{:S(2)}) collective-permute-start(f32[2,36864]{1,0:T(2,128)S(1)} %bitcast.132), channel_id=1, source_target_pairs={{0,64},{64,0},{128,192},{192,128},{1,65},{65,1},{129,193},{193,129... | collective-permute-start | bytes 884744 | tf_op jit(solution)/shard_map/ppermute | solution.py:30
  6.4 0.5 reshape_squeeze.3
  7.0 0.5 reshape_reshape.2
  7.5 0.7 constant_dynamic-slice_fusion.8
  8.2 0.3 copy.76
  8.6 0.3 bitcast_add_fusion.4
  9.3 1.0 collective-permute-done.3
  10.3 0.4 bitcast_add_fusion
  10.7 0.3 constant_dynamic-slice_fusion.5
  11.0 0.5 collective-permute-start.4
  11.6 2.6 %collective-permute-done.1 = f32[36864]{0:T(1024)S(1)} collective-permute-done((f32[36864]{0:T(1024)S(1)}, f32[36864]{0:T(1024)S(1)}, u32[]{:S(2)}, u32[]{:S(2)}) %collective-permute-start.1) | collective-permute-done | bytes 147488 | tf_op jit(solution)/shard_map/ppermute | solution.py:32
  14.3 1.1 %collective-permute-start.2 = (f32[36864]{0:T(1024)S(1)}, f32[36864]{0:T(1024)S(1)}, u32[]{:S(2)}, u32[]{:S(2)}) collective-permute-start(f32[36864]{0:T(1024)S(1)} %add.70), channel_id=1, source_target_pairs={{0,1},{1,0},{2,3},{3,2},{4,5},{5,4},{6,7},{7,6},{8,9},{9,8},{10,11... | collective-permute-start | bytes 442376 | tf_op jit(solution)/shard_map/ppermute | solution.py:119
  15.4 3.1 %collective-permute-done.4 = f32[49152]{0:T(1024)S(1)} collective-permute-done((f32[49152]{0:T(1024)S(1)}, f32[49152]{0:T(1024)S(1)}, u32[]{:S(2)}, u32[]{:S(2)}) %collective-permute-start.4) | collective-permute-done | bytes 196640 | tf_op jit(solution)/shard_map/ppermute | solution.py:32
  18.5 1.1 %collective-permute-start.5 = (f32[49152]{0:T(1024)S(1)}, f32[49152]{0:T(1024)S(1)}, u32[]{:S(2)}, u32[]{:S(2)}) collective-permute-start(f32[49152]{0:T(1024)S(1)} %add.72), channel_id=1, source_target_pairs={{0,1},{1,0},{2,3},{3,2},{4,5},{5,4},{6,7},{7,6},{8,9},{9,8},{10,11... | collective-permute-start | bytes 589832 | tf_op jit(solution)/shard_map/ppermute | solution.py:119
  19.7 1.8 %collective-permute-done.2 = f32[36864]{0:T(1024)S(1)} collective-permute-done((f32[36864]{0:T(1024)S(1)}, f32[36864]{0:T(1024)S(1)}, u32[]{:S(2)}, u32[]{:S(2)}) %collective-permute-start.2) | collective-permute-done | bytes 147488 | tf_op jit(solution)/shard_map/ppermute | solution.py:119
  21.9 2.9 %collective-permute-done.5 = f32[49152]{0:T(1024)S(1)} collective-permute-done((f32[49152]{0:T(1024)S(1)}, f32[49152]{0:T(1024)S(1)}, u32[]{:S(2)}, u32[]{:S(2)}) %collective-permute-start.5) | collective-permute-done | bytes 196640 | tf_op jit(solution)/shard_map/ppermute | solution.py:119
  25.1 1.6 %copy.40 = f32[32,1,5376]{2,1,0:T(1,128)} copy(f32[32,1,5376]{2,0,1:T(8,128)S(1)} %maximum_bitcast_fusion) | data formatting | bytes 1376256 | tf_op jit(solution)/shard_map/all_to_all | solution.py:127
  26.6 12.7 %all-to-all-start = ((f32[32,1,5376]{2,1,0:T(1,128)}), f32[32,1,5376]{2,1,0:T(1,128)S(1)}, u32[]{:S(2)}, u32[]{:S(2)}) async-start(f32[32,1,5376]{2,1,0:T(1,128)} %copy.40), calls=%async_computation | async-start | bytes 1376256 | tf_op jit(solution)/shard_map/all_to_all | solution.py:127
  39.3 1.1 %constant_dynamic-slice_fusion.3 = (f32[1,96,768]{2,1,0:T(8,128)S(1)}, f32[1,96,768]{2,1,0:T(8,128)S(1)}) fusion(f32[4,96,768]{2,1,0:T(8,128)} %refs_6_.2, s32[]{:T(128)S(6)} %select_n.107, f32[4,96,768]{2,1,0:T(8,128)} %refs_5_.2), kind=kLoop, calls=%fused_computation.36 | loop fusion | bytes 1179652 | tf_op jit(solution)/shard_map/jit(dynamic_index_in_dim)/dynamic_slice | solution.py:136
  40.8 1.2 %constant_dynamic-slice_fusion.1 = (f32[128,768]{1,0:T(8,128)S(1)}, f32[128,768]{1,0:T(8,128)S(1)}) fusion(f32[512,768]{1,0:T(8,128)} %refs_6_.3, s32[]{:T(128)S(6)} %select_n.108, f32[512,768]{1,0:T(8,128)} %refs_5_.3), kind=kLoop, calls=%fused_computation.34 | loop fusion | bytes 1572868 | tf_op jit(solution)/shard_map/dynamic_slice | solution.py:143
  42.3 15.6 %all-to-all-done = f32[32,1,5376]{2,1,0:T(1,128)S(1)} async-done(((f32[32,1,5376]{2,1,0:T(1,128)}), f32[32,1,5376]{2,1,0:T(1,128)S(1)}, u32[]{:S(2)}, u32[]{:S(2)}) %all-to-all-start) | async-done | bytes 688160 | tf_op jit(solution)/shard_map/all_to_all | solution.py:127
  58.1 0.3 div.34
  58.8 0.5 broadcast.40
  59.4 0.8 reduce
  60.2 0.8 reshape.159
  61.0 6.5 %all-to-all-start.1 = ((bf16[32,2,2688]{2,1,0:T(2,128)(2,1)}), bf16[32,2,2688]{2,1,0:T(2,128)(2,1)S(1)}, u32[]{:S(2)}, u32[]{:S(2)}) async-start(bf16[32,2,2688]{2,1,0:T(2,128)(2,1)} %reshape.159), calls=%async_computation.1 | async-start | bytes 688128 | tf_op jit(solution)/shard_map/all_to_all | solution.py:148
  67.5 0.3 reshape.149.refs_1_
  67.9 2.1 %collective-permute-start.6 = (f32[32,24,96]{2,1,0:T(8,128)S(1)}, f32[32,24,96]{2,1,0:T(8,128)S(1)}, u32[]{:S(2)}, u32[]{:S(2)}) collective-permute-start(f32[32,24,96]{2,1,0:T(8,128)S(1)} %reshape.149.refs_1_), channel_id=1, source_target_pairs={{0,64},{64,0},{128,192},{192,128},{1,65},{65,1},{129,193},{193,129... | collective-permute-start | bytes 884744 | tf_op jit(solution)/shard_map/ppermute | solution.py:55
  70.1 6.3 %collective-permute-done.7.refs_3_ = f32[32,24,96]{2,1,0:T(8,128)S(1)} collective-permute-done((f32[32,24,96]{2,1,0:T(8,128)S(1)}, f32[32,24,96]{2,1,0:T(8,128)S(1)}, u32[]{:S(2)}, u32[]{:S(2)}) %collective-permute-start.7) | collective-permute-done | bytes 294944 | tf_op jit(solution)/shard_map/ppermute | solution.py:54
  76.4 0.3 collective-permute-start.12
  76.7 3.0 %collective-permute-start.8 = (f32[32,24,96]{2,1,0:T(8,128)S(1)}, f32[32,24,96]{2,1,0:T(8,128)S(1)}, u32[]{:S(2)}, u32[]{:S(2)}) collective-permute-start(f32[32,24,96]{2,1,0:T(8,128)S(1)} %collective-permute-done.7.refs_3_), channel_id=1, source_target_pairs={{0,64},{64,0},{128,192},{192,128},{1,65},{65,1},{129,193},{193,129... | collective-permute-start | bytes 884744 | tf_op jit(solution)/shard_map/ppermute | solution.py:55
  79.7 0.3 reshape.160
  80.0 0.4 constant_dynamic-slice_fusion
  80.4 1.5 %collective-permute-start.9 = (bf16[16,5376]{1,0:T(8,128)(2,1)S(1)}, bf16[16,5376]{1,0:T(8,128)(2,1)S(1)}, u32[]{:S(2)}, u32[]{:S(2)}) collective-permute-start(bf16[16,5376]{1,0:T(8,128)(2,1)S(1)} %bitcast.119), channel_id=1, source_target_pairs={{0,128},{64,192},{128,0},{192,64},{1,129},{65,193},{129,1},{193,65... | collective-permute-start | bytes 516104 | tf_op jit(solution)/shard_map/ppermute | solution.py:40
  81.9 2.0 %collective-permute-start.11 = (f32[32,24,128]{2,1,0:T(8,128)S(1)}, f32[32,24,128]{2,1,0:T(8,128)S(1)}, u32[]{:S(2)}, u32[]{:S(2)}) collective-permute-start(f32[32,24,128]{2,1,0:T(8,128)S(1)} %bitcast.112), channel_id=1, source_target_pairs={{0,64},{64,0},{128,192},{192,128},{1,65},{65,1},{129,193},{193,129... | collective-permute-start | bytes 1179656 | tf_op jit(solution)/shard_map/ppermute | solution.py:55
  84.0 0.7 copy-done.5
  84.9 4.6 %shard_map.109 = (f32[4,96,768]{2,1,0:T(8,128)}, f32[4,96,768]{2,1,0:T(8,128)}) custom-call(s32[1]{0:T(128)} %bitcast.refs_0_, f32[32,24,96]{2,1,0:T(8,128)} %copy-done.1, f32[32,24,96]{2,1,0:T(8,128)} %copy-done.5, f32[32,24,96]{2,1,0:T(8,128)} %copy-done.4, f32[32,24,96]{2,1,0:T(8,128)} %copy-done.7, f32[4,96,768]{2,1,0:T(8,128)} %refs_5_.2, ...), custom_call_target="tpu_custom_call" | custom-call | tf_op jit(solution)/shard_map/pallas_call | solution.py:87
  89.5 0.3 collective-permute-start.13
  89.8 1.9 %collective-permute-start.10 = (bf16[2,16,5376]{2,1,0:T(8,128)(2,1)S(1)}, bf16[2,16,5376]{2,1,0:T(8,128)(2,1)S(1)}, u32[]{:S(2)}, u32[]{:S(2)}) collective-permute-start(bf16[2,16,5376]{2,1,0:T(8,128)(2,1)S(1)} %maximum_select_fusion.4), channel_id=1, source_target_pairs={{0,64},{64,0},{128,192},{192,128},{1,65},{65,1},{129,193},{193,129... | collective-permute-start | bytes 1032200 | tf_op jit(solution)/shard_map/ppermute | solution.py:44
  91.9 0.7 copy-done.6
  92.6 0.8 copy-done.8
  93.4 4.9 %shard_map.110 = (f32[512,768]{1,0:T(8,128)}, f32[512,768]{1,0:T(8,128)}) custom-call(s32[1]{0:T(128)} %bitcast.refs_0_, f32[32,24,128]{2,1,0:T(8,128)} %bitcast.113, f32[32,24,128]{2,1,0:T(8,128)} %copy-done.6, f32[32,24,128]{2,1,0:T(8,128)} %copy-done.3, f32[32,24,128]{2,1,0:T(8,128)} %copy-done.8, f32[512,768]{1,0:T(8,128)} %refs_5_.3, f32[512,768]{1,0:T(8,128)} %refs_6_.3), custom_call_target="tpu_custom_call" | custom-call | tf_op jit(solution)/shard_map/pallas_call | solution.py:87
  98.5 0.3 copy.48
  98.8 1.0 %reshape.158 = bf16[24,8192]{1,0:T(8,128)(2,1)} reshape(bf16[24,16,4,128]{3,2,1,0:T(4,128)(2,1)S(1)} %copy.48) | data formatting | bytes 786432 | tf_op jit(solution)/shard_map/reshape | solution.py:165
  99.8 0.6 reshape.154
  100.5 1.1 %reshape.155 = bf16[4,24,1536]{2,1,0:T(8,128)(2,1)} reshape(bf16[4,24,16,96]{3,2,1,0:T(8,128)(2,1)S(1)} %copy.47) | data formatting | bytes 589824 | tf_op jit(solution)/shard_map/reshape | solution.py:163
  (64 shorter events, 3.6 us)
Async XLA Ops:
  0.6 5.8 %copy-start.2 = (f32[1,24,8192]{2,1,0:T(8,128)S(1)}, f32[1,24,8192]{2,1,0:T(8,128)}, u32[]{:S(2)}) copy-start(f32[1,24,8192]{2,1,0:T(8,128)} %param.7) | copy-start | bytes 2359300
  3.1 5.5 %collective-permute-start = (f32[2,36864]{1,0:T(2,128)S(1)}, f32[2,36864]{1,0:T(2,128)S(1)}, u32[]{:S(2)}, u32[]{:S(2)}) collective-permute-start(f32[2,36864]{1,0:T(2,128)S(1)} %bitcast.132), channel_id=1, source_target_pairs={{0,64},{64,0},{128,192},{192,128},{1,65},{65,1},{129,193},{193,129... | collective-permute-start | bytes 884744 | tf_op jit(solution)/shard_map/ppermute | solution.py:30
  8.5 1.8 %collective-permute-start.3 = (f32[2,49152]{1,0:T(2,128)S(1)}, f32[2,49152]{1,0:T(2,128)S(1)}, u32[]{:S(2)}, u32[]{:S(2)}) collective-permute-start(f32[2,49152]{1,0:T(2,128)S(1)} %bitcast.130), channel_id=1, source_target_pairs={{0,64},{64,0},{128,192},{192,128},{1,65},{65,1},{129,193},{193,129... | collective-permute-start | bytes 1179656 | tf_op jit(solution)/shard_map/ppermute | solution.py:30
  9.2 5.0 %collective-permute-start.1 = (f32[36864]{0:T(1024)S(1)}, f32[36864]{0:T(1024)S(1)}, u32[]{:S(2)}, u32[]{:S(2)}) collective-permute-start(f32[36864]{0:T(1024)S(1)} %bitcast.135), channel_id=1, source_target_pairs={{0,128},{64,192},{128,0},{192,64},{1,129},{65,193},{129,1},{193,65... | collective-permute-start | bytes 442376 | tf_op jit(solution)/shard_map/ppermute | solution.py:32
  11.0 7.4 %collective-permute-start.4 = (f32[49152]{0:T(1024)S(1)}, f32[49152]{0:T(1024)S(1)}, u32[]{:S(2)}, u32[]{:S(2)}) collective-permute-start(f32[49152]{0:T(1024)S(1)} %bitcast.134), channel_id=1, source_target_pairs={{0,128},{64,192},{128,0},{192,64},{1,129},{65,193},{129,1},{193,65... | collective-permute-start | bytes 589832 | tf_op jit(solution)/shard_map/ppermute | solution.py:32
  14.3 7.2 %collective-permute-start.2 = (f32[36864]{0:T(1024)S(1)}, f32[36864]{0:T(1024)S(1)}, u32[]{:S(2)}, u32[]{:S(2)}) collective-permute-start(f32[36864]{0:T(1024)S(1)} %add.70), channel_id=1, source_target_pairs={{0,1},{1,0},{2,3},{3,2},{4,5},{5,4},{6,7},{7,6},{8,9},{9,8},{10,11... | collective-permute-start | bytes 442376 | tf_op jit(solution)/shard_map/ppermute | solution.py:119
  18.5 6.3 %collective-permute-start.5 = (f32[49152]{0:T(1024)S(1)}, f32[49152]{0:T(1024)S(1)}, u32[]{:S(2)}, u32[]{:S(2)}) collective-permute-start(f32[49152]{0:T(1024)S(1)} %add.72), channel_id=1, source_target_pairs={{0,1},{1,0},{2,3},{3,2},{4,5},{5,4},{6,7},{7,6},{8,9},{9,8},{10,11... | collective-permute-start | bytes 589832 | tf_op jit(solution)/shard_map/ppermute | solution.py:119
  26.6 31.3 %all-to-all-start = ((f32[32,1,5376]{2,1,0:T(1,128)}), f32[32,1,5376]{2,1,0:T(1,128)S(1)}, u32[]{:S(2)}, u32[]{:S(2)}) async-start(f32[32,1,5376]{2,1,0:T(1,128)} %copy.40), calls=%async_computation | async-start | bytes 1376256 | tf_op jit(solution)/shard_map/all_to_all | solution.py:127
  61.0 18.7 %all-to-all-start.1 = ((bf16[32,2,2688]{2,1,0:T(2,128)(2,1)}), bf16[32,2,2688]{2,1,0:T(2,128)(2,1)S(1)}, u32[]{:S(2)}, u32[]{:S(2)}) async-start(bf16[32,2,2688]{2,1,0:T(2,128)(2,1)} %reshape.159), calls=%async_computation.1 | async-start | bytes 688128 | tf_op jit(solution)/shard_map/all_to_all | solution.py:148
  67.8 16.2 %copy-start.1 = (f32[32,24,96]{2,1,0:T(8,128)}, f32[32,24,96]{2,1,0:T(8,128)S(1)}, u32[]{:S(2)}) copy-start(f32[32,24,96]{2,1,0:T(8,128)S(1)} %reshape.149.refs_1_) | copy-start | bytes 884740
  67.8 8.6 %collective-permute-start.7 = (f32[32,24,96]{2,1,0:T(8,128)S(1)}, f32[32,24,96]{2,1,0:T(8,128)S(1)}, u32[]{:S(2)}, u32[]{:S(2)}) collective-permute-start(f32[32,24,96]{2,1,0:T(8,128)S(1)} %reshape.149.refs_1_), channel_id=1, source_target_pairs={{0,128},{64,192},{128,0},{192,64},{1,129},{65,193},{129,1},{193,65... | collective-permute-start | bytes 884744 | tf_op jit(solution)/shard_map/ppermute | solution.py:54
  67.9 16.1 %collective-permute-start.6 = (f32[32,24,96]{2,1,0:T(8,128)S(1)}, f32[32,24,96]{2,1,0:T(8,128)S(1)}, u32[]{:S(2)}, u32[]{:S(2)}) collective-permute-start(f32[32,24,96]{2,1,0:T(8,128)S(1)} %reshape.149.refs_1_), channel_id=1, source_target_pairs={{0,64},{64,0},{128,192},{192,128},{1,65},{65,1},{129,193},{193,129... | collective-permute-start | bytes 884744 | tf_op jit(solution)/shard_map/ppermute | solution.py:55
  70.1 19.4 %copy-start = (f32[4,8,24,128]{3,2,1,0:T(8,128)}, f32[4,8,24,128]{3,2,1,0:T(8,128)S(1)}, u32[]{:S(2)}) copy-start(f32[4,8,24,128]{3,2,1,0:T(8,128)S(1)} %copy.60) | copy-start | bytes 1179652
  76.4 7.6 %copy-start.4 = (f32[32,24,96]{2,1,0:T(8,128)}, f32[32,24,96]{2,1,0:T(8,128)S(1)}, u32[]{:S(2)}) copy-start(f32[32,24,96]{2,1,0:T(8,128)S(1)} %collective-permute-done.7.refs_3_) | copy-start | bytes 884740
  76.4 13.0 %collective-permute-start.12 = (f32[32,24,128]{2,1,0:T(8,128)S(1)}, f32[32,24,128]{2,1,0:T(8,128)S(1)}, u32[]{:S(2)}, u32[]{:S(2)}) collective-permute-start(f32[32,24,128]{2,1,0:T(8,128)S(1)} %bitcast.111), channel_id=1, source_target_pairs={{0,128},{64,192},{128,0},{192,64},{1,129},{65,193},{129,1},{193,65... | collective-permute-start | bytes 1179656 | tf_op jit(solution)/shard_map/ppermute | solution.py:54
  76.7 7.3 %collective-permute-start.8 = (f32[32,24,96]{2,1,0:T(8,128)S(1)}, f32[32,24,96]{2,1,0:T(8,128)S(1)}, u32[]{:S(2)}, u32[]{:S(2)}) collective-permute-start(f32[32,24,96]{2,1,0:T(8,128)S(1)} %collective-permute-done.7.refs_3_), channel_id=1, source_target_pairs={{0,64},{64,0},{128,192},{192,128},{1,65},{65,1},{129,193},{193,129... | collective-permute-start | bytes 884744 | tf_op jit(solution)/shard_map/ppermute | solution.py:55
  80.4 9.4 %collective-permute-start.9 = (bf16[16,5376]{1,0:T(8,128)(2,1)S(1)}, bf16[16,5376]{1,0:T(8,128)(2,1)S(1)}, u32[]{:S(2)}, u32[]{:S(2)}) collective-permute-start(bf16[16,5376]{1,0:T(8,128)(2,1)S(1)} %bitcast.119), channel_id=1, source_target_pairs={{0,128},{64,192},{128,0},{192,64},{1,129},{65,193},{129,1},{193,65... | collective-permute-start | bytes 516104 | tf_op jit(solution)/shard_map/ppermute | solution.py:40
  81.9 9.9 %collective-permute-start.11 = (f32[32,24,128]{2,1,0:T(8,128)S(1)}, f32[32,24,128]{2,1,0:T(8,128)S(1)}, u32[]{:S(2)}, u32[]{:S(2)}) collective-permute-start(f32[32,24,128]{2,1,0:T(8,128)S(1)} %bitcast.112), channel_id=1, source_target_pairs={{0,64},{64,0},{128,192},{192,128},{1,65},{65,1},{129,193},{193,129... | collective-permute-start | bytes 1179656 | tf_op jit(solution)/shard_map/ppermute | solution.py:55
  84.0 0.7 copy-start.5
  84.0 0.9 copy-start.7
  89.5 2.4 %copy-start.3 = (f32[32,24,128]{2,1,0:T(8,128)}, f32[32,24,128]{2,1,0:T(8,128)S(1)}, u32[]{:S(2)}) copy-start(f32[32,24,128]{2,1,0:T(8,128)S(1)} %collective-permute-done.12.refs_3_) | copy-start | bytes 1179652
  89.5 2.4 %collective-permute-start.13 = (f32[32,24,128]{2,1,0:T(8,128)S(1)}, f32[32,24,128]{2,1,0:T(8,128)S(1)}, u32[]{:S(2)}, u32[]{:S(2)}) collective-permute-start(f32[32,24,128]{2,1,0:T(8,128)S(1)} %collective-permute-done.12.refs_3_), channel_id=1, source_target_pairs={{0,64},{64,0},{128,192},{192,128},{1,65},{65,1},{129,193},{193,129... | collective-permute-start | bytes 1179656 | tf_op jit(solution)/shard_map/ppermute | solution.py:55
  89.8 8.4 %collective-permute-start.10 = (bf16[2,16,5376]{2,1,0:T(8,128)(2,1)S(1)}, bf16[2,16,5376]{2,1,0:T(8,128)(2,1)S(1)}, u32[]{:S(2)}, u32[]{:S(2)}) collective-permute-start(bf16[2,16,5376]{2,1,0:T(8,128)(2,1)S(1)} %maximum_select_fusion.4), channel_id=1, source_target_pairs={{0,64},{64,0},{128,192},{192,128},{1,65},{65,1},{129,193},{193,129... | collective-permute-start | bytes 1032200 | tf_op jit(solution)/shard_map/ppermute | solution.py:44
  91.8 0.7 copy-start.6
  92.6 0.8 copy-start.8

commit v12 on v11

--- a/solution.py
+++ b/solution.py
@@ -153,9 +153,6 @@
     expert_weights, expert_velocity = fused_update(
         pieces_e, expert_master, expert_moment, 1.0 / groups
     )
-    table_weights, table_velocity = fused_update(
-        pieces_t, table_master, table_moment, 1.0 / groups
-    )
 
     back = lax.dynamic_slice_in_dim(back, t * per_half, per_half, 0)
     allq = rep_gather(back)
@@ -163,6 +160,12 @@
     expert_copies = jnp.transpose(ce, (0, 2, 1, 3)).reshape(mats, width, per_half * rows)
     ct = allq[:, :, width * rows :].reshape(groups, per_half, width, sub)
     table_copies = jnp.transpose(ct, (2, 1, 0, 3)).reshape(width, per_half * vrows)
+    pieces_t, expert_copies, table_copies = lax.optimization_barrier(
+        (pieces_t, expert_copies, table_copies)
+    )
+    table_weights, table_velocity = fused_update(
+        pieces_t, table_master, table_moment, 1.0 / groups
+    )
     return (
         expert_weights,
         expert_velocity,

time: 102 us -> 103 us (level)
  waiting for transfers between devices: 33.4 us -> 34.6 us
    ppermute x1, waiting for transfers between devices: 0.01 us -> 1.24 us  [rep_gather(): sib = lax.ppermute(pair, 'rep', pairs(n, 1))]
  transfers between devices with their start and end apart: 16 -> 16, of which waited for: 7 -> 8; matrix products, arithmetic and copies ran while one was open for 8% -> 11% of each run, Pallas kernels for 9% -> 4%
where the time goes in v12:
time: 103 us
  starting transfers between devices  36.7 us (36%)
  waiting for transfers between devices  34.6 us (34%)
  local copies, waits for them, and re-layouts  18.7 us (18%)
  Pallas kernels  9.48 us (9%)
  other arithmetic  2.17 us (2%)
  between operations  1.15 us (1%)
    all_to_all x1, waiting for transfers between devices, local(): lax.all_to_all(jnp.concatenate([he, ht], 1), 'shard', 0, 0, tiled=True)  15.6 us
    all_to_all x1, starting transfers between devices, local(): lax.all_to_all(jnp.concatenate([he, ht], 1), 'shard', 0, 0, tiled=True)  12.7 us
    pallas_call x2, Pallas kernels, fused_update(): pl.pallas_call(lambda *refs: update_kernel(scale, *refs), grid_spec=pltpu...  9.48 us
    ppermute x4, starting transfers between devices, gather_pieces(): sib, sib_cross = lax.ppermute((x, cross), 'rep', pairs(n, 1))  7.47 us
    all_to_all x1, starting transfers between devices, local(): back = lax.all_to_all(back, 'shard', 0, 0, tiled=True)  6.45 us
    ppermute x2, waiting for transfers between devices, gather_pieces(): cross = lax.ppermute(x, 'rep', pairs(n, 2))  6.33 us
    ppermute x2, waiting for transfers between devices, rep_scatter(): got = lax.ppermute(pick(a, 1 - x_lo, 0), 'rep', pairs(n, 2))  5.74 us
    unnamed x31, local copies, waits for them, and re-layouts  4.78 us
  transfers between devices with their start and end apart: 16, of which 8 were waited for; matrix products, arithmetic and copies ran while one was open for 11% of the time, Pallas kernels for 4%

profile of v12, /device:TPU:1, one launch (start us, length us, event | category | flops | bytes accessed | tf_op | source)
XLA Modules:
  0.0 102.9 jit_solution(12250251755667377451)
XLA Ops:
  0.7 1.6 %reshape_reshape_squeeze.3 = f32[2,2,36864]{2,1,0:T(2,128)S(1)} reshape(f32[1,4,24,1536]{3,2,1,0:T(8,128)} %param.6) | data formatting | bytes 1179648 | tf_op jit(solution)/shard_map/reshape;reshape;squeeze | solution.py:26
  2.3 0.5 constant_dynamic-slice_fusion.12
  3.1 3.3 %collective-permute-start = (f32[2,36864]{1,0:T(2,128)S(1)}, f32[2,36864]{1,0:T(2,128)S(1)}, u32[]{:S(2)}, u32[]{:S(2)}) collective-permute-start(f32[2,36864]{1,0:T(2,128)S(1)} %bitcast.132), channel_id=1, source_target_pairs={{0,64},{64,0},{128,192},{192,128},{1,65},{65,1},{129,193},{193,129... | collective-permute-start | bytes 884744 | tf_op jit(solution)/shard_map/ppermute | solution.py:30
  6.4 0.5 reshape_squeeze.3
  7.0 0.5 reshape_reshape.2
  7.5 0.7 constant_dynamic-slice_fusion.8
  8.2 0.3 copy.76
  8.6 0.3 bitcast_add_fusion.4
  9.3 1.0 collective-permute-done.3
  10.3 0.4 bitcast_add_fusion
  10.7 0.3 constant_dynamic-slice_fusion.5
  11.0 0.5 collective-permute-start.4
  11.6 2.6 %collective-permute-done.1 = f32[36864]{0:T(1024)S(1)} collective-permute-done((f32[36864]{0:T(1024)S(1)}, f32[36864]{0:T(1024)S(1)}, u32[]{:S(2)}, u32[]{:S(2)}) %collective-permute-start.1) | collective-permute-done | bytes 147488 | tf_op jit(solution)/shard_map/ppermute | solution.py:32
  14.3 1.1 %collective-permute-start.2 = (f32[36864]{0:T(1024)S(1)}, f32[36864]{0:T(1024)S(1)}, u32[]{:S(2)}, u32[]{:S(2)}) collective-permute-start(f32[36864]{0:T(1024)S(1)} %add.70), channel_id=1, source_target_pairs={{0,1},{1,0},{2,3},{3,2},{4,5},{5,4},{6,7},{7,6},{8,9},{9,8},{10,11... | collective-permute-start | bytes 442376 | tf_op jit(solution)/shard_map/ppermute | solution.py:119
  15.4 3.1 %collective-permute-done.4 = f32[49152]{0:T(1024)S(1)} collective-permute-done((f32[49152]{0:T(1024)S(1)}, f32[49152]{0:T(1024)S(1)}, u32[]{:S(2)}, u32[]{:S(2)}) %collective-permute-start.4) | collective-permute-done | bytes 196640 | tf_op jit(solution)/shard_map/ppermute | solution.py:32
  18.5 1.1 %collective-permute-start.5 = (f32[49152]{0:T(1024)S(1)}, f32[49152]{0:T(1024)S(1)}, u32[]{:S(2)}, u32[]{:S(2)}) collective-permute-start(f32[49152]{0:T(1024)S(1)} %add.72), channel_id=1, source_target_pairs={{0,1},{1,0},{2,3},{3,2},{4,5},{5,4},{6,7},{7,6},{8,9},{9,8},{10,11... | collective-permute-start | bytes 589832 | tf_op jit(solution)/shard_map/ppermute | solution.py:119
  19.7 1.8 %collective-permute-done.2 = f32[36864]{0:T(1024)S(1)} collective-permute-done((f32[36864]{0:T(1024)S(1)}, f32[36864]{0:T(1024)S(1)}, u32[]{:S(2)}, u32[]{:S(2)}) %collective-permute-start.2) | collective-permute-done | bytes 147488 | tf_op jit(solution)/shard_map/ppermute | solution.py:119
  21.9 2.9 %collective-permute-done.5 = f32[49152]{0:T(1024)S(1)} collective-permute-done((f32[49152]{0:T(1024)S(1)}, f32[49152]{0:T(1024)S(1)}, u32[]{:S(2)}, u32[]{:S(2)}) %collective-permute-start.5) | collective-permute-done | bytes 196640 | tf_op jit(solution)/shard_map/ppermute | solution.py:119
  25.1 1.6 %copy.40 = f32[32,1,5376]{2,1,0:T(1,128)} copy(f32[32,1,5376]{2,0,1:T(8,128)S(1)} %maximum_bitcast_fusion) | data formatting | bytes 1376256 | tf_op jit(solution)/shard_map/all_to_all | solution.py:127
  26.6 12.7 %all-to-all-start = ((f32[32,1,5376]{2,1,0:T(1,128)}), f32[32,1,5376]{2,1,0:T(1,128)S(1)}, u32[]{:S(2)}, u32[]{:S(2)}) async-start(f32[32,1,5376]{2,1,0:T(1,128)} %copy.40), calls=%async_computation | async-start | bytes 1376256 | tf_op jit(solution)/shard_map/all_to_all | solution.py:127
  39.3 1.1 %constant_dynamic-slice_fusion.3 = (f32[1,96,768]{2,1,0:T(8,128)S(1)}, f32[1,96,768]{2,1,0:T(8,128)S(1)}) fusion(f32[4,96,768]{2,1,0:T(8,128)} %refs_6_.2, s32[]{:T(128)S(6)} %select_n.107, f32[4,96,768]{2,1,0:T(8,128)} %refs_5_.2), kind=kLoop, calls=%fused_computation.36 | loop fusion | bytes 1179652 | tf_op jit(solution)/shard_map/jit(dynamic_index_in_dim)/dynamic_slice | solution.py:136
  40.8 1.2 %constant_dynamic-slice_fusion.1 = (f32[128,768]{1,0:T(8,128)S(1)}, f32[128,768]{1,0:T(8,128)S(1)}) fusion(f32[512,768]{1,0:T(8,128)} %refs_6_.3, s32[]{:T(128)S(6)} %select_n.108, f32[512,768]{1,0:T(8,128)} %refs_5_.3), kind=kLoop, calls=%fused_computation.34 | loop fusion | bytes 1572868 | tf_op jit(solution)/shard_map/dynamic_slice | solution.py:143
  42.3 15.6 %all-to-all-done = f32[32,1,5376]{2,1,0:T(1,128)S(1)} async-done(((f32[32,1,5376]{2,1,0:T(1,128)}), f32[32,1,5376]{2,1,0:T(1,128)S(1)}, u32[]{:S(2)}, u32[]{:S(2)}) %all-to-all-start) | async-done | bytes 688160 | tf_op jit(solution)/shard_map/all_to_all | solution.py:127
  58.8 0.5 broadcast.40
  59.4 0.8 reduce
  60.2 0.8 reshape.159
  61.0 6.5 %all-to-all-start.1 = ((bf16[32,2,2688]{2,1,0:T(2,128)(2,1)}), bf16[32,2,2688]{2,1,0:T(2,128)(2,1)S(1)}, u32[]{:S(2)}, u32[]{:S(2)}) async-start(bf16[32,2,2688]{2,1,0:T(2,128)(2,1)} %reshape.159), calls=%async_computation.1 | async-start | bytes 688128 | tf_op jit(solution)/shard_map/all_to_all | solution.py:148
  67.5 0.3 reshape.149.refs_1_
  67.9 2.1 %collective-permute-start.6 = (f32[32,24,96]{2,1,0:T(8,128)S(1)}, f32[32,24,96]{2,1,0:T(8,128)S(1)}, u32[]{:S(2)}, u32[]{:S(2)}) collective-permute-start(f32[32,24,96]{2,1,0:T(8,128)S(1)} %reshape.149.refs_1_), channel_id=1, source_target_pairs={{0,64},{64,0},{128,192},{192,128},{1,65},{65,1},{129,193},{193,129... | collective-permute-start | bytes 884744 | tf_op jit(solution)/shard_map/ppermute | solution.py:55
  70.1 6.3 %collective-permute-done.7.refs_3_ = f32[32,24,96]{2,1,0:T(8,128)S(1)} collective-permute-done((f32[32,24,96]{2,1,0:T(8,128)S(1)}, f32[32,24,96]{2,1,0:T(8,128)S(1)}, u32[]{:S(2)}, u32[]{:S(2)}) %collective-permute-start.7) | collective-permute-done | bytes 294944 | tf_op jit(solution)/shard_map/ppermute | solution.py:54
  76.4 0.3 collective-permute-start.10
  76.7 3.0 %collective-permute-start.8 = (f32[32,24,96]{2,1,0:T(8,128)S(1)}, f32[32,24,96]{2,1,0:T(8,128)S(1)}, u32[]{:S(2)}, u32[]{:S(2)}) collective-permute-start(f32[32,24,96]{2,1,0:T(8,128)S(1)} %collective-permute-done.7.refs_3_), channel_id=1, source_target_pairs={{0,64},{64,0},{128,192},{192,128},{1,65},{65,1},{129,193},{193,129... | collective-permute-start | bytes 884744 | tf_op jit(solution)/shard_map/ppermute | solution.py:55
  79.7 0.3 reshape.160
  80.0 0.4 constant_dynamic-slice_fusion
  80.4 1.5 %collective-permute-start.12 = (bf16[16,5376]{1,0:T(8,128)(2,1)S(1)}, bf16[16,5376]{1,0:T(8,128)(2,1)S(1)}, u32[]{:S(2)}, u32[]{:S(2)}) collective-permute-start(bf16[16,5376]{1,0:T(8,128)(2,1)S(1)} %bitcast.119), channel_id=1, source_target_pairs={{0,128},{64,192},{128,0},{192,64},{1,129},{65,193},{129,1},{193,65... | collective-permute-start | bytes 516104 | tf_op jit(solution)/shard_map/ppermute | solution.py:40
  81.9 2.0 %collective-permute-start.9 = (f32[32,24,128]{2,1,0:T(8,128)S(1)}, f32[32,24,128]{2,1,0:T(8,128)S(1)}, u32[]{:S(2)}, u32[]{:S(2)}) collective-permute-start(f32[32,24,128]{2,1,0:T(8,128)S(1)} %bitcast.112), channel_id=1, source_target_pairs={{0,64},{64,0},{128,192},{192,128},{1,65},{65,1},{129,193},{193,129... | collective-permute-start | bytes 1179656 | tf_op jit(solution)/shard_map/ppermute | solution.py:55
  84.0 0.7 copy-done.6
  84.9 4.6 %shard_map.109 = (f32[4,96,768]{2,1,0:T(8,128)}, f32[4,96,768]{2,1,0:T(8,128)}) custom-call(s32[1]{0:T(128)} %bitcast.refs_0_, f32[32,24,96]{2,1,0:T(8,128)} %copy-done.1, f32[32,24,96]{2,1,0:T(8,128)} %copy-done.6, f32[32,24,96]{2,1,0:T(8,128)} %copy-done.5, f32[32,24,96]{2,1,0:T(8,128)} %copy-done.8, f32[4,96,768]{2,1,0:T(8,128)} %refs_5_.2, ...), custom_call_target="tpu_custom_call" | custom-call | tf_op jit(solution)/shard_map/pallas_call | solution.py:87
  89.5 0.3 collective-permute-start.11
  89.8 1.9 %collective-permute-start.13 = (bf16[2,16,5376]{2,1,0:T(8,128)(2,1)S(1)}, bf16[2,16,5376]{2,1,0:T(8,128)(2,1)S(1)}, u32[]{:S(2)}, u32[]{:S(2)}) collective-permute-start(bf16[2,16,5376]{2,1,0:T(8,128)(2,1)S(1)} %maximum_select_fusion.4), channel_id=1, source_target_pairs={{0,64},{64,0},{128,192},{192,128},{1,65},{65,1},{129,193},{193,129... | collective-permute-start | bytes 1032200 | tf_op jit(solution)/shard_map/ppermute | solution.py:44
  91.8 1.2 %collective-permute-done.13 = bf16[2,16,5376]{2,1,0:T(8,128)(2,1)S(1)} collective-permute-done((bf16[2,16,5376]{2,1,0:T(8,128)(2,1)S(1)}, bf16[2,16,5376]{2,1,0:T(8,128)(2,1)S(1)}, u32[]{:S(2)}, u32[]{:S(2)}) %collective-permute-start.13) | collective-permute-done | bytes 344096 | tf_op jit(solution)/shard_map/ppermute | solution.py:44
  93.3 0.3 copy.48
  93.6 1.0 %reshape.158 = bf16[24,8192]{1,0:T(8,128)(2,1)} reshape(bf16[24,16,4,128]{3,2,1,0:T(4,128)(2,1)S(1)} %copy.48) | data formatting | bytes 786432 | tf_op jit(solution)/shard_map/reshape | solution.py:162
  94.7 0.6 reshape.155
  95.3 1.1 %reshape.156 = bf16[4,24,1536]{2,1,0:T(8,128)(2,1)} reshape(bf16[4,24,16,96]{3,2,1,0:T(8,128)(2,1)S(1)} %copy.47) | data formatting | bytes 589824 | tf_op jit(solution)/shard_map/reshape | solution.py:160
  96.5 0.8 copy-done.4
  97.2 0.7 copy-done.7
  98.0 4.9 %shard_map.110 = (f32[512,768]{1,0:T(8,128)}, f32[512,768]{1,0:T(8,128)}) custom-call(s32[1]{0:T(128)} %bitcast.refs_0_, f32[32,24,128]{2,1,0:T(8,128)} %bitcast.113, f32[32,24,128]{2,1,0:T(8,128)} %copy-done.4, f32[32,24,128]{2,1,0:T(8,128)} %copy-done.3, f32[32,24,128]{2,1,0:T(8,128)} %copy-done.7, f32[512,768]{1,0:T(8,128)} %refs_5_.3, f32[512,768]{1,0:T(8,128)} %refs_6_.3), custom_call_target="tpu_custom_call" | custom-call | tf_op jit(solution)/shard_map/pallas_call | solution.py:87
  (64 shorter events, 3.8 us)
Async XLA Ops:
  0.6 5.8 %copy-start.2 = (f32[1,24,8192]{2,1,0:T(8,128)S(1)}, f32[1,24,8192]{2,1,0:T(8,128)}, u32[]{:S(2)}) copy-start(f32[1,24,8192]{2,1,0:T(8,128)} %param.7) | copy-start | bytes 2359300
  3.1 5.5 %collective-permute-start = (f32[2,36864]{1,0:T(2,128)S(1)}, f32[2,36864]{1,0:T(2,128)S(1)}, u32[]{:S(2)}, u32[]{:S(2)}) collective-permute-start(f32[2,36864]{1,0:T(2,128)S(1)} %bitcast.132), channel_id=1, source_target_pairs={{0,64},{64,0},{128,192},{192,128},{1,65},{65,1},{129,193},{193,129... | collective-permute-start | bytes 884744 | tf_op jit(solution)/shard_map/ppermute | solution.py:30
  8.5 1.8 %collective-permute-start.3 = (f32[2,49152]{1,0:T(2,128)S(1)}, f32[2,49152]{1,0:T(2,128)S(1)}, u32[]{:S(2)}, u32[]{:S(2)}) collective-permute-start(f32[2,49152]{1,0:T(2,128)S(1)} %bitcast.130), channel_id=1, source_target_pairs={{0,64},{64,0},{128,192},{192,128},{1,65},{65,1},{129,193},{193,129... | collective-permute-start | bytes 1179656 | tf_op jit(solution)/shard_map/ppermute | solution.py:30
  9.2 5.0 %collective-permute-start.1 = (f32[36864]{0:T(1024)S(1)}, f32[36864]{0:T(1024)S(1)}, u32[]{:S(2)}, u32[]{:S(2)}) collective-permute-start(f32[36864]{0:T(1024)S(1)} %bitcast.135), channel_id=1, source_target_pairs={{0,128},{64,192},{128,0},{192,64},{1,129},{65,193},{129,1},{193,65... | collective-permute-start | bytes 442376 | tf_op jit(solution)/shard_map/ppermute | solution.py:32
  11.0 7.4 %collective-permute-start.4 = (f32[49152]{0:T(1024)S(1)}, f32[49152]{0:T(1024)S(1)}, u32[]{:S(2)}, u32[]{:S(2)}) collective-permute-start(f32[49152]{0:T(1024)S(1)} %bitcast.134), channel_id=1, source_target_pairs={{0,128},{64,192},{128,0},{192,64},{1,129},{65,193},{129,1},{193,65... | collective-permute-start | bytes 589832 | tf_op jit(solution)/shard_map/ppermute | solution.py:32
  14.3 7.2 %collective-permute-start.2 = (f32[36864]{0:T(1024)S(1)}, f32[36864]{0:T(1024)S(1)}, u32[]{:S(2)}, u32[]{:S(2)}) collective-permute-start(f32[36864]{0:T(1024)S(1)} %add.70), channel_id=1, source_target_pairs={{0,1},{1,0},{2,3},{3,2},{4,5},{5,4},{6,7},{7,6},{8,9},{9,8},{10,11... | collective-permute-start | bytes 442376 | tf_op jit(solution)/shard_map/ppermute | solution.py:119
  18.5 6.3 %collective-permute-start.5 = (f32[49152]{0:T(1024)S(1)}, f32[49152]{0:T(1024)S(1)}, u32[]{:S(2)}, u32[]{:S(2)}) collective-permute-start(f32[49152]{0:T(1024)S(1)} %add.72), channel_id=1, source_target_pairs={{0,1},{1,0},{2,3},{3,2},{4,5},{5,4},{6,7},{7,6},{8,9},{9,8},{10,11... | collective-permute-start | bytes 589832 | tf_op jit(solution)/shard_map/ppermute | solution.py:119
  26.6 31.3 %all-to-all-start = ((f32[32,1,5376]{2,1,0:T(1,128)}), f32[32,1,5376]{2,1,0:T(1,128)S(1)}, u32[]{:S(2)}, u32[]{:S(2)}) async-start(f32[32,1,5376]{2,1,0:T(1,128)} %copy.40), calls=%async_computation | async-start | bytes 1376256 | tf_op jit(solution)/shard_map/all_to_all | solution.py:127
  61.0 18.6 %all-to-all-start.1 = ((bf16[32,2,2688]{2,1,0:T(2,128)(2,1)}), bf16[32,2,2688]{2,1,0:T(2,128)(2,1)S(1)}, u32[]{:S(2)}, u32[]{:S(2)}) async-start(bf16[32,2,2688]{2,1,0:T(2,128)(2,1)} %reshape.159), calls=%async_computation.1 | async-start | bytes 688128 | tf_op jit(solution)/shard_map/all_to_all | solution.py:148
  67.8 16.2 %copy-start.1 = (f32[32,24,96]{2,1,0:T(8,128)}, f32[32,24,96]{2,1,0:T(8,128)S(1)}, u32[]{:S(2)}) copy-start(f32[32,24,96]{2,1,0:T(8,128)S(1)} %reshape.149.refs_1_) | copy-start | bytes 884740
  67.8 8.6 %collective-permute-start.7 = (f32[32,24,96]{2,1,0:T(8,128)S(1)}, f32[32,24,96]{2,1,0:T(8,128)S(1)}, u32[]{:S(2)}, u32[]{:S(2)}) collective-permute-start(f32[32,24,96]{2,1,0:T(8,128)S(1)} %reshape.149.refs_1_), channel_id=1, source_target_pairs={{0,128},{64,192},{128,0},{192,64},{1,129},{65,193},{129,1},{193,65... | collective-permute-start | bytes 884744 | tf_op jit(solution)/shard_map/ppermute | solution.py:54
  67.9 16.1 %collective-permute-start.6 = (f32[32,24,96]{2,1,0:T(8,128)S(1)}, f32[32,24,96]{2,1,0:T(8,128)S(1)}, u32[]{:S(2)}, u32[]{:S(2)}) collective-permute-start(f32[32,24,96]{2,1,0:T(8,128)S(1)} %reshape.149.refs_1_), channel_id=1, source_target_pairs={{0,64},{64,0},{128,192},{192,128},{1,65},{65,1},{129,193},{193,129... | collective-permute-start | bytes 884744 | tf_op jit(solution)/shard_map/ppermute | solution.py:55
  70.1 19.4 %copy-start = (f32[4,8,24,128]{3,2,1,0:T(8,128)}, f32[4,8,24,128]{3,2,1,0:T(8,128)S(1)}, u32[]{:S(2)}) copy-start(f32[4,8,24,128]{3,2,1,0:T(8,128)S(1)} %copy.59) | copy-start | bytes 1179652
  76.4 7.6 %copy-start.5 = (f32[32,24,96]{2,1,0:T(8,128)}, f32[32,24,96]{2,1,0:T(8,128)S(1)}, u32[]{:S(2)}) copy-start(f32[32,24,96]{2,1,0:T(8,128)S(1)} %collective-permute-done.7.refs_3_) | copy-start | bytes 884740
  76.4 13.0 %collective-permute-start.10 = (f32[32,24,128]{2,1,0:T(8,128)S(1)}, f32[32,24,128]{2,1,0:T(8,128)S(1)}, u32[]{:S(2)}, u32[]{:S(2)}) collective-permute-start(f32[32,24,128]{2,1,0:T(8,128)S(1)} %bitcast.111), channel_id=1, source_target_pairs={{0,128},{64,192},{128,0},{192,64},{1,129},{65,193},{129,1},{193,65... | collective-permute-start | bytes 1179656 | tf_op jit(solution)/shard_map/ppermute | solution.py:54
  76.7 7.3 %collective-permute-start.8 = (f32[32,24,96]{2,1,0:T(8,128)S(1)}, f32[32,24,96]{2,1,0:T(8,128)S(1)}, u32[]{:S(2)}, u32[]{:S(2)}) collective-permute-start(f32[32,24,96]{2,1,0:T(8,128)S(1)} %collective-permute-done.7.refs_3_), channel_id=1, source_target_pairs={{0,64},{64,0},{128,192},{192,128},{1,65},{65,1},{129,193},{193,129... | collective-permute-start | bytes 884744 | tf_op jit(solution)/shard_map/ppermute | solution.py:55
  80.4 9.4 %collective-permute-start.12 = (bf16[16,5376]{1,0:T(8,128)(2,1)S(1)}, bf16[16,5376]{1,0:T(8,128)(2,1)S(1)}, u32[]{:S(2)}, u32[]{:S(2)}) collective-permute-start(bf16[16,5376]{1,0:T(8,128)(2,1)S(1)} %bitcast.119), channel_id=1, source_target_pairs={{0,128},{64,192},{128,0},{192,64},{1,129},{65,193},{129,1},{193,65... | collective-permute-start | bytes 516104 | tf_op jit(solution)/shard_map/ppermute | solution.py:40
  81.9 14.6 %collective-permute-start.9 = (f32[32,24,128]{2,1,0:T(8,128)S(1)}, f32[32,24,128]{2,1,0:T(8,128)S(1)}, u32[]{:S(2)}, u32[]{:S(2)}) collective-permute-start(f32[32,24,128]{2,1,0:T(8,128)S(1)} %bitcast.112), channel_id=1, source_target_pairs={{0,64},{64,0},{128,192},{192,128},{1,65},{65,1},{129,193},{193,129... | collective-permute-start | bytes 1179656 | tf_op jit(solution)/shard_map/ppermute | solution.py:55
  84.0 0.7 copy-start.6
  84.0 0.9 copy-start.8
  89.5 3.7 %copy-start.3 = (f32[32,24,128]{2,1,0:T(8,128)}, f32[32,24,128]{2,1,0:T(8,128)S(1)}, u32[]{:S(2)}) copy-start(f32[32,24,128]{2,1,0:T(8,128)S(1)} %collective-permute-done.10.refs_3_) | copy-start | bytes 1179652
  89.5 7.0 %collective-permute-start.11 = (f32[32,24,128]{2,1,0:T(8,128)S(1)}, f32[32,24,128]{2,1,0:T(8,128)S(1)}, u32[]{:S(2)}, u32[]{:S(2)}) collective-permute-start(f32[32,24,128]{2,1,0:T(8,128)S(1)} %collective-permute-done.10.refs_3_), channel_id=1, source_target_pairs={{0,64},{64,0},{128,192},{192,128},{1,65},{65,1},{129,193},{193,129... | collective-permute-start | bytes 1179656 | tf_op jit(solution)/shard_map/ppermute | solution.py:55
  89.8 3.2 %collective-permute-start.13 = (bf16[2,16,5376]{2,1,0:T(8,128)(2,1)S(1)}, bf16[2,16,5376]{2,1,0:T(8,128)(2,1)S(1)}, u32[]{:S(2)}, u32[]{:S(2)}) collective-permute-start(bf16[2,16,5376]{2,1,0:T(8,128)(2,1)S(1)} %maximum_select_fusion.4), channel_id=1, source_target_pairs={{0,64},{64,0},{128,192},{192,128},{1,65},{65,1},{129,193},{193,129... | collective-permute-start | bytes 1032200 | tf_op jit(solution)/shard_map/ppermute | solution.py:44
  96.5 0.8 copy-start.4
  97.2 0.7 copy-start.7

commit v13 on v9

--- a/solution.py
+++ b/solution.py
@@ -23,13 +23,14 @@
     r = lax.axis_index("rep")
     n = lax.axis_size("rep")
     core, x_lo = r % 2, r // 2
-    x4 = x.reshape(2, 2, -1)
-    mine = lax.dynamic_index_in_dim(x4, core, 1, keepdims=False)
-    other = lax.dynamic_index_in_dim(x4, 1 - core, 1, keepdims=False)
-    a = mine + lax.ppermute(other, "rep", pairs(n, 1))
-    keep = lax.dynamic_index_in_dim(a, x_lo, 0, keepdims=False)
-    send = lax.dynamic_index_in_dim(a, 1 - x_lo, 0, keepdims=False)
-    return keep + lax.ppermute(send, "rep", pairs(n, 2))
+    x4 = jax.tree.map(lambda a: a.reshape(2, 2, -1), x)
+    pick = lambda tree, i, axis: jax.tree.map(
+        lambda a: lax.dynamic_index_in_dim(a, i, axis, keepdims=False), tree
+    )
+    got = lax.ppermute(pick(x4, 1 - core, 1), "rep", pairs(n, 1))
+    a = jax.tree.map(jnp.add, pick(x4, core, 1), got)
+    got = lax.ppermute(pick(a, 1 - x_lo, 0), "rep", pairs(n, 2))
+    return jax.tree.map(jnp.add, pick(a, x_lo, 0), got)
 
 
 def rep_gather(x):
@@ -126,13 +127,15 @@
     ex = expert_change[0].reshape(mats, esize)
     tx = table_change[0].reshape(width, per_half, groups, sub)
     tx = jnp.transpose(tx, (2, 0, 1, 3)).reshape(groups, -1)
-    q = rep_scatter(jnp.concatenate([ex, tx], axis=1))
+    q = rep_scatter((ex, tx))
 
     other = lax.ppermute(q, "tp", pairs(tensor, 1))
-    halves = jnp.where(t == 0, jnp.stack([q, other]), jnp.stack([other, q]))
-    he = halves[:, :esize].reshape(tensor, width, per_half, rows)
+    halves = jax.tree.map(
+        lambda a, b: jnp.where(t == 0, jnp.stack([a, b]), jnp.stack([b, a])), q, other
+    )
+    he = halves[0].reshape(tensor, width, per_half, rows)
     he = jnp.transpose(he, (0, 2, 1, 3)).reshape(shards, width * rows)
-    ht = halves[:, esize:].reshape(tensor, width, per_half, sub)
+    ht = halves[1].reshape(tensor, width, per_half, sub)
     ht = jnp.transpose(ht, (0, 2, 1, 3)).reshape(shards, width * sub)
     got = lax.all_to_all(jnp.concatenate([he, ht], 1), "shard", 0, 0, tiled=True)
 
@@ -158,6 +161,7 @@
     back = lax.all_to_all(back, "shard", 0, 0, tiled=True)
 
     pieces_e = gather_pieces(ge)
+    gt, _ = lax.optimization_barrier((gt, pieces_e[2]))
     pieces_t = gather_pieces(gt)
     scale = 1.0 / groups
     early_e = fused_update(pieces_e[:2], 0, expert_master, expert_moment, scale)

time: 112 us -> 102 us (0.911)
  waiting for transfers between devices: 48 us -> 34.7 us
  starting transfers between devices: 30.5 us -> 35.4 us
    ppermute x2, waiting for transfers between devices: 11.7 us -> 6.33 us  [gather_pieces(): cross = lax.ppermute(x, 'rep', pairs(n, 2))]
    ppermute x2 -> x4, waiting for transfers between devices: 11 us -> 6.74 us  [the longest x2 5.74 us: rep_scatter(): got = lax.ppermute(pick(a, 1 - x_lo, 0), 'rep', pairs(n, 2))]
    ppermute x1 -> x2, waiting for transfers between devices: 8.85 us -> 4.69 us  [local(): other = lax.ppermute(q, 'tp', pairs(tensor, 1))]
    all_to_all x1, starting transfers between devices: 9.47 us -> 12.7 us  [local(): lax.all_to_all(jnp.concatenate([he, ht], 1), 'shard', 0, 0, tiled=True)]
    another operation x0 -> x4, local copies, waits for them, and re-layouts: none -> 2.3 us  [the longest x2 2.1 us: rep_scatter(): x4 = jax.tree.map(lambda a: a.reshape(2, 2, -1), x)]
    ppermute x2, starting transfers between devices: 3.02 us -> 5.1 us  [gather_pieces(): sib = lax.ppermute(x, 'rep', pairs(n, 1))]
    ppermute x2, starting transfers between devices: 1.64 us -> 0.1 us  [gather_pieces(): cross = lax.ppermute(x, 'rep', pairs(n, 2))]
    ppermute x1, waiting for transfers between devices: 0.01 us -> 1.28 us  [rep_gather(): cross = lax.ppermute(x, 'rep', pairs(n, 2))]
  transfers between devices with their start and end apart: 13 -> 16, of which waited for: 6 -> 8; matrix products, arithmetic and copies ran while one was open for 4% -> 8% of each run, Pallas kernels for 9% -> 10%
where the time goes in v13:
time: 102 us
  starting transfers between devices  35.4 us (35%)
  waiting for transfers between devices  34.7 us (34%)
  local copies, waits for them, and re-layouts  17.8 us (17%)
  Pallas kernels  10.4 us (10%)
  other arithmetic  2.17 us (2%)
  between operations  1.15 us (1%)
    all_to_all x1, waiting for transfers between devices, local(): lax.all_to_all(jnp.concatenate([he, ht], 1), 'shard', 0, 0, tiled=True)  15.6 us
    all_to_all x1, starting transfers between devices, local(): lax.all_to_all(jnp.concatenate([he, ht], 1), 'shard', 0, 0, tiled=True)  12.7 us
    pallas_call x4, Pallas kernels, fused_update(): pl.pallas_call(lambda *refs: update_kernel(scale, count, *refs), grid_spe...  10.4 us
    all_to_all x1, starting transfers between devices, local(): back = lax.all_to_all(back, 'shard', 0, 0, tiled=True)  6.45 us
    ppermute x2, waiting for transfers between devices, gather_pieces(): cross = lax.ppermute(x, 'rep', pairs(n, 2))  6.33 us
    ppermute x2, waiting for transfers between devices, rep_scatter(): got = lax.ppermute(pick(a, 1 - x_lo, 0), 'rep', pairs(n, 2))  5.74 us
    ppermute x2, starting transfers between devices, gather_pieces(): sib = lax.ppermute(x, 'rep', pairs(n, 1))  5.1 us
    ppermute x2, waiting for transfers between devices, local(): other = lax.ppermute(q, 'tp', pairs(tensor, 1))  4.69 us
  transfers between devices with their start and end apart: 16, of which 8 were waited for; matrix products, arithmetic and copies ran while one was open for 8% of the time, Pallas kernels for 10%

profile of v13, /device:TPU:1, one launch (start us, length us, event | category | flops | bytes accessed | tf_op | source)
XLA Modules:
  0.0 101.6 jit_solution(4526879147560157761)
XLA Ops:
  0.7 1.6 %reshape_reshape_squeeze.3 = f32[2,2,36864]{2,1,0:T(2,128)S(1)} reshape(f32[1,4,24,1536]{3,2,1,0:T(8,128)} %param.6) | data formatting | bytes 1179648 | tf_op jit(solution)/shard_map/reshape;reshape;squeeze | solution.py:26
  2.3 0.5 constant_dynamic-slice_fusion.12
  3.1 3.3 %collective-permute-start = (f32[2,36864]{1,0:T(2,128)S(1)}, f32[2,36864]{1,0:T(2,128)S(1)}, u32[]{:S(2)}, u32[]{:S(2)}) collective-permute-start(f32[2,36864]{1,0:T(2,128)S(1)} %bitcast.132), channel_id=1, source_target_pairs={{0,64},{64,0},{128,192},{192,128},{1,65},{65,1},{129,193},{193,129... | collective-permute-start | bytes 884744 | tf_op jit(solution)/shard_map/ppermute | solution.py:30
  6.4 0.5 reshape_squeeze.3
  7.0 0.5 reshape_reshape.2
  7.5 0.7 constant_dynamic-slice_fusion.8
  8.2 0.3 copy.80
  8.6 0.3 bitcast_add_fusion.4
  9.3 1.0 collective-permute-done.3
  10.3 0.4 bitcast_add_fusion
  10.7 0.3 constant_dynamic-slice_fusion.5
  11.0 0.5 collective-permute-start.4
  11.6 2.6 %collective-permute-done.1 = f32[36864]{0:T(1024)S(1)} collective-permute-done((f32[36864]{0:T(1024)S(1)}, f32[36864]{0:T(1024)S(1)}, u32[]{:S(2)}, u32[]{:S(2)}) %collective-permute-start.1) | collective-permute-done | bytes 147488 | tf_op jit(solution)/shard_map/ppermute | solution.py:32
  14.3 1.1 %collective-permute-start.2 = (f32[36864]{0:T(1024)S(1)}, f32[36864]{0:T(1024)S(1)}, u32[]{:S(2)}, u32[]{:S(2)}) collective-permute-start(f32[36864]{0:T(1024)S(1)} %add.70), channel_id=1, source_target_pairs={{0,1},{1,0},{2,3},{3,2},{4,5},{5,4},{6,7},{7,6},{8,9},{9,8},{10,11... | collective-permute-start | bytes 442376 | tf_op jit(solution)/shard_map/ppermute | solution.py:132
  15.4 3.1 %collective-permute-done.4 = f32[49152]{0:T(1024)S(1)} collective-permute-done((f32[49152]{0:T(1024)S(1)}, f32[49152]{0:T(1024)S(1)}, u32[]{:S(2)}, u32[]{:S(2)}) %collective-permute-start.4) | collective-permute-done | bytes 196640 | tf_op jit(solution)/shard_map/ppermute | solution.py:32
  18.5 1.1 %collective-permute-start.5 = (f32[49152]{0:T(1024)S(1)}, f32[49152]{0:T(1024)S(1)}, u32[]{:S(2)}, u32[]{:S(2)}) collective-permute-start(f32[49152]{0:T(1024)S(1)} %add.72), channel_id=1, source_target_pairs={{0,1},{1,0},{2,3},{3,2},{4,5},{5,4},{6,7},{7,6},{8,9},{9,8},{10,11... | collective-permute-start | bytes 589832 | tf_op jit(solution)/shard_map/ppermute | solution.py:132
  19.7 1.8 %collective-permute-done.2 = f32[36864]{0:T(1024)S(1)} collective-permute-done((f32[36864]{0:T(1024)S(1)}, f32[36864]{0:T(1024)S(1)}, u32[]{:S(2)}, u32[]{:S(2)}) %collective-permute-start.2) | collective-permute-done | bytes 147488 | tf_op jit(solution)/shard_map/ppermute | solution.py:132
  21.9 2.9 %collective-permute-done.5 = f32[49152]{0:T(1024)S(1)} collective-permute-done((f32[49152]{0:T(1024)S(1)}, f32[49152]{0:T(1024)S(1)}, u32[]{:S(2)}, u32[]{:S(2)}) %collective-permute-start.5) | collective-permute-done | bytes 196640 | tf_op jit(solution)/shard_map/ppermute | solution.py:132
  25.1 1.6 %copy.44 = f32[32,1,5376]{2,1,0:T(1,128)} copy(f32[32,1,5376]{2,0,1:T(8,128)S(1)} %maximum_bitcast_fusion) | data formatting | bytes 1376256 | tf_op jit(solution)/shard_map/all_to_all | solution.py:140
  26.6 12.7 %all-to-all-start = ((f32[32,1,5376]{2,1,0:T(1,128)}), f32[32,1,5376]{2,1,0:T(1,128)S(1)}, u32[]{:S(2)}, u32[]{:S(2)}) async-start(f32[32,1,5376]{2,1,0:T(1,128)} %copy.44), calls=%async_computation | async-start | bytes 1376256 | tf_op jit(solution)/shard_map/all_to_all | solution.py:140
  39.4 1.2 %constant_dynamic-slice_fusion.1 = (f32[128,768]{1,0:T(8,128)S(1)}, f32[128,768]{1,0:T(8,128)S(1)}) fusion(f32[512,768]{1,0:T(8,128)} %refs_4_.7, s32[]{:T(128)S(6)} %select_n.108, f32[512,768]{1,0:T(8,128)} %refs_3_.7), kind=kLoop, calls=%fused_computation.34 | loop fusion | bytes 1572868 | tf_op jit(solution)/shard_map/dynamic_slice | solution.py:156
  40.9 1.1 %constant_dynamic-slice_fusion.3 = (f32[1,96,768]{2,1,0:T(8,128)S(1)}, f32[1,96,768]{2,1,0:T(8,128)S(1)}) fusion(f32[4,96,768]{2,1,0:T(8,128)} %refs_4_.5, s32[]{:T(128)S(6)} %select_n.107, f32[4,96,768]{2,1,0:T(8,128)} %refs_3_.5), kind=kLoop, calls=%fused_computation.36 | loop fusion | bytes 1179652 | tf_op jit(solution)/shard_map/jit(dynamic_index_in_dim)/dynamic_slice | solution.py:149
  42.3 15.6 %all-to-all-done = f32[32,1,5376]{2,1,0:T(1,128)S(1)} async-done(((f32[32,1,5376]{2,1,0:T(1,128)}), f32[32,1,5376]{2,1,0:T(1,128)S(1)}, u32[]{:S(2)}, u32[]{:S(2)}) %all-to-all-start) | async-done | bytes 688160 | tf_op jit(solution)/shard_map/all_to_all | solution.py:140
  58.3 0.3 div.34
  58.9 0.5 broadcast.40
  59.4 0.8 reduce
  60.2 0.8 reshape.161
  61.0 6.5 %all-to-all-start.1 = ((bf16[32,2,2688]{2,1,0:T(2,128)(2,1)}), bf16[32,2,2688]{2,1,0:T(2,128)(2,1)S(1)}, u32[]{:S(2)}, u32[]{:S(2)}) async-start(bf16[32,2,2688]{2,1,0:T(2,128)(2,1)} %reshape.161), calls=%async_computation.1 | async-start | bytes 688128 | tf_op jit(solution)/shard_map/all_to_all | solution.py:161
  67.9 2.1 %collective-permute-start.8 = (f32[32,24,96]{2,1,0:T(8,128)S(1)}, f32[32,24,96]{2,1,0:T(8,128)}, u32[]{:S(2)}, u32[]{:S(2)}) collective-permute-start(f32[32,24,96]{2,1,0:T(8,128)S(1)} %reshape.151.refs_1_), channel_id=1, source_target_pairs={{0,64},{64,0},{128,192},{192,128},{1,65},{65,1},{129,193},{193,129... | collective-permute-start | bytes 884744 | tf_op jit(solution)/shard_map/ppermute | solution.py:54
  70.1 6.3 %collective-permute-done.6.refs_1_ = f32[32,24,96]{2,1,0:T(8,128)S(1)} collective-permute-done((f32[32,24,96]{2,1,0:T(8,128)S(1)}, f32[32,24,96]{2,1,0:T(8,128)S(1)}, u32[]{:S(2)}, u32[]{:S(2)}) %collective-permute-start.6) | collective-permute-done | bytes 294944 | tf_op jit(solution)/shard_map/ppermute | solution.py:55
  76.4 3.0 %collective-permute-start.13 = (f32[32,24,128]{2,1,0:T(8,128)S(1)}, f32[32,24,128]{2,1,0:T(8,128)S(1)}, u32[]{:S(2)}, u32[]{:S(2)}) collective-permute-start(f32[32,24,128]{2,1,0:T(8,128)S(1)} %bitcast.111), channel_id=1, source_target_pairs={{0,64},{64,0},{128,192},{192,128},{1,65},{65,1},{129,193},{193,129... | collective-permute-start | bytes 1179656 | tf_op jit(solution)/shard_map/ppermute | solution.py:54
  79.4 0.3 collective-permute-start.7
  79.7 0.3 reshape.162
  80.0 0.4 constant_dynamic-slice_fusion
  80.4 1.5 %collective-permute-start.9 = (bf16[16,5376]{1,0:T(8,128)(2,1)S(1)}, bf16[16,5376]{1,0:T(8,128)(2,1)S(1)}, u32[]{:S(2)}, u32[]{:S(2)}) collective-permute-start(bf16[16,5376]{1,0:T(8,128)(2,1)S(1)} %bitcast.119), channel_id=1, source_target_pairs={{0,128},{64,192},{128,0},{192,64},{1,129},{65,193},{129,1},{193,65... | collective-permute-start | bytes 516104 | tf_op jit(solution)/shard_map/ppermute | solution.py:40
  81.9 2.5 %shard_map.109 = (f32[4,96,768]{2,1,0:T(8,128)}, f32[4,96,768]{2,1,0:T(8,128)}) custom-call(s32[1]{0:T(128)} %bitcast.refs_0_, f32[32,24,96]{2,1,0:T(8,128)} %copy-done.1, f32[32,24,96]{2,1,0:T(8,128)} %collective-permute-done.8.refs_2_, f32[4,96,768]{2,1,0:T(8,128)} %refs_3_.5, f32[4,96,768]{2,1,0:T(8,128)} %refs_4_.5), custom_call_target="tpu_custom_call" | custom-call | tf_op jit(solution)/shard_map/pallas_call | solution.py:99
  84.5 2.6 %shard_map.110 = (f32[4,96,768]{2,1,0:T(8,128)}, f32[4,96,768]{2,1,0:T(8,128)}) custom-call(s32[1]{0:T(128)} %bitcast.refs_0_, f32[32,24,96]{2,1,0:T(8,128)} %copy-done.5, f32[32,24,96]{2,1,0:T(8,128)} %collective-permute-done.7.refs_2_, f32[4,96,768]{2,1,0:T(8,128)} %refs_3_.5, ...), custom_call_target="tpu_custom_call", output_to_operand_aliasing={{0}: (5, {}), {1}: (6, {})} | custom-call | tf_op jit(solution)/shard_map/pallas_call | solution.py:99
  87.1 0.7 copy-done.6
  87.8 2.7 %shard_map.111 = (f32[512,768]{1,0:T(8,128)}, f32[512,768]{1,0:T(8,128)}) custom-call(s32[1]{0:T(128)} %bitcast.refs_0_, f32[32,24,128]{2,1,0:T(8,128)} %bitcast.113, f32[32,24,128]{2,1,0:T(8,128)} %copy-done.6, f32[512,768]{1,0:T(8,128)} %refs_3_.7, f32[512,768]{1,0:T(8,128)} %refs_4_.7), custom_call_target="tpu_custom_call" | custom-call | tf_op jit(solution)/shard_map/pallas_call | solution.py:99
  90.5 2.1 %collective-permute-start.12 = (f32[32,24,128]{2,1,0:T(8,128)S(1)}, f32[32,24,128]{2,1,0:T(8,128)S(1)}, u32[]{:S(2)}, u32[]{:S(2)}) collective-permute-start(f32[32,24,128]{2,1,0:T(8,128)S(1)} %collective-permute-done.11.refs_1_), channel_id=1, source_target_pairs={{0,64},{64,0},{128,192},{192,128},{1,65},{65,1},{129,193},{193,129... | collective-permute-start | bytes 1179656 | tf_op jit(solution)/shard_map/ppermute | solution.py:56
  92.5 1.3 %collective-permute-done.9 = bf16[16,5376]{1,0:T(8,128)(2,1)S(1)} collective-permute-done((bf16[16,5376]{1,0:T(8,128)(2,1)S(1)}, bf16[16,5376]{1,0:T(8,128)(2,1)S(1)}, u32[]{:S(2)}, u32[]{:S(2)}) %collective-permute-start.9) | collective-permute-done | bytes 172064 | tf_op jit(solution)/shard_map/ppermute | solution.py:40
  93.9 0.9 collective-permute-start.10
  94.8 0.7 copy-done.4
  95.5 2.7 %shard_map.112 = (f32[512,768]{1,0:T(8,128)}, f32[512,768]{1,0:T(8,128)}) custom-call(s32[1]{0:T(128)} %bitcast.refs_0_, f32[32,24,128]{2,1,0:T(8,128)} %copy-done.3, f32[32,24,128]{2,1,0:T(8,128)} %copy-done.4, f32[512,768]{1,0:T(8,128)} %refs_3_.7, f32[512,768]{1,0:T(8,128)} %refs_4_.7, ...), custom_call_target="tpu_custom_call", output_to_operand_aliasing={{0}: (5, {}), {1}: (6, {})} | custom-call | tf_op jit(solution)/shard_map/pallas_call | solution.py:99
  98.5 0.3 copy.52
  98.8 1.0 %reshape.160 = bf16[24,8192]{1,0:T(8,128)(2,1)} reshape(bf16[24,16,4,128]{3,2,1,0:T(4,128)(2,1)S(1)} %copy.52) | data formatting | bytes 786432 | tf_op jit(solution)/shard_map/reshape | solution.py:181
  99.8 0.6 reshape.156
  100.5 1.1 %reshape.157 = bf16[4,24,1536]{2,1,0:T(8,128)(2,1)} reshape(bf16[4,24,16,96]{3,2,1,0:T(8,128)(2,1)S(1)} %copy.51) | data formatting | bytes 589824 | tf_op jit(solution)/shard_map/reshape | solution.py:179
  (62 shorter events, 3.7 us)
Async XLA Ops:
  0.6 5.8 %copy-start.2 = (f32[1,24,8192]{2,1,0:T(8,128)S(1)}, f32[1,24,8192]{2,1,0:T(8,128)}, u32[]{:S(2)}) copy-start(f32[1,24,8192]{2,1,0:T(8,128)} %param.7) | copy-start | bytes 2359300
  3.1 5.5 %collective-permute-start = (f32[2,36864]{1,0:T(2,128)S(1)}, f32[2,36864]{1,0:T(2,128)S(1)}, u32[]{:S(2)}, u32[]{:S(2)}) collective-permute-start(f32[2,36864]{1,0:T(2,128)S(1)} %bitcast.132), channel_id=1, source_target_pairs={{0,64},{64,0},{128,192},{192,128},{1,65},{65,1},{129,193},{193,129... | collective-permute-start | bytes 884744 | tf_op jit(solution)/shard_map/ppermute | solution.py:30
  8.5 1.8 %collective-permute-start.3 = (f32[2,49152]{1,0:T(2,128)S(1)}, f32[2,49152]{1,0:T(2,128)S(1)}, u32[]{:S(2)}, u32[]{:S(2)}) collective-permute-start(f32[2,49152]{1,0:T(2,128)S(1)} %bitcast.130), channel_id=1, source_target_pairs={{0,64},{64,0},{128,192},{192,128},{1,65},{65,1},{129,193},{193,129... | collective-permute-start | bytes 1179656 | tf_op jit(solution)/shard_map/ppermute | solution.py:30
  9.2 5.0 %collective-permute-start.1 = (f32[36864]{0:T(1024)S(1)}, f32[36864]{0:T(1024)S(1)}, u32[]{:S(2)}, u32[]{:S(2)}) collective-permute-start(f32[36864]{0:T(1024)S(1)} %bitcast.135), channel_id=1, source_target_pairs={{0,128},{64,192},{128,0},{192,64},{1,129},{65,193},{129,1},{193,65... | collective-permute-start | bytes 442376 | tf_op jit(solution)/shard_map/ppermute | solution.py:32
  11.0 7.4 %collective-permute-start.4 = (f32[49152]{0:T(1024)S(1)}, f32[49152]{0:T(1024)S(1)}, u32[]{:S(2)}, u32[]{:S(2)}) collective-permute-start(f32[49152]{0:T(1024)S(1)} %bitcast.134), channel_id=1, source_target_pairs={{0,128},{64,192},{128,0},{192,64},{1,129},{65,193},{129,1},{193,65... | collective-permute-start | bytes 589832 | tf_op jit(solution)/shard_map/ppermute | solution.py:32
  14.3 7.2 %collective-permute-start.2 = (f32[36864]{0:T(1024)S(1)}, f32[36864]{0:T(1024)S(1)}, u32[]{:S(2)}, u32[]{:S(2)}) collective-permute-start(f32[36864]{0:T(1024)S(1)} %add.70), channel_id=1, source_target_pairs={{0,1},{1,0},{2,3},{3,2},{4,5},{5,4},{6,7},{7,6},{8,9},{9,8},{10,11... | collective-permute-start | bytes 442376 | tf_op jit(solution)/shard_map/ppermute | solution.py:132
  18.5 6.3 %collective-permute-start.5 = (f32[49152]{0:T(1024)S(1)}, f32[49152]{0:T(1024)S(1)}, u32[]{:S(2)}, u32[]{:S(2)}) collective-permute-start(f32[49152]{0:T(1024)S(1)} %add.72), channel_id=1, source_target_pairs={{0,1},{1,0},{2,3},{3,2},{4,5},{5,4},{6,7},{7,6},{8,9},{9,8},{10,11... | collective-permute-start | bytes 589832 | tf_op jit(solution)/shard_map/ppermute | solution.py:132
  26.6 31.3 %all-to-all-start = ((f32[32,1,5376]{2,1,0:T(1,128)}), f32[32,1,5376]{2,1,0:T(1,128)S(1)}, u32[]{:S(2)}, u32[]{:S(2)}) async-start(f32[32,1,5376]{2,1,0:T(1,128)} %copy.44), calls=%async_computation | async-start | bytes 1376256 | tf_op jit(solution)/shard_map/all_to_all | solution.py:140
  61.0 18.7 %all-to-all-start.1 = ((bf16[32,2,2688]{2,1,0:T(2,128)(2,1)}), bf16[32,2,2688]{2,1,0:T(2,128)(2,1)S(1)}, u32[]{:S(2)}, u32[]{:S(2)}) async-start(bf16[32,2,2688]{2,1,0:T(2,128)(2,1)} %reshape.161), calls=%async_computation.1 | async-start | bytes 688128 | tf_op jit(solution)/shard_map/all_to_all | solution.py:161
  67.8 14.2 %copy-start.1 = (f32[32,24,96]{2,1,0:T(8,128)}, f32[32,24,96]{2,1,0:T(8,128)S(1)}, u32[]{:S(2)}) copy-start(f32[32,24,96]{2,1,0:T(8,128)S(1)} %reshape.151.refs_1_) | copy-start | bytes 884740
  67.8 8.6 %collective-permute-start.6 = (f32[32,24,96]{2,1,0:T(8,128)S(1)}, f32[32,24,96]{2,1,0:T(8,128)S(1)}, u32[]{:S(2)}, u32[]{:S(2)}) collective-permute-start(f32[32,24,96]{2,1,0:T(8,128)S(1)} %reshape.151.refs_1_), channel_id=1, source_target_pairs={{0,128},{64,192},{128,0},{192,64},{1,129},{65,193},{129,1},{193,65... | collective-permute-start | bytes 884744 | tf_op jit(solution)/shard_map/ppermute | solution.py:55
  67.9 14.0 %collective-permute-start.8 = (f32[32,24,96]{2,1,0:T(8,128)S(1)}, f32[32,24,96]{2,1,0:T(8,128)}, u32[]{:S(2)}, u32[]{:S(2)}) collective-permute-start(f32[32,24,96]{2,1,0:T(8,128)S(1)} %reshape.151.refs_1_), channel_id=1, source_target_pairs={{0,64},{64,0},{128,192},{192,128},{1,65},{65,1},{129,193},{193,129... | collective-permute-start | bytes 884744 | tf_op jit(solution)/shard_map/ppermute | solution.py:54
  70.1 14.4 %copy-start = (f32[4,8,24,128]{3,2,1,0:T(8,128)}, f32[4,8,24,128]{3,2,1,0:T(8,128)S(1)}, u32[]{:S(2)}) copy-start(f32[4,8,24,128]{3,2,1,0:T(8,128)S(1)} %copy.64) | copy-start | bytes 1179652
  76.4 8.1 %copy-start.5 = (f32[32,24,96]{2,1,0:T(8,128)}, f32[32,24,96]{2,1,0:T(8,128)S(1)}, u32[]{:S(2)}) copy-start(f32[32,24,96]{2,1,0:T(8,128)S(1)} %collective-permute-done.6.refs_1_) | copy-start | bytes 884740
  76.4 10.6 %collective-permute-start.13 = (f32[32,24,128]{2,1,0:T(8,128)S(1)}, f32[32,24,128]{2,1,0:T(8,128)S(1)}, u32[]{:S(2)}, u32[]{:S(2)}) collective-permute-start(f32[32,24,128]{2,1,0:T(8,128)S(1)} %bitcast.111), channel_id=1, source_target_pairs={{0,64},{64,0},{128,192},{192,128},{1,65},{65,1},{129,193},{193,129... | collective-permute-start | bytes 1179656 | tf_op jit(solution)/shard_map/ppermute | solution.py:54
  79.4 11.1 %collective-permute-start.11 = (f32[32,24,128]{2,1,0:T(8,128)S(1)}, f32[32,24,128]{2,1,0:T(8,128)S(1)}, u32[]{:S(2)}, u32[]{:S(2)}) collective-permute-start(f32[32,24,128]{2,1,0:T(8,128)S(1)} %bitcast.112), channel_id=1, source_target_pairs={{0,128},{64,192},{128,0},{192,64},{1,129},{65,193},{129,1},{193,65... | collective-permute-start | bytes 1179656 | tf_op jit(solution)/shard_map/ppermute | solution.py:55
  79.4 5.1 %collective-permute-start.7 = (f32[32,24,96]{2,1,0:T(8,128)S(1)}, f32[32,24,96]{2,1,0:T(8,128)}, u32[]{:S(2)}, u32[]{:S(2)}) collective-permute-start(f32[32,24,96]{2,1,0:T(8,128)S(1)} %collective-permute-done.6.refs_1_), channel_id=1, source_target_pairs={{0,64},{64,0},{128,192},{192,128},{1,65},{65,1},{129,193},{193,129... | collective-permute-start | bytes 884744 | tf_op jit(solution)/shard_map/ppermute | solution.py:56
  80.4 13.5 %collective-permute-start.9 = (bf16[16,5376]{1,0:T(8,128)(2,1)S(1)}, bf16[16,5376]{1,0:T(8,128)(2,1)S(1)}, u32[]{:S(2)}, u32[]{:S(2)}) collective-permute-start(bf16[16,5376]{1,0:T(8,128)(2,1)S(1)} %bitcast.119), channel_id=1, source_target_pairs={{0,128},{64,192},{128,0},{192,64},{1,129},{65,193},{129,1},{193,65... | collective-permute-start | bytes 516104 | tf_op jit(solution)/shard_map/ppermute | solution.py:40
  87.0 0.7 copy-start.6
  90.5 4.3 %copy-start.3 = (f32[32,24,128]{2,1,0:T(8,128)}, f32[32,24,128]{2,1,0:T(8,128)S(1)}, u32[]{:S(2)}) copy-start(f32[32,24,128]{2,1,0:T(8,128)S(1)} %collective-permute-done.11.refs_1_) | copy-start | bytes 1179652
  90.5 4.3 %collective-permute-start.12 = (f32[32,24,128]{2,1,0:T(8,128)S(1)}, f32[32,24,128]{2,1,0:T(8,128)S(1)}, u32[]{:S(2)}, u32[]{:S(2)}) collective-permute-start(f32[32,24,128]{2,1,0:T(8,128)S(1)} %collective-permute-done.11.refs_1_), channel_id=1, source_target_pairs={{0,64},{64,0},{128,192},{192,128},{1,65},{65,1},{129,193},{193,129... | collective-permute-start | bytes 1179656 | tf_op jit(solution)/shard_map/ppermute | solution.py:56
  93.9 4.3 %collective-permute-start.10 = (bf16[2,16,5376]{2,1,0:T(8,128)(2,1)S(1)}, bf16[2,16,5376]{2,1,0:T(8,128)(2,1)S(1)}, u32[]{:S(2)}, u32[]{:S(2)}) collective-permute-start(bf16[2,16,5376]{2,1,0:T(8,128)(2,1)S(1)} %maximum_select_fusion.4), channel_id=1, source_target_pairs={{0,64},{64,0},{128,192},{192,128},{1,65},{65,1},{129,193},{193,129... | collective-permute-start | bytes 1032200 | tf_op jit(solution)/shard_map/ppermute | solution.py:44
  94.8 0.7 copy-start.4

commit v14 on v13

--- a/solution.py
+++ b/solution.py
@@ -161,16 +161,19 @@
     back = lax.all_to_all(back, "shard", 0, 0, tiled=True)
 
     pieces_e = gather_pieces(ge)
-    gt, _ = lax.optimization_barrier((gt, pieces_e[2]))
-    pieces_t = gather_pieces(gt)
+    n_rep = lax.axis_size("rep")
+    sib_t = lax.ppermute(gt, "rep", pairs(n_rep, 1))
+    gt_late, _ = lax.optimization_barrier((gt, pieces_e[2]))
+    cross_t = lax.ppermute(gt_late, "rep", pairs(n_rep, 2))
+    sib_cross_t = lax.ppermute(cross_t, "rep", pairs(n_rep, 1))
     scale = 1.0 / groups
-    early_e = fused_update(pieces_e[:2], 0, expert_master, expert_moment, scale)
-    early_t = fused_update(pieces_t[:2], 0, table_master, table_moment, scale)
+    early_t = fused_update((gt, sib_t), 0, table_master, table_moment, scale)
+    pieces_e, early_t = lax.optimization_barrier((pieces_e, early_t))
     expert_weights, expert_velocity = fused_update(
-        pieces_e[2:], 2, expert_master, expert_moment, scale, early_e
+        pieces_e, 0, expert_master, expert_moment, scale
     )
     table_weights, table_velocity = fused_update(
-        pieces_t[2:], 2, table_master, table_moment, scale, early_t
+        (cross_t, sib_cross_t), 2, table_master, table_moment, scale, early_t
     )
 
     back = lax.dynamic_slice_in_dim(back, t * per_half, per_half, 0)

time: 102 us -> 101 us (level)
    ppermute x2 -> x1, starting transfers between devices: 5.1 us -> 2.13 us  [gather_pieces(): sib = lax.ppermute(x, 'rep', pairs(n, 1))]
    ppermute x0 -> x3, starting transfers between devices: none -> 2.46 us  [the longest x1 2.07 us: local(): sib_cross_t = lax.ppermute(cross_t, 'rep', pairs(n_rep, 1))]
    ppermute x1, waiting for transfers between devices: 1.28 us -> 0.01 us  [rep_gather(): cross = lax.ppermute(x, 'rep', pairs(n, 2))]
    ppermute x0 -> x3, waiting for transfers between devices: none -> 1.15 us  [the longest x1 1.15 us: local(): sib_cross_t = lax.ppermute(cross_t, 'rep', pairs(n_rep, 1))]
    ppermute x2 -> x1, starting transfers between devices: 2.35 us -> 2.97 us  [gather_pieces(): sib_cross = lax.ppermute(cross, 'rep', pairs(n, 1))]
    pallas_call x4 -> x3, Pallas kernels: 10.4 us -> 9.98 us  [fused_update(): pl.pallas_call(lambda *refs: update_kernel(scale, count, *refs), grid_spe...]
    unnamed x27 -> x29, local copies, waits for them, and re-layouts: 3.9 us -> 4.07 us
    ppermute x2 -> x1, waiting for transfers between devices: 6.33 us -> 6.22 us  [gather_pieces(): cross = lax.ppermute(x, 'rep', pairs(n, 2))]
where the time goes in v14:
time: 101 us; the launch traced here: 100 us
  starting transfers between devices  34.7 us (34%)
  waiting for transfers between devices  34.4 us (34%)
  local copies, waits for them, and re-layouts  18 us (18%)
  Pallas kernels  9.98 us (10%)
  other arithmetic  2.17 us (2%)
  between operations  1.15 us (1%)
    all_to_all x1, waiting for transfers between devices, local(): lax.all_to_all(jnp.concatenate([he, ht], 1), 'shard', 0, 0, tiled=True)  15.6 us
    all_to_all x1, starting transfers between devices, local(): lax.all_to_all(jnp.concatenate([he, ht], 1), 'shard', 0, 0, tiled=True)  12.7 us
    pallas_call x3, Pallas kernels, fused_update(): pl.pallas_call(lambda *refs: update_kernel(scale, count, *refs), grid_spe...  9.98 us
    all_to_all x1, starting transfers between devices, local(): back = lax.all_to_all(back, 'shard', 0, 0, tiled=True)  6.45 us
    ppermute x1, waiting for transfers between devices, gather_pieces(): cross = lax.ppermute(x, 'rep', pairs(n, 2))  6.22 us
    ppermute x2, waiting for transfers between devices, rep_scatter(): got = lax.ppermute(pick(a, 1 - x_lo, 0), 'rep', pairs(n, 2))  5.74 us
    ppermute x2, waiting for transfers between devices, local(): other = lax.ppermute(q, 'tp', pairs(tensor, 1))  4.69 us
    unnamed x29, local copies, waits for them, and re-layouts  4.07 us
  transfers between devices with their start and end apart: 16, of which 8 were waited for; matrix products, arithmetic and copies ran while one was open for 8% of the time, Pallas kernels for 10%

profile of v14, /device:TPU:1, one launch (start us, length us, event | category | flops | bytes accessed | tf_op | source)
XLA Modules:
  0.0 100.4 jit_solution(7347831988900151718)
XLA Ops:
  0.7 1.6 %reshape_reshape_squeeze.3 = f32[2,2,36864]{2,1,0:T(2,128)S(1)} reshape(f32[1,4,24,1536]{3,2,1,0:T(8,128)} %param.6) | data formatting | bytes 1179648 | tf_op jit(solution)/shard_map/reshape;reshape;squeeze | solution.py:26
  2.3 0.5 constant_dynamic-slice_fusion.12
  3.1 3.3 %collective-permute-start = (f32[2,36864]{1,0:T(2,128)S(1)}, f32[2,36864]{1,0:T(2,128)S(1)}, u32[]{:S(2)}, u32[]{:S(2)}) collective-permute-start(f32[2,36864]{1,0:T(2,128)S(1)} %bitcast.132), channel_id=1, source_target_pairs={{0,64},{64,0},{128,192},{192,128},{1,65},{65,1},{129,193},{193,129... | collective-permute-start | bytes 884744 | tf_op jit(solution)/shard_map/ppermute | solution.py:30
  6.4 0.5 reshape_squeeze.3
  7.0 0.5 reshape_reshape.2
  7.5 0.7 constant_dynamic-slice_fusion.8
  8.2 0.3 copy.78
  8.6 0.3 bitcast_add_fusion.4
  8.9 0.3 constant_dynamic-slice_fusion.9
  9.3 1.0 collective-permute-done.3
  10.3 0.4 bitcast_add_fusion
  10.7 0.3 constant_dynamic-slice_fusion.5
  11.0 0.5 collective-permute-start.4
  11.6 2.6 %collective-permute-done.1 = f32[36864]{0:T(1024)S(1)} collective-permute-done((f32[36864]{0:T(1024)S(1)}, f32[36864]{0:T(1024)S(1)}, u32[]{:S(2)}, u32[]{:S(2)}) %collective-permute-start.1) | collective-permute-done | bytes 147488 | tf_op jit(solution)/shard_map/ppermute | solution.py:32
  14.3 1.1 %collective-permute-start.2 = (f32[36864]{0:T(1024)S(1)}, f32[36864]{0:T(1024)S(1)}, u32[]{:S(2)}, u32[]{:S(2)}) collective-permute-start(f32[36864]{0:T(1024)S(1)} %add.70), channel_id=1, source_target_pairs={{0,1},{1,0},{2,3},{3,2},{4,5},{5,4},{6,7},{7,6},{8,9},{9,8},{10,11... | collective-permute-start | bytes 442376 | tf_op jit(solution)/shard_map/ppermute | solution.py:132
  15.4 3.1 %collective-permute-done.4 = f32[49152]{0:T(1024)S(1)} collective-permute-done((f32[49152]{0:T(1024)S(1)}, f32[49152]{0:T(1024)S(1)}, u32[]{:S(2)}, u32[]{:S(2)}) %collective-permute-start.4) | collective-permute-done | bytes 196640 | tf_op jit(solution)/shard_map/ppermute | solution.py:32
  18.5 1.1 %collective-permute-start.5 = (f32[49152]{0:T(1024)S(1)}, f32[49152]{0:T(1024)S(1)}, u32[]{:S(2)}, u32[]{:S(2)}) collective-permute-start(f32[49152]{0:T(1024)S(1)} %add.72), channel_id=1, source_target_pairs={{0,1},{1,0},{2,3},{3,2},{4,5},{5,4},{6,7},{7,6},{8,9},{9,8},{10,11... | collective-permute-start | bytes 589832 | tf_op jit(solution)/shard_map/ppermute | solution.py:132
  19.7 1.8 %collective-permute-done.2 = f32[36864]{0:T(1024)S(1)} collective-permute-done((f32[36864]{0:T(1024)S(1)}, f32[36864]{0:T(1024)S(1)}, u32[]{:S(2)}, u32[]{:S(2)}) %collective-permute-start.2) | collective-permute-done | bytes 147488 | tf_op jit(solution)/shard_map/ppermute | solution.py:132
  21.9 2.9 %collective-permute-done.5 = f32[49152]{0:T(1024)S(1)} collective-permute-done((f32[49152]{0:T(1024)S(1)}, f32[49152]{0:T(1024)S(1)}, u32[]{:S(2)}, u32[]{:S(2)}) %collective-permute-start.5) | collective-permute-done | bytes 196640 | tf_op jit(solution)/shard_map/ppermute | solution.py:132
  25.1 1.6 %copy.42 = f32[32,1,5376]{2,1,0:T(1,128)} copy(f32[32,1,5376]{2,0,1:T(8,128)S(1)} %maximum_bitcast_fusion) | data formatting | bytes 1376256 | tf_op jit(solution)/shard_map/all_to_all | solution.py:140
  26.6 12.7 %all-to-all-start = ((f32[32,1,5376]{2,1,0:T(1,128)}), f32[32,1,5376]{2,1,0:T(1,128)S(1)}, u32[]{:S(2)}, u32[]{:S(2)}) async-start(f32[32,1,5376]{2,1,0:T(1,128)} %copy.42), calls=%async_computation | async-start | bytes 1376256 | tf_op jit(solution)/shard_map/all_to_all | solution.py:140
  39.4 1.2 %constant_dynamic-slice_fusion.1 = (f32[128,768]{1,0:T(8,128)S(1)}, f32[128,768]{1,0:T(8,128)S(1)}) fusion(f32[512,768]{1,0:T(8,128)} %refs_4_.3, s32[]{:T(128)S(6)} %select_n.108, f32[512,768]{1,0:T(8,128)} %refs_3_.3), kind=kLoop, calls=%fused_computation.34 | loop fusion | bytes 1572868 | tf_op jit(solution)/shard_map/dynamic_slice | solution.py:156
  40.9 1.1 %constant_dynamic-slice_fusion.3 = (f32[1,96,768]{2,1,0:T(8,128)S(1)}, f32[1,96,768]{2,1,0:T(8,128)S(1)}) fusion(f32[4,96,768]{2,1,0:T(8,128)} %refs_6_.1, s32[]{:T(128)S(6)} %select_n.107, f32[4,96,768]{2,1,0:T(8,128)} %refs_5_.1), kind=kLoop, calls=%fused_computation.36 | loop fusion | bytes 1179652 | tf_op jit(solution)/shard_map/jit(dynamic_index_in_dim)/dynamic_slice | solution.py:149
  42.3 15.6 %all-to-all-done = f32[32,1,5376]{2,1,0:T(1,128)S(1)} async-done(((f32[32,1,5376]{2,1,0:T(1,128)}), f32[32,1,5376]{2,1,0:T(1,128)S(1)}, u32[]{:S(2)}, u32[]{:S(2)}) %all-to-all-start) | async-done | bytes 688160 | tf_op jit(solution)/shard_map/all_to_all | solution.py:140
  58.3 0.3 div.34
  58.9 0.5 broadcast.40
  59.4 0.8 reduce
  60.2 0.8 reshape.160
  61.0 6.5 %all-to-all-start.1 = ((bf16[32,2,2688]{2,1,0:T(2,128)(2,1)}), bf16[32,2,2688]{2,1,0:T(2,128)(2,1)S(1)}, u32[]{:S(2)}, u32[]{:S(2)}) async-start(bf16[32,2,2688]{2,1,0:T(2,128)(2,1)} %reshape.160), calls=%async_computation.1 | async-start | bytes 688128 | tf_op jit(solution)/shard_map/all_to_all | solution.py:161
  67.5 0.3 reshape.150.refs_1_
  67.9 2.1 %collective-permute-start.6 = (f32[32,24,96]{2,1,0:T(8,128)S(1)}, f32[32,24,96]{2,1,0:T(8,128)S(1)}, u32[]{:S(2)}, u32[]{:S(2)}) collective-permute-start(f32[32,24,96]{2,1,0:T(8,128)S(1)} %reshape.150.refs_1_), channel_id=1, source_target_pairs={{0,64},{64,0},{128,192},{192,128},{1,65},{65,1},{129,193},{193,129... | collective-permute-start | bytes 884744 | tf_op jit(solution)/shard_map/ppermute | solution.py:54
  70.2 6.2 %collective-permute-done.7.refs_3_ = f32[32,24,96]{2,1,0:T(8,128)S(1)} collective-permute-done((f32[32,24,96]{2,1,0:T(8,128)S(1)}, f32[32,24,96]{2,1,0:T(8,128)S(1)}, u32[]{:S(2)}, u32[]{:S(2)}) %collective-permute-start.7) | collective-permute-done | bytes 294944 | tf_op jit(solution)/shard_map/ppermute | solution.py:55
  76.4 0.3 collective-permute-start.12
  76.7 3.0 %collective-permute-start.8 = (f32[32,24,96]{2,1,0:T(8,128)S(1)}, f32[32,24,96]{2,1,0:T(8,128)S(1)}, u32[]{:S(2)}, u32[]{:S(2)}) collective-permute-start(f32[32,24,96]{2,1,0:T(8,128)S(1)} %collective-permute-done.7.refs_3_), channel_id=1, source_target_pairs={{0,64},{64,0},{128,192},{192,128},{1,65},{65,1},{129,193},{193,129... | collective-permute-start | bytes 884744 | tf_op jit(solution)/shard_map/ppermute | solution.py:56
  79.7 0.3 reshape.161
  80.0 0.4 constant_dynamic-slice_fusion
  80.4 1.5 %collective-permute-start.10 = (bf16[16,5376]{1,0:T(8,128)(2,1)S(1)}, bf16[16,5376]{1,0:T(8,128)(2,1)S(1)}, u32[]{:S(2)}, u32[]{:S(2)}) collective-permute-start(bf16[16,5376]{1,0:T(8,128)(2,1)S(1)} %bitcast.119), channel_id=1, source_target_pairs={{0,128},{64,192},{128,0},{192,64},{1,129},{65,193},{129,1},{193,65... | collective-permute-start | bytes 516104 | tf_op jit(solution)/shard_map/ppermute | solution.py:40
  81.9 2.7 %shard_map.109 = (f32[512,768]{1,0:T(8,128)}, f32[512,768]{1,0:T(8,128)}) custom-call(s32[1]{0:T(128)} %bitcast.refs_0_, f32[32,24,128]{2,1,0:T(8,128)} %bitcast.113, f32[32,24,128]{2,1,0:T(8,128)} %collective-permute-done.9.refs_2_, f32[512,768]{1,0:T(8,128)} %refs_3_.3, f32[512,768]{1,0:T(8,128)} %refs_4_.3), custom_call_target="tpu_custom_call" | custom-call | tf_op jit(solution)/shard_map/pallas_call | solution.py:99
  84.7 0.7 copy-done.6
  85.6 4.6 %shard_map.110 = (f32[4,96,768]{2,1,0:T(8,128)}, f32[4,96,768]{2,1,0:T(8,128)}) custom-call(s32[1]{0:T(128)} %bitcast.refs_0_, f32[32,24,96]{2,1,0:T(8,128)} %copy-done, f32[32,24,96]{2,1,0:T(8,128)} %copy-done.6, f32[32,24,96]{2,1,0:T(8,128)} %copy-done.5, f32[32,24,96]{2,1,0:T(8,128)} %copy-done.7, f32[4,96,768]{2,1,0:T(8,128)} %refs_5_.1, ...), custom_call_target="tpu_custom_call" | custom-call | tf_op jit(solution)/shard_map/pallas_call | solution.py:99
  90.2 2.1 %collective-permute-start.13 = (f32[32,24,128]{2,1,0:T(8,128)S(1)}, f32[32,24,128]{2,1,0:T(8,128)S(1)}, u32[]{:S(2)}, u32[]{:S(2)}) collective-permute-start(f32[32,24,128]{2,1,0:T(8,128)S(1)} %collective-permute-done.12.refs_1_), channel_id=1, source_target_pairs={{0,64},{64,0},{128,192},{192,128},{1,65},{65,1},{129,193},{193,129... | collective-permute-start | bytes 1179656 | tf_op jit(solution)/shard_map/ppermute | solution.py:168
  92.5 1.1 %collective-permute-done.13.refs_2_ = f32[32,24,128]{2,1,0:T(8,128)S(1)} collective-permute-done((f32[32,24,128]{2,1,0:T(8,128)S(1)}, f32[32,24,128]{2,1,0:T(8,128)S(1)}, u32[]{:S(2)}, u32[]{:S(2)}) %collective-permute-start.13) | collective-permute-done | bytes 393248 | tf_op jit(solution)/shard_map/ppermute | solution.py:168
  93.6 0.7 copy-done.4
  94.3 2.7 %shard_map.111 = (f32[512,768]{1,0:T(8,128)}, f32[512,768]{1,0:T(8,128)}) custom-call(s32[1]{0:T(128)} %bitcast.refs_0_, f32[32,24,128]{2,1,0:T(8,128)} %copy-done.3, f32[32,24,128]{2,1,0:T(8,128)} %copy-done.4, f32[512,768]{1,0:T(8,128)} %refs_3_.3, f32[512,768]{1,0:T(8,128)} %refs_4_.3, ...), custom_call_target="tpu_custom_call", output_to_operand_aliasing={{0}: (5, {}), {1}: (6, {})} | custom-call | tf_op jit(solution)/shard_map/pallas_call | solution.py:99
  97.3 0.3 copy.50
  97.6 1.0 %reshape.159 = bf16[24,8192]{1,0:T(8,128)(2,1)} reshape(bf16[24,16,4,128]{3,2,1,0:T(4,128)(2,1)S(1)} %copy.50) | data formatting | bytes 786432 | tf_op jit(solution)/shard_map/reshape | solution.py:184
  98.6 0.6 reshape.156
  99.3 1.1 %reshape.157 = bf16[4,24,1536]{2,1,0:T(8,128)(2,1)} reshape(bf16[4,24,16,96]{3,2,1,0:T(8,128)(2,1)S(1)} %copy.49) | data formatting | bytes 589824 | tf_op jit(solution)/shard_map/reshape | solution.py:182
  (63 shorter events, 3.5 us)
Async XLA Ops:
  0.6 5.8 %copy-start.2 = (f32[1,24,8192]{2,1,0:T(8,128)S(1)}, f32[1,24,8192]{2,1,0:T(8,128)}, u32[]{:S(2)}) copy-start(f32[1,24,8192]{2,1,0:T(8,128)} %param.7) | copy-start | bytes 2359300
  3.1 5.5 %collective-permute-start = (f32[2,36864]{1,0:T(2,128)S(1)}, f32[2,36864]{1,0:T(2,128)S(1)}, u32[]{:S(2)}, u32[]{:S(2)}) collective-permute-start(f32[2,36864]{1,0:T(2,128)S(1)} %bitcast.132), channel_id=1, source_target_pairs={{0,64},{64,0},{128,192},{192,128},{1,65},{65,1},{129,193},{193,129... | collective-permute-start | bytes 884744 | tf_op jit(solution)/shard_map/ppermute | solution.py:30
  8.5 1.8 %collective-permute-start.3 = (f32[2,49152]{1,0:T(2,128)S(1)}, f32[2,49152]{1,0:T(2,128)S(1)}, u32[]{:S(2)}, u32[]{:S(2)}) collective-permute-start(f32[2,49152]{1,0:T(2,128)S(1)} %bitcast.130), channel_id=1, source_target_pairs={{0,64},{64,0},{128,192},{192,128},{1,65},{65,1},{129,193},{193,129... | collective-permute-start | bytes 1179656 | tf_op jit(solution)/shard_map/ppermute | solution.py:30
  9.2 5.0 %collective-permute-start.1 = (f32[36864]{0:T(1024)S(1)}, f32[36864]{0:T(1024)S(1)}, u32[]{:S(2)}, u32[]{:S(2)}) collective-permute-start(f32[36864]{0:T(1024)S(1)} %bitcast.135), channel_id=1, source_target_pairs={{0,128},{64,192},{128,0},{192,64},{1,129},{65,193},{129,1},{193,65... | collective-permute-start | bytes 442376 | tf_op jit(solution)/shard_map/ppermute | solution.py:32
  11.0 7.4 %collective-permute-start.4 = (f32[49152]{0:T(1024)S(1)}, f32[49152]{0:T(1024)S(1)}, u32[]{:S(2)}, u32[]{:S(2)}) collective-permute-start(f32[49152]{0:T(1024)S(1)} %bitcast.134), channel_id=1, source_target_pairs={{0,128},{64,192},{128,0},{192,64},{1,129},{65,193},{129,1},{193,65... | collective-permute-start | bytes 589832 | tf_op jit(solution)/shard_map/ppermute | solution.py:32
  14.3 7.2 %collective-permute-start.2 = (f32[36864]{0:T(1024)S(1)}, f32[36864]{0:T(1024)S(1)}, u32[]{:S(2)}, u32[]{:S(2)}) collective-permute-start(f32[36864]{0:T(1024)S(1)} %add.70), channel_id=1, source_target_pairs={{0,1},{1,0},{2,3},{3,2},{4,5},{5,4},{6,7},{7,6},{8,9},{9,8},{10,11... | collective-permute-start | bytes 442376 | tf_op jit(solution)/shard_map/ppermute | solution.py:132
  18.5 6.3 %collective-permute-start.5 = (f32[49152]{0:T(1024)S(1)}, f32[49152]{0:T(1024)S(1)}, u32[]{:S(2)}, u32[]{:S(2)}) collective-permute-start(f32[49152]{0:T(1024)S(1)} %add.72), channel_id=1, source_target_pairs={{0,1},{1,0},{2,3},{3,2},{4,5},{5,4},{6,7},{7,6},{8,9},{9,8},{10,11... | collective-permute-start | bytes 589832 | tf_op jit(solution)/shard_map/ppermute | solution.py:132
  26.6 31.3 %all-to-all-start = ((f32[32,1,5376]{2,1,0:T(1,128)}), f32[32,1,5376]{2,1,0:T(1,128)S(1)}, u32[]{:S(2)}, u32[]{:S(2)}) async-start(f32[32,1,5376]{2,1,0:T(1,128)} %copy.42), calls=%async_computation | async-start | bytes 1376256 | tf_op jit(solution)/shard_map/all_to_all | solution.py:140
  61.0 18.7 %all-to-all-start.1 = ((bf16[32,2,2688]{2,1,0:T(2,128)(2,1)}), bf16[32,2,2688]{2,1,0:T(2,128)(2,1)S(1)}, u32[]{:S(2)}, u32[]{:S(2)}) async-start(bf16[32,2,2688]{2,1,0:T(2,128)(2,1)} %reshape.160), calls=%async_computation.1 | async-start | bytes 688128 | tf_op jit(solution)/shard_map/all_to_all | solution.py:161
  67.8 16.9 %copy-start = (f32[32,24,96]{2,1,0:T(8,128)}, f32[32,24,96]{2,1,0:T(8,128)S(1)}, u32[]{:S(2)}) copy-start(f32[32,24,96]{2,1,0:T(8,128)S(1)} %reshape.150.refs_1_) | copy-start | bytes 884740
  67.8 8.6 %collective-permute-start.7 = (f32[32,24,96]{2,1,0:T(8,128)S(1)}, f32[32,24,96]{2,1,0:T(8,128)S(1)}, u32[]{:S(2)}, u32[]{:S(2)}) collective-permute-start(f32[32,24,96]{2,1,0:T(8,128)S(1)} %reshape.150.refs_1_), channel_id=1, source_target_pairs={{0,128},{64,192},{128,0},{192,64},{1,129},{65,193},{129,1},{193,65... | collective-permute-start | bytes 884744 | tf_op jit(solution)/shard_map/ppermute | solution.py:55
  67.9 16.8 %collective-permute-start.6 = (f32[32,24,96]{2,1,0:T(8,128)S(1)}, f32[32,24,96]{2,1,0:T(8,128)S(1)}, u32[]{:S(2)}, u32[]{:S(2)}) collective-permute-start(f32[32,24,96]{2,1,0:T(8,128)S(1)} %reshape.150.refs_1_), channel_id=1, source_target_pairs={{0,64},{64,0},{128,192},{192,128},{1,65},{65,1},{129,193},{193,129... | collective-permute-start | bytes 884744 | tf_op jit(solution)/shard_map/ppermute | solution.py:54
  70.1 11.8 %copy-start.1 = (f32[4,8,24,128]{3,2,1,0:T(8,128)}, f32[4,8,24,128]{3,2,1,0:T(8,128)S(1)}, u32[]{:S(2)}) copy-start(f32[4,8,24,128]{3,2,1,0:T(8,128)S(1)} %copy.61) | copy-start | bytes 1179652
  70.1 11.8 %collective-permute-start.9 = (f32[32,24,128]{2,1,0:T(8,128)S(1)}, f32[32,24,128]{2,1,0:T(8,128)}, u32[]{:S(2)}, u32[]{:S(2)}) collective-permute-start(f32[32,24,128]{2,1,0:T(8,128)S(1)} %bitcast.111), channel_id=1, source_target_pairs={{0,64},{64,0},{128,192},{192,128},{1,65},{65,1},{129,193},{193,129... | collective-permute-start | bytes 1179656 | tf_op jit(solution)/shard_map/ppermute | solution.py:165
  76.4 8.2 %copy-start.5 = (f32[32,24,96]{2,1,0:T(8,128)}, f32[32,24,96]{2,1,0:T(8,128)S(1)}, u32[]{:S(2)}) copy-start(f32[32,24,96]{2,1,0:T(8,128)S(1)} %collective-permute-done.7.refs_3_) | copy-start | bytes 884740
  76.4 13.7 %collective-permute-start.12 = (f32[32,24,128]{2,1,0:T(8,128)S(1)}, f32[32,24,128]{2,1,0:T(8,128)S(1)}, u32[]{:S(2)}, u32[]{:S(2)}) collective-permute-start(f32[32,24,128]{2,1,0:T(8,128)S(1)} %bitcast.112), channel_id=1, source_target_pairs={{0,128},{64,192},{128,0},{192,64},{1,129},{65,193},{129,1},{193,65... | collective-permute-start | bytes 1179656 | tf_op jit(solution)/shard_map/ppermute | solution.py:167
  76.7 8.0 %collective-permute-start.8 = (f32[32,24,96]{2,1,0:T(8,128)S(1)}, f32[32,24,96]{2,1,0:T(8,128)S(1)}, u32[]{:S(2)}, u32[]{:S(2)}) collective-permute-start(f32[32,24,96]{2,1,0:T(8,128)S(1)} %collective-permute-done.7.refs_3_), channel_id=1, source_target_pairs={{0,64},{64,0},{128,192},{192,128},{1,65},{65,1},{129,193},{193,129... | collective-permute-start | bytes 884744 | tf_op jit(solution)/shard_map/ppermute | solution.py:56
  80.4 11.9 %collective-permute-start.10 = (bf16[16,5376]{1,0:T(8,128)(2,1)S(1)}, bf16[16,5376]{1,0:T(8,128)(2,1)S(1)}, u32[]{:S(2)}, u32[]{:S(2)}) collective-permute-start(bf16[16,5376]{1,0:T(8,128)(2,1)S(1)} %bitcast.119), channel_id=1, source_target_pairs={{0,128},{64,192},{128,0},{192,64},{1,129},{65,193},{129,1},{193,65... | collective-permute-start | bytes 516104 | tf_op jit(solution)/shard_map/ppermute | solution.py:40
  84.6 0.8 copy-start.6
  84.7 0.9 copy-start.7
  90.2 3.4 %copy-start.3 = (f32[32,24,128]{2,1,0:T(8,128)}, f32[32,24,128]{2,1,0:T(8,128)S(1)}, u32[]{:S(2)}) copy-start(f32[32,24,128]{2,1,0:T(8,128)S(1)} %collective-permute-done.12.refs_1_) | copy-start | bytes 1179652
  90.2 3.4 %collective-permute-start.13 = (f32[32,24,128]{2,1,0:T(8,128)S(1)}, f32[32,24,128]{2,1,0:T(8,128)S(1)}, u32[]{:S(2)}, u32[]{:S(2)}) collective-permute-start(f32[32,24,128]{2,1,0:T(8,128)S(1)} %collective-permute-done.12.refs_1_), channel_id=1, source_target_pairs={{0,64},{64,0},{128,192},{192,128},{1,65},{65,1},{129,193},{193,129... | collective-permute-start | bytes 1179656 | tf_op jit(solution)/shard_map/ppermute | solution.py:168
  92.3 4.7 %collective-permute-start.11 = (bf16[2,16,5376]{2,1,0:T(8,128)(2,1)S(1)}, bf16[2,16,5376]{2,1,0:T(8,128)(2,1)S(1)}, u32[]{:S(2)}, u32[]{:S(2)}) collective-permute-start(bf16[2,16,5376]{2,1,0:T(8,128)(2,1)S(1)} %maximum_select_fusion.4), channel_id=1, source_target_pairs={{0,64},{64,0},{128,192},{192,128},{1,65},{65,1},{129,193},{193,129... | collective-permute-start | bytes 1032200 | tf_op jit(solution)/shard_map/ppermute | solution.py:44
  93.6 0.7 copy-start.4

commit v15 on v14

--- a/solution.py
+++ b/solution.py
@@ -172,9 +172,6 @@
     expert_weights, expert_velocity = fused_update(
         pieces_e, 0, expert_master, expert_moment, scale
     )
-    table_weights, table_velocity = fused_update(
-        (cross_t, sib_cross_t), 2, table_master, table_moment, scale, early_t
-    )
 
     back = lax.dynamic_slice_in_dim(back, t * per_half, per_half, 0)
     allq = rep_gather(back)
@@ -182,6 +179,12 @@
     expert_copies = jnp.transpose(ce, (0, 2, 1, 3)).reshape(mats, width, per_half * rows)
     ct = allq[:, :, width * rows :].reshape(groups, per_half, width, sub)
     table_copies = jnp.transpose(ct, (2, 1, 0, 3)).reshape(width, per_half * vrows)
+    late, expert_copies, table_copies = lax.optimization_barrier(
+        ((cross_t, sib_cross_t), expert_copies, table_copies)
+    )
+    table_weights, table_velocity = fused_update(
+        late, 2, table_master, table_moment, scale, early_t
+    )
     return (
         expert_weights,
         expert_velocity,

time: 101 us -> 101 us (level)
    ppermute x1, waiting for transfers between devices: 0.01 us -> 1.64 us  [rep_gather(): sib = lax.ppermute(pair, 'rep', pairs(n, 1))]
    ppermute x1, waiting for transfers between devices: 1.15 us -> 0.01 us  [local(): sib_cross_t = lax.ppermute(cross_t, 'rep', pairs(n_rep, 1))]
  transfers between devices with their start and end apart: 16 -> 16, of which waited for: 8 -> 8; matrix products, arithmetic and copies ran while one was open for 8% -> 11% of each run, Pallas kernels for 10% -> 7%
where the time goes in v15:
time: 101 us
  waiting for transfers between devices  34.9 us (35%)
  starting transfers between devices  34.7 us (34%)
  local copies, waits for them, and re-layouts  18 us (18%)
  Pallas kernels  9.98 us (10%)
  other arithmetic  2.17 us (2%)
  between operations  1.16 us (1%)
    all_to_all x1, waiting for transfers between devices, local(): lax.all_to_all(jnp.concatenate([he, ht], 1), 'shard', 0, 0, tiled=True)  15.6 us
    all_to_all x1, starting transfers between devices, local(): lax.all_to_all(jnp.concatenate([he, ht], 1), 'shard', 0, 0, tiled=True)  12.7 us
    pallas_call x3, Pallas kernels, fused_update(): pl.pallas_call(lambda *refs: update_kernel(scale, count, *refs), grid_spe...  9.98 us
    all_to_all x1, starting transfers between devices, local(): back = lax.all_to_all(back, 'shard', 0, 0, tiled=True)  6.45 us
    ppermute x1, waiting for transfers between devices, gather_pieces(): cross = lax.ppermute(x, 'rep', pairs(n, 2))  6.22 us
    ppermute x2, waiting for transfers between devices, rep_scatter(): got = lax.ppermute(pick(a, 1 - x_lo, 0), 'rep', pairs(n, 2))  5.74 us
    ppermute x2, waiting for transfers between devices, local(): other = lax.ppermute(q, 'tp', pairs(tensor, 1))  4.69 us
    unnamed x29, local copies, waits for them, and re-layouts  4.09 us
  transfers between devices with their start and end apart: 16, of which 8 were waited for; matrix products, arithmetic and copies ran while one was open for 11% of the time, Pallas kernels for 7%

profile of v15, /device:TPU:1, one launch (start us, length us, event | category | flops | bytes accessed | tf_op | source)
XLA Modules:
  0.0 100.9 jit_solution(10386981060281171111)
XLA Ops:
  0.7 1.6 %reshape_reshape_squeeze.3 = f32[2,2,36864]{2,1,0:T(2,128)S(1)} reshape(f32[1,4,24,1536]{3,2,1,0:T(8,128)} %param.6) | data formatting | bytes 1179648 | tf_op jit(solution)/shard_map/reshape;reshape;squeeze | solution.py:26
  2.3 0.5 constant_dynamic-slice_fusion.12
  3.1 3.3 %collective-permute-start = (f32[2,36864]{1,0:T(2,128)S(1)}, f32[2,36864]{1,0:T(2,128)S(1)}, u32[]{:S(2)}, u32[]{:S(2)}) collective-permute-start(f32[2,36864]{1,0:T(2,128)S(1)} %bitcast.132), channel_id=1, source_target_pairs={{0,64},{64,0},{128,192},{192,128},{1,65},{65,1},{129,193},{193,129... | collective-permute-start | bytes 884744 | tf_op jit(solution)/shard_map/ppermute | solution.py:30
  6.4 0.5 reshape_squeeze.3
  7.0 0.5 reshape_reshape.2
  7.5 0.7 constant_dynamic-slice_fusion.8
  8.2 0.3 copy.78
  8.6 0.3 bitcast_add_fusion.4
  8.9 0.3 constant_dynamic-slice_fusion.9
  9.3 1.0 collective-permute-done.3
  10.3 0.4 bitcast_add_fusion
  10.7 0.3 constant_dynamic-slice_fusion.5
  11.0 0.5 collective-permute-start.4
  11.6 2.6 %collective-permute-done.1 = f32[36864]{0:T(1024)S(1)} collective-permute-done((f32[36864]{0:T(1024)S(1)}, f32[36864]{0:T(1024)S(1)}, u32[]{:S(2)}, u32[]{:S(2)}) %collective-permute-start.1) | collective-permute-done | bytes 147488 | tf_op jit(solution)/shard_map/ppermute | solution.py:32
  14.3 1.1 %collective-permute-start.2 = (f32[36864]{0:T(1024)S(1)}, f32[36864]{0:T(1024)S(1)}, u32[]{:S(2)}, u32[]{:S(2)}) collective-permute-start(f32[36864]{0:T(1024)S(1)} %add.70), channel_id=1, source_target_pairs={{0,1},{1,0},{2,3},{3,2},{4,5},{5,4},{6,7},{7,6},{8,9},{9,8},{10,11... | collective-permute-start | bytes 442376 | tf_op jit(solution)/shard_map/ppermute | solution.py:132
  15.4 3.1 %collective-permute-done.4 = f32[49152]{0:T(1024)S(1)} collective-permute-done((f32[49152]{0:T(1024)S(1)}, f32[49152]{0:T(1024)S(1)}, u32[]{:S(2)}, u32[]{:S(2)}) %collective-permute-start.4) | collective-permute-done | bytes 196640 | tf_op jit(solution)/shard_map/ppermute | solution.py:32
  18.5 1.1 %collective-permute-start.5 = (f32[49152]{0:T(1024)S(1)}, f32[49152]{0:T(1024)S(1)}, u32[]{:S(2)}, u32[]{:S(2)}) collective-permute-start(f32[49152]{0:T(1024)S(1)} %add.72), channel_id=1, source_target_pairs={{0,1},{1,0},{2,3},{3,2},{4,5},{5,4},{6,7},{7,6},{8,9},{9,8},{10,11... | collective-permute-start | bytes 589832 | tf_op jit(solution)/shard_map/ppermute | solution.py:132
  19.7 1.8 %collective-permute-done.2 = f32[36864]{0:T(1024)S(1)} collective-permute-done((f32[36864]{0:T(1024)S(1)}, f32[36864]{0:T(1024)S(1)}, u32[]{:S(2)}, u32[]{:S(2)}) %collective-permute-start.2) | collective-permute-done | bytes 147488 | tf_op jit(solution)/shard_map/ppermute | solution.py:132
  21.9 2.9 %collective-permute-done.5 = f32[49152]{0:T(1024)S(1)} collective-permute-done((f32[49152]{0:T(1024)S(1)}, f32[49152]{0:T(1024)S(1)}, u32[]{:S(2)}, u32[]{:S(2)}) %collective-permute-start.5) | collective-permute-done | bytes 196640 | tf_op jit(solution)/shard_map/ppermute | solution.py:132
  25.1 1.6 %copy.42 = f32[32,1,5376]{2,1,0:T(1,128)} copy(f32[32,1,5376]{2,0,1:T(8,128)S(1)} %maximum_bitcast_fusion) | data formatting | bytes 1376256 | tf_op jit(solution)/shard_map/all_to_all | solution.py:140
  26.6 12.7 %all-to-all-start = ((f32[32,1,5376]{2,1,0:T(1,128)}), f32[32,1,5376]{2,1,0:T(1,128)S(1)}, u32[]{:S(2)}, u32[]{:S(2)}) async-start(f32[32,1,5376]{2,1,0:T(1,128)} %copy.42), calls=%async_computation | async-start | bytes 1376256 | tf_op jit(solution)/shard_map/all_to_all | solution.py:140
  39.4 1.2 %constant_dynamic-slice_fusion.1 = (f32[128,768]{1,0:T(8,128)S(1)}, f32[128,768]{1,0:T(8,128)S(1)}) fusion(f32[512,768]{1,0:T(8,128)} %refs_4_.3, s32[]{:T(128)S(6)} %select_n.108, f32[512,768]{1,0:T(8,128)} %refs_3_.3), kind=kLoop, calls=%fused_computation.34 | loop fusion | bytes 1572868 | tf_op jit(solution)/shard_map/dynamic_slice | solution.py:156
  40.9 1.1 %constant_dynamic-slice_fusion.3 = (f32[1,96,768]{2,1,0:T(8,128)S(1)}, f32[1,96,768]{2,1,0:T(8,128)S(1)}) fusion(f32[4,96,768]{2,1,0:T(8,128)} %refs_6_.1, s32[]{:T(128)S(6)} %select_n.107, f32[4,96,768]{2,1,0:T(8,128)} %refs_5_.1), kind=kLoop, calls=%fused_computation.36 | loop fusion | bytes 1179652 | tf_op jit(solution)/shard_map/jit(dynamic_index_in_dim)/dynamic_slice | solution.py:149
  42.3 15.6 %all-to-all-done = f32[32,1,5376]{2,1,0:T(1,128)S(1)} async-done(((f32[32,1,5376]{2,1,0:T(1,128)}), f32[32,1,5376]{2,1,0:T(1,128)S(1)}, u32[]{:S(2)}, u32[]{:S(2)}) %all-to-all-start) | async-done | bytes 688160 | tf_op jit(solution)/shard_map/all_to_all | solution.py:140
  58.3 0.3 div.34
  58.8 0.5 broadcast.40
  59.4 0.8 reduce
  60.2 0.8 reshape.160
  61.0 6.5 %all-to-all-start.1 = ((bf16[32,2,2688]{2,1,0:T(2,128)(2,1)}), bf16[32,2,2688]{2,1,0:T(2,128)(2,1)S(1)}, u32[]{:S(2)}, u32[]{:S(2)}) async-start(bf16[32,2,2688]{2,1,0:T(2,128)(2,1)} %reshape.160), calls=%async_computation.1 | async-start | bytes 688128 | tf_op jit(solution)/shard_map/all_to_all | solution.py:161
  67.5 0.3 reshape.150.refs_1_
  67.9 2.1 %collective-permute-start.6 = (f32[32,24,96]{2,1,0:T(8,128)S(1)}, f32[32,24,96]{2,1,0:T(8,128)S(1)}, u32[]{:S(2)}, u32[]{:S(2)}) collective-permute-start(f32[32,24,96]{2,1,0:T(8,128)S(1)} %reshape.150.refs_1_), channel_id=1, source_target_pairs={{0,64},{64,0},{128,192},{192,128},{1,65},{65,1},{129,193},{193,129... | collective-permute-start | bytes 884744 | tf_op jit(solution)/shard_map/ppermute | solution.py:54
  70.2 6.2 %collective-permute-done.7.refs_3_ = f32[32,24,96]{2,1,0:T(8,128)S(1)} collective-permute-done((f32[32,24,96]{2,1,0:T(8,128)S(1)}, f32[32,24,96]{2,1,0:T(8,128)S(1)}, u32[]{:S(2)}, u32[]{:S(2)}) %collective-permute-start.7) | collective-permute-done | bytes 294944 | tf_op jit(solution)/shard_map/ppermute | solution.py:55
  76.4 0.3 collective-permute-start.10
  76.7 3.0 %collective-permute-start.8 = (f32[32,24,96]{2,1,0:T(8,128)S(1)}, f32[32,24,96]{2,1,0:T(8,128)S(1)}, u32[]{:S(2)}, u32[]{:S(2)}) collective-permute-start(f32[32,24,96]{2,1,0:T(8,128)S(1)} %collective-permute-done.7.refs_3_), channel_id=1, source_target_pairs={{0,64},{64,0},{128,192},{192,128},{1,65},{65,1},{129,193},{193,129... | collective-permute-start | bytes 884744 | tf_op jit(solution)/shard_map/ppermute | solution.py:56
  79.7 0.3 reshape.161
  80.0 0.4 constant_dynamic-slice_fusion
  80.4 1.5 %collective-permute-start.12 = (bf16[16,5376]{1,0:T(8,128)(2,1)S(1)}, bf16[16,5376]{1,0:T(8,128)(2,1)S(1)}, u32[]{:S(2)}, u32[]{:S(2)}) collective-permute-start(bf16[16,5376]{1,0:T(8,128)(2,1)S(1)} %bitcast.119), channel_id=1, source_target_pairs={{0,128},{64,192},{128,0},{192,64},{1,129},{65,193},{129,1},{193,65... | collective-permute-start | bytes 516104 | tf_op jit(solution)/shard_map/ppermute | solution.py:40
  81.9 2.7 %shard_map.109 = (f32[512,768]{1,0:T(8,128)}, f32[512,768]{1,0:T(8,128)}) custom-call(s32[1]{0:T(128)} %bitcast.refs_0_, f32[32,24,128]{2,1,0:T(8,128)} %bitcast.113, f32[32,24,128]{2,1,0:T(8,128)} %collective-permute-done.9.refs_2_, f32[512,768]{1,0:T(8,128)} %refs_3_.3, f32[512,768]{1,0:T(8,128)} %refs_4_.3), custom_call_target="tpu_custom_call" | custom-call | tf_op jit(solution)/shard_map/pallas_call | solution.py:99
  84.7 0.7 copy-done.6
  85.6 4.6 %shard_map.110 = (f32[4,96,768]{2,1,0:T(8,128)}, f32[4,96,768]{2,1,0:T(8,128)}) custom-call(s32[1]{0:T(128)} %bitcast.refs_0_, f32[32,24,96]{2,1,0:T(8,128)} %copy-done, f32[32,24,96]{2,1,0:T(8,128)} %copy-done.6, f32[32,24,96]{2,1,0:T(8,128)} %copy-done.5, f32[32,24,96]{2,1,0:T(8,128)} %copy-done.7, f32[4,96,768]{2,1,0:T(8,128)} %refs_5_.1, ...), custom_call_target="tpu_custom_call" | custom-call | tf_op jit(solution)/shard_map/pallas_call | solution.py:99
  90.2 2.1 %collective-permute-start.11 = (f32[32,24,128]{2,1,0:T(8,128)S(1)}, f32[32,24,128]{2,1,0:T(8,128)S(1)}, u32[]{:S(2)}, u32[]{:S(2)}) collective-permute-start(f32[32,24,128]{2,1,0:T(8,128)S(1)} %collective-permute-done.10.refs_1_), channel_id=1, source_target_pairs={{0,64},{64,0},{128,192},{192,128},{1,65},{65,1},{129,193},{193,129... | collective-permute-start | bytes 1179656 | tf_op jit(solution)/shard_map/ppermute | solution.py:168
  92.5 1.6 %collective-permute-done.13 = bf16[2,16,5376]{2,1,0:T(8,128)(2,1)S(1)} collective-permute-done((bf16[2,16,5376]{2,1,0:T(8,128)(2,1)S(1)}, bf16[2,16,5376]{2,1,0:T(8,128)(2,1)S(1)}, u32[]{:S(2)}, u32[]{:S(2)}) %collective-permute-start.13) | collective-permute-done | bytes 344096 | tf_op jit(solution)/shard_map/ppermute | solution.py:44
  94.4 0.3 copy.50
  94.7 1.0 %reshape.159 = bf16[24,8192]{1,0:T(8,128)(2,1)} reshape(bf16[24,16,4,128]{3,2,1,0:T(4,128)(2,1)S(1)} %copy.50) | data formatting | bytes 786432 | tf_op jit(solution)/shard_map/reshape | solution.py:181
  95.7 0.6 reshape.156
  96.4 1.1 %reshape.157 = bf16[4,24,1536]{2,1,0:T(8,128)(2,1)} reshape(bf16[4,24,16,96]{3,2,1,0:T(8,128)(2,1)S(1)} %copy.49) | data formatting | bytes 589824 | tf_op jit(solution)/shard_map/reshape | solution.py:179
  97.5 0.8 copy-done.4
  98.3 2.7 %shard_map.111 = (f32[512,768]{1,0:T(8,128)}, f32[512,768]{1,0:T(8,128)}) custom-call(s32[1]{0:T(128)} %bitcast.refs_0_, f32[32,24,128]{2,1,0:T(8,128)} %copy-done.3, f32[32,24,128]{2,1,0:T(8,128)} %copy-done.4, f32[512,768]{1,0:T(8,128)} %refs_3_.3, f32[512,768]{1,0:T(8,128)} %refs_4_.3, ...), custom_call_target="tpu_custom_call", output_to_operand_aliasing={{0}: (5, {}), {1}: (6, {})} | custom-call | tf_op jit(solution)/shard_map/pallas_call | solution.py:99
  (63 shorter events, 3.5 us)
Async XLA Ops:
  0.6 5.8 %copy-start.2 = (f32[1,24,8192]{2,1,0:T(8,128)S(1)}, f32[1,24,8192]{2,1,0:T(8,128)}, u32[]{:S(2)}) copy-start(f32[1,24,8192]{2,1,0:T(8,128)} %param.7) | copy-start | bytes 2359300
  3.1 5.5 %collective-permute-start = (f32[2,36864]{1,0:T(2,128)S(1)}, f32[2,36864]{1,0:T(2,128)S(1)}, u32[]{:S(2)}, u32[]{:S(2)}) collective-permute-start(f32[2,36864]{1,0:T(2,128)S(1)} %bitcast.132), channel_id=1, source_target_pairs={{0,64},{64,0},{128,192},{192,128},{1,65},{65,1},{129,193},{193,129... | collective-permute-start | bytes 884744 | tf_op jit(solution)/shard_map/ppermute | solution.py:30
  8.5 1.8 %collective-permute-start.3 = (f32[2,49152]{1,0:T(2,128)S(1)}, f32[2,49152]{1,0:T(2,128)S(1)}, u32[]{:S(2)}, u32[]{:S(2)}) collective-permute-start(f32[2,49152]{1,0:T(2,128)S(1)} %bitcast.130), channel_id=1, source_target_pairs={{0,64},{64,0},{128,192},{192,128},{1,65},{65,1},{129,193},{193,129... | collective-permute-start | bytes 1179656 | tf_op jit(solution)/shard_map/ppermute | solution.py:30
  9.2 5.0 %collective-permute-start.1 = (f32[36864]{0:T(1024)S(1)}, f32[36864]{0:T(1024)S(1)}, u32[]{:S(2)}, u32[]{:S(2)}) collective-permute-start(f32[36864]{0:T(1024)S(1)} %bitcast.135), channel_id=1, source_target_pairs={{0,128},{64,192},{128,0},{192,64},{1,129},{65,193},{129,1},{193,65... | collective-permute-start | bytes 442376 | tf_op jit(solution)/shard_map/ppermute | solution.py:32
  11.0 7.4 %collective-permute-start.4 = (f32[49152]{0:T(1024)S(1)}, f32[49152]{0:T(1024)S(1)}, u32[]{:S(2)}, u32[]{:S(2)}) collective-permute-start(f32[49152]{0:T(1024)S(1)} %bitcast.134), channel_id=1, source_target_pairs={{0,128},{64,192},{128,0},{192,64},{1,129},{65,193},{129,1},{193,65... | collective-permute-start | bytes 589832 | tf_op jit(solution)/shard_map/ppermute | solution.py:32
  14.3 7.2 %collective-permute-start.2 = (f32[36864]{0:T(1024)S(1)}, f32[36864]{0:T(1024)S(1)}, u32[]{:S(2)}, u32[]{:S(2)}) collective-permute-start(f32[36864]{0:T(1024)S(1)} %add.70), channel_id=1, source_target_pairs={{0,1},{1,0},{2,3},{3,2},{4,5},{5,4},{6,7},{7,6},{8,9},{9,8},{10,11... | collective-permute-start | bytes 442376 | tf_op jit(solution)/shard_map/ppermute | solution.py:132
  18.5 6.3 %collective-permute-start.5 = (f32[49152]{0:T(1024)S(1)}, f32[49152]{0:T(1024)S(1)}, u32[]{:S(2)}, u32[]{:S(2)}) collective-permute-start(f32[49152]{0:T(1024)S(1)} %add.72), channel_id=1, source_target_pairs={{0,1},{1,0},{2,3},{3,2},{4,5},{5,4},{6,7},{7,6},{8,9},{9,8},{10,11... | collective-permute-start | bytes 589832 | tf_op jit(solution)/shard_map/ppermute | solution.py:132
  26.6 31.3 %all-to-all-start = ((f32[32,1,5376]{2,1,0:T(1,128)}), f32[32,1,5376]{2,1,0:T(1,128)S(1)}, u32[]{:S(2)}, u32[]{:S(2)}) async-start(f32[32,1,5376]{2,1,0:T(1,128)} %copy.42), calls=%async_computation | async-start | bytes 1376256 | tf_op jit(solution)/shard_map/all_to_all | solution.py:140
  61.0 18.7 %all-to-all-start.1 = ((bf16[32,2,2688]{2,1,0:T(2,128)(2,1)}), bf16[32,2,2688]{2,1,0:T(2,128)(2,1)S(1)}, u32[]{:S(2)}, u32[]{:S(2)}) async-start(bf16[32,2,2688]{2,1,0:T(2,128)(2,1)} %reshape.160), calls=%async_computation.1 | async-start | bytes 688128 | tf_op jit(solution)/shard_map/all_to_all | solution.py:161
  67.8 16.9 %copy-start = (f32[32,24,96]{2,1,0:T(8,128)}, f32[32,24,96]{2,1,0:T(8,128)S(1)}, u32[]{:S(2)}) copy-start(f32[32,24,96]{2,1,0:T(8,128)S(1)} %reshape.150.refs_1_) | copy-start | bytes 884740
  67.8 8.6 %collective-permute-start.7 = (f32[32,24,96]{2,1,0:T(8,128)S(1)}, f32[32,24,96]{2,1,0:T(8,128)S(1)}, u32[]{:S(2)}, u32[]{:S(2)}) collective-permute-start(f32[32,24,96]{2,1,0:T(8,128)S(1)} %reshape.150.refs_1_), channel_id=1, source_target_pairs={{0,128},{64,192},{128,0},{192,64},{1,129},{65,193},{129,1},{193,65... | collective-permute-start | bytes 884744 | tf_op jit(solution)/shard_map/ppermute | solution.py:55
  67.9 16.8 %collective-permute-start.6 = (f32[32,24,96]{2,1,0:T(8,128)S(1)}, f32[32,24,96]{2,1,0:T(8,128)S(1)}, u32[]{:S(2)}, u32[]{:S(2)}) collective-permute-start(f32[32,24,96]{2,1,0:T(8,128)S(1)} %reshape.150.refs_1_), channel_id=1, source_target_pairs={{0,64},{64,0},{128,192},{192,128},{1,65},{65,1},{129,193},{193,129... | collective-permute-start | bytes 884744 | tf_op jit(solution)/shard_map/ppermute | solution.py:54
  70.1 11.8 %copy-start.1 = (f32[4,8,24,128]{3,2,1,0:T(8,128)}, f32[4,8,24,128]{3,2,1,0:T(8,128)S(1)}, u32[]{:S(2)}) copy-start(f32[4,8,24,128]{3,2,1,0:T(8,128)S(1)} %copy.61) | copy-start | bytes 1179652
  70.1 11.8 %collective-permute-start.9 = (f32[32,24,128]{2,1,0:T(8,128)S(1)}, f32[32,24,128]{2,1,0:T(8,128)}, u32[]{:S(2)}, u32[]{:S(2)}) collective-permute-start(f32[32,24,128]{2,1,0:T(8,128)S(1)} %bitcast.111), channel_id=1, source_target_pairs={{0,64},{64,0},{128,192},{192,128},{1,65},{65,1},{129,193},{193,129... | collective-permute-start | bytes 1179656 | tf_op jit(solution)/shard_map/ppermute | solution.py:165
  76.4 8.2 %copy-start.5 = (f32[32,24,96]{2,1,0:T(8,128)}, f32[32,24,96]{2,1,0:T(8,128)S(1)}, u32[]{:S(2)}) copy-start(f32[32,24,96]{2,1,0:T(8,128)S(1)} %collective-permute-done.7.refs_3_) | copy-start | bytes 884740
  76.4 13.7 %collective-permute-start.10 = (f32[32,24,128]{2,1,0:T(8,128)S(1)}, f32[32,24,128]{2,1,0:T(8,128)S(1)}, u32[]{:S(2)}, u32[]{:S(2)}) collective-permute-start(f32[32,24,128]{2,1,0:T(8,128)S(1)} %bitcast.112), channel_id=1, source_target_pairs={{0,128},{64,192},{128,0},{192,64},{1,129},{65,193},{129,1},{193,65... | collective-permute-start | bytes 1179656 | tf_op jit(solution)/shard_map/ppermute | solution.py:167
  76.7 8.0 %collective-permute-start.8 = (f32[32,24,96]{2,1,0:T(8,128)S(1)}, f32[32,24,96]{2,1,0:T(8,128)S(1)}, u32[]{:S(2)}, u32[]{:S(2)}) collective-permute-start(f32[32,24,96]{2,1,0:T(8,128)S(1)} %collective-permute-done.7.refs_3_), channel_id=1, source_target_pairs={{0,64},{64,0},{128,192},{192,128},{1,65},{65,1},{129,193},{193,129... | collective-permute-start | bytes 884744 | tf_op jit(solution)/shard_map/ppermute | solution.py:56
  80.4 11.9 %collective-permute-start.12 = (bf16[16,5376]{1,0:T(8,128)(2,1)S(1)}, bf16[16,5376]{1,0:T(8,128)(2,1)S(1)}, u32[]{:S(2)}, u32[]{:S(2)}) collective-permute-start(bf16[16,5376]{1,0:T(8,128)(2,1)S(1)} %bitcast.119), channel_id=1, source_target_pairs={{0,128},{64,192},{128,0},{192,64},{1,129},{65,193},{129,1},{193,65... | collective-permute-start | bytes 516104 | tf_op jit(solution)/shard_map/ppermute | solution.py:40
  84.6 0.8 copy-start.6
  84.7 0.9 copy-start.7
  90.2 4.0 %copy-start.3 = (f32[32,24,128]{2,1,0:T(8,128)}, f32[32,24,128]{2,1,0:T(8,128)S(1)}, u32[]{:S(2)}) copy-start(f32[32,24,128]{2,1,0:T(8,128)S(1)} %collective-permute-done.10.refs_1_) | copy-start | bytes 1179652
  90.2 7.3 %collective-permute-start.11 = (f32[32,24,128]{2,1,0:T(8,128)S(1)}, f32[32,24,128]{2,1,0:T(8,128)S(1)}, u32[]{:S(2)}, u32[]{:S(2)}) collective-permute-start(f32[32,24,128]{2,1,0:T(8,128)S(1)} %collective-permute-done.10.refs_1_), channel_id=1, source_target_pairs={{0,64},{64,0},{128,192},{192,128},{1,65},{65,1},{129,193},{193,129... | collective-permute-start | bytes 1179656 | tf_op jit(solution)/shard_map/ppermute | solution.py:168
  92.3 1.8 %collective-permute-start.13 = (bf16[2,16,5376]{2,1,0:T(8,128)(2,1)S(1)}, bf16[2,16,5376]{2,1,0:T(8,128)(2,1)S(1)}, u32[]{:S(2)}, u32[]{:S(2)}) collective-permute-start(bf16[2,16,5376]{2,1,0:T(8,128)(2,1)S(1)} %maximum_select_fusion.4), channel_id=1, source_target_pairs={{0,64},{64,0},{128,192},{192,128},{1,65},{65,1},{129,193},{193,129... | collective-permute-start | bytes 1032200 | tf_op jit(solution)/shard_map/ppermute | solution.py:44
  97.5 0.8 copy-start.4

commit v16 on v14

--- a/solution.py
+++ b/solution.py
@@ -172,11 +172,12 @@
     expert_weights, expert_velocity = fused_update(
         pieces_e, 0, expert_master, expert_moment, scale
     )
+
+    back, early_t = lax.optimization_barrier((back, early_t))
+    back = lax.dynamic_slice_in_dim(back, t * per_half, per_half, 0)
     table_weights, table_velocity = fused_update(
         (cross_t, sib_cross_t), 2, table_master, table_moment, scale, early_t
     )
-
-    back = lax.dynamic_slice_in_dim(back, t * per_half, per_half, 0)
     allq = rep_gather(back)
     ce = allq[:, :, : width * rows].reshape(groups, per_half, width, rows)
     expert_copies = jnp.transpose(ce, (0, 2, 1, 3)).reshape(mats, width, per_half * rows)

time: 101 us -> 103 us (1.020)
  waiting for transfers between devices: 34.4 us -> 36.8 us
    ppermute x1, waiting for transfers between devices: 0.01 us -> 3.54 us  [rep_gather(): cross = lax.ppermute(x, 'rep', pairs(n, 2))]
    ppermute x1, starting transfers between devices: 2.13 us -> 0.1 us  [gather_pieces(): sib = lax.ppermute(x, 'rep', pairs(n, 1))]
    ppermute x1, starting transfers between devices: 0.11 us -> 2.13 us  [local(): sib_t = lax.ppermute(gt, 'rep', pairs(n_rep, 1))]
    ppermute x1, starting transfers between devices: 2.07 us -> 0.65 us  [local(): sib_cross_t = lax.ppermute(cross_t, 'rep', pairs(n_rep, 1))]
    ppermute x1, waiting for transfers between devices: 1.15 us -> 0.01 us  [local(): sib_cross_t = lax.ppermute(cross_t, 'rep', pairs(n_rep, 1))]
    ppermute x1, starting transfers between devices: 0.11 us -> 1.19 us  [rep_gather(): sib = lax.ppermute(pair, 'rep', pairs(n, 1))]
    unnamed x29 -> x31, local copies, waits for them, and re-layouts: 4.07 us -> 4.83 us
  transfers between devices with their start and end apart: 16 -> 16, of which waited for: 8 -> 8; matrix products, arithmetic and copies ran while one was open for 8% -> 7% of each run, Pallas kernels for 10% -> 10%
where the time goes in v16:
time: 103 us
  waiting for transfers between devices  36.8 us (36%)
  starting transfers between devices  34.1 us (33%)
  local copies, waits for them, and re-layouts  18.5 us (18%)
  Pallas kernels  9.95 us (10%)
  other arithmetic  2.21 us (2%)
  between operations  1.21 us (1%)
    all_to_all x1, waiting for transfers between devices, local(): lax.all_to_all(jnp.concatenate([he, ht], 1), 'shard', 0, 0, tiled=True)  15.6 us
    all_to_all x1, starting transfers between devices, local(): lax.all_to_all(jnp.concatenate([he, ht], 1), 'shard', 0, 0, tiled=True)  12.7 us
    pallas_call x3, Pallas kernels, fused_update(): pl.pallas_call(lambda *refs: update_kernel(scale, count, *refs), grid_spe...  9.95 us
    all_to_all x1, starting transfers between devices, local(): back = lax.all_to_all(back, 'shard', 0, 0, tiled=True)  6.45 us
    ppermute x1, waiting for transfers between devices, gather_pieces(): cross = lax.ppermute(x, 'rep', pairs(n, 2))  6.22 us
    ppermute x2, waiting for transfers between devices, rep_scatter(): got = lax.ppermute(pick(a, 1 - x_lo, 0), 'rep', pairs(n, 2))  5.74 us
    unnamed x31, local copies, waits for them, and re-layouts  4.83 us
    ppermute x2, waiting for transfers between devices, local(): other = lax.ppermute(q, 'tp', pairs(tensor, 1))  4.69 us
  transfers between devices with their start and end apart: 16, of which 8 were waited for; matrix products, arithmetic and copies ran while one was open for 7% of the time, Pallas kernels for 10%

profile of v16, /device:TPU:1, one launch (start us, length us, event | category | flops | bytes accessed | tf_op | source)
XLA Modules:
  0.0 102.8 jit_solution(14902333544747883879)
XLA Ops:
  0.7 1.6 %reshape_reshape_squeeze.3 = f32[2,2,36864]{2,1,0:T(2,128)S(1)} reshape(f32[1,4,24,1536]{3,2,1,0:T(8,128)} %param.6) | data formatting | bytes 1179648 | tf_op jit(solution)/shard_map/reshape;reshape;squeeze | solution.py:26
  2.3 0.5 constant_dynamic-slice_fusion.12
  3.1 3.3 %collective-permute-start = (f32[2,36864]{1,0:T(2,128)S(1)}, f32[2,36864]{1,0:T(2,128)S(1)}, u32[]{:S(2)}, u32[]{:S(2)}) collective-permute-start(f32[2,36864]{1,0:T(2,128)S(1)} %bitcast.132), channel_id=1, source_target_pairs={{0,64},{64,0},{128,192},{192,128},{1,65},{65,1},{129,193},{193,129... | collective-permute-start | bytes 884744 | tf_op jit(solution)/shard_map/ppermute | solution.py:30
  6.4 0.5 reshape_squeeze.3
  7.0 0.5 reshape_reshape.2
  7.5 0.7 constant_dynamic-slice_fusion.8
  8.2 0.3 copy.77
  8.6 0.3 bitcast_add_fusion.4
  8.9 0.3 constant_dynamic-slice_fusion.9
  9.3 1.0 collective-permute-done.3
  10.3 0.4 bitcast_add_fusion
  10.7 0.3 constant_dynamic-slice_fusion.5
  11.0 0.5 collective-permute-start.4
  11.6 2.6 %collective-permute-done.1 = f32[36864]{0:T(1024)S(1)} collective-permute-done((f32[36864]{0:T(1024)S(1)}, f32[36864]{0:T(1024)S(1)}, u32[]{:S(2)}, u32[]{:S(2)}) %collective-permute-start.1) | collective-permute-done | bytes 147488 | tf_op jit(solution)/shard_map/ppermute | solution.py:32
  14.3 1.1 %collective-permute-start.2 = (f32[36864]{0:T(1024)S(1)}, f32[36864]{0:T(1024)S(1)}, u32[]{:S(2)}, u32[]{:S(2)}) collective-permute-start(f32[36864]{0:T(1024)S(1)} %add.70), channel_id=1, source_target_pairs={{0,1},{1,0},{2,3},{3,2},{4,5},{5,4},{6,7},{7,6},{8,9},{9,8},{10,11... | collective-permute-start | bytes 442376 | tf_op jit(solution)/shard_map/ppermute | solution.py:132
  15.4 3.1 %collective-permute-done.4 = f32[49152]{0:T(1024)S(1)} collective-permute-done((f32[49152]{0:T(1024)S(1)}, f32[49152]{0:T(1024)S(1)}, u32[]{:S(2)}, u32[]{:S(2)}) %collective-permute-start.4) | collective-permute-done | bytes 196640 | tf_op jit(solution)/shard_map/ppermute | solution.py:32
  18.5 1.1 %collective-permute-start.5 = (f32[49152]{0:T(1024)S(1)}, f32[49152]{0:T(1024)S(1)}, u32[]{:S(2)}, u32[]{:S(2)}) collective-permute-start(f32[49152]{0:T(1024)S(1)} %add.72), channel_id=1, source_target_pairs={{0,1},{1,0},{2,3},{3,2},{4,5},{5,4},{6,7},{7,6},{8,9},{9,8},{10,11... | collective-permute-start | bytes 589832 | tf_op jit(solution)/shard_map/ppermute | solution.py:132
  19.7 1.8 %collective-permute-done.2 = f32[36864]{0:T(1024)S(1)} collective-permute-done((f32[36864]{0:T(1024)S(1)}, f32[36864]{0:T(1024)S(1)}, u32[]{:S(2)}, u32[]{:S(2)}) %collective-permute-start.2) | collective-permute-done | bytes 147488 | tf_op jit(solution)/shard_map/ppermute | solution.py:132
  21.9 2.9 %collective-permute-done.5 = f32[49152]{0:T(1024)S(1)} collective-permute-done((f32[49152]{0:T(1024)S(1)}, f32[49152]{0:T(1024)S(1)}, u32[]{:S(2)}, u32[]{:S(2)}) %collective-permute-start.5) | collective-permute-done | bytes 196640 | tf_op jit(solution)/shard_map/ppermute | solution.py:132
  25.1 1.6 %copy.43 = f32[32,1,5376]{2,1,0:T(1,128)} copy(f32[32,1,5376]{2,0,1:T(8,128)S(1)} %maximum_bitcast_fusion) | data formatting | bytes 1376256 | tf_op jit(solution)/shard_map/all_to_all | solution.py:140
  26.6 12.7 %all-to-all-start = ((f32[32,1,5376]{2,1,0:T(1,128)}), f32[32,1,5376]{2,1,0:T(1,128)S(1)}, u32[]{:S(2)}, u32[]{:S(2)}) async-start(f32[32,1,5376]{2,1,0:T(1,128)} %copy.43), calls=%async_computation | async-start | bytes 1376256 | tf_op jit(solution)/shard_map/all_to_all | solution.py:140
  39.3 1.1 %constant_dynamic-slice_fusion.3 = (f32[1,96,768]{2,1,0:T(8,128)S(1)}, f32[1,96,768]{2,1,0:T(8,128)S(1)}) fusion(f32[4,96,768]{2,1,0:T(8,128)} %refs_6_.1, s32[]{:T(128)S(6)} %select_n.107, f32[4,96,768]{2,1,0:T(8,128)} %refs_5_.1), kind=kLoop, calls=%fused_computation.37 | loop fusion | bytes 1179652 | tf_op jit(solution)/shard_map/jit(dynamic_index_in_dim)/dynamic_slice | solution.py:149
  40.8 1.2 %constant_dynamic-slice_fusion.1 = (f32[128,768]{1,0:T(8,128)S(1)}, f32[128,768]{1,0:T(8,128)S(1)}) fusion(f32[512,768]{1,0:T(8,128)} %refs_4_.3, s32[]{:T(128)S(6)} %select_n.108, f32[512,768]{1,0:T(8,128)} %refs_3_.3), kind=kLoop, calls=%fused_computation.35 | loop fusion | bytes 1572868 | tf_op jit(solution)/shard_map/dynamic_slice | solution.py:156
  42.3 15.6 %all-to-all-done = f32[32,1,5376]{2,1,0:T(1,128)S(1)} async-done(((f32[32,1,5376]{2,1,0:T(1,128)}), f32[32,1,5376]{2,1,0:T(1,128)S(1)}, u32[]{:S(2)}, u32[]{:S(2)}) %all-to-all-start) | async-done | bytes 688160 | tf_op jit(solution)/shard_map/all_to_all | solution.py:140
  58.1 0.3 div.34
  58.8 0.5 broadcast.40
  59.4 0.8 reduce
  60.2 0.8 reshape.158
  61.0 6.5 %all-to-all-start.1 = ((bf16[32,2,2688]{2,1,0:T(2,128)(2,1)}), bf16[32,2,2688]{2,1,0:T(2,128)(2,1)S(1)}, u32[]{:S(2)}, u32[]{:S(2)}) async-start(bf16[32,2,2688]{2,1,0:T(2,128)(2,1)} %reshape.158), calls=%async_computation.1 | async-start | bytes 688128 | tf_op jit(solution)/shard_map/all_to_all | solution.py:161
  67.5 0.3 reshape.148.refs_1_
  68.0 2.1 %collective-permute-start.9 = (f32[32,24,128]{2,1,0:T(8,128)S(1)}, f32[32,24,128]{2,1,0:T(8,128)S(1)}, u32[]{:S(2)}, u32[]{:S(2)}) collective-permute-start(f32[32,24,128]{2,1,0:T(8,128)S(1)} %bitcast.114), channel_id=1, source_target_pairs={{0,64},{64,0},{128,192},{192,128},{1,65},{65,1},{129,193},{193,129... | collective-permute-start | bytes 1179656 | tf_op jit(solution)/shard_map/ppermute | solution.py:165
  70.2 6.2 %collective-permute-done.7.refs_3_ = f32[32,24,96]{2,1,0:T(8,128)S(1)} collective-permute-done((f32[32,24,96]{2,1,0:T(8,128)S(1)}, f32[32,24,96]{2,1,0:T(8,128)S(1)}, u32[]{:S(2)}, u32[]{:S(2)}) %collective-permute-start.7) | collective-permute-done | bytes 294944 | tf_op jit(solution)/shard_map/ppermute | solution.py:55
  76.4 3.0 %collective-permute-start.8 = (f32[32,24,96]{2,1,0:T(8,128)S(1)}, f32[32,24,96]{2,1,0:T(8,128)S(1)}, u32[]{:S(2)}, u32[]{:S(2)}) collective-permute-start(f32[32,24,96]{2,1,0:T(8,128)S(1)} %collective-permute-done.7.refs_3_), channel_id=1, source_target_pairs={{0,64},{64,0},{128,192},{192,128},{1,65},{65,1},{129,193},{193,129... | collective-permute-start | bytes 884744 | tf_op jit(solution)/shard_map/ppermute | solution.py:56
  79.4 0.7 copy-done.8
  80.2 2.7 %shard_map.109 = (f32[512,768]{1,0:T(8,128)}, f32[512,768]{1,0:T(8,128)}) custom-call(s32[1]{0:T(128)} %bitcast.refs_0_, f32[32,24,128]{2,1,0:T(8,128)} %bitcast.116, f32[32,24,128]{2,1,0:T(8,128)} %copy-done.8, f32[512,768]{1,0:T(8,128)} %refs_3_.3, f32[512,768]{1,0:T(8,128)} %refs_4_.3), custom_call_target="tpu_custom_call" | custom-call | tf_op jit(solution)/shard_map/pallas_call | solution.py:99
  82.9 0.7 copy-done.6
  83.7 4.6 %shard_map.110 = (f32[4,96,768]{2,1,0:T(8,128)}, f32[4,96,768]{2,1,0:T(8,128)}) custom-call(s32[1]{0:T(128)} %bitcast.refs_0_, f32[32,24,96]{2,1,0:T(8,128)} %copy-done.1, f32[32,24,96]{2,1,0:T(8,128)} %copy-done.6, f32[32,24,96]{2,1,0:T(8,128)} %copy-done.5, f32[32,24,96]{2,1,0:T(8,128)} %copy-done.7, f32[4,96,768]{2,1,0:T(8,128)} %refs_5_.1, ...), custom_call_target="tpu_custom_call" | custom-call | tf_op jit(solution)/shard_map/pallas_call | solution.py:99
  88.4 0.3 reshape.159
  88.8 1.5 %collective-permute-start.10 = (bf16[16,5376]{1,0:T(8,128)(2,1)S(1)}, bf16[16,5376]{1,0:T(8,128)(2,1)S(1)}, u32[]{:S(2)}, u32[]{:S(2)}) collective-permute-start(bf16[16,5376]{1,0:T(8,128)(2,1)S(1)} %constant_dynamic-slice_fusion), channel_id=1, source_target_pairs={{0,128},{64,192},{128,0},{192,64},{1,129},{65,193},{129,1},{193,65... | collective-permute-start | bytes 516104 | tf_op jit(solution)/shard_map/ppermute | solution.py:40
  90.4 0.7 collective-permute-start.13
  91.0 3.5 %collective-permute-done.10 = bf16[16,5376]{1,0:T(8,128)(2,1)S(1)} collective-permute-done((bf16[16,5376]{1,0:T(8,128)(2,1)S(1)}, bf16[16,5376]{1,0:T(8,128)(2,1)S(1)}, u32[]{:S(2)}, u32[]{:S(2)}) %collective-permute-start.10) | collective-permute-done | bytes 172064 | tf_op jit(solution)/shard_map/ppermute | solution.py:40
  94.6 1.2 %collective-permute-start.11 = (bf16[2,16,5376]{2,1,0:T(8,128)(2,1)S(1)}, bf16[2,16,5376]{2,1,0:T(8,128)(2,1)S(1)}, u32[]{:S(2)}, u32[]{:S(2)}) collective-permute-start(bf16[2,16,5376]{2,1,0:T(8,128)(2,1)S(1)} %maximum_select_fusion.4), channel_id=1, source_target_pairs={{0,64},{64,0},{128,192},{192,128},{1,65},{65,1},{129,193},{193,129... | collective-permute-start | bytes 1032200 | tf_op jit(solution)/shard_map/ppermute | solution.py:44
  95.8 0.7 copy-done.4
  96.6 2.7 %shard_map.111 = (f32[512,768]{1,0:T(8,128)}, f32[512,768]{1,0:T(8,128)}) custom-call(s32[1]{0:T(128)} %bitcast.refs_0_, f32[32,24,128]{2,1,0:T(8,128)} %copy-done.3, f32[32,24,128]{2,1,0:T(8,128)} %copy-done.4, f32[512,768]{1,0:T(8,128)} %refs_3_.3, f32[512,768]{1,0:T(8,128)} %refs_4_.3, ...), custom_call_target="tpu_custom_call", output_to_operand_aliasing={{0}: (5, {}), {1}: (6, {})} | custom-call | tf_op jit(solution)/shard_map/pallas_call | solution.py:99
  99.6 0.3 copy.51
  99.9 1.0 %reshape.157 = bf16[24,8192]{1,0:T(8,128)(2,1)} reshape(bf16[24,16,4,128]{3,2,1,0:T(4,128)(2,1)S(1)} %copy.51) | data formatting | bytes 786432 | tf_op jit(solution)/shard_map/reshape | solution.py:185
  101.0 0.6 reshape.154
  101.6 1.1 %reshape.155 = bf16[4,24,1536]{2,1,0:T(8,128)(2,1)} reshape(bf16[4,24,16,96]{3,2,1,0:T(8,128)(2,1)S(1)} %copy.50) | data formatting | bytes 589824 | tf_op jit(solution)/shard_map/reshape | solution.py:183
  (68 shorter events, 3.6 us)
Async XLA Ops:
  0.6 5.8 %copy-start.2 = (f32[1,24,8192]{2,1,0:T(8,128)S(1)}, f32[1,24,8192]{2,1,0:T(8,128)}, u32[]{:S(2)}) copy-start(f32[1,24,8192]{2,1,0:T(8,128)} %param.7) | copy-start | bytes 2359300
  3.1 5.5 %collective-permute-start = (f32[2,36864]{1,0:T(2,128)S(1)}, f32[2,36864]{1,0:T(2,128)S(1)}, u32[]{:S(2)}, u32[]{:S(2)}) collective-permute-start(f32[2,36864]{1,0:T(2,128)S(1)} %bitcast.132), channel_id=1, source_target_pairs={{0,64},{64,0},{128,192},{192,128},{1,65},{65,1},{129,193},{193,129... | collective-permute-start | bytes 884744 | tf_op jit(solution)/shard_map/ppermute | solution.py:30
  8.5 1.8 %collective-permute-start.3 = (f32[2,49152]{1,0:T(2,128)S(1)}, f32[2,49152]{1,0:T(2,128)S(1)}, u32[]{:S(2)}, u32[]{:S(2)}) collective-permute-start(f32[2,49152]{1,0:T(2,128)S(1)} %bitcast.130), channel_id=1, source_target_pairs={{0,64},{64,0},{128,192},{192,128},{1,65},{65,1},{129,193},{193,129... | collective-permute-start | bytes 1179656 | tf_op jit(solution)/shard_map/ppermute | solution.py:30
  9.2 5.0 %collective-permute-start.1 = (f32[36864]{0:T(1024)S(1)}, f32[36864]{0:T(1024)S(1)}, u32[]{:S(2)}, u32[]{:S(2)}) collective-permute-start(f32[36864]{0:T(1024)S(1)} %bitcast.135), channel_id=1, source_target_pairs={{0,128},{64,192},{128,0},{192,64},{1,129},{65,193},{129,1},{193,65... | collective-permute-start | bytes 442376 | tf_op jit(solution)/shard_map/ppermute | solution.py:32
  11.0 7.4 %collective-permute-start.4 = (f32[49152]{0:T(1024)S(1)}, f32[49152]{0:T(1024)S(1)}, u32[]{:S(2)}, u32[]{:S(2)}) collective-permute-start(f32[49152]{0:T(1024)S(1)} %bitcast.134), channel_id=1, source_target_pairs={{0,128},{64,192},{128,0},{192,64},{1,129},{65,193},{129,1},{193,65... | collective-permute-start | bytes 589832 | tf_op jit(solution)/shard_map/ppermute | solution.py:32
  14.3 7.2 %collective-permute-start.2 = (f32[36864]{0:T(1024)S(1)}, f32[36864]{0:T(1024)S(1)}, u32[]{:S(2)}, u32[]{:S(2)}) collective-permute-start(f32[36864]{0:T(1024)S(1)} %add.70), channel_id=1, source_target_pairs={{0,1},{1,0},{2,3},{3,2},{4,5},{5,4},{6,7},{7,6},{8,9},{9,8},{10,11... | collective-permute-start | bytes 442376 | tf_op jit(solution)/shard_map/ppermute | solution.py:132
  18.5 6.3 %collective-permute-start.5 = (f32[49152]{0:T(1024)S(1)}, f32[49152]{0:T(1024)S(1)}, u32[]{:S(2)}, u32[]{:S(2)}) collective-permute-start(f32[49152]{0:T(1024)S(1)} %add.72), channel_id=1, source_target_pairs={{0,1},{1,0},{2,3},{3,2},{4,5},{5,4},{6,7},{7,6},{8,9},{9,8},{10,11... | collective-permute-start | bytes 589832 | tf_op jit(solution)/shard_map/ppermute | solution.py:132
  26.6 31.3 %all-to-all-start = ((f32[32,1,5376]{2,1,0:T(1,128)}), f32[32,1,5376]{2,1,0:T(1,128)S(1)}, u32[]{:S(2)}, u32[]{:S(2)}) async-start(f32[32,1,5376]{2,1,0:T(1,128)} %copy.43), calls=%async_computation | async-start | bytes 1376256 | tf_op jit(solution)/shard_map/all_to_all | solution.py:140
  61.0 27.3 %all-to-all-start.1 = ((bf16[32,2,2688]{2,1,0:T(2,128)(2,1)}), bf16[32,2,2688]{2,1,0:T(2,128)(2,1)S(1)}, u32[]{:S(2)}, u32[]{:S(2)}) async-start(bf16[32,2,2688]{2,1,0:T(2,128)(2,1)} %reshape.158), calls=%async_computation.1 | async-start | bytes 688128 | tf_op jit(solution)/shard_map/all_to_all | solution.py:161
  67.8 15.1 %copy-start.1 = (f32[32,24,96]{2,1,0:T(8,128)}, f32[32,24,96]{2,1,0:T(8,128)S(1)}, u32[]{:S(2)}) copy-start(f32[32,24,96]{2,1,0:T(8,128)S(1)} %reshape.148.refs_1_) | copy-start | bytes 884740
  67.8 8.6 %collective-permute-start.7 = (f32[32,24,96]{2,1,0:T(8,128)S(1)}, f32[32,24,96]{2,1,0:T(8,128)S(1)}, u32[]{:S(2)}, u32[]{:S(2)}) collective-permute-start(f32[32,24,96]{2,1,0:T(8,128)S(1)} %reshape.148.refs_1_), channel_id=1, source_target_pairs={{0,128},{64,192},{128,0},{192,64},{1,129},{65,193},{129,1},{193,65... | collective-permute-start | bytes 884744 | tf_op jit(solution)/shard_map/ppermute | solution.py:55
  68.0 11.5 %copy-start = (f32[4,8,24,128]{3,2,1,0:T(8,128)}, f32[4,8,24,128]{3,2,1,0:T(8,128)S(1)}, u32[]{:S(2)}) copy-start(f32[4,8,24,128]{3,2,1,0:T(8,128)S(1)} %copy.62) | copy-start | bytes 1179652
  68.0 11.4 %collective-permute-start.9 = (f32[32,24,128]{2,1,0:T(8,128)S(1)}, f32[32,24,128]{2,1,0:T(8,128)S(1)}, u32[]{:S(2)}, u32[]{:S(2)}) collective-permute-start(f32[32,24,128]{2,1,0:T(8,128)S(1)} %bitcast.114), channel_id=1, source_target_pairs={{0,64},{64,0},{128,192},{192,128},{1,65},{65,1},{129,193},{193,129... | collective-permute-start | bytes 1179656 | tf_op jit(solution)/shard_map/ppermute | solution.py:165
  70.1 12.7 %collective-permute-start.6 = (f32[32,24,96]{2,1,0:T(8,128)S(1)}, f32[32,24,96]{2,1,0:T(8,128)S(1)}, u32[]{:S(2)}, u32[]{:S(2)}) collective-permute-start(f32[32,24,96]{2,1,0:T(8,128)S(1)} %reshape.148.refs_1_), channel_id=1, source_target_pairs={{0,64},{64,0},{128,192},{192,128},{1,65},{65,1},{129,193},{193,129... | collective-permute-start | bytes 884744 | tf_op jit(solution)/shard_map/ppermute | solution.py:54
  76.4 6.4 %copy-start.5 = (f32[32,24,96]{2,1,0:T(8,128)}, f32[32,24,96]{2,1,0:T(8,128)S(1)}, u32[]{:S(2)}) copy-start(f32[32,24,96]{2,1,0:T(8,128)S(1)} %collective-permute-done.7.refs_3_) | copy-start | bytes 884740
  76.4 6.4 %collective-permute-start.8 = (f32[32,24,96]{2,1,0:T(8,128)S(1)}, f32[32,24,96]{2,1,0:T(8,128)S(1)}, u32[]{:S(2)}, u32[]{:S(2)}) collective-permute-start(f32[32,24,96]{2,1,0:T(8,128)S(1)} %collective-permute-done.7.refs_3_), channel_id=1, source_target_pairs={{0,64},{64,0},{128,192},{192,128},{1,65},{65,1},{129,193},{193,129... | collective-permute-start | bytes 884744 | tf_op jit(solution)/shard_map/ppermute | solution.py:56
  79.4 10.9 %collective-permute-start.12 = (f32[32,24,128]{2,1,0:T(8,128)S(1)}, f32[32,24,128]{2,1,0:T(8,128)S(1)}, u32[]{:S(2)}, u32[]{:S(2)}) collective-permute-start(f32[32,24,128]{2,1,0:T(8,128)S(1)} %bitcast.115), channel_id=1, source_target_pairs={{0,128},{64,192},{128,0},{192,64},{1,129},{65,193},{129,1},{193,65... | collective-permute-start | bytes 1179656 | tf_op jit(solution)/shard_map/ppermute | solution.py:167
  79.4 0.7 copy-start.8
  82.8 0.7 copy-start.6
  82.9 0.9 copy-start.7
  88.8 5.8 %collective-permute-start.10 = (bf16[16,5376]{1,0:T(8,128)(2,1)S(1)}, bf16[16,5376]{1,0:T(8,128)(2,1)S(1)}, u32[]{:S(2)}, u32[]{:S(2)}) collective-permute-start(bf16[16,5376]{1,0:T(8,128)(2,1)S(1)} %constant_dynamic-slice_fusion), channel_id=1, source_target_pairs={{0,128},{64,192},{128,0},{192,64},{1,129},{65,193},{129,1},{193,65... | collective-permute-start | bytes 516104 | tf_op jit(solution)/shard_map/ppermute | solution.py:40
  90.3 5.5 %copy-start.3 = (f32[32,24,128]{2,1,0:T(8,128)}, f32[32,24,128]{2,1,0:T(8,128)S(1)}, u32[]{:S(2)}) copy-start(f32[32,24,128]{2,1,0:T(8,128)S(1)} %collective-permute-done.12.refs_1_) | copy-start | bytes 1179652
  90.4 5.5 %collective-permute-start.13 = (f32[32,24,128]{2,1,0:T(8,128)S(1)}, f32[32,24,128]{2,1,0:T(8,128)S(1)}, u32[]{:S(2)}, u32[]{:S(2)}) collective-permute-start(f32[32,24,128]{2,1,0:T(8,128)S(1)} %collective-permute-done.12.refs_1_), channel_id=1, source_target_pairs={{0,64},{64,0},{128,192},{192,128},{1,65},{65,1},{129,193},{193,129... | collective-permute-start | bytes 1179656 | tf_op jit(solution)/shard_map/ppermute | solution.py:168
  94.6 4.7 %collective-permute-start.11 = (bf16[2,16,5376]{2,1,0:T(8,128)(2,1)S(1)}, bf16[2,16,5376]{2,1,0:T(8,128)(2,1)S(1)}, u32[]{:S(2)}, u32[]{:S(2)}) collective-permute-start(bf16[2,16,5376]{2,1,0:T(8,128)(2,1)S(1)} %maximum_select_fusion.4), channel_id=1, source_target_pairs={{0,64},{64,0},{128,192},{192,128},{1,65},{65,1},{129,193},{193,129... | collective-permute-start | bytes 1032200 | tf_op jit(solution)/shard_map/ppermute | solution.py:44
  95.8 0.7 copy-start.4

commit v17 on v14

--- a/solution.py
+++ b/solution.py
@@ -172,8 +172,9 @@
     expert_weights, expert_velocity = fused_update(
         pieces_e, 0, expert_master, expert_moment, scale
     )
+    mid_t = fused_update((cross_t,), 2, table_master, table_moment, scale, early_t)
     table_weights, table_velocity = fused_update(
-        (cross_t, sib_cross_t), 2, table_master, table_moment, scale, early_t
+        (sib_cross_t,), 3, table_master, table_moment, scale, mid_t
     )
 
     back = lax.dynamic_slice_in_dim(back, t * per_half, per_half, 0)

time: 101 us -> 102 us (level)
  Pallas kernels: 9.98 us -> 11.8 us
  waiting for transfers between devices: 34.4 us -> 33.3 us
    pallas_call x3 -> x4, Pallas kernels: 9.98 us -> 11.8 us  [fused_update(): pl.pallas_call(lambda *refs: update_kernel(scale, count, *refs), grid_spe...]
    ppermute x1, waiting for transfers between devices: 1.15 us -> 0.01 us  [local(): sib_cross_t = lax.ppermute(cross_t, 'rep', pairs(n_rep, 1))]
  transfers between devices with their start and end apart: 16 -> 16, of which waited for: 8 -> 7; matrix products, arithmetic and copies ran while one was open for 8% -> 8% of each run, Pallas kernels for 10% -> 12%
where the time goes in v17:
time: 102 us
  starting transfers between devices  34.7 us (34%)
  waiting for transfers between devices  33.3 us (33%)
  local copies, waits for them, and re-layouts  18.7 us (18%)
  Pallas kernels  11.8 us (12%)
  other arithmetic  2.17 us (2%)
  between operations  1.16 us (1%)
    all_to_all x1, waiting for transfers between devices, local(): lax.all_to_all(jnp.concatenate([he, ht], 1), 'shard', 0, 0, tiled=True)  15.6 us
    all_to_all x1, starting transfers between devices, local(): lax.all_to_all(jnp.concatenate([he, ht], 1), 'shard', 0, 0, tiled=True)  12.7 us
    pallas_call x4, Pallas kernels, fused_update(): pl.pallas_call(lambda *refs: update_kernel(scale, count, *refs), grid_spe...  11.8 us
    all_to_all x1, starting transfers between devices, local(): back = lax.all_to_all(back, 'shard', 0, 0, tiled=True)  6.45 us
    ppermute x1, waiting for transfers between devices, gather_pieces(): cross = lax.ppermute(x, 'rep', pairs(n, 2))  6.22 us
    ppermute x2, waiting for transfers between devices, rep_scatter(): got = lax.ppermute(pick(a, 1 - x_lo, 0), 'rep', pairs(n, 2))  5.74 us
    unnamed x29, local copies, waits for them, and re-layouts  4.8 us
    ppermute x2, waiting for transfers between devices, local(): other = lax.ppermute(q, 'tp', pairs(tensor, 1))  4.69 us
  transfers between devices with their start and end apart: 16, of which 7 were waited for; matrix products, arithmetic and copies ran while one was open for 8% of the time, Pallas kernels for 12%

profile of v17, /device:TPU:1, one launch (start us, length us, event | category | flops | bytes accessed | tf_op | source)
XLA Modules:
  0.0 101.9 jit_solution(1172121418570339455)
XLA Ops:
  0.7 1.6 %reshape_reshape_squeeze.3 = f32[2,2,36864]{2,1,0:T(2,128)S(1)} reshape(f32[1,4,24,1536]{3,2,1,0:T(8,128)} %param.6) | data formatting | bytes 1179648 | tf_op jit(solution)/shard_map/reshape;reshape;squeeze | solution.py:26
  2.3 0.5 constant_dynamic-slice_fusion.12
  3.1 3.3 %collective-permute-start = (f32[2,36864]{1,0:T(2,128)S(1)}, f32[2,36864]{1,0:T(2,128)S(1)}, u32[]{:S(2)}, u32[]{:S(2)}) collective-permute-start(f32[2,36864]{1,0:T(2,128)S(1)} %bitcast.132), channel_id=1, source_target_pairs={{0,64},{64,0},{128,192},{192,128},{1,65},{65,1},{129,193},{193,129... | collective-permute-start | bytes 884744 | tf_op jit(solution)/shard_map/ppermute | solution.py:30
  6.4 0.5 reshape_squeeze.3
  7.0 0.5 reshape_reshape.2
  7.5 0.7 constant_dynamic-slice_fusion.8
  8.2 0.3 copy.80
  8.6 0.3 bitcast_add_fusion.4
  9.3 1.0 collective-permute-done.3
  10.3 0.4 bitcast_add_fusion
  10.7 0.3 constant_dynamic-slice_fusion.5
  11.0 0.5 collective-permute-start.4
  11.6 2.6 %collective-permute-done.1 = f32[36864]{0:T(1024)S(1)} collective-permute-done((f32[36864]{0:T(1024)S(1)}, f32[36864]{0:T(1024)S(1)}, u32[]{:S(2)}, u32[]{:S(2)}) %collective-permute-start.1) | collective-permute-done | bytes 147488 | tf_op jit(solution)/shard_map/ppermute | solution.py:32
  14.3 1.1 %collective-permute-start.2 = (f32[36864]{0:T(1024)S(1)}, f32[36864]{0:T(1024)S(1)}, u32[]{:S(2)}, u32[]{:S(2)}) collective-permute-start(f32[36864]{0:T(1024)S(1)} %add.70), channel_id=1, source_target_pairs={{0,1},{1,0},{2,3},{3,2},{4,5},{5,4},{6,7},{7,6},{8,9},{9,8},{10,11... | collective-permute-start | bytes 442376 | tf_op jit(solution)/shard_map/ppermute | solution.py:132
  15.4 3.1 %collective-permute-done.4 = f32[49152]{0:T(1024)S(1)} collective-permute-done((f32[49152]{0:T(1024)S(1)}, f32[49152]{0:T(1024)S(1)}, u32[]{:S(2)}, u32[]{:S(2)}) %collective-permute-start.4) | collective-permute-done | bytes 196640 | tf_op jit(solution)/shard_map/ppermute | solution.py:32
  18.5 1.1 %collective-permute-start.5 = (f32[49152]{0:T(1024)S(1)}, f32[49152]{0:T(1024)S(1)}, u32[]{:S(2)}, u32[]{:S(2)}) collective-permute-start(f32[49152]{0:T(1024)S(1)} %add.72), channel_id=1, source_target_pairs={{0,1},{1,0},{2,3},{3,2},{4,5},{5,4},{6,7},{7,6},{8,9},{9,8},{10,11... | collective-permute-start | bytes 589832 | tf_op jit(solution)/shard_map/ppermute | solution.py:132
  19.7 1.8 %collective-permute-done.2 = f32[36864]{0:T(1024)S(1)} collective-permute-done((f32[36864]{0:T(1024)S(1)}, f32[36864]{0:T(1024)S(1)}, u32[]{:S(2)}, u32[]{:S(2)}) %collective-permute-start.2) | collective-permute-done | bytes 147488 | tf_op jit(solution)/shard_map/ppermute | solution.py:132
  21.9 2.9 %collective-permute-done.5 = f32[49152]{0:T(1024)S(1)} collective-permute-done((f32[49152]{0:T(1024)S(1)}, f32[49152]{0:T(1024)S(1)}, u32[]{:S(2)}, u32[]{:S(2)}) %collective-permute-start.5) | collective-permute-done | bytes 196640 | tf_op jit(solution)/shard_map/ppermute | solution.py:132
  25.1 1.6 %copy.44 = f32[32,1,5376]{2,1,0:T(1,128)} copy(f32[32,1,5376]{2,0,1:T(8,128)S(1)} %maximum_bitcast_fusion) | data formatting | bytes 1376256 | tf_op jit(solution)/shard_map/all_to_all | solution.py:140
  26.6 12.7 %all-to-all-start = ((f32[32,1,5376]{2,1,0:T(1,128)}), f32[32,1,5376]{2,1,0:T(1,128)S(1)}, u32[]{:S(2)}, u32[]{:S(2)}) async-start(f32[32,1,5376]{2,1,0:T(1,128)} %copy.44), calls=%async_computation | async-start | bytes 1376256 | tf_op jit(solution)/shard_map/all_to_all | solution.py:140
  39.4 1.2 %constant_dynamic-slice_fusion.1 = (f32[128,768]{1,0:T(8,128)S(1)}, f32[128,768]{1,0:T(8,128)S(1)}) fusion(f32[512,768]{1,0:T(8,128)} %refs_3_.5, s32[]{:T(128)S(6)} %select_n.108, f32[512,768]{1,0:T(8,128)} %refs_2_.3), kind=kLoop, calls=%fused_computation.34 | loop fusion | bytes 1572868 | tf_op jit(solution)/shard_map/dynamic_slice | solution.py:156
  40.9 1.1 %constant_dynamic-slice_fusion.3 = (f32[1,96,768]{2,1,0:T(8,128)S(1)}, f32[1,96,768]{2,1,0:T(8,128)S(1)}) fusion(f32[4,96,768]{2,1,0:T(8,128)} %refs_6_.1, s32[]{:T(128)S(6)} %select_n.107, f32[4,96,768]{2,1,0:T(8,128)} %refs_5_.1), kind=kLoop, calls=%fused_computation.36 | loop fusion | bytes 1179652 | tf_op jit(solution)/shard_map/jit(dynamic_index_in_dim)/dynamic_slice | solution.py:149
  42.3 15.6 %all-to-all-done = f32[32,1,5376]{2,1,0:T(1,128)S(1)} async-done(((f32[32,1,5376]{2,1,0:T(1,128)}), f32[32,1,5376]{2,1,0:T(1,128)S(1)}, u32[]{:S(2)}, u32[]{:S(2)}) %all-to-all-start) | async-done | bytes 688160 | tf_op jit(solution)/shard_map/all_to_all | solution.py:140
  58.3 0.3 div.34
  58.9 0.5 broadcast.40
  59.4 0.8 reduce
  60.2 0.8 reshape.161
  61.0 6.5 %all-to-all-start.1 = ((bf16[32,2,2688]{2,1,0:T(2,128)(2,1)}), bf16[32,2,2688]{2,1,0:T(2,128)(2,1)S(1)}, u32[]{:S(2)}, u32[]{:S(2)}) async-start(bf16[32,2,2688]{2,1,0:T(2,128)(2,1)} %reshape.161), calls=%async_computation.1 | async-start | bytes 688128 | tf_op jit(solution)/shard_map/all_to_all | solution.py:161
  67.5 0.3 reshape.151.refs_1_
  67.9 2.1 %collective-permute-start.6 = (f32[32,24,96]{2,1,0:T(8,128)S(1)}, f32[32,24,96]{2,1,0:T(8,128)S(1)}, u32[]{:S(2)}, u32[]{:S(2)}) collective-permute-start(f32[32,24,96]{2,1,0:T(8,128)S(1)} %reshape.151.refs_1_), channel_id=1, source_target_pairs={{0,64},{64,0},{128,192},{192,128},{1,65},{65,1},{129,193},{193,129... | collective-permute-start | bytes 884744 | tf_op jit(solution)/shard_map/ppermute | solution.py:54
  70.2 6.2 %collective-permute-done.7.refs_3_ = f32[32,24,96]{2,1,0:T(8,128)S(1)} collective-permute-done((f32[32,24,96]{2,1,0:T(8,128)S(1)}, f32[32,24,96]{2,1,0:T(8,128)S(1)}, u32[]{:S(2)}, u32[]{:S(2)}) %collective-permute-start.7) | collective-permute-done | bytes 294944 | tf_op jit(solution)/shard_map/ppermute | solution.py:55
  76.4 0.3 collective-permute-start.12
  76.7 3.0 %collective-permute-start.8 = (f32[32,24,96]{2,1,0:T(8,128)S(1)}, f32[32,24,96]{2,1,0:T(8,128)S(1)}, u32[]{:S(2)}, u32[]{:S(2)}) collective-permute-start(f32[32,24,96]{2,1,0:T(8,128)S(1)} %collective-permute-done.7.refs_3_), channel_id=1, source_target_pairs={{0,64},{64,0},{128,192},{192,128},{1,65},{65,1},{129,193},{193,129... | collective-permute-start | bytes 884744 | tf_op jit(solution)/shard_map/ppermute | solution.py:56
  79.7 0.3 reshape.162
  80.0 0.4 constant_dynamic-slice_fusion
  80.4 1.5 %collective-permute-start.10 = (bf16[16,5376]{1,0:T(8,128)(2,1)S(1)}, bf16[16,5376]{1,0:T(8,128)(2,1)S(1)}, u32[]{:S(2)}, u32[]{:S(2)}) collective-permute-start(bf16[16,5376]{1,0:T(8,128)(2,1)S(1)} %bitcast.119), channel_id=1, source_target_pairs={{0,128},{64,192},{128,0},{192,64},{1,129},{65,193},{129,1},{193,65... | collective-permute-start | bytes 516104 | tf_op jit(solution)/shard_map/ppermute | solution.py:40
  81.9 0.7 copy-done.6
  82.7 2.7 %shard_map.109 = (f32[512,768]{1,0:T(8,128)}, f32[512,768]{1,0:T(8,128)}) custom-call(s32[1]{0:T(128)} %bitcast.refs_0_, f32[32,24,128]{2,1,0:T(8,128)} %bitcast.113, f32[32,24,128]{2,1,0:T(8,128)} %copy-done.6, f32[512,768]{1,0:T(8,128)} %refs_2_.3, f32[512,768]{1,0:T(8,128)} %refs_3_.5), custom_call_target="tpu_custom_call" | custom-call | tf_op jit(solution)/shard_map/pallas_call | solution.py:99
  85.4 0.7 copy-done.4
  86.3 4.6 %shard_map.110 = (f32[4,96,768]{2,1,0:T(8,128)}, f32[4,96,768]{2,1,0:T(8,128)}) custom-call(s32[1]{0:T(128)} %bitcast.refs_0_, f32[32,24,96]{2,1,0:T(8,128)} %copy-done, f32[32,24,96]{2,1,0:T(8,128)} %copy-done.4, f32[32,24,96]{2,1,0:T(8,128)} %copy-done.3, f32[32,24,96]{2,1,0:T(8,128)} %copy-done.5, f32[4,96,768]{2,1,0:T(8,128)} %refs_5_.1, ...), custom_call_target="tpu_custom_call" | custom-call | tf_op jit(solution)/shard_map/pallas_call | solution.py:99
  90.9 2.1 %collective-permute-start.13 = (f32[32,24,128]{2,1,0:T(8,128)}, f32[32,24,128]{2,1,0:T(8,128)S(1)}, u32[]{:S(2)}, u32[]{:S(2)}) collective-permute-start(f32[32,24,128]{2,1,0:T(8,128)} %collective-permute-done.12.refs_1_), channel_id=1, source_target_pairs={{0,64},{64,0},{128,192},{192,128},{1,65},{65,1},{129,193},{193,129... | collective-permute-start | bytes 1179656 | tf_op jit(solution)/shard_map/ppermute | solution.py:168
  92.9 2.3 %shard_map.111 = (f32[512,768]{1,0:T(8,128)}, f32[512,768]{1,0:T(8,128)}) custom-call(s32[1]{0:T(128)} %bitcast.refs_0_, f32[32,24,128]{2,1,0:T(8,128)} %collective-permute-done.12.refs_1_, f32[512,768]{1,0:T(8,128)} %refs_2_.3, f32[512,768]{1,0:T(8,128)} %refs_3_.5, ...), custom_call_target="tpu_custom_call", output_to_operand_aliasing={{0}: (4, {}), {1}: (5, {})} | custom-call | tf_op jit(solution)/shard_map/pallas_call | solution.py:99
  95.4 0.7 copy-done.7
  96.2 2.3 %shard_map.112 = (f32[512,768]{1,0:T(8,128)}, f32[512,768]{1,0:T(8,128)}) custom-call(s32[1]{0:T(128)} %bitcast.refs_0_, f32[32,24,128]{2,1,0:T(8,128)} %copy-done.7, f32[512,768]{1,0:T(8,128)} %refs_2_.3, f32[512,768]{1,0:T(8,128)} %refs_3_.5, f32[512,768]{1,0:T(8,128)} %get-tuple-element.32.refs_4_, ...), custom_call_target="tpu_custom_call", output_to_operand_aliasing={{0}: (4, {}), {1}: (5, {})} | custom-call | tf_op jit(solution)/shard_map/pallas_call | solution.py:99
  98.7 0.3 copy.52
  99.0 1.0 %reshape.160 = bf16[24,8192]{1,0:T(8,128)(2,1)} reshape(bf16[24,16,4,128]{3,2,1,0:T(4,128)(2,1)S(1)} %copy.52) | data formatting | bytes 786432 | tf_op jit(solution)/shard_map/reshape | solution.py:185
  100.1 0.6 reshape.157
  100.7 1.1 %reshape.158 = bf16[4,24,1536]{2,1,0:T(8,128)(2,1)} reshape(bf16[4,24,16,96]{3,2,1,0:T(8,128)(2,1)S(1)} %copy.51) | data formatting | bytes 589824 | tf_op jit(solution)/shard_map/reshape | solution.py:183
  (64 shorter events, 3.8 us)
Async XLA Ops:
  0.6 5.8 %copy-start.2 = (f32[1,24,8192]{2,1,0:T(8,128)S(1)}, f32[1,24,8192]{2,1,0:T(8,128)}, u32[]{:S(2)}) copy-start(f32[1,24,8192]{2,1,0:T(8,128)} %param.7) | copy-start | bytes 2359300
  3.1 5.5 %collective-permute-start = (f32[2,36864]{1,0:T(2,128)S(1)}, f32[2,36864]{1,0:T(2,128)S(1)}, u32[]{:S(2)}, u32[]{:S(2)}) collective-permute-start(f32[2,36864]{1,0:T(2,128)S(1)} %bitcast.132), channel_id=1, source_target_pairs={{0,64},{64,0},{128,192},{192,128},{1,65},{65,1},{129,193},{193,129... | collective-permute-start | bytes 884744 | tf_op jit(solution)/shard_map/ppermute | solution.py:30
  8.5 1.8 %collective-permute-start.3 = (f32[2,49152]{1,0:T(2,128)S(1)}, f32[2,49152]{1,0:T(2,128)S(1)}, u32[]{:S(2)}, u32[]{:S(2)}) collective-permute-start(f32[2,49152]{1,0:T(2,128)S(1)} %bitcast.130), channel_id=1, source_target_pairs={{0,64},{64,0},{128,192},{192,128},{1,65},{65,1},{129,193},{193,129... | collective-permute-start | bytes 1179656 | tf_op jit(solution)/shard_map/ppermute | solution.py:30
  9.2 5.0 %collective-permute-start.1 = (f32[36864]{0:T(1024)S(1)}, f32[36864]{0:T(1024)S(1)}, u32[]{:S(2)}, u32[]{:S(2)}) collective-permute-start(f32[36864]{0:T(1024)S(1)} %bitcast.135), channel_id=1, source_target_pairs={{0,128},{64,192},{128,0},{192,64},{1,129},{65,193},{129,1},{193,65... | collective-permute-start | bytes 442376 | tf_op jit(solution)/shard_map/ppermute | solution.py:32
  11.0 7.4 %collective-permute-start.4 = (f32[49152]{0:T(1024)S(1)}, f32[49152]{0:T(1024)S(1)}, u32[]{:S(2)}, u32[]{:S(2)}) collective-permute-start(f32[49152]{0:T(1024)S(1)} %bitcast.134), channel_id=1, source_target_pairs={{0,128},{64,192},{128,0},{192,64},{1,129},{65,193},{129,1},{193,65... | collective-permute-start | bytes 589832 | tf_op jit(solution)/shard_map/ppermute | solution.py:32
  14.3 7.2 %collective-permute-start.2 = (f32[36864]{0:T(1024)S(1)}, f32[36864]{0:T(1024)S(1)}, u32[]{:S(2)}, u32[]{:S(2)}) collective-permute-start(f32[36864]{0:T(1024)S(1)} %add.70), channel_id=1, source_target_pairs={{0,1},{1,0},{2,3},{3,2},{4,5},{5,4},{6,7},{7,6},{8,9},{9,8},{10,11... | collective-permute-start | bytes 442376 | tf_op jit(solution)/shard_map/ppermute | solution.py:132
  18.5 6.3 %collective-permute-start.5 = (f32[49152]{0:T(1024)S(1)}, f32[49152]{0:T(1024)S(1)}, u32[]{:S(2)}, u32[]{:S(2)}) collective-permute-start(f32[49152]{0:T(1024)S(1)} %add.72), channel_id=1, source_target_pairs={{0,1},{1,0},{2,3},{3,2},{4,5},{5,4},{6,7},{7,6},{8,9},{9,8},{10,11... | collective-permute-start | bytes 589832 | tf_op jit(solution)/shard_map/ppermute | solution.py:132
  26.6 31.3 %all-to-all-start = ((f32[32,1,5376]{2,1,0:T(1,128)}), f32[32,1,5376]{2,1,0:T(1,128)S(1)}, u32[]{:S(2)}, u32[]{:S(2)}) async-start(f32[32,1,5376]{2,1,0:T(1,128)} %copy.44), calls=%async_computation | async-start | bytes 1376256 | tf_op jit(solution)/shard_map/all_to_all | solution.py:140
  61.0 18.7 %all-to-all-start.1 = ((bf16[32,2,2688]{2,1,0:T(2,128)(2,1)}), bf16[32,2,2688]{2,1,0:T(2,128)(2,1)S(1)}, u32[]{:S(2)}, u32[]{:S(2)}) async-start(bf16[32,2,2688]{2,1,0:T(2,128)(2,1)} %reshape.161), calls=%async_computation.1 | async-start | bytes 688128 | tf_op jit(solution)/shard_map/all_to_all | solution.py:161
  67.8 17.6 %copy-start = (f32[32,24,96]{2,1,0:T(8,128)}, f32[32,24,96]{2,1,0:T(8,128)S(1)}, u32[]{:S(2)}) copy-start(f32[32,24,96]{2,1,0:T(8,128)S(1)} %reshape.151.refs_1_) | copy-start | bytes 884740
  67.8 8.6 %collective-permute-start.7 = (f32[32,24,96]{2,1,0:T(8,128)S(1)}, f32[32,24,96]{2,1,0:T(8,128)S(1)}, u32[]{:S(2)}, u32[]{:S(2)}) collective-permute-start(f32[32,24,96]{2,1,0:T(8,128)S(1)} %reshape.151.refs_1_), channel_id=1, source_target_pairs={{0,128},{64,192},{128,0},{192,64},{1,129},{65,193},{129,1},{193,65... | collective-permute-start | bytes 884744 | tf_op jit(solution)/shard_map/ppermute | solution.py:55
  67.9 17.5 %collective-permute-start.6 = (f32[32,24,96]{2,1,0:T(8,128)S(1)}, f32[32,24,96]{2,1,0:T(8,128)S(1)}, u32[]{:S(2)}, u32[]{:S(2)}) collective-permute-start(f32[32,24,96]{2,1,0:T(8,128)S(1)} %reshape.151.refs_1_), channel_id=1, source_target_pairs={{0,64},{64,0},{128,192},{192,128},{1,65},{65,1},{129,193},{193,129... | collective-permute-start | bytes 884744 | tf_op jit(solution)/shard_map/ppermute | solution.py:54
  70.1 11.8 %copy-start.1 = (f32[4,8,24,128]{3,2,1,0:T(8,128)}, f32[4,8,24,128]{3,2,1,0:T(8,128)S(1)}, u32[]{:S(2)}) copy-start(f32[4,8,24,128]{3,2,1,0:T(8,128)S(1)} %copy.63) | copy-start | bytes 1179652
  70.1 11.8 %collective-permute-start.9 = (f32[32,24,128]{2,1,0:T(8,128)S(1)}, f32[32,24,128]{2,1,0:T(8,128)S(1)}, u32[]{:S(2)}, u32[]{:S(2)}) collective-permute-start(f32[32,24,128]{2,1,0:T(8,128)S(1)} %bitcast.111), channel_id=1, source_target_pairs={{0,64},{64,0},{128,192},{192,128},{1,65},{65,1},{129,193},{193,129... | collective-permute-start | bytes 1179656 | tf_op jit(solution)/shard_map/ppermute | solution.py:165
  76.4 8.9 %copy-start.3 = (f32[32,24,96]{2,1,0:T(8,128)}, f32[32,24,96]{2,1,0:T(8,128)S(1)}, u32[]{:S(2)}) copy-start(f32[32,24,96]{2,1,0:T(8,128)S(1)} %collective-permute-done.7.refs_3_) | copy-start | bytes 884740
  76.4 14.5 %collective-permute-start.12 = (f32[32,24,128]{2,1,0:T(8,128)S(1)}, f32[32,24,128]{2,1,0:T(8,128)}, u32[]{:S(2)}, u32[]{:S(2)}) collective-permute-start(f32[32,24,128]{2,1,0:T(8,128)S(1)} %bitcast.112), channel_id=1, source_target_pairs={{0,128},{64,192},{128,0},{192,64},{1,129},{65,193},{129,1},{193,65... | collective-permute-start | bytes 1179656 | tf_op jit(solution)/shard_map/ppermute | solution.py:167
  76.7 8.7 %collective-permute-start.8 = (f32[32,24,96]{2,1,0:T(8,128)S(1)}, f32[32,24,96]{2,1,0:T(8,128)S(1)}, u32[]{:S(2)}, u32[]{:S(2)}) collective-permute-start(f32[32,24,96]{2,1,0:T(8,128)S(1)} %collective-permute-done.7.refs_3_), channel_id=1, source_target_pairs={{0,64},{64,0},{128,192},{192,128},{1,65},{65,1},{129,193},{193,129... | collective-permute-start | bytes 884744 | tf_op jit(solution)/shard_map/ppermute | solution.py:56
  80.4 14.8 %collective-permute-start.10 = (bf16[16,5376]{1,0:T(8,128)(2,1)S(1)}, bf16[16,5376]{1,0:T(8,128)(2,1)S(1)}, u32[]{:S(2)}, u32[]{:S(2)}) collective-permute-start(bf16[16,5376]{1,0:T(8,128)(2,1)S(1)} %bitcast.119), channel_id=1, source_target_pairs={{0,128},{64,192},{128,0},{192,64},{1,129},{65,193},{129,1},{193,65... | collective-permute-start | bytes 516104 | tf_op jit(solution)/shard_map/ppermute | solution.py:40
  81.9 0.7 copy-start.6
  85.4 0.8 copy-start.4
  85.4 0.9 copy-start.5
  90.9 4.5 %collective-permute-start.13 = (f32[32,24,128]{2,1,0:T(8,128)}, f32[32,24,128]{2,1,0:T(8,128)S(1)}, u32[]{:S(2)}, u32[]{:S(2)}) collective-permute-start(f32[32,24,128]{2,1,0:T(8,128)} %collective-permute-done.12.refs_1_), channel_id=1, source_target_pairs={{0,64},{64,0},{128,192},{192,128},{1,65},{65,1},{129,193},{193,129... | collective-permute-start | bytes 1179656 | tf_op jit(solution)/shard_map/ppermute | solution.py:168
  95.3 3.2 %collective-permute-start.11 = (bf16[2,16,5376]{2,1,0:T(8,128)(2,1)S(1)}, bf16[2,16,5376]{2,1,0:T(8,128)(2,1)S(1)}, u32[]{:S(2)}, u32[]{:S(2)}) collective-permute-start(bf16[2,16,5376]{2,1,0:T(8,128)(2,1)S(1)} %maximum_select_fusion.4), channel_id=1, source_target_pairs={{0,64},{64,0},{128,192},{192,128},{1,65},{65,1},{129,193},{193,129... | collective-permute-start | bytes 1032200 | tf_op jit(solution)/shard_map/ppermute | solution.py:44
  95.4 0.7 copy-start.7

commit v18 on v14

--- a/solution.py
+++ b/solution.py
@@ -158,7 +158,8 @@
     )
     lt = jnp.transpose(own_t.astype(jnp.bfloat16).reshape(sub, shards, width), (1, 2, 0))
     back = jnp.concatenate([le.reshape(shards, -1), lt.reshape(shards, -1)], 1)
-    back = lax.all_to_all(back, "shard", 0, 0, tiled=True)
+    back = lax.all_to_all(back.reshape(shards, 2, -1), "shard", 0, 0, tiled=True)
+    back = back.reshape(shards, -1)
 
     pieces_e = gather_pieces(ge)
     n_rep = lax.axis_size("rep")

time: 101 us -> 101 us (level)
  waiting for transfers between devices: 34.4 us -> 36.7 us
    ppermute x1, waiting for transfers between devices: 0.01 us -> 3.31 us  [rep_gather(): cross = lax.ppermute(x, 'rep', pairs(n, 2))]
    ppermute x1, starting transfers between devices: 2.13 us -> 0.1 us  [gather_pieces(): sib = lax.ppermute(x, 'rep', pairs(n, 1))]
    ppermute x1, starting transfers between devices: 0.11 us -> 2.13 us  [local(): sib_t = lax.ppermute(gt, 'rep', pairs(n_rep, 1))]
    ppermute x1, starting transfers between devices: 2.07 us -> 0.78 us  [local(): sib_cross_t = lax.ppermute(cross_t, 'rep', pairs(n_rep, 1))]
    ppermute x1, waiting for transfers between devices: 1.15 us -> 0.01 us  [local(): sib_cross_t = lax.ppermute(cross_t, 'rep', pairs(n_rep, 1))]
    ppermute x1, starting transfers between devices: 0.11 us -> 1.19 us  [rep_gather(): sib = lax.ppermute(pair, 'rep', pairs(n, 1))]
  transfers between devices with their start and end apart: 16 -> 16, of which waited for: 8 -> 9; matrix products, arithmetic and copies ran while one was open for 8% -> 7% of each run, Pallas kernels for 10% -> 10%
where the time goes in v18:
time: 101 us
  waiting for transfers between devices  36.7 us (36%)
  starting transfers between devices  34.1 us (34%)
  local copies, waits for them, and re-layouts  17.6 us (17%)
  Pallas kernels  9.95 us (10%)
  other arithmetic  1.33 us (1%)
  between operations  1.17 us (1%)
    all_to_all x1, waiting for transfers between devices, local(): lax.all_to_all(jnp.concatenate([he, ht], 1), 'shard', 0, 0, tiled=True)  15.6 us
    all_to_all x1, starting transfers between devices, local(): lax.all_to_all(jnp.concatenate([he, ht], 1), 'shard', 0, 0, tiled=True)  12.7 us
    pallas_call x3, Pallas kernels, fused_update(): pl.pallas_call(lambda *refs: update_kernel(scale, count, *refs), grid_spe...  9.95 us
    all_to_all x1, starting transfers between devices, local(): lax.all_to_all(back.reshape(shards, 2, -1), 'shard', 0, 0, tiled=True)  6.27 us
    ppermute x1, waiting for transfers between devices, gather_pieces(): cross = lax.ppermute(x, 'rep', pairs(n, 2))  6.22 us
    ppermute x2, waiting for transfers between devices, rep_scatter(): got = lax.ppermute(pick(a, 1 - x_lo, 0), 'rep', pairs(n, 2))  5.74 us
    ppermute x2, waiting for transfers between devices, local(): other = lax.ppermute(q, 'tp', pairs(tensor, 1))  4.69 us
    unnamed x29, local copies, waits for them, and re-layouts  3.72 us
  transfers between devices with their start and end apart: 16, of which 9 were waited for; matrix products, arithmetic and copies ran while one was open for 7% of the time, Pallas kernels for 10%

profile of v18, /device:TPU:1, one launch (start us, length us, event | category | flops | bytes accessed | tf_op | source)
XLA Modules:
  0.0 100.8 jit_solution(8859655306483435987)
XLA Ops:
  0.7 1.6 %reshape_reshape_squeeze.3 = f32[2,2,36864]{2,1,0:T(2,128)S(1)} reshape(f32[1,4,24,1536]{3,2,1,0:T(8,128)} %param.6) | data formatting | bytes 1179648 | tf_op jit(solution)/shard_map/reshape;reshape;squeeze | solution.py:26
  2.3 0.5 constant_dynamic-slice_fusion.12
  2.8 0.2 copy.63
  3.1 3.3 %collective-permute-start = (f32[2,36864]{1,0:T(2,128)S(1)}, f32[2,36864]{1,0:T(2,128)S(1)}, u32[]{:S(2)}, u32[]{:S(2)}) collective-permute-start(f32[2,36864]{1,0:T(2,128)S(1)} %bitcast.130), channel_id=1, source_target_pairs={{0,64},{64,0},{128,192},{192,128},{1,65},{65,1},{129,193},{193,129... | collective-permute-start | bytes 884744 | tf_op jit(solution)/shard_map/ppermute | solution.py:30
  6.4 0.5 reshape_squeeze.3
  7.0 0.5 reshape_reshape.2
  7.5 0.7 constant_dynamic-slice_fusion.8
  8.2 0.3 copy.62
  8.6 0.3 bitcast_add_fusion.4
  8.9 0.3 constant_dynamic-slice_fusion.9
  9.3 1.0 collective-permute-done.3
  10.3 0.4 bitcast_add_fusion
  10.7 0.3 constant_dynamic-slice_fusion.5
  11.0 0.5 collective-permute-start.4
  11.6 2.6 %collective-permute-done.1 = f32[36864]{0:T(1024)S(1)} collective-permute-done((f32[36864]{0:T(1024)S(1)}, f32[36864]{0:T(1024)S(1)}, u32[]{:S(2)}, u32[]{:S(2)}) %collective-permute-start.1) | collective-permute-done | bytes 147488 | tf_op jit(solution)/shard_map/ppermute | solution.py:32
  14.3 1.1 %collective-permute-start.2 = (f32[36864]{0:T(1024)S(1)}, f32[36864]{0:T(1024)S(1)}, u32[]{:S(2)}, u32[]{:S(2)}) collective-permute-start(f32[36864]{0:T(1024)S(1)} %add.70), channel_id=1, source_target_pairs={{0,1},{1,0},{2,3},{3,2},{4,5},{5,4},{6,7},{7,6},{8,9},{9,8},{10,11... | collective-permute-start | bytes 442376 | tf_op jit(solution)/shard_map/ppermute | solution.py:132
  15.4 3.1 %collective-permute-done.4 = f32[49152]{0:T(1024)S(1)} collective-permute-done((f32[49152]{0:T(1024)S(1)}, f32[49152]{0:T(1024)S(1)}, u32[]{:S(2)}, u32[]{:S(2)}) %collective-permute-start.4) | collective-permute-done | bytes 196640 | tf_op jit(solution)/shard_map/ppermute | solution.py:32
  18.5 1.1 %collective-permute-start.5 = (f32[49152]{0:T(1024)S(1)}, f32[49152]{0:T(1024)S(1)}, u32[]{:S(2)}, u32[]{:S(2)}) collective-permute-start(f32[49152]{0:T(1024)S(1)} %add.72), channel_id=1, source_target_pairs={{0,1},{1,0},{2,3},{3,2},{4,5},{5,4},{6,7},{7,6},{8,9},{9,8},{10,11... | collective-permute-start | bytes 589832 | tf_op jit(solution)/shard_map/ppermute | solution.py:132
  19.7 1.8 %collective-permute-done.2 = f32[36864]{0:T(1024)S(1)} collective-permute-done((f32[36864]{0:T(1024)S(1)}, f32[36864]{0:T(1024)S(1)}, u32[]{:S(2)}, u32[]{:S(2)}) %collective-permute-start.2) | collective-permute-done | bytes 147488 | tf_op jit(solution)/shard_map/ppermute | solution.py:132
  21.9 2.9 %collective-permute-done.5 = f32[49152]{0:T(1024)S(1)} collective-permute-done((f32[49152]{0:T(1024)S(1)}, f32[49152]{0:T(1024)S(1)}, u32[]{:S(2)}, u32[]{:S(2)}) %collective-permute-start.5) | collective-permute-done | bytes 196640 | tf_op jit(solution)/shard_map/ppermute | solution.py:132
  25.1 1.6 %copy.31 = f32[32,1,5376]{2,1,0:T(1,128)} copy(f32[32,1,5376]{2,0,1:T(8,128)S(1)} %maximum_bitcast_fusion) | data formatting | bytes 1376256 | tf_op jit(solution)/shard_map/all_to_all | solution.py:140
  26.6 12.7 %all-to-all-start = ((f32[32,1,5376]{2,1,0:T(1,128)}), f32[32,1,5376]{2,1,0:T(1,128)S(1)}, u32[]{:S(2)}, u32[]{:S(2)}) async-start(f32[32,1,5376]{2,1,0:T(1,128)} %copy.31), calls=%async_computation | async-start | bytes 1376256 | tf_op jit(solution)/shard_map/all_to_all | solution.py:140
  39.4 1.2 %constant_dynamic-slice_fusion.1 = (f32[128,768]{1,0:T(8,128)S(1)}, f32[128,768]{1,0:T(8,128)S(1)}) fusion(f32[512,768]{1,0:T(8,128)} %refs_4_.3, s32[]{:T(128)S(6)} %select_n.108, f32[512,768]{1,0:T(8,128)} %refs_3_.3), kind=kLoop, calls=%fused_computation.34 | loop fusion | bytes 1572868 | tf_op jit(solution)/shard_map/dynamic_slice | solution.py:156
  40.9 1.1 %constant_dynamic-slice_fusion.3 = (f32[1,96,768]{2,1,0:T(8,128)S(1)}, f32[1,96,768]{2,1,0:T(8,128)S(1)}) fusion(f32[4,96,768]{2,1,0:T(8,128)} %refs_6_.1, s32[]{:T(128)S(6)} %select_n.107, f32[4,96,768]{2,1,0:T(8,128)} %refs_5_.1), kind=kLoop, calls=%fused_computation.36 | loop fusion | bytes 1179652 | tf_op jit(solution)/shard_map/jit(dynamic_index_in_dim)/dynamic_slice | solution.py:149
  42.0 0.2 copy.32
  42.1 0.2 copy.43
  42.3 15.6 %all-to-all-done = f32[32,1,5376]{2,1,0:T(1,128)S(1)} async-done(((f32[32,1,5376]{2,1,0:T(1,128)}), f32[32,1,5376]{2,1,0:T(1,128)S(1)}, u32[]{:S(2)}, u32[]{:S(2)}) %all-to-all-start) | async-done | bytes 688160 | tf_op jit(solution)/shard_map/all_to_all | solution.py:140
  58.3 0.3 div.34
  58.8 0.8 reshape.158
  59.7 6.3 %all-to-all-start.1 = ((bf16[32,2,2688]{2,1,0:T(2,128)(2,1)}), bf16[32,2,2688]{2,1,0:T(2,128)(2,1)S(1)}, u32[]{:S(2)}, u32[]{:S(2)}) async-start(bf16[32,2,2688]{2,1,0:T(2,128)(2,1)} %reshape.158), calls=%async_computation.1 | async-start | bytes 688128 | tf_op jit(solution)/shard_map/all_to_all | solution.py:161
  65.9 0.3 reshape.152.refs_1_
  66.4 2.1 %collective-permute-start.9 = (f32[32,24,128]{2,1,0:T(8,128)S(1)}, f32[32,24,128]{2,1,0:T(8,128)S(1)}, u32[]{:S(2)}, u32[]{:S(2)}) collective-permute-start(f32[32,24,128]{2,1,0:T(8,128)S(1)} %bitcast.111), channel_id=1, source_target_pairs={{0,64},{64,0},{128,192},{192,128},{1,65},{65,1},{129,193},{193,129... | collective-permute-start | bytes 1179656 | tf_op jit(solution)/shard_map/ppermute | solution.py:166
  68.6 6.2 %collective-permute-done.7.refs_3_ = f32[32,24,96]{2,1,0:T(8,128)S(1)} collective-permute-done((f32[32,24,96]{2,1,0:T(8,128)S(1)}, f32[32,24,96]{2,1,0:T(8,128)S(1)}, u32[]{:S(2)}, u32[]{:S(2)}) %collective-permute-start.7) | collective-permute-done | bytes 294944 | tf_op jit(solution)/shard_map/ppermute | solution.py:55
  74.9 3.0 %collective-permute-start.8 = (f32[32,24,96]{2,1,0:T(8,128)S(1)}, f32[32,24,96]{2,1,0:T(8,128)S(1)}, u32[]{:S(2)}, u32[]{:S(2)}) collective-permute-start(f32[32,24,96]{2,1,0:T(8,128)S(1)} %collective-permute-done.7.refs_3_), channel_id=1, source_target_pairs={{0,64},{64,0},{128,192},{192,128},{1,65},{65,1},{129,193},{193,129... | collective-permute-start | bytes 884744 | tf_op jit(solution)/shard_map/ppermute | solution.py:56
  77.9 0.7 copy-done.8
  78.6 2.7 %shard_map.109 = (f32[512,768]{1,0:T(8,128)}, f32[512,768]{1,0:T(8,128)}) custom-call(s32[1]{0:T(128)} %bitcast.refs_0_, f32[32,24,128]{2,1,0:T(8,128)} %bitcast.113, f32[32,24,128]{2,1,0:T(8,128)} %copy-done.8, f32[512,768]{1,0:T(8,128)} %refs_3_.3, f32[512,768]{1,0:T(8,128)} %refs_4_.3), custom_call_target="tpu_custom_call" | custom-call | tf_op jit(solution)/shard_map/pallas_call | solution.py:99
  81.3 0.7 copy-done.6
  82.2 4.6 %shard_map.110 = (f32[4,96,768]{2,1,0:T(8,128)}, f32[4,96,768]{2,1,0:T(8,128)}) custom-call(s32[1]{0:T(128)} %bitcast.refs_0_, f32[32,24,96]{2,1,0:T(8,128)} %copy-done.1, f32[32,24,96]{2,1,0:T(8,128)} %copy-done.6, f32[32,24,96]{2,1,0:T(8,128)} %copy-done.5, f32[32,24,96]{2,1,0:T(8,128)} %copy-done.7, f32[4,96,768]{2,1,0:T(8,128)} %refs_5_.1, ...), custom_call_target="tpu_custom_call" | custom-call | tf_op jit(solution)/shard_map/pallas_call | solution.py:99
  86.9 1.5 %collective-permute-start.10 = (bf16[16,5376]{1,0:T(8,128)(2,1)S(1)}, bf16[16,5376]{1,0:T(8,128)(2,1)S(1)}, u32[]{:S(2)}, u32[]{:S(2)}) collective-permute-start(bf16[16,5376]{1,0:T(8,128)(2,1)S(1)} %constant_dynamic-slice_fusion), channel_id=1, source_target_pairs={{0,128},{64,192},{128,0},{192,64},{1,129},{65,193},{129,1},{193,65... | collective-permute-start | bytes 516104 | tf_op jit(solution)/shard_map/ppermute | solution.py:40
  88.6 0.8 collective-permute-start.13
  89.4 3.3 %collective-permute-done.10 = bf16[16,5376]{1,0:T(8,128)(2,1)S(1)} collective-permute-done((bf16[16,5376]{1,0:T(8,128)(2,1)S(1)}, bf16[16,5376]{1,0:T(8,128)(2,1)S(1)}, u32[]{:S(2)}, u32[]{:S(2)}) %collective-permute-start.10) | collective-permute-done | bytes 172064 | tf_op jit(solution)/shard_map/ppermute | solution.py:40
  92.7 1.2 %collective-permute-start.11 = (bf16[2,16,5376]{2,1,0:T(8,128)(2,1)S(1)}, bf16[2,16,5376]{2,1,0:T(8,128)(2,1)S(1)}, u32[]{:S(2)}, u32[]{:S(2)}) collective-permute-start(bf16[2,16,5376]{2,1,0:T(8,128)(2,1)S(1)} %maximum_select_fusion.4), channel_id=1, source_target_pairs={{0,64},{64,0},{128,192},{192,128},{1,65},{65,1},{129,193},{193,129... | collective-permute-start | bytes 1032200 | tf_op jit(solution)/shard_map/ppermute | solution.py:44
  94.0 0.7 copy-done.4
  94.7 2.7 %shard_map.111 = (f32[512,768]{1,0:T(8,128)}, f32[512,768]{1,0:T(8,128)}) custom-call(s32[1]{0:T(128)} %bitcast.refs_0_, f32[32,24,128]{2,1,0:T(8,128)} %copy-done.3, f32[32,24,128]{2,1,0:T(8,128)} %copy-done.4, f32[512,768]{1,0:T(8,128)} %refs_3_.3, f32[512,768]{1,0:T(8,128)} %refs_4_.3, ...), custom_call_target="tpu_custom_call", output_to_operand_aliasing={{0}: (5, {}), {1}: (6, {})} | custom-call | tf_op jit(solution)/shard_map/pallas_call | solution.py:99
  97.7 0.3 copy.37
  98.0 1.0 %reshape.163 = bf16[24,8192]{1,0:T(8,128)(2,1)} reshape(bf16[24,16,4,128]{3,2,1,0:T(4,128)(2,1)S(1)} %copy.37) | data formatting | bytes 786432 | tf_op jit(solution)/shard_map/reshape | solution.py:185
  99.0 0.6 reshape.160
  99.7 1.1 %reshape.161 = bf16[4,24,1536]{2,1,0:T(8,128)(2,1)} reshape(bf16[4,24,16,96]{3,2,1,0:T(8,128)(2,1)S(1)} %copy.36) | data formatting | bytes 589824 | tf_op jit(solution)/shard_map/reshape | solution.py:183
  (64 shorter events, 3.1 us)
Async XLA Ops:
  0.6 5.8 %copy-start.2 = (f32[1,24,8192]{2,1,0:T(8,128)S(1)}, f32[1,24,8192]{2,1,0:T(8,128)}, u32[]{:S(2)}) copy-start(f32[1,24,8192]{2,1,0:T(8,128)} %param.7) | copy-start | bytes 2359300
  3.1 5.5 %collective-permute-start = (f32[2,36864]{1,0:T(2,128)S(1)}, f32[2,36864]{1,0:T(2,128)S(1)}, u32[]{:S(2)}, u32[]{:S(2)}) collective-permute-start(f32[2,36864]{1,0:T(2,128)S(1)} %bitcast.130), channel_id=1, source_target_pairs={{0,64},{64,0},{128,192},{192,128},{1,65},{65,1},{129,193},{193,129... | collective-permute-start | bytes 884744 | tf_op jit(solution)/shard_map/ppermute | solution.py:30
  8.5 1.8 %collective-permute-start.3 = (f32[2,49152]{1,0:T(2,128)S(1)}, f32[2,49152]{1,0:T(2,128)S(1)}, u32[]{:S(2)}, u32[]{:S(2)}) collective-permute-start(f32[2,49152]{1,0:T(2,128)S(1)} %bitcast.128), channel_id=1, source_target_pairs={{0,64},{64,0},{128,192},{192,128},{1,65},{65,1},{129,193},{193,129... | collective-permute-start | bytes 1179656 | tf_op jit(solution)/shard_map/ppermute | solution.py:30
  9.2 5.0 %collective-permute-start.1 = (f32[36864]{0:T(1024)S(1)}, f32[36864]{0:T(1024)S(1)}, u32[]{:S(2)}, u32[]{:S(2)}) collective-permute-start(f32[36864]{0:T(1024)S(1)} %bitcast.133), channel_id=1, source_target_pairs={{0,128},{64,192},{128,0},{192,64},{1,129},{65,193},{129,1},{193,65... | collective-permute-start | bytes 442376 | tf_op jit(solution)/shard_map/ppermute | solution.py:32
  11.0 7.4 %collective-permute-start.4 = (f32[49152]{0:T(1024)S(1)}, f32[49152]{0:T(1024)S(1)}, u32[]{:S(2)}, u32[]{:S(2)}) collective-permute-start(f32[49152]{0:T(1024)S(1)} %bitcast.132), channel_id=1, source_target_pairs={{0,128},{64,192},{128,0},{192,64},{1,129},{65,193},{129,1},{193,65... | collective-permute-start | bytes 589832 | tf_op jit(solution)/shard_map/ppermute | solution.py:32
  14.3 7.2 %collective-permute-start.2 = (f32[36864]{0:T(1024)S(1)}, f32[36864]{0:T(1024)S(1)}, u32[]{:S(2)}, u32[]{:S(2)}) collective-permute-start(f32[36864]{0:T(1024)S(1)} %add.70), channel_id=1, source_target_pairs={{0,1},{1,0},{2,3},{3,2},{4,5},{5,4},{6,7},{7,6},{8,9},{9,8},{10,11... | collective-permute-start | bytes 442376 | tf_op jit(solution)/shard_map/ppermute | solution.py:132
  18.5 6.3 %collective-permute-start.5 = (f32[49152]{0:T(1024)S(1)}, f32[49152]{0:T(1024)S(1)}, u32[]{:S(2)}, u32[]{:S(2)}) collective-permute-start(f32[49152]{0:T(1024)S(1)} %add.72), channel_id=1, source_target_pairs={{0,1},{1,0},{2,3},{3,2},{4,5},{5,4},{6,7},{7,6},{8,9},{9,8},{10,11... | collective-permute-start | bytes 589832 | tf_op jit(solution)/shard_map/ppermute | solution.py:132
  26.6 31.3 %all-to-all-start = ((f32[32,1,5376]{2,1,0:T(1,128)}), f32[32,1,5376]{2,1,0:T(1,128)S(1)}, u32[]{:S(2)}, u32[]{:S(2)}) async-start(f32[32,1,5376]{2,1,0:T(1,128)} %copy.31), calls=%async_computation | async-start | bytes 1376256 | tf_op jit(solution)/shard_map/all_to_all | solution.py:140
  59.7 27.1 %all-to-all-start.1 = ((bf16[32,2,2688]{2,1,0:T(2,128)(2,1)}), bf16[32,2,2688]{2,1,0:T(2,128)(2,1)S(1)}, u32[]{:S(2)}, u32[]{:S(2)}) async-start(bf16[32,2,2688]{2,1,0:T(2,128)(2,1)} %reshape.158), calls=%async_computation.1 | async-start | bytes 688128 | tf_op jit(solution)/shard_map/all_to_all | solution.py:161
  66.2 15.1 %copy-start.1 = (f32[32,24,96]{2,1,0:T(8,128)}, f32[32,24,96]{2,1,0:T(8,128)S(1)}, u32[]{:S(2)}) copy-start(f32[32,24,96]{2,1,0:T(8,128)S(1)} %reshape.152.refs_1_) | copy-start | bytes 884740
  66.2 8.6 %collective-permute-start.7 = (f32[32,24,96]{2,1,0:T(8,128)S(1)}, f32[32,24,96]{2,1,0:T(8,128)S(1)}, u32[]{:S(2)}, u32[]{:S(2)}) collective-permute-start(f32[32,24,96]{2,1,0:T(8,128)S(1)} %reshape.152.refs_1_), channel_id=1, source_target_pairs={{0,128},{64,192},{128,0},{192,64},{1,129},{65,193},{129,1},{193,65... | collective-permute-start | bytes 884744 | tf_op jit(solution)/shard_map/ppermute | solution.py:55
  66.4 11.5 %copy-start = (f32[4,8,24,128]{3,2,1,0:T(8,128)}, f32[4,8,24,128]{3,2,1,0:T(8,128)S(1)}, u32[]{:S(2)}) copy-start(f32[4,8,24,128]{3,2,1,0:T(8,128)S(1)} %copy.47) | copy-start | bytes 1179652
  66.4 11.4 %collective-permute-start.9 = (f32[32,24,128]{2,1,0:T(8,128)S(1)}, f32[32,24,128]{2,1,0:T(8,128)S(1)}, u32[]{:S(2)}, u32[]{:S(2)}) collective-permute-start(f32[32,24,128]{2,1,0:T(8,128)S(1)} %bitcast.111), channel_id=1, source_target_pairs={{0,64},{64,0},{128,192},{192,128},{1,65},{65,1},{129,193},{193,129... | collective-permute-start | bytes 1179656 | tf_op jit(solution)/shard_map/ppermute | solution.py:166
  68.5 12.7 %collective-permute-start.6 = (f32[32,24,96]{2,1,0:T(8,128)S(1)}, f32[32,24,96]{2,1,0:T(8,128)S(1)}, u32[]{:S(2)}, u32[]{:S(2)}) collective-permute-start(f32[32,24,96]{2,1,0:T(8,128)S(1)} %reshape.152.refs_1_), channel_id=1, source_target_pairs={{0,64},{64,0},{128,192},{192,128},{1,65},{65,1},{129,193},{193,129... | collective-permute-start | bytes 884744 | tf_op jit(solution)/shard_map/ppermute | solution.py:54
  74.9 6.4 %copy-start.5 = (f32[32,24,96]{2,1,0:T(8,128)}, f32[32,24,96]{2,1,0:T(8,128)S(1)}, u32[]{:S(2)}) copy-start(f32[32,24,96]{2,1,0:T(8,128)S(1)} %collective-permute-done.7.refs_3_) | copy-start | bytes 884740
  74.9 6.4 %collective-permute-start.8 = (f32[32,24,96]{2,1,0:T(8,128)S(1)}, f32[32,24,96]{2,1,0:T(8,128)S(1)}, u32[]{:S(2)}, u32[]{:S(2)}) collective-permute-start(f32[32,24,96]{2,1,0:T(8,128)S(1)} %collective-permute-done.7.refs_3_), channel_id=1, source_target_pairs={{0,64},{64,0},{128,192},{192,128},{1,65},{65,1},{129,193},{193,129... | collective-permute-start | bytes 884744 | tf_op jit(solution)/shard_map/ppermute | solution.py:56
  77.8 10.7 %collective-permute-start.12 = (f32[32,24,128]{2,1,0:T(8,128)S(1)}, f32[32,24,128]{2,1,0:T(8,128)S(1)}, u32[]{:S(2)}, u32[]{:S(2)}) collective-permute-start(f32[32,24,128]{2,1,0:T(8,128)S(1)} %bitcast.112), channel_id=1, source_target_pairs={{0,128},{64,192},{128,0},{192,64},{1,129},{65,193},{129,1},{193,65... | collective-permute-start | bytes 1179656 | tf_op jit(solution)/shard_map/ppermute | solution.py:168
  77.8 0.7 copy-start.8
  81.3 0.7 copy-start.6
  81.3 0.9 copy-start.7
  86.9 5.8 %collective-permute-start.10 = (bf16[16,5376]{1,0:T(8,128)(2,1)S(1)}, bf16[16,5376]{1,0:T(8,128)(2,1)S(1)}, u32[]{:S(2)}, u32[]{:S(2)}) collective-permute-start(bf16[16,5376]{1,0:T(8,128)(2,1)S(1)} %constant_dynamic-slice_fusion), channel_id=1, source_target_pairs={{0,128},{64,192},{128,0},{192,64},{1,129},{65,193},{129,1},{193,65... | collective-permute-start | bytes 516104 | tf_op jit(solution)/shard_map/ppermute | solution.py:40
  88.6 5.4 %copy-start.3 = (f32[32,24,128]{2,1,0:T(8,128)}, f32[32,24,128]{2,1,0:T(8,128)S(1)}, u32[]{:S(2)}) copy-start(f32[32,24,128]{2,1,0:T(8,128)S(1)} %collective-permute-done.12.refs_1_) | copy-start | bytes 1179652
  88.6 5.4 %collective-permute-start.13 = (f32[32,24,128]{2,1,0:T(8,128)S(1)}, f32[32,24,128]{2,1,0:T(8,128)S(1)}, u32[]{:S(2)}, u32[]{:S(2)}) collective-permute-start(f32[32,24,128]{2,1,0:T(8,128)S(1)} %collective-permute-done.12.refs_1_), channel_id=1, source_target_pairs={{0,64},{64,0},{128,192},{192,128},{1,65},{65,1},{129,193},{193,129... | collective-permute-start | bytes 1179656 | tf_op jit(solution)/shard_map/ppermute | solution.py:169
  92.7 4.7 %collective-permute-start.11 = (bf16[2,16,5376]{2,1,0:T(8,128)(2,1)S(1)}, bf16[2,16,5376]{2,1,0:T(8,128)(2,1)S(1)}, u32[]{:S(2)}, u32[]{:S(2)}) collective-permute-start(bf16[2,16,5376]{2,1,0:T(8,128)(2,1)S(1)} %maximum_select_fusion.4), channel_id=1, source_target_pairs={{0,64},{64,0},{128,192},{192,128},{1,65},{65,1},{129,193},{193,129... | collective-permute-start | bytes 1032200 | tf_op jit(solution)/shard_map/ppermute | solution.py:44
  94.0 0.7 copy-start.4

commit v19 on v18

--- a/solution.py
+++ b/solution.py
@@ -178,7 +178,15 @@
     )
 
     back = lax.dynamic_slice_in_dim(back, t * per_half, per_half, 0)
-    allq = rep_gather(back)
+    bp = gather_pieces(back)
+
+    def quarter(q):
+        pick = lambda p: (r ^ q) == p
+        return jnp.where(
+            pick(0), bp[0], jnp.where(pick(1), bp[1], jnp.where(pick(2), bp[2], bp[3]))
+        )
+
+    allq = jnp.stack([quarter(q) for q in range(groups)])
     ce = allq[:, :, : width * rows].reshape(groups, per_half, width, rows)
     expert_copies = jnp.transpose(ce, (0, 2, 1, 3)).reshape(mats, width, per_half * rows)
     ct = allq[:, :, width * rows :].reshape(groups, per_half, width, sub)

time: 101 us -> 106 us (1.050)
  starting transfers between devices: 34.1 us -> 36.8 us
  waiting for transfers between devices: 36.7 us -> 39.3 us
    ppermute x1 -> x2, starting transfers between devices: 0.1 us -> 4.86 us  [gather_pieces(): sib = lax.ppermute(x, 'rep', pairs(n, 1))]
    ppermute x1 -> x2, waiting for transfers between devices: 6.22 us -> 10.2 us  [gather_pieces(): cross = lax.ppermute(x, 'rep', pairs(n, 2))]
    ppermute x2 -> x0, waiting for transfers between devices: 3.31 us -> none  [the longest x1 3.31 us: rep_gather(): cross = lax.ppermute(x, 'rep', pairs(n, 2))]
    ppermute x2 -> x0, starting transfers between devices: 2.74 us -> none  [the longest x1 1.55 us: rep_gather(): cross = lax.ppermute(x, 'rep', pairs(n, 2))]
    all_to_all x1, waiting for transfers between devices: 0.01 us -> 2 us  [local(): lax.all_to_all(back.reshape(shards, 2, -1), 'shard', 0, 0, tiled=True)]
    ppermute x1 -> x2, starting transfers between devices: 2.97 us -> 3.99 us  [gather_pieces(): sib_cross = lax.ppermute(cross, 'rep', pairs(n, 1))]
    unnamed x29 -> x27, local copies, waits for them, and re-layouts: 3.72 us -> 3.16 us
  transfers between devices with their start and end apart: 16 -> 17, of which waited for: 9 -> 9; matrix products, arithmetic and copies ran while one was open for 7% -> 10% of each run, Pallas kernels for 10% -> 7%
where the time goes in v19:
time: 106 us
  waiting for transfers between devices  39.3 us (37%)
  starting transfers between devices  36.8 us (35%)
  local copies, waits for them, and re-layouts  17 us (16%)
  Pallas kernels  9.98 us (9%)
  other arithmetic  1.43 us (1%)
  between operations  1.14 us (1%)
    all_to_all x1, waiting for transfers between devices, local(): lax.all_to_all(jnp.concatenate([he, ht], 1), 'shard', 0, 0, tiled=True)  15.6 us
    all_to_all x1, starting transfers between devices, local(): lax.all_to_all(jnp.concatenate([he, ht], 1), 'shard', 0, 0, tiled=True)  12.7 us
    ppermute x2, waiting for transfers between devices, gather_pieces(): cross = lax.ppermute(x, 'rep', pairs(n, 2))  10.2 us
    pallas_call x3, Pallas kernels, fused_update(): pl.pallas_call(lambda *refs: update_kernel(scale, count, *refs), grid_spe...  9.98 us
    all_to_all x1, starting transfers between devices, local(): lax.all_to_all(back.reshape(shards, 2, -1), 'shard', 0, 0, tiled=True)  6.27 us
    ppermute x2, waiting for transfers between devices, rep_scatter(): got = lax.ppermute(pick(a, 1 - x_lo, 0), 'rep', pairs(n, 2))  5.74 us
    ppermute x2, starting transfers between devices, gather_pieces(): sib = lax.ppermute(x, 'rep', pairs(n, 1))  4.86 us
    ppermute x2, waiting for transfers between devices, local(): other = lax.ppermute(q, 'tp', pairs(tensor, 1))  4.69 us
  transfers between devices with their start and end apart: 17, of which 9 were waited for; matrix products, arithmetic and copies ran while one was open for 10% of the time, Pallas kernels for 7%

profile of v19, /device:TPU:1, one launch (start us, length us, event | category | flops | bytes accessed | tf_op | source)
XLA Modules:
  0.0 105.6 jit_solution(4965827281696255221)
XLA Ops:
  0.7 1.6 %reshape_reshape_squeeze.3 = f32[2,2,36864]{2,1,0:T(2,128)S(1)} reshape(f32[1,4,24,1536]{3,2,1,0:T(8,128)} %param.6) | data formatting | bytes 1179648 | tf_op jit(solution)/shard_map/reshape;reshape;squeeze | solution.py:26
  2.3 0.5 constant_dynamic-slice_fusion.12
  2.8 0.2 copy.63
  3.1 3.3 %collective-permute-start = (f32[2,36864]{1,0:T(2,128)S(1)}, f32[2,36864]{1,0:T(2,128)S(1)}, u32[]{:S(2)}, u32[]{:S(2)}) collective-permute-start(f32[2,36864]{1,0:T(2,128)S(1)} %bitcast.124), channel_id=1, source_target_pairs={{0,64},{64,0},{128,192},{192,128},{1,65},{65,1},{129,193},{193,129... | collective-permute-start | bytes 884744 | tf_op jit(solution)/shard_map/ppermute | solution.py:30
  6.4 0.5 reshape_squeeze.3
  7.0 0.5 reshape_reshape.2
  7.5 0.7 constant_dynamic-slice_fusion.8
  8.2 0.3 copy.62
  8.6 0.3 bitcast_add_fusion.4
  8.9 0.3 constant_dynamic-slice_fusion.9
  9.3 1.0 collective-permute-done.3
  10.3 0.4 bitcast_add_fusion
  10.7 0.3 constant_dynamic-slice_fusion.5
  11.0 0.5 collective-permute-start.4
  11.6 2.6 %collective-permute-done.1 = f32[36864]{0:T(1024)S(1)} collective-permute-done((f32[36864]{0:T(1024)S(1)}, f32[36864]{0:T(1024)S(1)}, u32[]{:S(2)}, u32[]{:S(2)}) %collective-permute-start.1) | collective-permute-done | bytes 147488 | tf_op jit(solution)/shard_map/ppermute | solution.py:32
  14.3 1.1 %collective-permute-start.2 = (f32[36864]{0:T(1024)S(1)}, f32[36864]{0:T(1024)S(1)}, u32[]{:S(2)}, u32[]{:S(2)}) collective-permute-start(f32[36864]{0:T(1024)S(1)} %add.69), channel_id=1, source_target_pairs={{0,1},{1,0},{2,3},{3,2},{4,5},{5,4},{6,7},{7,6},{8,9},{9,8},{10,11... | collective-permute-start | bytes 442376 | tf_op jit(solution)/shard_map/ppermute | solution.py:132
  15.4 3.1 %collective-permute-done.4 = f32[49152]{0:T(1024)S(1)} collective-permute-done((f32[49152]{0:T(1024)S(1)}, f32[49152]{0:T(1024)S(1)}, u32[]{:S(2)}, u32[]{:S(2)}) %collective-permute-start.4) | collective-permute-done | bytes 196640 | tf_op jit(solution)/shard_map/ppermute | solution.py:32
  18.5 1.1 %collective-permute-start.5 = (f32[49152]{0:T(1024)S(1)}, f32[49152]{0:T(1024)S(1)}, u32[]{:S(2)}, u32[]{:S(2)}) collective-permute-start(f32[49152]{0:T(1024)S(1)} %add.71), channel_id=1, source_target_pairs={{0,1},{1,0},{2,3},{3,2},{4,5},{5,4},{6,7},{7,6},{8,9},{9,8},{10,11... | collective-permute-start | bytes 589832 | tf_op jit(solution)/shard_map/ppermute | solution.py:132
  19.7 1.8 %collective-permute-done.2 = f32[36864]{0:T(1024)S(1)} collective-permute-done((f32[36864]{0:T(1024)S(1)}, f32[36864]{0:T(1024)S(1)}, u32[]{:S(2)}, u32[]{:S(2)}) %collective-permute-start.2) | collective-permute-done | bytes 147488 | tf_op jit(solution)/shard_map/ppermute | solution.py:132
  21.9 2.9 %collective-permute-done.5 = f32[49152]{0:T(1024)S(1)} collective-permute-done((f32[49152]{0:T(1024)S(1)}, f32[49152]{0:T(1024)S(1)}, u32[]{:S(2)}, u32[]{:S(2)}) %collective-permute-start.5) | collective-permute-done | bytes 196640 | tf_op jit(solution)/shard_map/ppermute | solution.py:132
  25.1 1.6 %copy.31 = f32[32,1,5376]{2,1,0:T(1,128)} copy(f32[32,1,5376]{2,0,1:T(8,128)S(1)} %maximum_bitcast_fusion) | data formatting | bytes 1376256 | tf_op jit(solution)/shard_map/all_to_all | solution.py:140
  26.6 12.7 %all-to-all-start = ((f32[32,1,5376]{2,1,0:T(1,128)}), f32[32,1,5376]{2,1,0:T(1,128)S(1)}, u32[]{:S(2)}, u32[]{:S(2)}) async-start(f32[32,1,5376]{2,1,0:T(1,128)} %copy.31), calls=%async_computation | async-start | bytes 1376256 | tf_op jit(solution)/shard_map/all_to_all | solution.py:140
  39.4 1.2 %constant_dynamic-slice_fusion.1 = (f32[128,768]{1,0:T(8,128)S(1)}, f32[128,768]{1,0:T(8,128)S(1)}) fusion(f32[512,768]{1,0:T(8,128)} %refs_4_.3, s32[]{:T(128)S(6)} %select_n.147, f32[512,768]{1,0:T(8,128)} %refs_3_.3), kind=kLoop, calls=%fused_computation.39 | loop fusion | bytes 1572868 | tf_op jit(solution)/shard_map/dynamic_slice | solution.py:156
  40.9 1.1 %constant_dynamic-slice_fusion.3 = (f32[1,96,768]{2,1,0:T(8,128)S(1)}, f32[1,96,768]{2,1,0:T(8,128)S(1)}) fusion(f32[4,96,768]{2,1,0:T(8,128)} %refs_6_.1, s32[]{:T(128)S(6)} %select_n.146, f32[4,96,768]{2,1,0:T(8,128)} %refs_5_.1), kind=kLoop, calls=%fused_computation.41 | loop fusion | bytes 1179652 | tf_op jit(solution)/shard_map/jit(dynamic_index_in_dim)/dynamic_slice | solution.py:149
  42.3 15.6 %all-to-all-done = f32[32,1,5376]{2,1,0:T(1,128)S(1)} async-done(((f32[32,1,5376]{2,1,0:T(1,128)}), f32[32,1,5376]{2,1,0:T(1,128)S(1)}, u32[]{:S(2)}, u32[]{:S(2)}) %all-to-all-start) | async-done | bytes 688160 | tf_op jit(solution)/shard_map/all_to_all | solution.py:140
  58.3 0.3 div.33
  58.9 0.8 reshape.94
  59.7 6.3 %all-to-all-start.1 = ((bf16[32,2,2688]{2,1,0:T(2,128)(2,1)}), bf16[32,2,2688]{2,1,0:T(2,128)(2,1)S(1)}, u32[]{:S(2)}, u32[]{:S(2)}) async-start(bf16[32,2,2688]{2,1,0:T(2,128)(2,1)} %reshape.94), calls=%async_computation.1 | async-start | bytes 688128 | tf_op jit(solution)/shard_map/all_to_all | solution.py:161
  65.9 0.3 reshape.88.refs_1_
  66.4 2.1 %collective-permute-start.9 = (f32[32,24,128]{2,1,0:T(8,128)S(1)}, f32[32,24,128]{2,1,0:T(8,128)S(1)}, u32[]{:S(2)}, u32[]{:S(2)}) collective-permute-start(f32[32,24,128]{2,1,0:T(8,128)S(1)} %bitcast.106), channel_id=1, source_target_pairs={{0,64},{64,0},{128,192},{192,128},{1,65},{65,1},{129,193},{193,129... | collective-permute-start | bytes 1179656 | tf_op jit(solution)/shard_map/ppermute | solution.py:166
  68.6 6.3 %collective-permute-done.7.refs_3_ = f32[32,24,96]{2,1,0:T(8,128)S(1)} collective-permute-done((f32[32,24,96]{2,1,0:T(8,128)S(1)}, f32[32,24,96]{2,1,0:T(8,128)S(1)}, u32[]{:S(2)}, u32[]{:S(2)}) %collective-permute-start.7) | collective-permute-done | bytes 294944 | tf_op jit(solution)/shard_map/ppermute | solution.py:55
  74.9 0.3 collective-permute-start.13
  75.2 2.0 %all-to-all-done.1 = bf16[32,2,2688]{2,1,0:T(2,128)(2,1)S(1)} async-done(((bf16[32,2,2688]{2,1,0:T(2,128)(2,1)}), bf16[32,2,2688]{2,1,0:T(2,128)(2,1)S(1)}, u32[]{:S(2)}, u32[]{:S(2)}) %all-to-all-start.1) | async-done | bytes 344096 | tf_op jit(solution)/shard_map/all_to_all | solution.py:161
  77.3 4.4 %collective-permute-start.6 = (f32[32,24,96]{2,1,0:T(8,128)S(1)}, f32[32,24,96]{2,1,0:T(8,128)S(1)}, u32[]{:S(2)}, u32[]{:S(2)}) collective-permute-start(f32[32,24,96]{2,1,0:T(8,128)S(1)} %reshape.88.refs_1_), channel_id=1, source_target_pairs={{0,64},{64,0},{128,192},{192,128},{1,65},{65,1},{129,193},{193,129... | collective-permute-start | bytes 884744 | tf_op jit(solution)/shard_map/ppermute | solution.py:54
  81.9 0.4 collective-permute-start.10
  82.3 3.9 %collective-permute-done.11 = bf16[16,5376]{1,0:T(8,128)(2,1)S(1)} collective-permute-done((bf16[16,5376]{1,0:T(8,128)(2,1)S(1)}, bf16[16,5376]{1,0:T(8,128)(2,1)S(1)}, u32[]{:S(2)}, u32[]{:S(2)}) %collective-permute-start.11) | collective-permute-done | bytes 172064 | tf_op jit(solution)/shard_map/ppermute | solution.py:55
  86.2 3.9 %collective-permute-start.12 = (bf16[16,5376]{1,0:T(8,128)(2,1)S(1)}, bf16[16,5376]{1,0:T(8,128)(2,1)S(1)}, u32[]{:S(2)}, u32[]{:S(2)}) collective-permute-start(bf16[16,5376]{1,0:T(8,128)(2,1)S(1)} %collective-permute-done.11), channel_id=1, source_target_pairs={{0,64},{64,0},{128,192},{192,128},{1,65},{65,1},{129,193},{193,129... | collective-permute-start | bytes 516104 | tf_op jit(solution)/shard_map/ppermute | solution.py:56
  90.1 2.7 %shard_map.109 = (f32[512,768]{1,0:T(8,128)}, f32[512,768]{1,0:T(8,128)}) custom-call(s32[1]{0:T(128)} %bitcast.refs_0_, f32[32,24,128]{2,1,0:T(8,128)} %bitcast.108, f32[32,24,128]{2,1,0:T(8,128)} %copy-done.6, f32[512,768]{1,0:T(8,128)} %refs_3_.3, f32[512,768]{1,0:T(8,128)} %refs_4_.3), custom_call_target="tpu_custom_call" | custom-call | tf_op jit(solution)/shard_map/pallas_call | solution.py:99
  92.8 0.7 copy-done.7
  93.6 4.6 %shard_map.110 = (f32[4,96,768]{2,1,0:T(8,128)}, f32[4,96,768]{2,1,0:T(8,128)}) custom-call(s32[1]{0:T(128)} %bitcast.refs_0_, f32[32,24,96]{2,1,0:T(8,128)} %copy-done, f32[32,24,96]{2,1,0:T(8,128)} %copy-done.7, f32[32,24,96]{2,1,0:T(8,128)} %copy-done.5, f32[32,24,96]{2,1,0:T(8,128)} %collective-permute-done.8.refs_4_, f32[4,96,768]{2,1,0:T(8,128)} %refs_5_.1, ...), custom_call_target="tpu_custom_call" | custom-call | tf_op jit(solution)/shard_map/pallas_call | solution.py:99
  98.3 0.2 select_bitcast_fusion.3
  98.6 0.3 copy-done.3
  99.0 0.3 copy.37
  99.3 1.0 reshape.99
  100.4 0.6 reshape.96
  101.1 1.1 %reshape.97 = bf16[4,24,1536]{2,1,0:T(8,128)(2,1)} reshape(bf16[4,24,16,96]{3,2,1,0:T(8,128)(2,1)S(1)} %copy.36) | data formatting | bytes 589824 | tf_op jit(solution)/shard_map/reshape | solution.py:191
  102.2 0.8 copy-done.4
  102.9 2.7 %shard_map.111 = (f32[512,768]{1,0:T(8,128)}, f32[512,768]{1,0:T(8,128)}) custom-call(s32[1]{0:T(128)} %bitcast.refs_0_, f32[32,24,128]{2,1,0:T(8,128)} %copy-done.3, f32[32,24,128]{2,1,0:T(8,128)} %copy-done.4, f32[512,768]{1,0:T(8,128)} %refs_3_.3, f32[512,768]{1,0:T(8,128)} %refs_4_.3, ...), custom_call_target="tpu_custom_call", output_to_operand_aliasing={{0}: (5, {}), {1}: (6, {})} | custom-call | tf_op jit(solution)/shard_map/pallas_call | solution.py:99
  (60 shorter events, 3.1 us)
Async XLA Ops:
  0.6 5.8 %copy-start.2 = (f32[1,24,8192]{2,1,0:T(8,128)S(1)}, f32[1,24,8192]{2,1,0:T(8,128)}, u32[]{:S(2)}) copy-start(f32[1,24,8192]{2,1,0:T(8,128)} %param.7) | copy-start | bytes 2359300
  3.1 5.5 %collective-permute-start = (f32[2,36864]{1,0:T(2,128)S(1)}, f32[2,36864]{1,0:T(2,128)S(1)}, u32[]{:S(2)}, u32[]{:S(2)}) collective-permute-start(f32[2,36864]{1,0:T(2,128)S(1)} %bitcast.124), channel_id=1, source_target_pairs={{0,64},{64,0},{128,192},{192,128},{1,65},{65,1},{129,193},{193,129... | collective-permute-start | bytes 884744 | tf_op jit(solution)/shard_map/ppermute | solution.py:30
  8.5 1.8 %collective-permute-start.3 = (f32[2,49152]{1,0:T(2,128)S(1)}, f32[2,49152]{1,0:T(2,128)S(1)}, u32[]{:S(2)}, u32[]{:S(2)}) collective-permute-start(f32[2,49152]{1,0:T(2,128)S(1)} %bitcast.123), channel_id=1, source_target_pairs={{0,64},{64,0},{128,192},{192,128},{1,65},{65,1},{129,193},{193,129... | collective-permute-start | bytes 1179656 | tf_op jit(solution)/shard_map/ppermute | solution.py:30
  9.2 5.0 %collective-permute-start.1 = (f32[36864]{0:T(1024)S(1)}, f32[36864]{0:T(1024)S(1)}, u32[]{:S(2)}, u32[]{:S(2)}) collective-permute-start(f32[36864]{0:T(1024)S(1)} %bitcast.127), channel_id=1, source_target_pairs={{0,128},{64,192},{128,0},{192,64},{1,129},{65,193},{129,1},{193,65... | collective-permute-start | bytes 442376 | tf_op jit(solution)/shard_map/ppermute | solution.py:32
  11.0 7.4 %collective-permute-start.4 = (f32[49152]{0:T(1024)S(1)}, f32[49152]{0:T(1024)S(1)}, u32[]{:S(2)}, u32[]{:S(2)}) collective-permute-start(f32[49152]{0:T(1024)S(1)} %bitcast.126), channel_id=1, source_target_pairs={{0,128},{64,192},{128,0},{192,64},{1,129},{65,193},{129,1},{193,65... | collective-permute-start | bytes 589832 | tf_op jit(solution)/shard_map/ppermute | solution.py:32
  14.3 7.2 %collective-permute-start.2 = (f32[36864]{0:T(1024)S(1)}, f32[36864]{0:T(1024)S(1)}, u32[]{:S(2)}, u32[]{:S(2)}) collective-permute-start(f32[36864]{0:T(1024)S(1)} %add.69), channel_id=1, source_target_pairs={{0,1},{1,0},{2,3},{3,2},{4,5},{5,4},{6,7},{7,6},{8,9},{9,8},{10,11... | collective-permute-start | bytes 442376 | tf_op jit(solution)/shard_map/ppermute | solution.py:132
  18.5 6.3 %collective-permute-start.5 = (f32[49152]{0:T(1024)S(1)}, f32[49152]{0:T(1024)S(1)}, u32[]{:S(2)}, u32[]{:S(2)}) collective-permute-start(f32[49152]{0:T(1024)S(1)} %add.71), channel_id=1, source_target_pairs={{0,1},{1,0},{2,3},{3,2},{4,5},{5,4},{6,7},{7,6},{8,9},{9,8},{10,11... | collective-permute-start | bytes 589832 | tf_op jit(solution)/shard_map/ppermute | solution.py:132
  26.6 31.3 %all-to-all-start = ((f32[32,1,5376]{2,1,0:T(1,128)}), f32[32,1,5376]{2,1,0:T(1,128)S(1)}, u32[]{:S(2)}, u32[]{:S(2)}) async-start(f32[32,1,5376]{2,1,0:T(1,128)} %copy.31), calls=%async_computation | async-start | bytes 1376256 | tf_op jit(solution)/shard_map/all_to_all | solution.py:140
  59.7 17.5 %all-to-all-start.1 = ((bf16[32,2,2688]{2,1,0:T(2,128)(2,1)}), bf16[32,2,2688]{2,1,0:T(2,128)(2,1)S(1)}, u32[]{:S(2)}, u32[]{:S(2)}) async-start(bf16[32,2,2688]{2,1,0:T(2,128)(2,1)} %reshape.94), calls=%async_computation.1 | async-start | bytes 688128 | tf_op jit(solution)/shard_map/all_to_all | solution.py:161
  66.2 26.6 %copy-start = (f32[32,24,96]{2,1,0:T(8,128)}, f32[32,24,96]{2,1,0:T(8,128)S(1)}, u32[]{:S(2)}) copy-start(f32[32,24,96]{2,1,0:T(8,128)S(1)} %reshape.88.refs_1_) | copy-start | bytes 884740
  66.2 8.6 %collective-permute-start.7 = (f32[32,24,96]{2,1,0:T(8,128)S(1)}, f32[32,24,96]{2,1,0:T(8,128)S(1)}, u32[]{:S(2)}, u32[]{:S(2)}) collective-permute-start(f32[32,24,96]{2,1,0:T(8,128)S(1)} %reshape.88.refs_1_), channel_id=1, source_target_pairs={{0,128},{64,192},{128,0},{192,64},{1,129},{65,193},{129,1},{193,65... | collective-permute-start | bytes 884744 | tf_op jit(solution)/shard_map/ppermute | solution.py:55
  66.4 23.7 %copy-start.1 = (f32[4,8,24,128]{3,2,1,0:T(8,128)}, f32[4,8,24,128]{3,2,1,0:T(8,128)S(1)}, u32[]{:S(2)}) copy-start(f32[4,8,24,128]{3,2,1,0:T(8,128)S(1)} %copy.47) | copy-start | bytes 1179652
  66.4 15.5 %collective-permute-start.9 = (f32[32,24,128]{2,1,0:T(8,128)S(1)}, f32[32,24,128]{2,1,0:T(8,128)S(1)}, u32[]{:S(2)}, u32[]{:S(2)}) collective-permute-start(f32[32,24,128]{2,1,0:T(8,128)S(1)} %bitcast.106), channel_id=1, source_target_pairs={{0,64},{64,0},{128,192},{192,128},{1,65},{65,1},{129,193},{193,129... | collective-permute-start | bytes 1179656 | tf_op jit(solution)/shard_map/ppermute | solution.py:166
  74.9 17.9 %copy-start.5 = (f32[32,24,96]{2,1,0:T(8,128)}, f32[32,24,96]{2,1,0:T(8,128)S(1)}, u32[]{:S(2)}) copy-start(f32[32,24,96]{2,1,0:T(8,128)S(1)} %collective-permute-done.7.refs_3_) | copy-start | bytes 884740
  74.9 23.3 %collective-permute-start.13 = (f32[32,24,128]{2,1,0:T(8,128)S(1)}, f32[32,24,128]{2,1,0:T(8,128)S(1)}, u32[]{:S(2)}, u32[]{:S(2)}) collective-permute-start(f32[32,24,128]{2,1,0:T(8,128)S(1)} %bitcast.107), channel_id=1, source_target_pairs={{0,128},{64,192},{128,0},{192,64},{1,129},{65,193},{129,1},{193,65... | collective-permute-start | bytes 1179656 | tf_op jit(solution)/shard_map/ppermute | solution.py:168
  77.2 9.0 %collective-permute-start.11 = (bf16[16,5376]{1,0:T(8,128)(2,1)S(1)}, bf16[16,5376]{1,0:T(8,128)(2,1)S(1)}, u32[]{:S(2)}, u32[]{:S(2)}) collective-permute-start(bf16[16,5376]{1,0:T(8,128)(2,1)S(1)} %constant_dynamic-slice_fusion), channel_id=1, source_target_pairs={{0,128},{64,192},{128,0},{192,64},{1,129},{65,193},{129,1},{193,65... | collective-permute-start | bytes 516104 | tf_op jit(solution)/shard_map/ppermute | solution.py:55
  77.3 15.5 %collective-permute-start.6 = (f32[32,24,96]{2,1,0:T(8,128)S(1)}, f32[32,24,96]{2,1,0:T(8,128)S(1)}, u32[]{:S(2)}, u32[]{:S(2)}) collective-permute-start(f32[32,24,96]{2,1,0:T(8,128)S(1)} %reshape.88.refs_1_), channel_id=1, source_target_pairs={{0,64},{64,0},{128,192},{192,128},{1,65},{65,1},{129,193},{193,129... | collective-permute-start | bytes 884744 | tf_op jit(solution)/shard_map/ppermute | solution.py:54
  81.8 11.0 %collective-permute-start.8 = (f32[32,24,96]{2,1,0:T(8,128)S(1)}, f32[32,24,96]{2,1,0:T(8,128)}, u32[]{:S(2)}, u32[]{:S(2)}) collective-permute-start(f32[32,24,96]{2,1,0:T(8,128)S(1)} %collective-permute-done.7.refs_3_), channel_id=1, source_target_pairs={{0,64},{64,0},{128,192},{192,128},{1,65},{65,1},{129,193},{193,129... | collective-permute-start | bytes 884744 | tf_op jit(solution)/shard_map/ppermute | solution.py:56
  81.9 8.2 %copy-start.6 = (f32[32,24,128]{2,1,0:T(8,128)}, f32[32,24,128]{2,1,0:T(8,128)S(1)}, u32[]{:S(2)}) copy-start(f32[32,24,128]{2,1,0:T(8,128)S(1)} %collective-permute-done.9.refs_2_) | copy-start | bytes 1179652
  81.9 16.4 %collective-permute-start.10 = (bf16[16,5376]{1,0:T(8,128)(2,1)S(1)}, bf16[16,5376]{1,0:T(8,128)(2,1)S(1)}, u32[]{:S(2)}, u32[]{:S(2)}) collective-permute-start(bf16[16,5376]{1,0:T(8,128)(2,1)S(1)} %constant_dynamic-slice_fusion), channel_id=1, source_target_pairs={{0,64},{64,0},{128,192},{192,128},{1,65},{65,1},{129,193},{193,129... | collective-permute-start | bytes 516104 | tf_op jit(solution)/shard_map/ppermute | solution.py:54
  86.2 12.1 %collective-permute-start.12 = (bf16[16,5376]{1,0:T(8,128)(2,1)S(1)}, bf16[16,5376]{1,0:T(8,128)(2,1)S(1)}, u32[]{:S(2)}, u32[]{:S(2)}) collective-permute-start(bf16[16,5376]{1,0:T(8,128)(2,1)S(1)} %collective-permute-done.11), channel_id=1, source_target_pairs={{0,64},{64,0},{128,192},{192,128},{1,65},{65,1},{129,193},{193,129... | collective-permute-start | bytes 516104 | tf_op jit(solution)/shard_map/ppermute | solution.py:56
  92.8 0.8 copy-start.7
  98.2 0.8 copy-start.3
  98.2 4.0 %collective-permute-start.14 = (f32[32,24,128]{2,1,0:T(8,128)S(1)}, f32[32,24,128]{2,1,0:T(8,128)S(1)}, u32[]{:S(2)}, u32[]{:S(2)}) collective-permute-start(f32[32,24,128]{2,1,0:T(8,128)S(1)} %collective-permute-done.13.refs_1_), channel_id=1, source_target_pairs={{0,64},{64,0},{128,192},{192,128},{1,65},{65,1},{129,193},{193,129... | collective-permute-start | bytes 1179656 | tf_op jit(solution)/shard_map/ppermute | solution.py:169
  102.2 0.8 copy-start.4
